TPU v7x, 256 devices: a whole 4x4x8 slice. The times are simulated.
256 devices in a mesh: ctx: 16 (over x, z_hi, core), tp: 16 (over y, z_lo).
Axes of the slice: x: 4, y: 4, z: 8 (z_hi: 2, z_lo: 4; z = z_hi * 4 + z_lo), core: 2. Of those that a mesh axis runs over, the one named last changes fastest.
Arguments:
- inputs: bfloat16 [4096, 8192], P('tp', 'ctx'), may hold values from -6 to 6
- gates: bfloat16 [4096, 8192], P('tp', 'ctx'), may hold values from -6 to 6
- filters: bfloat16 [4096, 8192], P('tp', 'ctx'), may hold values from -6 to 6
- out_grad: bfloat16 [4096, 8192], P('tp', 'ctx'), may hold values from -6 to 6
- out_weight: bfloat16 [4096, 4096], P('ctx', 'tp'), may hold values from -0.09375 to 0.09375
Outputs:
- input_grad: bfloat16 [4096, 8192], P('tp', 'ctx')
- gate_grad: bfloat16 [4096, 8192], P('tp', 'ctx')
- filter_grad: bfloat16 [4096, 8192], P('tp', 'ctx')
- weight_grad: bfloat16 [4096, 4096], P('ctx', 'tp')
All inputs are finite; a program needn't handle non-finite values.
Results may differ from a plain program's by a relative error of at most 0.019.
Values may be sent and summed in bfloat16 or wider, within the bound.
No kernel may reach another device: no remote copies, remote signals or barrier semaphores. Data moves between devices by JAX's collectives and lax.ppermute only.
A program may use at most 128 MiB of HBM per device.

v0:
```python
import math

import jax
import jax.numpy as jnp
from jax import lax
from jax.sharding import PartitionSpec as P

HIGHEST = lax.Precision.HIGHEST


def dft_matrix(length_n, sign):
    positions = jnp.arange(length_n, dtype=jnp.int32)
    angles = (positions[:, None] * positions[None, :] % length_n).astype(jnp.float32) * (
        2.0 * math.pi / length_n
    )
    return (jnp.cos(angles), sign * jnp.sin(angles))


def twiddle_matrix(radix_len, rest_len, sign):
    row_ids = jnp.arange(radix_len, dtype=jnp.int32)
    col_ids = jnp.arange(rest_len, dtype=jnp.int32)
    angles = (row_ids[:, None] * col_ids[None, :] % (radix_len * rest_len)).astype(jnp.float32)
    angles = angles * (2.0 * math.pi / (radix_len * rest_len))
    return (jnp.cos(angles), sign * jnp.sin(angles))


def mix_rows(matrix, operand):
    return jnp.einsum("kr,...rm->...km", matrix, operand, precision=HIGHEST)


def mix_last(matrix, operand):
    return jnp.einsum("...r,kr->...k", operand, matrix, precision=HIGHEST)


def split_radix(length_n):
    if length_n <= 128 or length_n % 128 != 0:
        return length_n
    return min(32, length_n // 128)


def complex_mix(mixer, cos_part, sin_part, real_part, imag_part):
    if imag_part is None:
        return (mixer(cos_part, real_part), mixer(sin_part, real_part))
    return (
        mixer(cos_part, real_part) - mixer(sin_part, imag_part),
        mixer(cos_part, imag_part) + mixer(sin_part, real_part),
    )


def forward(real_part, imag_part):
    length_n = real_part.shape[-1]
    lead_shape = real_part.shape[:-1]
    radix_len = split_radix(length_n)
    cos_part, sin_part = dft_matrix(radix_len, -1.0)
    if radix_len == length_n:
        return complex_mix(mix_last, cos_part, sin_part, real_part, imag_part)
    rest_len = length_n // radix_len
    new_shape = lead_shape + (radix_len, rest_len)
    real_part = real_part.reshape(new_shape)
    imag_part = None if imag_part is None else imag_part.reshape(new_shape)
    out_re, out_im = complex_mix(mix_rows, cos_part, sin_part, real_part, imag_part)
    turn_re, turn_im = twiddle_matrix(radix_len, rest_len, -1.0)
    deep_re, deep_im = forward(
        out_re * turn_re - out_im * turn_im, out_re * turn_im + out_im * turn_re
    )
    return (deep_re.reshape(lead_shape + (length_n,)), deep_im.reshape(lead_shape + (length_n,)))


def inverse(real_part, imag_part):
    length_n = real_part.shape[-1]
    lead_shape = real_part.shape[:-1]
    radix_len = split_radix(length_n)
    cos_part, sin_part = dft_matrix(radix_len, 1.0)
    if radix_len == length_n:
        return complex_mix(mix_last, cos_part, sin_part, real_part, imag_part)
    rest_len = length_n // radix_len
    new_shape = lead_shape + (radix_len, rest_len)
    inner_re, inner_im = inverse(real_part.reshape(new_shape), imag_part.reshape(new_shape))
    turn_re, turn_im = twiddle_matrix(radix_len, rest_len, 1.0)
    turned_re = inner_re * turn_re - inner_im * turn_im
    turned_im = inner_re * turn_im + inner_im * turn_re
    out_re, out_im = complex_mix(mix_rows, cos_part, sin_part, turned_re, turned_im)
    return (out_re.reshape(lead_shape + (length_n,)), out_im.reshape(lead_shape + (length_n,)))


def spectrum(operand):
    widened = jnp.concatenate(
        [operand.astype(jnp.float32), jnp.zeros(operand.shape, jnp.float32)], axis=1
    )
    return forward(widened, None)


def back_to_time(real_part, imag_part, length):
    time_re, _ = inverse(real_part, imag_part)
    factor = length ** (-0.5) / (2.0 * length)
    return (time_re[:, :length] * factor).astype(jnp.bfloat16)


def conv_forward(input_spec, filter_spec, length):
    in_re, in_im = input_spec
    fil_re, fil_im = filter_spec
    return back_to_time(in_re * fil_re - in_im * fil_im, in_re * fil_im + in_im * fil_re, length)


def correlate(product_spec, other_spec, length):
    pro_re, pro_im = product_spec
    oth_re, oth_im = other_spec
    return back_to_time(
        pro_re * oth_re + pro_im * oth_im, pro_im * oth_re - pro_re * oth_im, length
    )


def on_device(inputs, gates, filters, out_grad, out_weight):
    tokens_here = inputs.shape[1]
    seq_len = tokens_here * lax.axis_size("ctx")
    weight_cols = lax.all_gather(out_weight, "ctx", axis=0, tiled=True)
    dims_t = (((0,), (0,)), ((), ()))
    dout_full = lax.all_gather(out_grad, "tp", axis=0, tiled=True)
    slope_f = lax.dot_general(weight_cols, dout_full, dims_t, preferred_element_type=jnp.float32)
    slope = slope_f.astype(jnp.bfloat16)
    input_chan, filter_chan = (
        lax.all_to_all(inputs, "ctx", split_axis=0, concat_axis=1, tiled=True),
        lax.all_to_all(filters, "ctx", split_axis=0, concat_axis=1, tiled=True),
    )
    input_spec = spectrum(input_chan)
    filter_spec = spectrum(filter_chan)
    mixed_chan = conv_forward(input_spec, filter_spec, seq_len)
    mixed = lax.all_to_all(mixed_chan, "ctx", split_axis=1, concat_axis=0, tiled=True)
    mixed_f = mixed.astype(jnp.float32)
    gates_f = gates.astype(jnp.float32)
    slope_w = slope.astype(jnp.float32)
    gated_out = (gates_f * mixed_f).astype(jnp.bfloat16)
    gate_grad = (slope_w * mixed_f).astype(jnp.bfloat16)
    product = (slope_w * gates_f).astype(jnp.bfloat16)
    product_chan = lax.all_to_all(product, "ctx", split_axis=0, concat_axis=1, tiled=True)
    product_spec = spectrum(product_chan)
    dinput_chan = correlate(product_spec, filter_spec, seq_len)
    dfilter_chan = correlate(product_spec, input_spec, seq_len)
    input_grad, filter_grad = (
        lax.all_to_all(dinput_chan, "ctx", split_axis=1, concat_axis=0, tiled=True),
        lax.all_to_all(dfilter_chan, "ctx", split_axis=1, concat_axis=0, tiled=True),
    )
    weight_scale = seq_len ** (-0.5)
    dims_n = (((1,), (1,)), ((), ()))
    weight_grad = lax.psum_scatter(
        (
            lax.dot_general(dout_full, gated_out, dims_n, preferred_element_type=jnp.float32)
            * weight_scale
        ).astype(jnp.bfloat16),
        "ctx",
        scatter_dimension=0,
        tiled=True,
    )
    return (input_grad, gate_grad, filter_grad, weight_grad)


def solution(mesh):
    in_specs = (P("tp", "ctx"), P("tp", "ctx"), P("tp", "ctx"), P("tp", "ctx"), P("ctx", "tp"))
    out_specs = (P("tp", "ctx"), P("tp", "ctx"), P("tp", "ctx"), P("ctx", "tp"))
    return jax.shard_map(
        on_device, mesh=mesh, in_specs=in_specs, out_specs=out_specs, check_vma=False
    )
```

profile of v0, /device:TPU:8, one launch (start us, length us, event | category | flops | bytes accessed | tf_op | source)
XLA Modules:
  0.0 476.1 jit_solution(17296696927362269976)
XLA Ops:
  8.7 23.1 %all_to_all.90 = bf16[16,16,512]{2,1,0:T(8,128)(2,1)S(1)} all-to-all(bf16[16,16,512]{2,1,0:T(8,128)(2,1)} %bitcast.309), channel_id=1, replica_groups=mesh['ctx'=16,'tp'=16] {'ctx'}, dimensions={0} | all-to-all | bytes 524288 | tf_op jit(solution)/shard_map/all_to_all | solution.py:122
  31.8 3.5 all-to-all-start.1
  36.8 10.5 %all-to-all-done.1 = bf16[16,16,512]{2,1,0:T(8,128)(2,1)S(1)} async-done(((bf16[16,16,512]{2,1,0:T(8,128)(2,1)}), bf16[16,16,512]{2,1,0:T(8,128)(2,1)S(1)}, u32[]{:S(2)}, u32[]{:S(2)}) %all-to-all-start.1) | async-done | bytes 262176 | tf_op jit(solution)/shard_map/all_to_all | solution.py:123
  48.3 29.8 %all-gather.3.cloned.1.call-done = bf16[4096,256]{1,0:T(8,128)(2,1)} async-done(((bf16[256,256]{1,0:T(8,128)(2,1)}), bf16[4096,256]{1,0:T(8,128)(2,1)}) %all-gather.3.cloned.1.call-update) | async-done | bytes 2097168 | tf_op jit(solution)/shard_map/all_gather | solution.py:116
  78.0 97.2 %all-gather.5.cloned.1.call-done = bf16[4096,512]{1,0:T(8,128)(2,1)} async-done(((bf16[256,512]{1,0:T(8,128)(2,1)}), bf16[4096,512]{1,0:T(8,128)(2,1)}) %all-gather.5.cloned.1.call-update) | async-done | bytes 4194320 | tf_op jit(solution)/shard_map/all_gather | solution.py:118
  175.3 5.0 %fusion.54 = (bf16[256,512]{1,0:T(8,128)(2,1)}, f32[256,512]{1,0:T(8,128)}) fusion(bf16[256,512]{1,0:T(8,128)(2,1)S(1)} %copy-done.10, bf16[4096,256]{1,0:T(8,128)(2,1)} %all-gather.3.cloned.1.call-done, bf16[4096,512]{1,0:T(8,128)(2,1)} %all-gather.5.cloned.1.call-done), kind=kOutput, calls=%fused_computation.115 | convolution fusion | flops 1074397184 | bytes 7340032 | tf_op jit(solution)/shard_map/dot_general | solution.py:119
  180.2 7.5 %all-to-all-start = ((bf16[16,16,512]{2,1,0:T(8,128)(2,1)}), bf16[16,16,512]{2,1,0:T(8,128)(2,1)S(1)}, u32[]{:S(2)}, u32[]{:S(2)}) async-start(bf16[16,16,512]{2,1,0:T(8,128)(2,1)} %bitcast), calls=%async_computation | async-start | bytes 524288 | tf_op jit(solution)/shard_map/all_to_all | solution.py:135
  188.5 1.7 convolution_bitcast_fusion.1
  190.2 9.5 %all-to-all-done = bf16[16,16,512]{2,1,0:T(8,128)(2,1)S(1)} async-done(((bf16[16,16,512]{2,1,0:T(8,128)(2,1)}), bf16[16,16,512]{2,1,0:T(8,128)(2,1)S(1)}, u32[]{:S(2)}, u32[]{:S(2)}) %all-to-all-start) | async-done | bytes 262176 | tf_op jit(solution)/shard_map/all_to_all | solution.py:135
  201.3 4.5 multiply_subtract_fusion.5
  205.8 1.7 reshape.195
  207.4 2.9 fusion.234
  210.7 1.9 fusion.232
  212.6 3.2 fusion.11
  215.9 3.5 fusion.10
  219.3 1.6 reshape.191
  220.9 3.0 fusion.238
  223.9 1.6 reshape.192
  225.4 1.9 fusion.236
  227.4 4.2 fusion.13
  231.6 3.1 fusion.12
  234.7 1.6 reshape.202
  236.3 3.1 fusion.226
  239.4 1.6 reshape.203
  241.0 1.9 fusion.224
  243.0 3.2 fusion.7
  246.2 3.7 multiply_subtract_fusion.4
  261.0 1.7 convolution_subtract_fusion.10
  263.9 1.8 multiply_add_fusion.1
  266.9 1.2 fusion.82
  273.1 1.4 fusion.106
  280.8 13.6 %multiply_subtract_fusion = (f32[16,32,4,128]{3,2,1,0:T(4,128)S(1)}, f32[16,32,4,128]{3,2,1,0:T(4,128)S(1)}, f32[16,32,4,128]{3,2,1,0:T(4,128)}, f32[16,32,4,128...) fusion(f32[4,128]{1,0:T(4,128)S(1)} %fusion.240, ...), kind=kLoop, calls=%fused_computation.58 | loop fusion | flops 6291456 | bytes 18878464 | tf_op jit(solution)/shard_map/sub | solution.py:80
  295.3 1.9 fusion.218
  297.3 3.0 fusion.216
  300.3 3.1 fusion.3
  303.4 2.6 reshape.207
  306.0 4.6 fusion.2
  310.5 2.6 reshape.208
  313.2 2.8 fusion.18
  316.0 2.9 convolution_subtract_fusion
  320.5 1.9 fusion.222
  322.4 2.9 fusion.220
  325.3 3.0 fusion.5
  328.4 2.7 reshape.204
  331.0 4.2 fusion.4
  335.2 2.7 reshape.205
  337.9 2.8 fusion.25
  340.7 2.5 convolution_subtract_fusion.2
  344.9 3.5 all-to-all-start.4
  348.4 1.9 fusion.230
  350.3 3.0 fusion.9
  353.3 1.6 reshape.197
  355.0 2.9 fusion.228
  357.9 2.5 all-to-all-done.4
  361.1 7.0 %all-to-all-start.5 = ((bf16[16,16,512]{2,0,1:T(8,128)(2,1)}), bf16[16,16,512]{2,0,1:T(8,128)(2,1)S(1)}, u32[]{:S(2)}, u32[]{:S(2)}) async-start(bf16[16,16,512]{2,0,1:T(8,128)(2,1)} %bitcast.280), calls=%async_computation.5 | async-start | bytes 524288 | tf_op jit(solution)/shard_map/all_to_all | solution.py:141
  368.5 2.0 fusion.55
  370.5 5.0 %fusion.1 = bf16[4096,256]{0,1:T(8,128)(2,1)} fusion(bf16[256,512]{1,0:T(8,128)(2,1)S(1)} %get-tuple-element.44, bf16[4096,512]{1,0:T(8,128)(2,1)} %all-gather.5.cloned.1.call-done), kind=kOutput, calls=%fused_computation.2 | convolution fusion | flops 1075838976 | bytes 6553600 | tf_op jit(solution)/shard_map/dot_general | solution.py:147
  375.5 3.0 fusion.8
  378.5 1.6 reshape.198
  381.4 1.3 convolution_subtract_fusion.6
  384.1 9.6 %all-to-all-start.2 = ((bf16[16,16,512]{2,0,1:T(8,128)(2,1)}), bf16[16,16,512]{2,0,1:T(8,128)(2,1)S(1)}, u32[]{:S(2)}, u32[]{:S(2)}) async-start(bf16[16,16,512]{2,0,1:T(8,128)(2,1)} %bitcast.282), calls=%async_computation.2 | async-start | bytes 524288 | tf_op jit(solution)/shard_map/all_to_all | solution.py:140
  393.7 12.1 %all-to-all-done.2 = bf16[16,16,512]{2,0,1:T(8,128)(2,1)S(1)} async-done(((bf16[16,16,512]{2,0,1:T(8,128)(2,1)}), bf16[16,16,512]{2,0,1:T(8,128)(2,1)S(1)}, u32[]{:S(2)}, u32[]{:S(2)}) %all-to-all-start.2) | async-done | bytes 262176 | tf_op jit(solution)/shard_map/all_to_all | solution.py:140
  405.8 60.5 %reduce-scatter.2.cloned.1.call-done = bf16[256,256]{0,1:T(8,128)(2,1)} async-done(((bf16[4096,256]{0,1:T(8,128)(2,1)}), bf16[256,256]{0,1:T(8,128)(2,1)}) %reduce-scatter.2.cloned.1.call-update) | async-done | bytes 131088 | tf_op jit(solution)/shard_map/reduce_scatter | solution.py:145
  466.2 1.7 copy.99
  (79 shorter events, 40.2 us)
Async XLA Ops:
  7.2 168.1 %copy-start.10 = (bf16[256,512]{1,0:T(8,128)(2,1)S(1)}, bf16[256,512]{1,0:T(8,128)(2,1)}, u32[]{:S(2)}) copy-start(bf16[256,512]{1,0:T(8,128)(2,1)} %param.6) | copy-start | bytes 786436
  7.2 70.9 %all-gather.3.cloned.1.call-start = ((), (), s32[]{:S(2)}) async-start(), calls=%async_computation.7 | async-start | bytes 2228224 | tf_op jit(solution)/shard_map/all_gather | solution.py:116
  7.9 167.4 %all-gather.5.cloned.1.call-start = ((), (), s32[]{:S(2)}) async-start(), calls=%async_computation.8 | async-start | bytes 4456448 | tf_op jit(solution)/shard_map/all_gather | solution.py:118
  31.8 15.6 %all-to-all-start.1 = ((bf16[16,16,512]{2,1,0:T(8,128)(2,1)}), bf16[16,16,512]{2,1,0:T(8,128)(2,1)S(1)}, u32[]{:S(2)}, u32[]{:S(2)}) async-start(bf16[16,16,512]{2,1,0:T(8,128)(2,1)} %bitcast.310), calls=%async_computation.1 | async-start | bytes 524288 | tf_op jit(solution)/shard_map/all_to_all | solution.py:123
  180.2 19.4 %all-to-all-start = ((bf16[16,16,512]{2,1,0:T(8,128)(2,1)}), bf16[16,16,512]{2,1,0:T(8,128)(2,1)S(1)}, u32[]{:S(2)}, u32[]{:S(2)}) async-start(bf16[16,16,512]{2,1,0:T(8,128)(2,1)} %bitcast), calls=%async_computation | async-start | bytes 524288 | tf_op jit(solution)/shard_map/all_to_all | solution.py:135
  199.7 1.6 copy-start.7
  205.8 4.6 copy-start.8
  241.0 5.2 %copy-start.3 = (f32[16,32,4,128]{3,2,1,0:T(4,128)S(1)}, f32[16,32,4,128]{3,2,1,0:T(4,128)}, u32[]{:S(2)}) copy-start(f32[16,32,4,128]{3,2,1,0:T(4,128)} %fusion.10) | copy-start | bytes 3145732
  241.0 5.2 %copy-start.4 = (f32[16,32,4,128]{3,2,1,0:T(4,128)S(1)}, f32[16,32,4,128]{3,2,1,0:T(4,128)}, u32[]{:S(2)}) copy-start(f32[16,32,4,128]{3,2,1,0:T(4,128)} %fusion.13) | copy-start | bytes 3145732
  241.0 5.2 %copy-start.5 = (f32[16,32,4,128]{3,2,1,0:T(4,128)S(1)}, f32[16,32,4,128]{3,2,1,0:T(4,128)}, u32[]{:S(2)}) copy-start(f32[16,32,4,128]{3,2,1,0:T(4,128)} %fusion.12) | copy-start | bytes 3145732
  294.3 1.0 copy-start.1
  315.9 6.5 %copy-start = (f32[16,32,4,128]{3,2,1,0:T(4,128)S(1)}, f32[16,32,4,128]{3,2,1,0:T(4,128)}, u32[]{:S(2)}) copy-start(f32[16,32,4,128]{3,2,1,0:T(4,128)} %get-tuple-element.50) | copy-start | bytes 3145732
  335.2 5.5 %copy-start.2 = (f32[16,32,512]{2,1,0:T(8,128)S(1)}, f32[16,32,512]{2,1,0:T(8,128)}, u32[]{:S(2)}) copy-start(f32[16,32,512]{2,1,0:T(8,128)} %reshape.204) | copy-start | bytes 3145732
  344.9 15.6 %all-to-all-start.4 = ((bf16[16,16,512]{2,0,1:T(8,128)(2,1)}), bf16[16,16,512]{2,0,1:T(8,128)(2,1)S(1)}, u32[]{:S(2)}, u32[]{:S(2)}) async-start(bf16[16,16,512]{2,0,1:T(8,128)(2,1)} %bitcast.281), calls=%async_computation.4 | async-start | bytes 524288 | tf_op jit(solution)/shard_map/all_to_all | solution.py:128
  360.4 0.7 copy-start.9
  361.1 22.9 %all-to-all-start.5 = ((bf16[16,16,512]{2,0,1:T(8,128)(2,1)}), bf16[16,16,512]{2,0,1:T(8,128)(2,1)S(1)}, u32[]{:S(2)}, u32[]{:S(2)}) async-start(bf16[16,16,512]{2,0,1:T(8,128)(2,1)} %bitcast.280), calls=%async_computation.5 | async-start | bytes 524288 | tf_op jit(solution)/shard_map/all_to_all | solution.py:141
  368.2 98.1 %reduce-scatter.2.cloned.1.call-start = ((), (), s32[]{:S(2)}) async-start(), calls=%async_computation.9 | async-start | bytes 2228224 | tf_op jit(solution)/shard_map/reduce_scatter | solution.py:145
  370.5 5.0 %copy-start.6 = (f32[16,32,128,4]{2,3,1,0:T(4,128)S(1)}, f32[16,32,128,4]{2,3,1,0:T(4,128)}, u32[]{:S(2)}) copy-start(f32[16,32,128,4]{2,3,1,0:T(4,128)} %fusion.228) | copy-start | bytes 3145732
  384.1 21.7 %all-to-all-start.2 = ((bf16[16,16,512]{2,0,1:T(8,128)(2,1)}), bf16[16,16,512]{2,0,1:T(8,128)(2,1)S(1)}, u32[]{:S(2)}, u32[]{:S(2)}) async-start(bf16[16,16,512]{2,0,1:T(8,128)(2,1)} %bitcast.282), calls=%async_computation.2 | async-start | bytes 524288 | tf_op jit(solution)/shard_map/all_to_all | solution.py:140
Sparse Core Ops, SparseCore 0:
  10.7 67.2 all-gather.2
  79.8 95.4 all-gather.4
  375.6 90.5 reduce-scatter.1
where the time goes:
time: 481 us; the launch traced here: 476 us
  waiting for transfers between devices  224 us (47%)
  matrix products  134 us (28%)
  local copies, waits for them, and re-layouts  32 us (7%)
  starting transfers between devices  31.6 us (7%)
  blocking collectives  23.1 us (5%)
  other arithmetic  17 us (4%)
  between operations  14.7 us (3%)
    all_gather x1, waiting for transfers between devices, on_device(): dout_full = lax.all_gather(out_grad, 'tp', axis=0, tiled=True)  97.2 us
    dot_general x36, matrix products, mix_rows(): return jnp.einsum('kr,...rm->...km', matrix, operand, precision=HIGHEST)  93.6 us
    reduce_scatter x1, waiting for transfers between devices, on_device(): lax.psum_scatter((lax.dot_general(dout_full, gated_out, dims_n, preferred...  60.5 us
    dot_general x24, matrix products, mix_last(): return jnp.einsum('...r,kr->...k', operand, matrix, precision=HIGHEST)  30.6 us
    all_gather x1, waiting for transfers between devices, on_device(): weight_cols = lax.all_gather(out_weight, 'ctx', axis=0, tiled=True)  29.8 us
    all_to_all x1, blocking collectives, on_device(): lax.all_to_all(inputs, 'ctx', split_axis=0, concat_axis=1, tiled=True)  23.1 us
    sub x1, other arithmetic, inverse(): turned_re = inner_re * turn_re - inner_im * turn_im  13.6 us
    all_to_all x1, waiting for transfers between devices, on_device(): lax.all_to_all(dinput_chan, 'ctx', split_axis=1, concat_axis=0, tiled=True)  12.1 us
  transfers between devices with their start and end apart: 8, of which 7 were waited for; matrix products, arithmetic and copies ran while one was open for 6% of the time, Pallas kernels for 0%

commit v1 on v0

v1 whole, which is shorter than its diff:
```python
import functools

import jax
import jax.numpy as jnp
import ml_dtypes
import numpy as np
from jax import lax
from jax.experimental import pallas as pl
from jax.experimental.pallas import tpu as pltpu
from jax.sharding import PartitionSpec as P

CH = 256
TOK = 512
FEW = 16
SEQ = 8192
ROWS = 64
LANES = 128
GROUP = 4
BF = jnp.bfloat16
F32 = jnp.float32


def shift_pairs(stride, size, by):
    pairs = []
    for i in range(16):
        at = (i // stride) % size
        pairs.append((i, i + ((at + by) % size - at) * stride))
    return pairs


def send(value, axis, stride, size, by):
    return lax.ppermute(value, axis, shift_pairs(stride, size, by))


def split_hi_lo(matrix):
    hi = matrix.astype(ml_dtypes.bfloat16)
    lo = (matrix - hi.astype(np.float64)).astype(ml_dtypes.bfloat16)
    return hi, lo


@functools.cache
def constants():
    n1 = np.arange(ROWS)
    k1 = np.arange(ROWS)
    n2 = np.arange(LANES)
    k2 = np.arange(LANES)
    first = np.exp(-2j * np.pi * np.outer(k1 + 0.25, n1) / ROWS)
    turn = np.exp(-2j * np.pi * np.outer(k1 + 0.25, n2) / SEQ)
    second = np.exp(-2j * np.pi * np.outer(n2, k2) / LANES)
    lhs = np.concatenate([first.real, first.imag], axis=0)
    hi, lo = split_hi_lo(lhs)
    first_c = np.concatenate([hi, lo], axis=1)

    def square(m):
        full = np.block([[m.real, m.imag], [-m.imag, m.real]])
        hi, lo = split_hi_lo(full)
        return np.concatenate([hi, hi, lo], axis=0)

    second_c = square(second)
    back_c = square(np.conj(second))
    scale = SEQ**-0.5 / SEQ
    last = np.conj(first).T * scale
    hi, lo = split_hi_lo(np.concatenate([last.real, -last.imag], axis=1))
    last_c = np.concatenate([hi, lo, hi], axis=1)
    turn_c = np.stack([turn.real, turn.imag]).astype(np.float32)
    return first_c, second_c, back_c, last_c, turn_c


def hi_lo(value):
    hi = value.astype(BF)
    lo = (value - hi.astype(F32)).astype(BF)
    return hi, lo


def dot(a, b):
    return jnp.dot(a, b, preferred_element_type=F32)


def spread(load, rows_ref):
    for s in range(16):
        block = load(s).astype(F32)
        for q in range(4):
            rows_ref[pl.ds((4 * s + q) * FEW, FEW), :] = block[:, q * LANES : (q + 1) * LANES]


def collect(rows_ref, store):
    for s in range(16):
        parts = [rows_ref[pl.ds((4 * s + q) * FEW, FEW), :] for q in range(4)]
        store(s, jnp.concatenate(parts, axis=1).astype(BF))


def forward_group(rows_ref, base, first_ref, second_ref, turn_ref):
    turn_re = turn_ref[0]
    turn_im = turn_ref[1]
    pieces = []
    for c in range(0, GROUP, 2):
        pair = [rows_ref[pl.ds(base + c + i, ROWS, stride=FEW), :].astype(BF) for i in range(2)]
        both = jnp.concatenate(pair, axis=1)
        out = dot(first_ref[...], jnp.concatenate([both, both], axis=0))
        for i in range(2):
            re = out[:ROWS, i * LANES : (i + 1) * LANES]
            im = out[ROWS:, i * LANES : (i + 1) * LANES]
            pieces.append(
                jnp.concatenate([re * turn_re - im * turn_im, re * turn_im + im * turn_re], axis=1)
            )
    hi, lo = hi_lo(jnp.concatenate(pieces, axis=0))
    spec = dot(jnp.concatenate([hi, lo, hi], axis=1), second_ref[...])
    return spec[:, :LANES], spec[:, LANES:]


def inverse_group(re, im, base, rows_ref, back_ref, last_ref, turn_ref):
    turn_re = turn_ref[0]
    turn_im = turn_ref[1]
    hi, lo = hi_lo(jnp.concatenate([re, im], axis=1))
    out = dot(jnp.concatenate([hi, lo, hi], axis=1), back_ref[...])
    for c in range(0, GROUP, 2):
        cols = []
        for i in range(2):
            d = out[(c + i) * ROWS : (c + i + 1) * ROWS]
            d_re, d_im = d[:, :LANES], d[:, LANES:]
            cols.append(
                jnp.concatenate([d_re * turn_re + d_im * turn_im, d_im * turn_re - d_re * turn_im], axis=0)
            )
        hi, lo = hi_lo(jnp.concatenate(cols, axis=1))
        time = dot(last_ref[...], jnp.concatenate([hi, hi, lo], axis=0))
        for i in range(2):
            rows_ref[pl.ds(base + c + i, ROWS, stride=FEW), :] = time[:, i * LANES : (i + 1) * LANES]


def conv_kernel(xf_ref, first_ref, second_ref, back_ref, last_ref, turn_ref, mixed_ref, spec_ref, x_rows, f_rows, m_rows):
    spread(lambda s: xf_ref[s, :FEW], x_rows)
    spread(lambda s: xf_ref[s, FEW:], f_rows)
    for base in range(0, FEW, GROUP):
        x_re, x_im = forward_group(x_rows, base, first_ref, second_ref, turn_ref)
        f_re, f_im = forward_group(f_rows, base, first_ref, second_ref, turn_ref)
        here = pl.ds(base * ROWS, GROUP * ROWS)
        spec_ref[0, here, :] = x_re
        spec_ref[1, here, :] = x_im
        spec_ref[2, here, :] = f_re
        spec_ref[3, here, :] = f_im
        inverse_group(
            x_re * f_re - x_im * f_im, x_re * f_im + x_im * f_re, base, m_rows, back_ref, last_ref, turn_ref
        )

    def store(s, value):
        mixed_ref[s] = value

    collect(m_rows, store)


def grads_kernel(p_ref, spec_ref, first_ref, second_ref, back_ref, last_ref, turn_ref, out_ref, p_rows, i_rows, f_rows):
    spread(lambda s: p_ref[s], p_rows)
    for base in range(0, FEW, GROUP):
        p_re, p_im = forward_group(p_rows, base, first_ref, second_ref, turn_ref)
        here = pl.ds(base * ROWS, GROUP * ROWS)
        for slot, rows in ((2, i_rows), (0, f_rows)):
            o_re = spec_ref[slot, here, :]
            o_im = spec_ref[slot + 1, here, :]
            inverse_group(
                p_re * o_re + p_im * o_im, p_im * o_re - p_re * o_im, base, rows, back_ref, last_ref, turn_ref
            )

    def store_at(first):
        def store(s, value):
            out_ref[s, first : first + FEW] = value

        return store

    collect(i_rows, store_at(0))
    collect(f_rows, store_at(FEW))


def params(mib):
    return pltpu.CompilerParams(vmem_limit_bytes=mib << 20)


def whole_vmem():
    return pl.BlockSpec(memory_space=pltpu.VMEM)


ROWS_SCRATCH = pltpu.VMEM((ROWS * FEW, LANES), F32)


def transform_cost(count, moved):
    return pl.CostEstimate(flops=count * 3 * 10**8, bytes_accessed=moved, transcendentals=0)


def conv_call(xf):
    consts = constants()
    return pl.pallas_call(
        conv_kernel,
        out_shape=(
            jax.ShapeDtypeStruct((16, FEW, TOK), BF),
            jax.ShapeDtypeStruct((4, FEW * ROWS, LANES), F32),
        ),
        in_specs=[whole_vmem()] * 6,
        out_specs=(whole_vmem(), whole_vmem()),
        scratch_shapes=[ROWS_SCRATCH] * 3,
        compiler_params=params(32),
        cost_estimate=transform_cost(3, 4 << 20),
        name="conv",
    )(xf, *consts)


def grads_call(product, spec):
    consts = constants()
    return pl.pallas_call(
        grads_kernel,
        out_shape=jax.ShapeDtypeStruct((16, 2 * FEW, TOK), BF),
        in_specs=[whole_vmem()] * 7,
        out_specs=whole_vmem(),
        scratch_shapes=[ROWS_SCRATCH] * 3,
        compiler_params=params(32),
        cost_estimate=transform_cost(3, 4 << 20),
        name="grads",
    )(product, spec, *consts)


def place_of(where_ref, dy, dz):
    x, zh, core, y, zl = (where_ref[i] for i in range(5))
    y_from = jnp.bitwise_and(y + 4 - dy, 3)
    zl_from = jnp.bitwise_and(zl + 4 - dz, 3)
    zh_from = jnp.right_shift(zl_from, 1)
    core_from = jnp.bitwise_and(zl_from, 1)
    return jnp.bitwise_xor(core, core_from), (x, y_from), jnp.bitwise_xor(zh, zh_from)


def grad_blocks(refs):
    for dy in range(4):
        own, rest = refs[2 * dy], refs[2 * dy + 1]
        for dz in range(4):
            yield dy, dz, (own[...] if dz == 0 else rest[dz - 1])


def slope_kernel(where_ref, *refs):
    grads = refs[:8]
    w_same, w_other, gates_ref, slope_ref, product_ref = refs[8:]
    total = None
    for dy, dz, block in grad_blocks(grads):
        other, (x, x_from), dzh = place_of(where_ref, dy, dz)
        slot = jnp.bitwise_and(x + 4 - x_from, 3) * 2 + dzh
        weight = jnp.where(other == 0, w_same[slot], w_other[slot])
        part = dot(weight, block)
        total = part if total is None else total + part
    slope = total.astype(BF)
    slope_ref[...] = slope
    product_ref[...] = (slope.astype(F32) * gates_ref[...].astype(F32)).astype(BF)


def weight_kernel(where_ref, *refs):
    grads = refs[:8]
    gates_ref, mixed_ref, slope_ref, gate_grad_ref, out_ref = refs[8:]
    mixed = mixed_ref[...].astype(F32)
    gated = (gates_ref[...].astype(F32) * mixed).astype(BF)
    gate_grad_ref[...] = (slope_ref[...].astype(F32) * mixed).astype(BF)
    for dy, dz, block in grad_blocks(grads):
        other, (x, x_to), dzh = place_of(where_ref, dy, dz)
        slot = jnp.bitwise_and(x_to + 4 - x, 3) * 2 + dzh
        part = lax.dot_general(block, gated, (((1,), (1,)), ((), ())), preferred_element_type=F32)
        out_ref[other, slot] = (part * (SEQ**-0.5)).astype(BF)


def matmul_cost(moved):
    return pl.CostEstimate(flops=2 * CH * TOK * 4096, bytes_accessed=moved, transcendentals=0)


def slope_call(where, grads, w_same, w_other, gates):
    shape = jax.ShapeDtypeStruct((CH, TOK), BF)
    return pl.pallas_call(
        slope_kernel,
        out_shape=(shape, shape),
        in_specs=[pl.BlockSpec(memory_space=pltpu.SMEM)] + [whole_vmem()] * 11,
        out_specs=(whole_vmem(), whole_vmem()),
        compiler_params=params(32),
        cost_estimate=matmul_cost(7 << 20),
        name="slope",
    )(where, *grads, w_same, w_other, gates)


def weight_call(where, grads, gates, mixed, slope):
    return pl.pallas_call(
        weight_kernel,
        out_shape=(
            jax.ShapeDtypeStruct((CH, TOK), BF),
            jax.ShapeDtypeStruct((2, 8, 256, 256), BF),
        ),
        in_specs=[pl.BlockSpec(memory_space=pltpu.SMEM)] + [whole_vmem()] * 11,
        out_specs=(whole_vmem(), whole_vmem()),
        compiler_params=params(32),
        cost_estimate=matmul_cost(7 << 20),
        name="weight",
    )(where, *grads, gates, mixed, slope)


def exchange(value):
    return lax.all_to_all(value, "ctx", split_axis=0, concat_axis=0, tiled=True)


def add(*parts):
    total = parts[0].astype(F32)
    for part in parts[1:]:
        total = total + part.astype(F32)
    return total.astype(BF)


def on_device(inputs, gates, filters, out_grad, out_weight):
    ctx = lax.axis_index("ctx")
    tp = lax.axis_index("tp")
    where = jnp.stack([ctx // 4, (ctx // 2) % 2, ctx % 2, tp // 4, tp % 4]).astype(jnp.int32)

    own = [send(out_grad, "tp", 4, 4, dy) for dy in (1, 2, 3)]
    rest = jnp.stack([send(out_grad, "tp", 1, 4, dz) for dz in (1, 2, 3)])
    rests = [send(rest, "tp", 4, 4, dy) for dy in (1, 2, 3)]
    grads = [out_grad, rest]
    for o, r in zip(own, rests):
        grads += [o, r]

    w_own = out_weight.T
    w_pair = jnp.stack([w_own, send(w_own, "ctx", 2, 2, 1)])
    w_same = jnp.concatenate([w_pair] + [send(w_pair, "ctx", 4, 4, dx) for dx in (1, 2, 3)])
    w_other = send(w_same, "ctx", 1, 2, 1)

    both = jnp.concatenate([inputs.reshape(16, FEW, TOK), filters.reshape(16, FEW, TOK)], axis=1)
    mixed_rows, spec = conv_call(exchange(both))
    mixed = exchange(mixed_rows).reshape(CH, TOK)

    slope, product = slope_call(where, grads, w_same, w_other, gates)
    grad_rows = grads_call(exchange(product.reshape(16, FEW, TOK)), spec)
    gate_grad, partial = weight_call(where, grads, gates, mixed, slope)
    both_grads = exchange(grad_rows)
    input_grad = both_grads[:, :FEW].reshape(CH, TOK)
    filter_grad = both_grads[:, FEW:].reshape(CH, TOK)

    chip = add(partial[0], send(partial[1], "ctx", 1, 2, 1)).reshape(4, 2, 256, 256)
    line = add(chip[0], *[send(chip[dx], "ctx", 4, 4, dx) for dx in (1, 2, 3)])
    weight_grad = add(line[0], send(line[1], "ctx", 2, 2, 1))
    return (input_grad, gate_grad, filter_grad, weight_grad)


def solution(mesh):
    in_specs = (P("tp", "ctx"), P("tp", "ctx"), P("tp", "ctx"), P("tp", "ctx"), P("ctx", "tp"))
    out_specs = (P("tp", "ctx"), P("tp", "ctx"), P("tp", "ctx"), P("ctx", "tp"))
    return jax.shard_map(
        on_device, mesh=mesh, in_specs=in_specs, out_specs=out_specs, check_vma=False
    )
```

time: 481 us -> 172 us (0.36)
  the two profiles are of different devices: /device:TPU:8 before, /device:TPU:67 now
where the time goes in v1:
time: 172 us; the launch traced here: 169 us
  waiting for transfers between devices  64.4 us (37%)
  starting transfers between devices  59.7 us (35%)
  local copies, waits for them, and re-layouts  21.4 us (12%)
  Pallas kernels  17.1 us (10%)
  other arithmetic  5.86 us (3%)
    ppermute x19, waiting for transfers between devices, send(): return lax.ppermute(value, axis, shift_pairs(stride, size, by))  59.3 us
    ppermute x19, starting transfers between devices, send(): return lax.ppermute(value, axis, shift_pairs(stride, size, by))  32.8 us
    all_to_all x4, starting transfers between devices, exchange(): return lax.all_to_all(value, 'ctx', split_axis=0, concat_axis=0, tiled=True)  26.9 us
    unnamed x49, local copies, waits for them, and re-layouts  17.7 us
    pallas_call x1, Pallas kernels, grads_call(): pl.pallas_call(grads_kernel, out_shape=jax.ShapeDtypeStruct((16, 2 * FEW,...  5.74 us
    all_to_all x4, waiting for transfers between devices, exchange(): return lax.all_to_all(value, 'ctx', split_axis=0, concat_axis=0, tiled=True)  5.14 us
    pallas_call x1, Pallas kernels, conv_call(): pl.pallas_call(conv_kernel, out_shape=(jax.ShapeDtypeStruct((16, FEW, TOK...  4.76 us
    convert_element_type x3, other arithmetic, add(): return total.astype(BF)  3.87 us
  transfers between devices with their start and end apart: 23, of which 8 were waited for; matrix products, arithmetic and copies ran while one was open for 6% of the time, Pallas kernels for 8%

profile of v1, /device:TPU:67, one launch (start us, length us, event | category | flops | bytes accessed | tf_op | source)
XLA Modules:
  0.0 169.3 jit_solution(5381095684813812689)
XLA Ops:
  0.6 1.0 copy.14
  1.6 5.2 %collective-permute-start.9 = (bf16[256,256]{1,0:T(8,128)(2,1)S(1)}, bf16[256,256]{1,0:T(8,128)(2,1)S(1)}, u32[]{:S(2)}, u32[]{:S(2)}) collective-permute-start(bf16[256,256]{1,0:T(8,128)(2,1)S(1)} %bitcast.33), channel_id=1, source_target_pairs={{0,32},{16,48},{32,0},{48,16},{64,96},{80,112},{96,64},{112,80},{1... | collective-permute-start | bytes 393224 | tf_op jit(solution)/shard_map/ppermute | solution.py:32
  6.8 0.7 collective-permute-start.2
  7.6 2.1 %collective-permute-start.1 = (bf16[256,512]{1,0:T(8,128)(2,1)}, bf16[256,512]{1,0:T(8,128)(2,1)S(1)}, u32[]{:S(2)}, u32[]{:S(2)}) collective-permute-start(bf16[256,512]{1,0:T(8,128)(2,1)} %refs_0_.3), channel_id=1, source_target_pairs={{0,2},{1,3},{2,0},{3,1},{4,6},{5,7},{6,4},{7,5},{8,10},{9,11},{10,... | collective-permute-start | bytes 786440 | tf_op jit(solution)/shard_map/ppermute | solution.py:32
  9.7 1.9 %pad_maximum_fusion.1 = bf16[16,32,512]{2,1,0:T(8,128)(2,1)} fusion(bf16[16,16,512]{2,1,0:T(8,128)(2,1)} %bitcast.36, bf16[16,16,512]{2,1,0:T(8,128)(2,1)} %bitcast.37), kind=kLoop, calls=%fused_computation.4 | loop fusion | flops 1048576 | bytes 1048576 | tf_op jit(solution)/shard_map/concatenate | solution.py:323
  11.5 6.9 %all-to-all-start.1 = ((bf16[16,32,512]{2,1,0:T(8,128)(2,1)}), bf16[16,32,512]{2,1,0:T(8,128)(2,1)}, u32[]{:S(2)}, u32[]{:S(2)}) async-start(bf16[16,32,512]{2,1,0:T(8,128)(2,1)} %pad_maximum_fusion.1), calls=%async_computation.1 | async-start | bytes 1048576 | tf_op jit(solution)/shard_map/all_to_all | solution.py:296
  18.5 1.3 collective-permute-start.10
  19.7 0.7 constant_dynamic-update-slice_fusion.4
  20.4 0.7 collective-permute-start.11
  21.1 2.0 %collective-permute-start.12 = (bf16[2,256,256]{2,1,0:T(8,128)(2,1)S(1)}, bf16[2,256,256]{2,1,0:T(8,128)(2,1)S(1)}, u32[]{:S(2)}, u32[]{:S(2)}) collective-permute-start(bf16[2,256,256]{2,1,0:T(8,128)(2,1)S(1)} %pad_maximum_fusion.2), channel_id=1, source_target_pairs={{0,192},{16,208},{32,224},{48,240},{64,0},{80,16},{96,32},{112,48}... | collective-permute-start | bytes 786440 | tf_op jit(solution)/shard_map/ppermute | solution.py:32
  23.1 0.7 constant_dynamic-update-slice_fusion.3
  23.7 6.9 %collective-permute-done.10 = bf16[2,256,256]{2,1,0:T(8,128)(2,1)S(1)} collective-permute-done((bf16[2,256,256]{2,1,0:T(8,128)(2,1)S(1)}, bf16[2,256,256]{2,1,0:T(8,128)(2,1)S(1)}, u32[]{:S(2)}, u32[]{:S(2)}) %collective-permute-start.10) | collective-permute-done | bytes 262176 | tf_op jit(solution)/shard_map/ppermute | solution.py:32
  30.7 0.7 constant_dynamic-update-slice_fusion.2
  31.4 0.7 constant_dynamic-update-slice_fusion.1
  32.1 5.2 %collective-permute-done.12 = bf16[2,256,256]{2,1,0:T(8,128)(2,1)S(1)} collective-permute-done((bf16[2,256,256]{2,1,0:T(8,128)(2,1)S(1)}, bf16[2,256,256]{2,1,0:T(8,128)(2,1)S(1)}, u32[]{:S(2)}, u32[]{:S(2)}) %collective-permute-start.12) | collective-permute-done | bytes 262176 | tf_op jit(solution)/shard_map/ppermute | solution.py:32
  37.3 0.7 constant_dynamic-update-slice_fusion.refs_8_
  38.0 1.2 collective-permute-start.13
  39.2 1.3 collective-permute-start.3
  40.5 5.5 %collective-permute-done.1 = bf16[256,512]{1,0:T(8,128)(2,1)S(1)} collective-permute-done((bf16[256,512]{1,0:T(8,128)(2,1)}, bf16[256,512]{1,0:T(8,128)(2,1)S(1)}, u32[]{:S(2)}, u32[]{:S(2)}) %collective-permute-start.1) | collective-permute-done | bytes 262176 | tf_op jit(solution)/shard_map/ppermute | solution.py:32
  45.9 1.9 %collective-permute-done = bf16[256,512]{1,0:T(8,128)(2,1)S(1)} collective-permute-done((bf16[256,512]{1,0:T(8,128)(2,1)}, bf16[256,512]{1,0:T(8,128)(2,1)S(1)}, u32[]{:S(2)}, u32[]{:S(2)}) %collective-permute-start) | collective-permute-done | bytes 262176 | tf_op jit(solution)/shard_map/ppermute | solution.py:32
  47.9 0.1 pad_maximum_fusion.refs_1_
  48.0 1.4 collective-permute-start.4
  49.3 2.6 %collective-permute-start.6 = (bf16[3,256,512]{2,1,0:T(8,128)(2,1)S(1)}, bf16[3,256,512]{2,1,0:T(8,128)(2,1)S(1)}, u32[]{:S(2)}, u32[]{:S(2)}) collective-permute-start(bf16[3,256,512]{2,1,0:T(8,128)(2,1)S(1)} %pad_maximum_fusion.refs_1_), channel_id=1, source_target_pairs={{0,8},{1,9},{2,10},{3,11},{4,12},{5,13},{6,14},{7,15},{8,0},{9,1},... | collective-permute-start | bytes 2359304 | tf_op jit(solution)/shard_map/ppermute | solution.py:32
  52.0 1.1 collective-permute-start.8
  53.0 0.7 copy-done.5
  53.7 0.2 collective-permute-start.5
  54.0 1.0 copy-done.10
  55.0 0.8 copy-done.15
  55.8 0.8 copy-done.17
  56.6 0.8 copy-done.19
  57.3 4.8 %conv.1 = (bf16[16,16,512]{2,1,0:T(8,128)(2,1)S(1)}, f32[4,1024,128]{2,1,0:T(8,128)S(1)}) custom-call(bf16[16,32,512]{2,1,0:T(8,128)(2,1)} %all-to-all-done.1.xf_ref, bf16[128,128]{1,0:T(8,128)(2,1)S(1)} %copy-done.19, bf16[768,256]{1,0:T(8,128)(2,1)S(1)} %copy-done.8, bf16[768,256]{1,0:T(8,128)(2,1)S(1)} %copy-done.10, bf16[64,384]{1,0:T(8,128)(2,1)S(1)} %copy-done.17, ...), custom_call_target="tpu_custom_call" | custom-call | flops 900000000 | bytes 4194304 | tf_op jit(solution)/shard_map/conv/pallas_call | solution.py:190
  62.1 1.3 copy-done.1
  63.5 0.7 copy-done.14
  64.2 7.4 %all-to-all-start.3 = ((bf16[16,16,512]{2,1,0:T(8,128)(2,1)}), bf16[16,16,512]{2,1,0:T(8,128)(2,1)S(1)}, u32[]{:S(2)}, u32[]{:S(2)}) async-start(bf16[16,16,512]{2,1,0:T(8,128)(2,1)} %copy-done.14), calls=%async_computation.3 | async-start | bytes 524288 | tf_op jit(solution)/shard_map/all_to_all | solution.py:296
  71.5 20.1 %collective-permute-done.5.refs_4_ = bf16[256,512]{1,0:T(8,128)(2,1)} collective-permute-done((bf16[256,512]{1,0:T(8,128)(2,1)}, bf16[256,512]{1,0:T(8,128)(2,1)}, u32[]{:S(2)}, u32[]{:S(2)}) %collective-permute-start.5) | collective-permute-done | bytes 262176 | tf_op jit(solution)/shard_map/ppermute | solution.py:32
  91.7 1.8 %collective-permute-start.7 = (bf16[256,512]{1,0:T(8,128)(2,1)}, bf16[256,512]{1,0:T(8,128)(2,1)}, u32[]{:S(2)}, u32[]{:S(2)}) collective-permute-start(bf16[256,512]{1,0:T(8,128)(2,1)} %refs_0_.3), channel_id=1, source_target_pairs={{0,12},{1,13},{2,14},{3,15},{4,0},{5,1},{6,2},{7,3},{8,4},{9,5},{1... | collective-permute-start | bytes 786440 | tf_op jit(solution)/shard_map/ppermute | solution.py:32
  93.5 0.1 stack.44.where_ref
  93.6 4.9 %collective-permute-done.7.refs_6_ = bf16[256,512]{1,0:T(8,128)(2,1)} collective-permute-done((bf16[256,512]{1,0:T(8,128)(2,1)}, bf16[256,512]{1,0:T(8,128)(2,1)}, u32[]{:S(2)}, u32[]{:S(2)}) %collective-permute-start.7) | collective-permute-done | bytes 262176 | tf_op jit(solution)/shard_map/ppermute | solution.py:32
  98.5 0.9 copy-done.3
  99.4 0.9 copy-done.6
  100.4 3.8 %slope.1 = (bf16[256,512]{1,0:T(8,128)(2,1)S(1)}, bf16[256,512]{1,0:T(8,128)(2,1)}) custom-call(s32[5]{0:T(128)S(1)} %stack.44.where_ref, bf16[256,512]{1,0:T(8,128)(2,1)} %refs_0_.3, bf16[3,256,512]{2,1,0:T(8,128)(2,1)S(1)} %pad_maximum_fusion.refs_1_, bf16[256,512]{1,0:T(8,128)(2,1)S(1)} %copy-done.6, ...), custom_call_target="tpu_custom_call" | custom-call | flops 1073741824 | bytes 7340032 | tf_op jit(solution)/shard_map/slope/pallas_call | solution.py:269
  104.2 0.7 copy-done.12
  104.9 0.9 copy-done.4
  105.8 0.9 copy-done.7
  106.8 0.9 copy-done.13
  107.7 2.9 %weight.1 = (bf16[256,512]{1,0:T(8,128)(2,1)}, bf16[2,8,256,256]{3,2,1,0:T(8,128)(2,1)S(1)}) custom-call(s32[5]{0:T(128)S(1)} %stack.44.where_ref, bf16[256,512]{1,0:T(8,128)(2,1)} %refs_0_.3, bf16[3,256,512]{2,1,0:T(8,128)(2,1)S(1)} %pad_maximum_fusion.refs_1_, bf16[256,512]{1,0:T(8,128)(2,1)S(1)} %copy-done.7, ...), custom_call_target="tpu_custom_call" | custom-call | flops 1073741824 | bytes 7340032 | tf_op jit(solution)/shard_map/weight/pallas_call | solution.py:281
  110.6 1.3 copy-done
  111.9 1.1 slice_bitcast_fusion
  113.0 2.3 %collective-permute-start.14 = (bf16[8,256,256]{2,1,0:T(8,128)(2,1)}, bf16[8,256,256]{2,1,0:T(8,128)(2,1)}, u32[]{:S(2)}, u32[]{:S(2)}) collective-permute-start(bf16[8,256,256]{2,1,0:T(8,128)(2,1)} %slice_bitcast_fusion), channel_id=1, source_target_pairs={{0,16},{16,0},{32,48},{48,32},{64,80},{80,64},{96,112},{112,96},{1... | collective-permute-start | bytes 3145736 | tf_op jit(solution)/shard_map/ppermute | solution.py:32
  115.2 6.6 %all-to-all-start = ((bf16[16,16,512]{2,1,0:T(8,128)(2,1)}), bf16[16,16,512]{2,1,0:T(8,128)(2,1)S(1)}, u32[]{:S(2)}, u32[]{:S(2)}) async-start(bf16[16,16,512]{2,1,0:T(8,128)(2,1)} %bitcast.12), calls=%async_computation | async-start | bytes 524288 | tf_op jit(solution)/shard_map/all_to_all | solution.py:296
  121.9 1.9 %fusion = bf16[8,256,256]{2,1,0:T(8,128)(2,1)S(1)} fusion(bf16[8,256,256]{2,1,0:T(8,128)(2,1)} %collective-permute-done.14, bf16[2,8,256,256]{3,2,1,0:T(8,128)(2,1)} %copy-done), kind=kLoop, calls=%fused_computation.1 | loop fusion | flops 2097152 | bytes 3145728 | tf_op jit(solution)/shard_map/convert_element_type | solution.py:303
  123.9 1.0 fusion.2
  124.8 0.1 collective-permute-start.17
  124.9 2.3 %collective-permute-start.16 = (bf16[2,256,256]{2,1,0:T(8,128)(2,1)}, bf16[2,256,256]{2,1,0:T(8,128)(2,1)}, u32[]{:S(2)}, u32[]{:S(2)}) collective-permute-start(bf16[2,256,256]{2,1,0:T(8,128)(2,1)} %get-tuple-element.18), channel_id=1, source_target_pairs={{0,128},{16,144},{32,160},{48,176},{64,192},{80,208},{96,224},{112... | collective-permute-start | bytes 786440 | tf_op jit(solution)/shard_map/ppermute | solution.py:32
  127.2 1.5 collective-permute-start.15
  128.7 5.1 %all-to-all-done.p_ref = bf16[16,16,512]{2,1,0:T(8,128)(2,1)S(1)} async-done(((bf16[16,16,512]{2,1,0:T(8,128)(2,1)}), bf16[16,16,512]{2,1,0:T(8,128)(2,1)S(1)}, u32[]{:S(2)}, u32[]{:S(2)}) %all-to-all-start) | async-done | bytes 262176 | tf_op jit(solution)/shard_map/all_to_all | solution.py:296
  133.9 1.0 copy-done.11
  134.9 5.7 %grads.1 = bf16[16,32,512]{2,1,0:T(8,128)(2,1)} custom-call(bf16[16,16,512]{2,1,0:T(8,128)(2,1)S(1)} %all-to-all-done.p_ref, f32[4,1024,128]{2,1,0:T(8,128)S(1)} %copy-done.2, bf16[128,128]{1,0:T(8,128)(2,1)S(1)} %copy-done.20, bf16[768,256]{1,0:T(8,128)(2,1)S(1)} %copy-done.9, bf16[768,256]{1,0:T(8,128)(2,1)S(1)} %copy-done.11, ...), custom_call_target="tpu_custom_call" | custom-call | flops 900000000 | bytes 4194304 | tf_op jit(solution)/shard_map/grads/pallas_call | solution.py:207
  140.6 6.0 %all-to-all-start.2 = ((bf16[16,32,512]{2,1,0:T(8,128)(2,1)}), bf16[16,32,512]{2,1,0:T(8,128)(2,1)S(1)}, u32[]{:S(2)}, u32[]{:S(2)}) async-start(bf16[16,32,512]{2,1,0:T(8,128)(2,1)} %grads.1), calls=%async_computation.2 | async-start | bytes 1048576 | tf_op jit(solution)/shard_map/all_to_all | solution.py:296
  146.7 1.2 add_convert_fusion
  147.9 5.2 %collective-permute-start.18 = (bf16[256,256]{1,0:T(8,128)(2,1)S(1)}, bf16[256,256]{1,0:T(8,128)(2,1)S(1)}, u32[]{:S(2)}, u32[]{:S(2)}) collective-permute-start(bf16[256,256]{1,0:T(8,128)(2,1)S(1)} %slice_bitcast_fusion.1), channel_id=1, source_target_pairs={{0,32},{16,48},{32,0},{48,16},{64,96},{80,112},{96,64},{112,80},{1... | collective-permute-start | bytes 393224 | tf_op jit(solution)/shard_map/ppermute | solution.py:32
  153.1 14.7 %collective-permute-done.18 = bf16[256,256]{1,0:T(8,128)(2,1)S(1)} collective-permute-done((bf16[256,256]{1,0:T(8,128)(2,1)S(1)}, bf16[256,256]{1,0:T(8,128)(2,1)S(1)}, u32[]{:S(2)}, u32[]{:S(2)}) %collective-permute-start.18) | collective-permute-done | bytes 131104 | tf_op jit(solution)/shard_map/ppermute | solution.py:32
  167.8 0.7 fusion.1
  168.5 0.8 fusion.3
  (47 shorter events, 0.2 us)
Async XLA Ops:
  1.6 16.8 %collective-permute-start.9 = (bf16[256,256]{1,0:T(8,128)(2,1)S(1)}, bf16[256,256]{1,0:T(8,128)(2,1)S(1)}, u32[]{:S(2)}, u32[]{:S(2)}) collective-permute-start(bf16[256,256]{1,0:T(8,128)(2,1)S(1)} %bitcast.33), channel_id=1, source_target_pairs={{0,32},{16,48},{32,0},{48,16},{64,96},{80,112},{96,64},{112,80},{1... | collective-permute-start | bytes 393224 | tf_op jit(solution)/shard_map/ppermute | solution.py:32
  6.8 33.6 %collective-permute-start.2 = (bf16[256,512]{1,0:T(8,128)(2,1)}, bf16[256,512]{1,0:T(8,128)(2,1)S(1)}, u32[]{:S(2)}, u32[]{:S(2)}) collective-permute-start(bf16[256,512]{1,0:T(8,128)(2,1)} %refs_0_.3), channel_id=1, source_target_pairs={{0,3},{1,0},{2,1},{3,2},{4,7},{5,4},{6,5},{7,6},{8,11},{9,8},{10,9... | collective-permute-start | bytes 786440 | tf_op jit(solution)/shard_map/ppermute | solution.py:32
  7.6 38.4 %collective-permute-start.1 = (bf16[256,512]{1,0:T(8,128)(2,1)}, bf16[256,512]{1,0:T(8,128)(2,1)S(1)}, u32[]{:S(2)}, u32[]{:S(2)}) collective-permute-start(bf16[256,512]{1,0:T(8,128)(2,1)} %refs_0_.3), channel_id=1, source_target_pairs={{0,2},{1,3},{2,0},{3,1},{4,6},{5,7},{6,4},{7,5},{8,10},{9,11},{10,... | collective-permute-start | bytes 786440 | tf_op jit(solution)/shard_map/ppermute | solution.py:32
  11.5 42.4 %all-to-all-start.1 = ((bf16[16,32,512]{2,1,0:T(8,128)(2,1)}), bf16[16,32,512]{2,1,0:T(8,128)(2,1)}, u32[]{:S(2)}, u32[]{:S(2)}) async-start(bf16[16,32,512]{2,1,0:T(8,128)(2,1)} %pad_maximum_fusion.1), calls=%async_computation.1 | async-start | bytes 1048576 | tf_op jit(solution)/shard_map/all_to_all | solution.py:296
  18.4 35.5 %copy-start.8 = (bf16[768,256]{1,0:T(8,128)(2,1)S(1)}, bf16[768,256]{1,0:T(8,128)(2,1)}, u32[]{:S(2)}) copy-start(bf16[768,256]{1,0:T(8,128)(2,1)} %constant.71.clone.second_ref) | copy-start | bytes 1179652
  18.5 12.2 %collective-permute-start.10 = (bf16[2,256,256]{2,1,0:T(8,128)(2,1)S(1)}, bf16[2,256,256]{2,1,0:T(8,128)(2,1)S(1)}, u32[]{:S(2)}, u32[]{:S(2)}) collective-permute-start(bf16[2,256,256]{2,1,0:T(8,128)(2,1)S(1)} %pad_maximum_fusion.2), channel_id=1, source_target_pairs={{0,64},{16,80},{32,96},{48,112},{64,128},{80,144},{96,160},{112,17... | collective-permute-start | bytes 786440 | tf_op jit(solution)/shard_map/ppermute | solution.py:32
  20.4 11.0 %collective-permute-start.11 = (bf16[2,256,256]{2,1,0:T(8,128)(2,1)S(1)}, bf16[2,256,256]{2,1,0:T(8,128)(2,1)S(1)}, u32[]{:S(2)}, u32[]{:S(2)}) collective-permute-start(bf16[2,256,256]{2,1,0:T(8,128)(2,1)S(1)} %pad_maximum_fusion.2), channel_id=1, source_target_pairs={{0,128},{16,144},{32,160},{48,176},{64,192},{80,208},{96,224},{112... | collective-permute-start | bytes 786440 | tf_op jit(solution)/shard_map/ppermute | solution.py:32
  21.1 16.2 %collective-permute-start.12 = (bf16[2,256,256]{2,1,0:T(8,128)(2,1)S(1)}, bf16[2,256,256]{2,1,0:T(8,128)(2,1)S(1)}, u32[]{:S(2)}, u32[]{:S(2)}) collective-permute-start(bf16[2,256,256]{2,1,0:T(8,128)(2,1)S(1)} %pad_maximum_fusion.2), channel_id=1, source_target_pairs={{0,192},{16,208},{32,224},{48,240},{64,0},{80,16},{96,32},{112,48}... | collective-permute-start | bytes 786440 | tf_op jit(solution)/shard_map/ppermute | solution.py:32
  30.7 17.2 %collective-permute-start = (bf16[256,512]{1,0:T(8,128)(2,1)}, bf16[256,512]{1,0:T(8,128)(2,1)S(1)}, u32[]{:S(2)}, u32[]{:S(2)}) collective-permute-start(bf16[256,512]{1,0:T(8,128)(2,1)} %refs_0_.3), channel_id=1, source_target_pairs={{0,1},{1,2},{2,3},{3,0},{4,5},{5,6},{6,7},{7,4},{8,9},{9,10},{10,1... | collective-permute-start | bytes 786440 | tf_op jit(solution)/shard_map/ppermute | solution.py:32
  38.0 60.5 %collective-permute-start.13 = (bf16[8,256,256]{2,1,0:T(8,128)(2,1)}, bf16[8,256,256]{2,1,0:T(8,128)(2,1)}, u32[]{:S(2)}, u32[]{:S(2)}) collective-permute-start(bf16[8,256,256]{2,1,0:T(8,128)(2,1)} %constant_dynamic-update-slice_fusion.refs_8_), channel_id=1, source_target_pairs={{0,16},{16,0},{32,48},{48,32},{64,80},{80,64},{96,112},{112,96},{1... | collective-permute-start | bytes 3145736 | tf_op jit(solution)/shard_map/ppermute | solution.py:32
  39.2 13.9 %collective-permute-start.3 = (bf16[256,512]{1,0:T(8,128)(2,1)}, bf16[256,512]{1,0:T(8,128)(2,1)S(1)}, u32[]{:S(2)}, u32[]{:S(2)}) collective-permute-start(bf16[256,512]{1,0:T(8,128)(2,1)} %refs_0_.3), channel_id=1, source_target_pairs={{0,4},{1,5},{2,6},{3,7},{4,8},{5,9},{6,10},{7,11},{8,12},{9,13},{1... | collective-permute-start | bytes 786440 | tf_op jit(solution)/shard_map/ppermute | solution.py:32
  48.0 50.5 %collective-permute-start.4 = (bf16[3,256,512]{2,1,0:T(8,128)(2,1)S(1)}, bf16[3,256,512]{2,1,0:T(8,128)(2,1)S(1)}, u32[]{:S(2)}, u32[]{:S(2)}) collective-permute-start(bf16[3,256,512]{2,1,0:T(8,128)(2,1)S(1)} %pad_maximum_fusion.refs_1_), channel_id=1, source_target_pairs={{0,4},{1,5},{2,6},{3,7},{4,8},{5,9},{6,10},{7,11},{8,12},{9,13},{1... | collective-permute-start | bytes 2359304 | tf_op jit(solution)/shard_map/ppermute | solution.py:32
  49.3 49.1 %collective-permute-start.6 = (bf16[3,256,512]{2,1,0:T(8,128)(2,1)S(1)}, bf16[3,256,512]{2,1,0:T(8,128)(2,1)S(1)}, u32[]{:S(2)}, u32[]{:S(2)}) collective-permute-start(bf16[3,256,512]{2,1,0:T(8,128)(2,1)S(1)} %pad_maximum_fusion.refs_1_), channel_id=1, source_target_pairs={{0,8},{1,9},{2,10},{3,11},{4,12},{5,13},{6,14},{7,15},{8,0},{9,1},... | collective-permute-start | bytes 2359304 | tf_op jit(solution)/shard_map/ppermute | solution.py:32
  52.0 46.5 %collective-permute-start.8 = (bf16[3,256,512]{2,1,0:T(8,128)(2,1)S(1)}, bf16[3,256,512]{2,1,0:T(8,128)(2,1)S(1)}, u32[]{:S(2)}, u32[]{:S(2)}) collective-permute-start(bf16[3,256,512]{2,1,0:T(8,128)(2,1)S(1)} %pad_maximum_fusion.refs_1_), channel_id=1, source_target_pairs={{0,12},{1,13},{2,14},{3,15},{4,0},{5,1},{6,2},{7,3},{8,4},{9,5},{1... | collective-permute-start | bytes 2359304 | tf_op jit(solution)/shard_map/ppermute | solution.py:32
  53.0 0.7 copy-start.5
  53.7 38.0 %collective-permute-start.5 = (bf16[256,512]{1,0:T(8,128)(2,1)}, bf16[256,512]{1,0:T(8,128)(2,1)}, u32[]{:S(2)}, u32[]{:S(2)}) collective-permute-start(bf16[256,512]{1,0:T(8,128)(2,1)} %refs_0_.3), channel_id=1, source_target_pairs={{0,8},{1,9},{2,10},{3,11},{4,12},{5,13},{6,14},{7,15},{8,0},{9,1},... | collective-permute-start | bytes 786440 | tf_op jit(solution)/shard_map/ppermute | solution.py:32
  54.0 1.0 copy-start.10
  55.0 0.8 copy-start.15
  55.8 0.8 copy-start.17
  56.6 0.8 copy-start.19
  62.1 1.3 copy-start.1
  63.5 0.7 copy-start.14
  64.2 40.7 %all-to-all-start.3 = ((bf16[16,16,512]{2,1,0:T(8,128)(2,1)}), bf16[16,16,512]{2,1,0:T(8,128)(2,1)S(1)}, u32[]{:S(2)}, u32[]{:S(2)}) async-start(bf16[16,16,512]{2,1,0:T(8,128)(2,1)} %copy-done.14), calls=%async_computation.3 | async-start | bytes 524288 | tf_op jit(solution)/shard_map/all_to_all | solution.py:296
  91.7 6.8 %collective-permute-start.7 = (bf16[256,512]{1,0:T(8,128)(2,1)}, bf16[256,512]{1,0:T(8,128)(2,1)}, u32[]{:S(2)}, u32[]{:S(2)}) collective-permute-start(bf16[256,512]{1,0:T(8,128)(2,1)} %refs_0_.3), channel_id=1, source_target_pairs={{0,12},{1,13},{2,14},{3,15},{4,0},{5,1},{6,2},{7,3},{8,4},{9,5},{1... | collective-permute-start | bytes 786440 | tf_op jit(solution)/shard_map/ppermute | solution.py:32
  98.5 1.0 copy-start.3
  99.4 0.9 copy-start.6
  104.1 0.7 copy-start.12
  104.9 1.0 copy-start.4
  105.8 0.9 copy-start.7
  106.8 0.9 copy-start.13
  110.6 1.3 copy-start
  113.0 8.9 %collective-permute-start.14 = (bf16[8,256,256]{2,1,0:T(8,128)(2,1)}, bf16[8,256,256]{2,1,0:T(8,128)(2,1)}, u32[]{:S(2)}, u32[]{:S(2)}) collective-permute-start(bf16[8,256,256]{2,1,0:T(8,128)(2,1)} %slice_bitcast_fusion), channel_id=1, source_target_pairs={{0,16},{16,0},{32,48},{48,32},{64,80},{80,64},{96,112},{112,96},{1... | collective-permute-start | bytes 3145736 | tf_op jit(solution)/shard_map/ppermute | solution.py:32
  115.2 18.6 %all-to-all-start = ((bf16[16,16,512]{2,1,0:T(8,128)(2,1)}), bf16[16,16,512]{2,1,0:T(8,128)(2,1)S(1)}, u32[]{:S(2)}, u32[]{:S(2)}) async-start(bf16[16,16,512]{2,1,0:T(8,128)(2,1)} %bitcast.12), calls=%async_computation | async-start | bytes 524288 | tf_op jit(solution)/shard_map/all_to_all | solution.py:296
  121.8 12.0 %copy-start.2 = (f32[4,1024,128]{2,1,0:T(8,128)S(1)}, f32[4,1024,128]{2,1,0:T(8,128)}, u32[]{:S(2)}) copy-start(f32[4,1024,128]{2,1,0:T(8,128)} %copy-done.1) | copy-start | bytes 6291460
  121.8 12.0 %copy-start.9 = (bf16[768,256]{1,0:T(8,128)(2,1)S(1)}, bf16[768,256]{1,0:T(8,128)(2,1)}, u32[]{:S(2)}) copy-start(bf16[768,256]{1,0:T(8,128)(2,1)} %constant.71.clone.second_ref) | copy-start | bytes 1179652
  121.9 12.0 %copy-start.16 = (f32[2,64,128]{2,1,0:T(8,128)S(1)}, f32[2,64,128]{2,1,0:T(8,128)}, u32[]{:S(2)}) copy-start(f32[2,64,128]{2,1,0:T(8,128)} %constant.74.clone.turn_ref) | copy-start | bytes 196612
  121.9 12.0 %copy-start.18 = (bf16[64,384]{1,0:T(8,128)(2,1)S(1)}, bf16[64,384]{1,0:T(8,128)(2,1)}, u32[]{:S(2)}) copy-start(bf16[64,384]{1,0:T(8,128)(2,1)} %constant.73.clone.last_ref) | copy-start | bytes 147460
  121.9 12.0 %copy-start.20 = (bf16[128,128]{1,0:T(8,128)(2,1)S(1)}, bf16[128,128]{1,0:T(8,128)(2,1)}, u32[]{:S(2)}) copy-start(bf16[128,128]{1,0:T(8,128)(2,1)} %constant.70.clone.first_ref) | copy-start | bytes 98308
  123.8 3.4 %copy-start.21 = (bf16[8,256,256]{2,1,0:T(8,128)(2,1)}, bf16[8,256,256]{2,1,0:T(8,128)(2,1)S(1)}, u32[]{:S(2)}) copy-start(bf16[8,256,256]{2,1,0:T(8,128)(2,1)S(1)} %fusion) | copy-start | bytes 3145732
  124.8 21.8 %collective-permute-start.17 = (bf16[2,256,256]{2,1,0:T(8,128)(2,1)}, bf16[2,256,256]{2,1,0:T(8,128)(2,1)S(1)}, u32[]{:S(2)}, u32[]{:S(2)}) collective-permute-start(bf16[2,256,256]{2,1,0:T(8,128)(2,1)} %get-tuple-element.17), channel_id=1, source_target_pairs={{0,192},{16,208},{32,224},{48,240},{64,0},{80,16},{96,32},{112,48}... | collective-permute-start | bytes 786440 | tf_op jit(solution)/shard_map/ppermute | solution.py:32
  124.9 21.7 %collective-permute-start.16 = (bf16[2,256,256]{2,1,0:T(8,128)(2,1)}, bf16[2,256,256]{2,1,0:T(8,128)(2,1)}, u32[]{:S(2)}, u32[]{:S(2)}) collective-permute-start(bf16[2,256,256]{2,1,0:T(8,128)(2,1)} %get-tuple-element.18), channel_id=1, source_target_pairs={{0,128},{16,144},{32,160},{48,176},{64,192},{80,208},{96,224},{112... | collective-permute-start | bytes 786440 | tf_op jit(solution)/shard_map/ppermute | solution.py:32
  127.2 19.5 %collective-permute-start.15 = (bf16[2,256,256]{2,1,0:T(8,128)(2,1)}, bf16[2,256,256]{2,1,0:T(8,128)(2,1)}, u32[]{:S(2)}, u32[]{:S(2)}) collective-permute-start(bf16[2,256,256]{2,1,0:T(8,128)(2,1)} %get-tuple-element.16), channel_id=1, source_target_pairs={{0,64},{16,80},{32,96},{48,112},{64,128},{80,144},{96,160},{112,17... | collective-permute-start | bytes 786440 | tf_op jit(solution)/shard_map/ppermute | solution.py:32
  133.9 1.0 copy-start.11
  140.6 27.9 %all-to-all-start.2 = ((bf16[16,32,512]{2,1,0:T(8,128)(2,1)}), bf16[16,32,512]{2,1,0:T(8,128)(2,1)S(1)}, u32[]{:S(2)}, u32[]{:S(2)}) async-start(bf16[16,32,512]{2,1,0:T(8,128)(2,1)} %grads.1), calls=%async_computation.2 | async-start | bytes 1048576 | tf_op jit(solution)/shard_map/all_to_all | solution.py:296
  147.9 19.9 %collective-permute-start.18 = (bf16[256,256]{1,0:T(8,128)(2,1)S(1)}, bf16[256,256]{1,0:T(8,128)(2,1)S(1)}, u32[]{:S(2)}, u32[]{:S(2)}) collective-permute-start(bf16[256,256]{1,0:T(8,128)(2,1)S(1)} %slice_bitcast_fusion.1), channel_id=1, source_target_pairs={{0,32},{16,48},{32,0},{48,16},{64,96},{80,112},{96,64},{112,80},{1... | collective-permute-start | bytes 393224 | tf_op jit(solution)/shard_map/ppermute | solution.py:32

commit v2 on v1

--- a/solution.py
+++ b/solution.py
@@ -30,6 +30,9 @@
 
 def send(value, axis, stride, size, by):
     return lax.ppermute(value, axis, shift_pairs(stride, size, by))
+
+
+LINES_X = [[4 * x + i for x in range(4)] for i in range(4)]
 
 
 def split_hi_lo(matrix):
@@ -127,9 +130,29 @@
             rows_ref[pl.ds(base + c + i, ROWS, stride=FEW), :] = time[:, i * LANES : (i + 1) * LANES]
 
 
-def conv_kernel(xf_ref, first_ref, second_ref, back_ref, last_ref, turn_ref, mixed_ref, spec_ref, x_rows, f_rows, m_rows):
+CONSTS = 5
+
+
+def fetch(sources, targets, sems):
+    copies = [pltpu.make_async_copy(src, dst, sems.at[i]) for i, (src, dst) in enumerate(zip(sources, targets))]
+    for copy in copies:
+        copy.start()
+    return copies
+
+
+def conv_kernel(xf_ref, *refs):
+    hbm, (mixed_out, spec_out) = refs[:CONSTS], refs[CONSTS : CONSTS + 2]
+    consts, (mixed_ref, spec_ref, x_rows, f_rows, m_rows, sems, mixed_sem, spec_sems) = (
+        refs[CONSTS + 2 : 2 * CONSTS + 2],
+        refs[2 * CONSTS + 2 :],
+    )
+    first_ref, second_ref, back_ref, last_ref, turn_ref = consts
+    copies = fetch(hbm, consts, sems)
     spread(lambda s: xf_ref[s, :FEW], x_rows)
     spread(lambda s: xf_ref[s, FEW:], f_rows)
+    for copy in copies:
+        copy.wait()
+    outs = []
     for base in range(0, FEW, GROUP):
         x_re, x_im = forward_group(x_rows, base, first_ref, second_ref, turn_ref)
         f_re, f_im = forward_group(f_rows, base, first_ref, second_ref, turn_ref)
@@ -138,6 +161,9 @@
         spec_ref[1, here, :] = x_im
         spec_ref[2, here, :] = f_re
         spec_ref[3, here, :] = f_im
+        out = pltpu.make_async_copy(spec_ref.at[:, here, :], spec_out.at[:, here, :], spec_sems.at[base // GROUP])
+        out.start()
+        outs.append(out)
         inverse_group(
             x_re * f_re - x_im * f_im, x_re * f_im + x_im * f_re, base, m_rows, back_ref, last_ref, turn_ref
         )
@@ -146,10 +172,21 @@
         mixed_ref[s] = value
 
     collect(m_rows, store)
-
-
-def grads_kernel(p_ref, spec_ref, first_ref, second_ref, back_ref, last_ref, turn_ref, out_ref, p_rows, i_rows, f_rows):
+    out = pltpu.make_async_copy(mixed_ref, mixed_out, mixed_sem)
+    out.start()
+    outs.append(out)
+    for out in outs:
+        out.wait()
+
+
+def grads_kernel(p_ref, *refs):
+    hbm, out_hbm = refs[: CONSTS + 1], refs[CONSTS + 1]
+    held, (out_ref, p_rows, i_rows, f_rows, sems, out_sem) = refs[CONSTS + 2 : 2 * CONSTS + 3], refs[2 * CONSTS + 3 :]
+    first_ref, second_ref, back_ref, last_ref, turn_ref, spec_ref = held
+    copies = fetch(hbm, held, sems)
     spread(lambda s: p_ref[s], p_rows)
+    for copy in copies:
+        copy.wait()
     for base in range(0, FEW, GROUP):
         p_re, p_im = forward_group(p_rows, base, first_ref, second_ref, turn_ref)
         here = pl.ds(base * ROWS, GROUP * ROWS)
@@ -168,6 +205,9 @@
 
     collect(i_rows, store_at(0))
     collect(f_rows, store_at(FEW))
+    out = pltpu.make_async_copy(out_ref, out_hbm, out_sem)
+    out.start()
+    out.wait()
 
 
 def params(mib):
@@ -178,42 +218,49 @@
     return pl.BlockSpec(memory_space=pltpu.VMEM)
 
 
+def in_hbm():
+    return pl.BlockSpec(memory_space=pltpu.HBM)
+
+
 ROWS_SCRATCH = pltpu.VMEM((ROWS * FEW, LANES), F32)
-
-
-def transform_cost(count, moved):
-    return pl.CostEstimate(flops=count * 3 * 10**8, bytes_accessed=moved, transcendentals=0)
+SPEC_SHAPE = (4, FEW * ROWS, LANES)
+DMA = pltpu.SemaphoreType.DMA
+
+
+def const_scratch():
+    return [pltpu.VMEM(c.shape, c.dtype) for c in constants()]
 
 
 def conv_call(xf):
-    consts = constants()
     return pl.pallas_call(
         conv_kernel,
-        out_shape=(
-            jax.ShapeDtypeStruct((16, FEW, TOK), BF),
-            jax.ShapeDtypeStruct((4, FEW * ROWS, LANES), F32),
-        ),
-        in_specs=[whole_vmem()] * 6,
-        out_specs=(whole_vmem(), whole_vmem()),
-        scratch_shapes=[ROWS_SCRATCH] * 3,
-        compiler_params=params(32),
-        cost_estimate=transform_cost(3, 4 << 20),
+        out_shape=(jax.ShapeDtypeStruct((16, FEW, TOK), BF), jax.ShapeDtypeStruct(SPEC_SHAPE, F32)),
+        in_specs=[whole_vmem()] + [in_hbm()] * CONSTS,
+        out_specs=(in_hbm(), in_hbm()),
+        scratch_shapes=const_scratch()
+        + [pltpu.VMEM((16, FEW, TOK), BF), pltpu.VMEM(SPEC_SHAPE, F32)]
+        + [ROWS_SCRATCH] * 3
+        + [DMA((CONSTS,)), DMA, DMA((FEW // GROUP,))],
+        compiler_params=params(60),
+        cost_estimate=pl.CostEstimate(flops=10**9, bytes_accessed=4 << 20, transcendentals=0),
         name="conv",
-    )(xf, *consts)
+    )(xf, *constants())
 
 
 def grads_call(product, spec):
-    consts = constants()
     return pl.pallas_call(
         grads_kernel,
         out_shape=jax.ShapeDtypeStruct((16, 2 * FEW, TOK), BF),
-        in_specs=[whole_vmem()] * 7,
-        out_specs=whole_vmem(),
-        scratch_shapes=[ROWS_SCRATCH] * 3,
-        compiler_params=params(32),
-        cost_estimate=transform_cost(3, 4 << 20),
+        in_specs=[whole_vmem()] + [in_hbm()] * (CONSTS + 1),
+        out_specs=in_hbm(),
+        scratch_shapes=const_scratch()
+        + [pltpu.VMEM(SPEC_SHAPE, F32), pltpu.VMEM((16, 2 * FEW, TOK), BF)]
+        + [ROWS_SCRATCH] * 3
+        + [DMA((CONSTS + 1,)), DMA],
+        compiler_params=params(57),
+        cost_estimate=pl.CostEstimate(flops=4 * 10**10, bytes_accessed=4 << 20, transcendentals=0),
         name="grads",
-    )(product, spec, *consts)
+    )(product, *constants(), spec)
 
 
 def place_of(where_ref, dy, dz):
@@ -225,69 +272,107 @@
     return jnp.bitwise_xor(core, core_from), (x, y_from), jnp.bitwise_xor(zh, zh_from)
 
 
-def grad_blocks(refs):
+def fetch_grads(grads, held, sems):
+    copies = []
     for dy in range(4):
-        own, rest = refs[2 * dy], refs[2 * dy + 1]
+        for part, target in enumerate((held.at[4 * dy], held.at[pl.ds(4 * dy + 1, 3)])):
+            copies.append(pltpu.make_async_copy(grads[2 * dy + part], target, sems.at[2 * dy + part]))
+    for copy in copies:
+        copy.start()
+    return copies
+
+
+def slots(copies):
+    for dy in range(4):
         for dz in range(4):
-            yield dy, dz, (own[...] if dz == 0 else rest[dz - 1])
+            if dz < 2:
+                copies[2 * dy + dz].wait()
+            yield dy, dz, 4 * dy + dz
 
 
 def slope_kernel(where_ref, *refs):
-    grads = refs[:8]
-    w_same, w_other, gates_ref, slope_ref, product_ref = refs[8:]
+    grads, ins_hbm, (slope_hbm, product_hbm) = refs[:8], refs[8:13], refs[13:15]
+    held, weights, gates_ref, slope_ref, product_ref, grad_sems, sems = refs[15:]
+    ins = fetch(ins_hbm, [weights.at[pl.ds(4 * i, 4)] for i in range(4)] + [gates_ref], sems)
+    copies = fetch_grads(grads, held, grad_sems)
+    for copy in ins[:4]:
+        copy.wait()
     total = None
-    for dy, dz, block in grad_blocks(grads):
-        other, (x, x_from), dzh = place_of(where_ref, dy, dz)
-        slot = jnp.bitwise_and(x + 4 - x_from, 3) * 2 + dzh
-        weight = jnp.where(other == 0, w_same[slot], w_other[slot])
-        part = dot(weight, block)
+    for dy, dz, at in slots(copies):
+        other, (_, x_from), dzh = place_of(where_ref, dy, dz)
+        slot = other * 8 + dzh * 4 + x_from
+        part = dot(weights[slot], held[at])
         total = part if total is None else total + part
     slope = total.astype(BF)
     slope_ref[...] = slope
+    ins[4].wait()
     product_ref[...] = (slope.astype(F32) * gates_ref[...].astype(F32)).astype(BF)
+    outs = [
+        pltpu.make_async_copy(product_ref, product_hbm, sems.at[5]),
+        pltpu.make_async_copy(slope_ref, slope_hbm, sems.at[6]),
+    ]
+    for out in outs:
+        out.start()
+    for out in outs:
+        out.wait()
 
 
 def weight_kernel(where_ref, *refs):
-    grads = refs[:8]
-    gates_ref, mixed_ref, slope_ref, gate_grad_ref, out_ref = refs[8:]
+    grads, ins_hbm, outs_hbm = refs[:8], refs[8:11], refs[11:14]
+    held, gates_ref, mixed_ref, slope_ref, gate_grad_ref, sums, grad_sems, sems = refs[14:]
+    ins = fetch(ins_hbm, (gates_ref, mixed_ref, slope_ref), sems)
+    copies = fetch_grads(grads, held, grad_sems)
+    for copy in ins:
+        copy.wait()
     mixed = mixed_ref[...].astype(F32)
     gated = (gates_ref[...].astype(F32) * mixed).astype(BF)
     gate_grad_ref[...] = (slope_ref[...].astype(F32) * mixed).astype(BF)
-    for dy, dz, block in grad_blocks(grads):
+    for dy, dz, at in slots(copies):
         other, (x, x_to), dzh = place_of(where_ref, dy, dz)
-        slot = jnp.bitwise_and(x_to + 4 - x, 3) * 2 + dzh
-        part = lax.dot_general(block, gated, (((1,), (1,)), ((), ())), preferred_element_type=F32)
-        out_ref[other, slot] = (part * (SEQ**-0.5)).astype(BF)
-
-
-def matmul_cost(moved):
-    return pl.CostEstimate(flops=2 * CH * TOK * 4096, bytes_accessed=moved, transcendentals=0)
-
-
-def slope_call(where, grads, w_same, w_other, gates):
+        slot = other * 8 + jnp.bitwise_and(x_to + 4 - x, 3) * 2 + dzh
+        part = lax.dot_general(held[at], gated, (((1,), (1,)), ((), ())), preferred_element_type=F32)
+        sums[slot] = (part * (SEQ**-0.5)).astype(BF)
+    sources = (gate_grad_ref, sums.at[:8], sums.at[8:])
+    outs = [pltpu.make_async_copy(src, dst, sems.at[3 + i]) for i, (src, dst) in enumerate(zip(sources, outs_hbm))]
+    for out in outs:
+        out.start()
+    for out in outs:
+        out.wait()
+
+
+HELD = pltpu.VMEM((16, CH, TOK), BF)
+SQUARES = pltpu.VMEM((16, 256, 256), BF)
+TILE = pltpu.VMEM((CH, TOK), BF)
+
+
+def matmul_cost():
+    return pl.CostEstimate(flops=2 * CH * TOK * 4096, bytes_accessed=7 << 20, transcendentals=0)
+
+
+def slope_call(where, grads, weights, gates):
     shape = jax.ShapeDtypeStruct((CH, TOK), BF)
     return pl.pallas_call(
         slope_kernel,
         out_shape=(shape, shape),
-        in_specs=[pl.BlockSpec(memory_space=pltpu.SMEM)] + [whole_vmem()] * 11,
-        out_specs=(whole_vmem(), whole_vmem()),
-        compiler_params=params(32),
-        cost_estimate=matmul_cost(7 << 20),
+        in_specs=[pl.BlockSpec(memory_space=pltpu.SMEM)] + [in_hbm()] * 13,
+        out_specs=(in_hbm(),) * 2,
+        scratch_shapes=[HELD, SQUARES, TILE, TILE, TILE, DMA((8,)), DMA((7,))],
+        compiler_params=params(57),
+        cost_estimate=matmul_cost(),
         name="slope",
-    )(where, *grads, w_same, w_other, gates)
+    )(where, *grads, *weights, gates)
 
 
 def weight_call(where, grads, gates, mixed, slope):
+    eight = jax.ShapeDtypeStruct((8, 256, 256), BF)
     return pl.pallas_call(
         weight_kernel,
-        out_shape=(
-            jax.ShapeDtypeStruct((CH, TOK), BF),
-            jax.ShapeDtypeStruct((2, 8, 256, 256), BF),
-        ),
-        in_specs=[pl.BlockSpec(memory_space=pltpu.SMEM)] + [whole_vmem()] * 11,
-        out_specs=(whole_vmem(), whole_vmem()),
-        compiler_params=params(32),
-        cost_estimate=matmul_cost(7 << 20),
+        out_shape=(jax.ShapeDtypeStruct((CH, TOK), BF), eight, eight),
+        in_specs=[pl.BlockSpec(memory_space=pltpu.SMEM)] + [in_hbm()] * 11,
+        out_specs=(in_hbm(),) * 3,
+        scratch_shapes=[HELD, TILE, TILE, TILE, TILE, SQUARES, DMA((8,)), DMA((6,))],
+        compiler_params=params(57),
+        cost_estimate=matmul_cost(),
         name="weight",
     )(where, *grads, gates, mixed, slope)
 
@@ -308,30 +393,35 @@
     tp = lax.axis_index("tp")
     where = jnp.stack([ctx // 4, (ctx // 2) % 2, ctx % 2, tp // 4, tp % 4]).astype(jnp.int32)
 
-    own = [send(out_grad, "tp", 4, 4, dy) for dy in (1, 2, 3)]
+    w_line = lax.all_gather(out_weight.T, "ctx", axis_index_groups=LINES_X)
+
     rest = jnp.stack([send(out_grad, "tp", 1, 4, dz) for dz in (1, 2, 3)])
+    up, down = send(out_grad, "tp", 4, 4, 1), send(out_grad, "tp", 4, 4, 3)
+    up, w_line, own = lax.optimization_barrier((up, w_line, out_grad))
+    near = [up, send(own, "tp", 4, 4, 2), down]
+    rest, near, w_line, inputs, filters = lax.optimization_barrier((rest, near, w_line, inputs, filters))
     rests = [send(rest, "tp", 4, 4, dy) for dy in (1, 2, 3)]
     grads = [out_grad, rest]
-    for o, r in zip(own, rests):
-        grads += [o, r]
-
-    w_own = out_weight.T
-    w_pair = jnp.stack([w_own, send(w_own, "ctx", 2, 2, 1)])
-    w_same = jnp.concatenate([w_pair] + [send(w_pair, "ctx", 4, 4, dx) for dx in (1, 2, 3)])
-    w_other = send(w_same, "ctx", 1, 2, 1)
+    for n, r in zip(near, rests):
+        grads += [n, r]
+
+    w_far = send(w_line, "ctx", 2, 2, 1)
+    weights = [w_line, w_far, send(w_line, "ctx", 1, 2, 1), send(w_far, "ctx", 1, 2, 1)]
 
     both = jnp.concatenate([inputs.reshape(16, FEW, TOK), filters.reshape(16, FEW, TOK)], axis=1)
     mixed_rows, spec = conv_call(exchange(both))
     mixed = exchange(mixed_rows).reshape(CH, TOK)
 
-    slope, product = slope_call(where, grads, w_same, w_other, gates)
-    grad_rows = grads_call(exchange(product.reshape(16, FEW, TOK)), spec)
-    gate_grad, partial = weight_call(where, grads, gates, mixed, slope)
+    slope, product = slope_call(where, grads, weights, gates)
+    product_rows = exchange(product.reshape(16, FEW, TOK))
+    gate_grad, part_same, part_other = weight_call(where, grads, gates, mixed, slope)
+    product_rows, part_same = lax.optimization_barrier((product_rows, part_same))
+    chip = add(part_same, send(part_other, "ctx", 1, 2, 1)).reshape(4, 2, 256, 256)
+    grad_rows = grads_call(product_rows, spec)
     both_grads = exchange(grad_rows)
     input_grad = both_grads[:, :FEW].reshape(CH, TOK)
     filter_grad = both_grads[:, FEW:].reshape(CH, TOK)
 
-    chip = add(partial[0], send(partial[1], "ctx", 1, 2, 1)).reshape(4, 2, 256, 256)
     line = add(chip[0], *[send(chip[dx], "ctx", 4, 4, dx) for dx in (1, 2, 3)])
     weight_grad = add(line[0], send(line[1], "ctx", 2, 2, 1))
     return (input_grad, gate_grad, filter_grad, weight_grad)

time: 172 us -> 172 us (level)
  the two profiles are of different devices: /device:TPU:67 before, /device:TPU:33 now
where the time goes in v2:
time: 172 us; the launch traced here: 171 us
  waiting for transfers between devices  69.8 us (41%)
  starting transfers between devices  54.5 us (32%)
  Pallas kernels  28.6 us (17%)
  blocking collectives  10.7 us (6%)
  local copies, waits for them, and re-layouts  4.57 us (3%)
  other arithmetic  2.1 us (1%)
    ppermute x17, waiting for transfers between devices, send(): return lax.ppermute(value, axis, shift_pairs(stride, size, by))  58.4 us
    ppermute x17, starting transfers between devices, send(): return lax.ppermute(value, axis, shift_pairs(stride, size, by))  30 us
    all_to_all x4, starting transfers between devices, exchange(): return lax.all_to_all(value, 'ctx', split_axis=0, concat_axis=0, tiled=True)  24.6 us
    all_to_all x4, waiting for transfers between devices, exchange(): return lax.all_to_all(value, 'ctx', split_axis=0, concat_axis=0, tiled=True)  11.4 us
    all_gather x1, blocking collectives, on_device(): w_line = lax.all_gather(out_weight.T, 'ctx', axis_index_groups=LINES_X)  10.7 us
    pallas_call x1, Pallas kernels, grads_call(): pl.pallas_call(grads_kernel, out_shape=jax.ShapeDtypeStruct((16, 2 * FEW,...  8.72 us
    pallas_call x1, Pallas kernels, weight_call(): pl.pallas_call(weight_kernel, out_shape=(jax.ShapeDtypeStruct((CH, TOK),...  7.53 us
    pallas_call x1, Pallas kernels, conv_call(): pl.pallas_call(conv_kernel, out_shape=(jax.ShapeDtypeStruct((16, FEW, TOK...  6.67 us
  transfers between devices with their start and end apart: 21, of which 8 were waited for; matrix products, arithmetic and copies ran while one was open for 2% of the time, Pallas kernels for 17%

profile of v2, /device:TPU:33, one launch (start us, length us, event | category | flops | bytes accessed | tf_op | source)
XLA Modules:
  0.0 171.2 jit_solution(5294530017313053092)
XLA Ops:
  0.6 0.0 copy-start.9
  0.6 0.0 copy-start.10
  0.7 1.4 collective-permute-start.3
  2.0 1.5 collective-permute-start.5
  3.6 0.0 collective-permute-start.2
  3.6 3.0 %collective-permute-start.1 = (bf16[256,512]{1,0:T(8,128)(2,1)}, bf16[256,512]{1,0:T(8,128)(2,1)S(1)}, u32[]{:S(2)}, u32[]{:S(2)}) collective-permute-start(bf16[256,512]{1,0:T(8,128)(2,1)} %refs_0_.5), channel_id=1, source_target_pairs={{0,2},{1,3},{2,0},{3,1},{4,6},{5,7},{6,4},{7,5},{8,10},{9,11},{10,... | collective-permute-start | bytes 786440 | tf_op jit(solution)/shard_map/ppermute | solution.py:32
  6.5 2.4 %collective-permute-start = (bf16[256,512]{1,0:T(8,128)(2,1)}, bf16[256,512]{1,0:T(8,128)(2,1)S(1)}, u32[]{:S(2)}, u32[]{:S(2)}) collective-permute-start(bf16[256,512]{1,0:T(8,128)(2,1)} %refs_0_.5), channel_id=1, source_target_pairs={{0,1},{1,2},{2,3},{3,0},{4,5},{5,6},{6,7},{7,4},{8,9},{9,10},{10,1... | collective-permute-start | bytes 786440 | tf_op jit(solution)/shard_map/ppermute | solution.py:32
  8.9 10.7 %all-gather = bf16[1024,256]{0,1:T(8,128)(2,1)S(1)} all-gather(bf16[256,256]{0,1:T(8,128)(2,1)} %bitcast.32), channel_id=2, replica_groups={{0,64,128,192},{16,80,144,208},{32,96,160,224},{48,112,176,240},{1,65,1..., dimensions={0}, use_global_device_ids=true | all-gather | bytes 655360 | tf_op jit(solution)/shard_map/all_gather | solution.py:396
  19.6 1.0 copy.14
  20.6 0.0 collective-permute-done.3.refs_2_
  20.6 1.6 collective-permute-start.4
  22.2 0.0 collective-permute-done.2
  22.2 1.0 collective-permute-done.1
  23.2 5.6 %collective-permute-done = bf16[256,512]{1,0:T(8,128)(2,1)S(1)} collective-permute-done((bf16[256,512]{1,0:T(8,128)(2,1)}, bf16[256,512]{1,0:T(8,128)(2,1)S(1)}, u32[]{:S(2)}, u32[]{:S(2)}) %collective-permute-start) | collective-permute-done | bytes 262176 | tf_op jit(solution)/shard_map/ppermute | solution.py:32
  28.8 0.1 pad_maximum_fusion.refs_1_
  28.9 0.0 collective-permute-done.5.refs_6_
  28.9 0.0 copy-start.7
  28.9 0.0 collective-permute-done.4.refs_4_
  29.0 0.9 pad_maximum_fusion.1
  29.9 11.9 %all-to-all-start.1 = ((bf16[16,32,512]{2,1,0:T(8,128)(2,1)}), bf16[16,32,512]{2,1,0:T(8,128)(2,1)}, u32[]{:S(2)}, u32[]{:S(2)}) async-start(bf16[16,32,512]{2,1,0:T(8,128)(2,1)} %pad_maximum_fusion.1), calls=%async_computation.1 | async-start | bytes 1048576 | tf_op jit(solution)/shard_map/all_to_all | solution.py:381
  41.9 5.4 %collective-permute-start.9 = (bf16[4,256,256]{2,1,0:T(8,128)(2,1)}, bf16[4,256,256]{2,1,0:T(8,128)(2,1)}, u32[]{:S(2)}, u32[]{:S(2)}) collective-permute-start(bf16[4,256,256]{2,1,0:T(8,128)(2,1)} %bitcast.9.refs_8_), channel_id=1, source_target_pairs={{0,32},{16,48},{32,0},{48,16},{64,96},{80,112},{96,64},{112,80},{1... | collective-permute-start | bytes 1572872 | tf_op jit(solution)/shard_map/ppermute | solution.py:32
  47.2 1.5 collective-permute-start.8
  48.8 0.3 collective-permute-start.7
  49.1 0.7 collective-permute-start.6
  49.8 1.5 collective-permute-start.10
  51.3 30.5 %collective-permute-done.9.refs_9_ = bf16[4,256,256]{2,1,0:T(8,128)(2,1)} collective-permute-done((bf16[4,256,256]{2,1,0:T(8,128)(2,1)}, bf16[4,256,256]{2,1,0:T(8,128)(2,1)}, u32[]{:S(2)}, u32[]{:S(2)}) %collective-permute-start.9) | collective-permute-done | bytes 524320 | tf_op jit(solution)/shard_map/ppermute | solution.py:32
  81.8 0.9 collective-permute-start.11
  82.7 0.0 all-to-all-done.1.xf_ref
  82.7 6.7 %conv.1 = (bf16[16,16,512]{2,1,0:T(8,128)(2,1)}, f32[4,1024,128]{2,1,0:T(8,128)}) custom-call(bf16[16,32,512]{2,1,0:T(8,128)(2,1)} %all-to-all-done.1.xf_ref, bf16[128,128]{1,0:T(8,128)(2,1)} %constant.70.clone.refs_0_, bf16[768,256]{1,0:T(8,128)(2,1)} %constant.71.clone.refs_1_, bf16[768,256]{1,0:T(8,128)(2,1)} %constant.72.clone.refs_2_, ...), custom_call_target="tpu_custom_call" | custom-call | flops 1000000000 | bytes 4194304 | tf_op jit(solution)/shard_map/conv/pallas_call | solution.py:235
  89.4 4.6 %all-to-all-start.2 = ((bf16[16,16,512]{2,1,0:T(8,128)(2,1)}), bf16[16,16,512]{2,1,0:T(8,128)(2,1)S(1)}, u32[]{:S(2)}, u32[]{:S(2)}) async-start(bf16[16,16,512]{2,1,0:T(8,128)(2,1)} %get-tuple-element.34), calls=%async_computation.2 | async-start | bytes 524288 | tf_op jit(solution)/shard_map/all_to_all | solution.py:381
  94.0 0.6 stack.35.where_ref
  94.6 0.0 collective-permute-done.10.refs_10_
  94.6 0.0 collective-permute-done.8.refs_7_
  94.6 0.0 collective-permute-done.7.refs_5_
  94.6 0.0 collective-permute-done.6.refs_3_
  94.6 0.0 collective-permute-done.11.refs_11_
  94.7 0.8 copy-done.1
  95.5 0.3 copy-done.2
  95.7 0.3 copy-done.3
  96.0 5.7 %slope.1 = (bf16[256,512]{1,0:T(8,128)(2,1)}, bf16[256,512]{1,0:T(8,128)(2,1)}) custom-call(s32[5]{0:T(128)} %stack.35.where_ref, bf16[256,512]{1,0:T(8,128)(2,1)} %refs_0_.5, bf16[3,256,512]{2,1,0:T(8,128)(2,1)} %copy-done, bf16[256,512]{1,0:T(8,128)(2,1)} %copy-done.6, bf16[3,256,512]{2,1,0:T(8,128)(2,1)} %copy-done.3, ...), custom_call_target="tpu_custom_call" | custom-call | flops 1073741824 | bytes 7340032 | tf_op jit(solution)/shard_map/slope/pallas_call | solution.py:354
  101.7 5.7 %all-to-all-done.2 = bf16[16,16,512]{2,1,0:T(8,128)(2,1)S(1)} async-done(((bf16[16,16,512]{2,1,0:T(8,128)(2,1)}), bf16[16,16,512]{2,1,0:T(8,128)(2,1)S(1)}, u32[]{:S(2)}, u32[]{:S(2)}) %all-to-all-start.2) | async-done | bytes 262176 | tf_op jit(solution)/shard_map/all_to_all | solution.py:381
  107.4 4.0 %all-to-all-start = ((bf16[16,16,512]{2,1,0:T(8,128)(2,1)}), bf16[16,16,512]{2,1,0:T(8,128)(2,1)S(1)}, u32[]{:S(2)}, u32[]{:S(2)}) async-start(bf16[16,16,512]{2,1,0:T(8,128)(2,1)} %bitcast.24), calls=%async_computation | async-start | bytes 524288 | tf_op jit(solution)/shard_map/all_to_all | solution.py:381
  111.4 0.0 copy-done.5
  111.4 7.5 %weight.1 = (bf16[256,512]{1,0:T(8,128)(2,1)}, bf16[8,256,256]{2,1,0:T(8,128)(2,1)}, bf16[8,256,256]{2,1,0:T(8,128)(2,1)}) custom-call(s32[5]{0:T(128)} %stack.35.where_ref, bf16[256,512]{1,0:T(8,128)(2,1)} %refs_0_.5, bf16[3,256,512]{2,1,0:T(8,128)(2,1)} %copy-done, bf16[256,512]{1,0:T(8,128)(2,1)} %copy-done.6, bf16[3,256,512]{2,1,0:T(8,128)(2,1)} %copy-done.3, ...), custom_call_target="tpu_custom_call" | custom-call | flops 1073741824 | bytes 7340032 | tf_op jit(solution)/shard_map/weight/pallas_call | solution.py:368
  118.9 0.2 collective-permute-start.12
  119.2 5.7 %all-to-all-done.p_ref = bf16[16,16,512]{2,1,0:T(8,128)(2,1)S(1)} async-done(((bf16[16,16,512]{2,1,0:T(8,128)(2,1)}), bf16[16,16,512]{2,1,0:T(8,128)(2,1)S(1)}, u32[]{:S(2)}, u32[]{:S(2)}) %all-to-all-start) | async-done | bytes 262176 | tf_op jit(solution)/shard_map/all_to_all | solution.py:381
  124.8 0.7 copy-done.8
  125.5 8.7 %grads.1 = bf16[16,32,512]{2,1,0:T(8,128)(2,1)} custom-call(bf16[16,16,512]{2,1,0:T(8,128)(2,1)} %copy-done.8, bf16[128,128]{1,0:T(8,128)(2,1)} %constant.70.clone.refs_0_, bf16[768,256]{1,0:T(8,128)(2,1)} %constant.71.clone.refs_1_, bf16[768,256]{1,0:T(8,128)(2,1)} %constant.72.clone.refs_2_, bf16[64,384]{1,0:T(8,128)(2,1)} %constant.73.clone.refs_3_, ...), custom_call_target="tpu_custom_call" | custom-call | flops 40000000000 | bytes 4194304 | tf_op jit(solution)/shard_map/grads/pallas_call | solution.py:251
  134.3 4.0 %all-to-all-start.3 = ((bf16[16,32,512]{2,1,0:T(8,128)(2,1)}), bf16[16,32,512]{2,1,0:T(8,128)(2,1)S(1)}, u32[]{:S(2)}, u32[]{:S(2)}) async-start(bf16[16,32,512]{2,1,0:T(8,128)(2,1)} %grads.1), calls=%async_computation.3 | async-start | bytes 1048576 | tf_op jit(solution)/shard_map/all_to_all | solution.py:381
  138.3 0.0 collective-permute-done.12
  138.3 0.3 add_convert_fusion
  138.6 0.1 fusion.1
  138.6 1.5 collective-permute-start.13
  140.1 1.3 collective-permute-start.15
  141.4 1.7 collective-permute-start.14
  143.1 7.3 %collective-permute-done.13 = bf16[2,256,256]{2,1,0:T(8,128)(2,1)S(1)} collective-permute-done((bf16[2,256,256]{2,1,0:T(8,128)(2,1)S(1)}, bf16[2,256,256]{2,1,0:T(8,128)(2,1)S(1)}, u32[]{:S(2)}, u32[]{:S(2)}) %collective-permute-start.13) | collective-permute-done | bytes 262176 | tf_op jit(solution)/shard_map/ppermute | solution.py:32
  150.4 0.0 collective-permute-done.15
  150.4 8.6 %collective-permute-done.14 = bf16[2,256,256]{2,1,0:T(8,128)(2,1)S(1)} collective-permute-done((bf16[2,256,256]{2,1,0:T(8,128)(2,1)S(1)}, bf16[2,256,256]{2,1,0:T(8,128)(2,1)S(1)}, u32[]{:S(2)}, u32[]{:S(2)}) %collective-permute-start.14) | collective-permute-done | bytes 262176 | tf_op jit(solution)/shard_map/ppermute | solution.py:32
  159.0 0.1 add_convert_fusion.1
  159.2 5.2 %collective-permute-start.16 = (bf16[256,256]{1,0:T(8,128)(2,1)S(1)}, bf16[256,256]{1,0:T(8,128)(2,1)S(1)}, u32[]{:S(2)}, u32[]{:S(2)}) collective-permute-start(bf16[256,256]{1,0:T(8,128)(2,1)S(1)} %slice_bitcast_fusion), channel_id=1, source_target_pairs={{0,32},{16,48},{32,0},{48,16},{64,96},{80,112},{96,64},{112,80},{1... | collective-permute-start | bytes 393224 | tf_op jit(solution)/shard_map/ppermute | solution.py:32
  164.4 0.0 all-to-all-done.3
  164.4 0.8 fusion.2
  165.2 5.3 %collective-permute-done.16 = bf16[256,256]{1,0:T(8,128)(2,1)S(1)} collective-permute-done((bf16[256,256]{1,0:T(8,128)(2,1)S(1)}, bf16[256,256]{1,0:T(8,128)(2,1)S(1)}, u32[]{:S(2)}, u32[]{:S(2)}) %collective-permute-start.16) | collective-permute-done | bytes 131104 | tf_op jit(solution)/shard_map/ppermute | solution.py:32
  170.5 0.7 fusion
  (15 shorter events, 0.0 us)
Async XLA Ops:
  0.6 28.3 %copy-start.9 = (bf16[256,512]{1,0:T(8,128)(2,1)S(1)}, bf16[256,512]{1,0:T(8,128)(2,1)}, u32[]{:S(2)}) copy-start(bf16[256,512]{1,0:T(8,128)(2,1)} %param.12) | copy-start | bytes 786436
  0.6 28.3 %copy-start.10 = (bf16[256,512]{1,0:T(8,128)(2,1)S(1)}, bf16[256,512]{1,0:T(8,128)(2,1)}, u32[]{:S(2)}) copy-start(bf16[256,512]{1,0:T(8,128)(2,1)} %param.10) | copy-start | bytes 786436
  0.7 20.0 %collective-permute-start.3 = (bf16[256,512]{1,0:T(8,128)(2,1)}, bf16[256,512]{1,0:T(8,128)(2,1)S(1)}, u32[]{:S(2)}, u32[]{:S(2)}) collective-permute-start(bf16[256,512]{1,0:T(8,128)(2,1)} %refs_0_.5), channel_id=1, source_target_pairs={{0,4},{1,5},{2,6},{3,7},{4,8},{5,9},{6,10},{7,11},{8,12},{9,13},{1... | collective-permute-start | bytes 786440 | tf_op jit(solution)/shard_map/ppermute | solution.py:32
  2.0 26.9 %collective-permute-start.5 = (bf16[256,512]{1,0:T(8,128)(2,1)}, bf16[256,512]{1,0:T(8,128)(2,1)S(1)}, u32[]{:S(2)}, u32[]{:S(2)}) collective-permute-start(bf16[256,512]{1,0:T(8,128)(2,1)} %refs_0_.5), channel_id=1, source_target_pairs={{0,12},{1,13},{2,14},{3,15},{4,0},{5,1},{6,2},{7,3},{8,4},{9,5},{1... | collective-permute-start | bytes 786440 | tf_op jit(solution)/shard_map/ppermute | solution.py:32
  3.6 18.7 %collective-permute-start.2 = (bf16[256,512]{1,0:T(8,128)(2,1)}, bf16[256,512]{1,0:T(8,128)(2,1)S(1)}, u32[]{:S(2)}, u32[]{:S(2)}) collective-permute-start(bf16[256,512]{1,0:T(8,128)(2,1)} %refs_0_.5), channel_id=1, source_target_pairs={{0,3},{1,0},{2,1},{3,2},{4,7},{5,4},{6,5},{7,6},{8,11},{9,8},{10,9... | collective-permute-start | bytes 786440 | tf_op jit(solution)/shard_map/ppermute | solution.py:32
  3.6 19.6 %collective-permute-start.1 = (bf16[256,512]{1,0:T(8,128)(2,1)}, bf16[256,512]{1,0:T(8,128)(2,1)S(1)}, u32[]{:S(2)}, u32[]{:S(2)}) collective-permute-start(bf16[256,512]{1,0:T(8,128)(2,1)} %refs_0_.5), channel_id=1, source_target_pairs={{0,2},{1,3},{2,0},{3,1},{4,6},{5,7},{6,4},{7,5},{8,10},{9,11},{10,... | collective-permute-start | bytes 786440 | tf_op jit(solution)/shard_map/ppermute | solution.py:32
  6.5 22.3 %collective-permute-start = (bf16[256,512]{1,0:T(8,128)(2,1)}, bf16[256,512]{1,0:T(8,128)(2,1)S(1)}, u32[]{:S(2)}, u32[]{:S(2)}) collective-permute-start(bf16[256,512]{1,0:T(8,128)(2,1)} %refs_0_.5), channel_id=1, source_target_pairs={{0,1},{1,2},{2,3},{3,0},{4,5},{5,6},{6,7},{7,4},{8,9},{9,10},{10,1... | collective-permute-start | bytes 786440 | tf_op jit(solution)/shard_map/ppermute | solution.py:32
  20.6 8.2 %copy-start.6 = (bf16[256,512]{1,0:T(8,128)(2,1)}, bf16[256,512]{1,0:T(8,128)(2,1)S(1)}, u32[]{:S(2)}) copy-start(bf16[256,512]{1,0:T(8,128)(2,1)S(1)} %collective-permute-done.3.refs_2_) | copy-start | bytes 786436
  20.6 8.3 %collective-permute-start.4 = (bf16[256,512]{1,0:T(8,128)(2,1)}, bf16[256,512]{1,0:T(8,128)(2,1)}, u32[]{:S(2)}, u32[]{:S(2)}) collective-permute-start(bf16[256,512]{1,0:T(8,128)(2,1)} %refs_0_.5), channel_id=1, source_target_pairs={{0,8},{1,9},{2,10},{3,11},{4,12},{5,13},{6,14},{7,15},{8,0},{9,1},... | collective-permute-start | bytes 786440 | tf_op jit(solution)/shard_map/ppermute | solution.py:32
  28.9 60.4 %copy-start = (bf16[3,256,512]{2,1,0:T(8,128)(2,1)}, bf16[3,256,512]{2,1,0:T(8,128)(2,1)S(1)}, u32[]{:S(2)}) copy-start(bf16[3,256,512]{2,1,0:T(8,128)(2,1)S(1)} %pad_maximum_fusion.refs_1_) | copy-start | bytes 2359300
  28.9 12.9 %copy-start.7 = (bf16[256,512]{1,0:T(8,128)(2,1)}, bf16[256,512]{1,0:T(8,128)(2,1)S(1)}, u32[]{:S(2)}) copy-start(bf16[256,512]{1,0:T(8,128)(2,1)S(1)} %collective-permute-done.5.refs_6_) | copy-start | bytes 786436
  29.9 52.8 %all-to-all-start.1 = ((bf16[16,32,512]{2,1,0:T(8,128)(2,1)}), bf16[16,32,512]{2,1,0:T(8,128)(2,1)}, u32[]{:S(2)}, u32[]{:S(2)}) async-start(bf16[16,32,512]{2,1,0:T(8,128)(2,1)} %pad_maximum_fusion.1), calls=%async_computation.1 | async-start | bytes 1048576 | tf_op jit(solution)/shard_map/all_to_all | solution.py:381
  41.9 39.9 %collective-permute-start.9 = (bf16[4,256,256]{2,1,0:T(8,128)(2,1)}, bf16[4,256,256]{2,1,0:T(8,128)(2,1)}, u32[]{:S(2)}, u32[]{:S(2)}) collective-permute-start(bf16[4,256,256]{2,1,0:T(8,128)(2,1)} %bitcast.9.refs_8_), channel_id=1, source_target_pairs={{0,32},{16,48},{32,0},{48,16},{64,96},{80,112},{96,64},{112,80},{1... | collective-permute-start | bytes 1572872 | tf_op jit(solution)/shard_map/ppermute | solution.py:32
  47.2 47.4 %collective-permute-start.8 = (bf16[3,256,512]{2,1,0:T(8,128)(2,1)S(1)}, bf16[3,256,512]{2,1,0:T(8,128)(2,1)S(1)}, u32[]{:S(2)}, u32[]{:S(2)}) collective-permute-start(bf16[3,256,512]{2,1,0:T(8,128)(2,1)S(1)} %pad_maximum_fusion.refs_1_), channel_id=1, source_target_pairs={{0,12},{1,13},{2,14},{3,15},{4,0},{5,1},{6,2},{7,3},{8,4},{9,5},{1... | collective-permute-start | bytes 2359304 | tf_op jit(solution)/shard_map/ppermute | solution.py:32
  48.8 45.8 %collective-permute-start.7 = (bf16[3,256,512]{2,1,0:T(8,128)(2,1)S(1)}, bf16[3,256,512]{2,1,0:T(8,128)(2,1)S(1)}, u32[]{:S(2)}, u32[]{:S(2)}) collective-permute-start(bf16[3,256,512]{2,1,0:T(8,128)(2,1)S(1)} %pad_maximum_fusion.refs_1_), channel_id=1, source_target_pairs={{0,8},{1,9},{2,10},{3,11},{4,12},{5,13},{6,14},{7,15},{8,0},{9,1},... | collective-permute-start | bytes 2359304 | tf_op jit(solution)/shard_map/ppermute | solution.py:32
  49.1 45.5 %collective-permute-start.6 = (bf16[3,256,512]{2,1,0:T(8,128)(2,1)S(1)}, bf16[3,256,512]{2,1,0:T(8,128)(2,1)S(1)}, u32[]{:S(2)}, u32[]{:S(2)}) collective-permute-start(bf16[3,256,512]{2,1,0:T(8,128)(2,1)S(1)} %pad_maximum_fusion.refs_1_), channel_id=1, source_target_pairs={{0,4},{1,5},{2,6},{3,7},{4,8},{5,9},{6,10},{7,11},{8,12},{9,13},{1... | collective-permute-start | bytes 2359304 | tf_op jit(solution)/shard_map/ppermute | solution.py:32
  49.8 44.8 %collective-permute-start.10 = (bf16[4,256,256]{2,1,0:T(8,128)(2,1)}, bf16[4,256,256]{2,1,0:T(8,128)(2,1)}, u32[]{:S(2)}, u32[]{:S(2)}) collective-permute-start(bf16[4,256,256]{2,1,0:T(8,128)(2,1)} %bitcast.9.refs_8_), channel_id=1, source_target_pairs={{0,16},{16,0},{32,48},{48,32},{64,80},{80,64},{96,112},{112,96},{1... | collective-permute-start | bytes 1572872 | tf_op jit(solution)/shard_map/ppermute | solution.py:32
  81.8 12.8 %collective-permute-start.11 = (bf16[4,256,256]{2,1,0:T(8,128)(2,1)}, bf16[4,256,256]{2,1,0:T(8,128)(2,1)}, u32[]{:S(2)}, u32[]{:S(2)}) collective-permute-start(bf16[4,256,256]{2,1,0:T(8,128)(2,1)} %collective-permute-done.9.refs_9_), channel_id=1, source_target_pairs={{0,16},{16,0},{32,48},{48,32},{64,80},{80,64},{96,112},{112,96},{1... | collective-permute-start | bytes 1572872 | tf_op jit(solution)/shard_map/ppermute | solution.py:32
  89.4 18.1 %all-to-all-start.2 = ((bf16[16,16,512]{2,1,0:T(8,128)(2,1)}), bf16[16,16,512]{2,1,0:T(8,128)(2,1)S(1)}, u32[]{:S(2)}, u32[]{:S(2)}) async-start(bf16[16,16,512]{2,1,0:T(8,128)(2,1)} %get-tuple-element.34), calls=%async_computation.2 | async-start | bytes 524288 | tf_op jit(solution)/shard_map/all_to_all | solution.py:381
  94.6 0.9 copy-start.1
  94.6 1.1 copy-start.2
  94.6 1.4 copy-start.3
  107.4 4.0 %copy-start.5 = (bf16[16,16,512]{2,1,0:T(8,128)(2,1)}, bf16[16,16,512]{2,1,0:T(8,128)(2,1)S(1)}, u32[]{:S(2)}) copy-start(bf16[16,16,512]{2,1,0:T(8,128)(2,1)S(1)} %all-to-all-done.2) | copy-start | bytes 786436
  107.4 17.4 %all-to-all-start = ((bf16[16,16,512]{2,1,0:T(8,128)(2,1)}), bf16[16,16,512]{2,1,0:T(8,128)(2,1)S(1)}, u32[]{:S(2)}, u32[]{:S(2)}) async-start(bf16[16,16,512]{2,1,0:T(8,128)(2,1)} %bitcast.24), calls=%async_computation | async-start | bytes 524288 | tf_op jit(solution)/shard_map/all_to_all | solution.py:381
  118.9 19.3 %collective-permute-start.12 = (bf16[8,256,256]{2,1,0:T(8,128)(2,1)}, bf16[8,256,256]{2,1,0:T(8,128)(2,1)S(1)}, u32[]{:S(2)}, u32[]{:S(2)}) collective-permute-start(bf16[8,256,256]{2,1,0:T(8,128)(2,1)} %get-tuple-element.41), channel_id=1, source_target_pairs={{0,16},{16,0},{32,48},{48,32},{64,80},{80,64},{96,112},{112,96},{1... | collective-permute-start | bytes 3145736 | tf_op jit(solution)/shard_map/ppermute | solution.py:32
  124.8 0.7 copy-start.8
  125.5 12.8 %copy-start.4 = (bf16[8,256,256]{2,1,0:T(8,128)(2,1)S(1)}, bf16[8,256,256]{2,1,0:T(8,128)(2,1)}, u32[]{:S(2)}) copy-start(bf16[8,256,256]{2,1,0:T(8,128)(2,1)} %get-tuple-element.40) | copy-start | bytes 3145732
  134.3 30.1 %all-to-all-start.3 = ((bf16[16,32,512]{2,1,0:T(8,128)(2,1)}), bf16[16,32,512]{2,1,0:T(8,128)(2,1)S(1)}, u32[]{:S(2)}, u32[]{:S(2)}) async-start(bf16[16,32,512]{2,1,0:T(8,128)(2,1)} %grads.1), calls=%async_computation.3 | async-start | bytes 1048576 | tf_op jit(solution)/shard_map/all_to_all | solution.py:381
  138.6 11.8 %collective-permute-start.13 = (bf16[2,256,256]{2,1,0:T(8,128)(2,1)S(1)}, bf16[2,256,256]{2,1,0:T(8,128)(2,1)S(1)}, u32[]{:S(2)}, u32[]{:S(2)}) collective-permute-start(bf16[2,256,256]{2,1,0:T(8,128)(2,1)S(1)} %get-tuple-element.42), channel_id=1, source_target_pairs={{0,64},{16,80},{32,96},{48,112},{64,128},{80,144},{96,160},{112,17... | collective-permute-start | bytes 786440 | tf_op jit(solution)/shard_map/ppermute | solution.py:32
  140.1 10.3 %collective-permute-start.15 = (bf16[2,256,256]{2,1,0:T(8,128)(2,1)S(1)}, bf16[2,256,256]{2,1,0:T(8,128)(2,1)S(1)}, u32[]{:S(2)}, u32[]{:S(2)}) collective-permute-start(bf16[2,256,256]{2,1,0:T(8,128)(2,1)S(1)} %get-tuple-element.43), channel_id=1, source_target_pairs={{0,192},{16,208},{32,224},{48,240},{64,0},{80,16},{96,32},{112,48}... | collective-permute-start | bytes 786440 | tf_op jit(solution)/shard_map/ppermute | solution.py:32
  141.4 17.6 %collective-permute-start.14 = (bf16[2,256,256]{2,1,0:T(8,128)(2,1)S(1)}, bf16[2,256,256]{2,1,0:T(8,128)(2,1)S(1)}, u32[]{:S(2)}, u32[]{:S(2)}) collective-permute-start(bf16[2,256,256]{2,1,0:T(8,128)(2,1)S(1)} %get-tuple-element.44), channel_id=1, source_target_pairs={{0,128},{16,144},{32,160},{48,176},{64,192},{80,208},{96,224},{112... | collective-permute-start | bytes 786440 | tf_op jit(solution)/shard_map/ppermute | solution.py:32
  159.2 11.4 %collective-permute-start.16 = (bf16[256,256]{1,0:T(8,128)(2,1)S(1)}, bf16[256,256]{1,0:T(8,128)(2,1)S(1)}, u32[]{:S(2)}, u32[]{:S(2)}) collective-permute-start(bf16[256,256]{1,0:T(8,128)(2,1)S(1)} %slice_bitcast_fusion), channel_id=1, source_target_pairs={{0,32},{16,48},{32,0},{48,16},{64,96},{80,112},{96,64},{112,80},{1... | collective-permute-start | bytes 393224 | tf_op jit(solution)/shard_map/ppermute | solution.py:32

commit v3 on v2

--- a/solution.py
+++ b/solution.py
@@ -179,14 +179,10 @@
         out.wait()
 
 
-def grads_kernel(p_ref, *refs):
-    hbm, out_hbm = refs[: CONSTS + 1], refs[CONSTS + 1]
-    held, (out_ref, p_rows, i_rows, f_rows, sems, out_sem) = refs[CONSTS + 2 : 2 * CONSTS + 3], refs[2 * CONSTS + 3 :]
-    first_ref, second_ref, back_ref, last_ref, turn_ref, spec_ref = held
-    copies = fetch(hbm, held, sems)
+def grads_kernel(
+    p_ref, first_ref, second_ref, back_ref, last_ref, turn_ref, spec_ref, out_ref, p_rows, i_rows, f_rows
+):
     spread(lambda s: p_ref[s], p_rows)
-    for copy in copies:
-        copy.wait()
     for base in range(0, FEW, GROUP):
         p_re, p_im = forward_group(p_rows, base, first_ref, second_ref, turn_ref)
         here = pl.ds(base * ROWS, GROUP * ROWS)
@@ -205,9 +201,6 @@
 
     collect(i_rows, store_at(0))
     collect(f_rows, store_at(FEW))
-    out = pltpu.make_async_copy(out_ref, out_hbm, out_sem)
-    out.start()
-    out.wait()
 
 
 def params(mib):
@@ -251,25 +244,13 @@
     return pl.pallas_call(
         grads_kernel,
         out_shape=jax.ShapeDtypeStruct((16, 2 * FEW, TOK), BF),
-        in_specs=[whole_vmem()] + [in_hbm()] * (CONSTS + 1),
-        out_specs=in_hbm(),
-        scratch_shapes=const_scratch()
-        + [pltpu.VMEM(SPEC_SHAPE, F32), pltpu.VMEM((16, 2 * FEW, TOK), BF)]
-        + [ROWS_SCRATCH] * 3
-        + [DMA((CONSTS + 1,)), DMA],
-        compiler_params=params(57),
-        cost_estimate=pl.CostEstimate(flops=4 * 10**10, bytes_accessed=4 << 20, transcendentals=0),
+        in_specs=[whole_vmem()] * (CONSTS + 2),
+        out_specs=whole_vmem(),
+        scratch_shapes=[ROWS_SCRATCH] * 3,
+        compiler_params=params(24),
+        cost_estimate=pl.CostEstimate(flops=10**10, bytes_accessed=4 << 20, transcendentals=0),
         name="grads",
     )(product, *constants(), spec)
-
-
-def place_of(where_ref, dy, dz):
-    x, zh, core, y, zl = (where_ref[i] for i in range(5))
-    y_from = jnp.bitwise_and(y + 4 - dy, 3)
-    zl_from = jnp.bitwise_and(zl + 4 - dz, 3)
-    zh_from = jnp.right_shift(zl_from, 1)
-    core_from = jnp.bitwise_and(zl_from, 1)
-    return jnp.bitwise_xor(core, core_from), (x, y_from), jnp.bitwise_xor(zh, zh_from)
 
 
 def fetch_grads(grads, held, sems):
@@ -282,60 +263,60 @@
     return copies
 
 
-def slots(copies):
-    for dy in range(4):
-        for dz in range(4):
-            if dz < 2:
-                copies[2 * dy + dz].wait()
-            yield dy, dz, 4 * dy + dz
-
-
-def slope_kernel(where_ref, *refs):
-    grads, ins_hbm, (slope_hbm, product_hbm) = refs[:8], refs[8:13], refs[13:15]
-    held, weights, gates_ref, slope_ref, product_ref, grad_sems, sems = refs[15:]
-    ins = fetch(ins_hbm, [weights.at[pl.ds(4 * i, 4)] for i in range(4)] + [gates_ref], sems)
+def weight_slot(where_ref, dy, dz):
+    zh, core, y, zl = (where_ref[i] for i in range(1, 5))
+    x_from = jnp.bitwise_and(y + 4 - dy, 3)
+    zl_from = jnp.bitwise_and(zl + 4 - dz, 3)
+    zh_from = jnp.right_shift(zl_from, 1)
+    core_from = jnp.bitwise_and(zl_from, 1)
+    return jnp.bitwise_xor(core, core_from) * 8 + jnp.bitwise_xor(zh, zh_from) * 4 + x_from
+
+
+def grad_slot(where_ref, other, dx, dzh):
+    x, zh, core, y, zl = (where_ref[i] for i in range(5))
+    y_from = jnp.bitwise_and(x + dx, 3)
+    zl_from = jnp.bitwise_xor(zh, dzh) * 2 + jnp.bitwise_xor(core, other)
+    return jnp.bitwise_and(y + 4 - y_from, 3) * 4 + jnp.bitwise_and(zl + 4 - zl_from, 3)
+
+
+def products_kernel(where_ref, *refs):
+    grads, ins_hbm = refs[:8], refs[8:14]
+    product_hbm, gate_grad_hbm, other_hbm, same_hbm = refs[14:18]
+    held, weights, gates_ref, mixed_ref, product_ref, gate_grad_ref, sums, grad_sems, sems, out_sems = refs[18:]
+    targets = [weights.at[pl.ds(4 * i, 4)] for i in range(4)] + [gates_ref, mixed_ref]
+    ins = fetch(ins_hbm, targets, sems)
     copies = fetch_grads(grads, held, grad_sems)
     for copy in ins[:4]:
         copy.wait()
     total = None
-    for dy, dz, at in slots(copies):
-        other, (_, x_from), dzh = place_of(where_ref, dy, dz)
-        slot = other * 8 + dzh * 4 + x_from
-        part = dot(weights[slot], held[at])
+    for dy in range(4):
+        copies[2 * dy].wait()
+        copies[2 * dy + 1].wait()
+        weight = jnp.concatenate([weights[weight_slot(where_ref, dy, dz)] for dz in range(4)], axis=1)
+        part = dot(weight, held[4 * dy : 4 * dy + 4].reshape(4 * CH, TOK))
         total = part if total is None else total + part
-    slope = total.astype(BF)
-    slope_ref[...] = slope
+    slope = total.astype(BF).astype(F32)
     ins[4].wait()
-    product_ref[...] = (slope.astype(F32) * gates_ref[...].astype(F32)).astype(BF)
-    outs = [
-        pltpu.make_async_copy(product_ref, product_hbm, sems.at[5]),
-        pltpu.make_async_copy(slope_ref, slope_hbm, sems.at[6]),
-    ]
-    for out in outs:
-        out.start()
-    for out in outs:
-        out.wait()
-
-
-def weight_kernel(where_ref, *refs):
-    grads, ins_hbm, outs_hbm = refs[:8], refs[8:11], refs[11:14]
-    held, gates_ref, mixed_ref, slope_ref, gate_grad_ref, sums, grad_sems, sems = refs[14:]
-    ins = fetch(ins_hbm, (gates_ref, mixed_ref, slope_ref), sems)
-    copies = fetch_grads(grads, held, grad_sems)
-    for copy in ins:
-        copy.wait()
+    gates = gates_ref[...].astype(F32)
+    product_ref[...] = (slope * gates).astype(BF)
+    outs = [pltpu.make_async_copy(product_ref, product_hbm, out_sems.at[0])]
+    outs[0].start()
+    ins[5].wait()
     mixed = mixed_ref[...].astype(F32)
-    gated = (gates_ref[...].astype(F32) * mixed).astype(BF)
-    gate_grad_ref[...] = (slope_ref[...].astype(F32) * mixed).astype(BF)
-    for dy, dz, at in slots(copies):
-        other, (x, x_to), dzh = place_of(where_ref, dy, dz)
-        slot = other * 8 + jnp.bitwise_and(x_to + 4 - x, 3) * 2 + dzh
-        part = lax.dot_general(held[at], gated, (((1,), (1,)), ((), ())), preferred_element_type=F32)
-        sums[slot] = (part * (SEQ**-0.5)).astype(BF)
-    sources = (gate_grad_ref, sums.at[:8], sums.at[8:])
-    outs = [pltpu.make_async_copy(src, dst, sems.at[3 + i]) for i, (src, dst) in enumerate(zip(sources, outs_hbm))]
-    for out in outs:
-        out.start()
+    gate_grad_ref[...] = (slope * mixed).astype(BF)
+    outs.append(pltpu.make_async_copy(gate_grad_ref, gate_grad_hbm, out_sems.at[1]))
+    outs[1].start()
+    gated = (gates * mixed).astype(BF).T
+    for other, target in ((1, other_hbm), (0, same_hbm)):
+        for dx in range(4):
+            at = other * 8 + 2 * dx
+            for dzh in range(2):
+                part = dot(held[grad_slot(where_ref, other, dx, dzh)], gated)
+                sums[at + dzh] = (part * (SEQ**-0.5)).astype(BF)
+            sem = out_sems.at[2 + other * 4 + dx]
+            out = pltpu.make_async_copy(sums.at[pl.ds(at, 2)], target.at[pl.ds(2 * dx, 2)], sem)
+            out.start()
+            outs.append(out)
     for out in outs:
         out.wait()
 
@@ -345,36 +326,19 @@
 TILE = pltpu.VMEM((CH, TOK), BF)
 
 
-def matmul_cost():
-    return pl.CostEstimate(flops=2 * CH * TOK * 4096, bytes_accessed=7 << 20, transcendentals=0)
-
-
-def slope_call(where, grads, weights, gates):
-    shape = jax.ShapeDtypeStruct((CH, TOK), BF)
-    return pl.pallas_call(
-        slope_kernel,
-        out_shape=(shape, shape),
-        in_specs=[pl.BlockSpec(memory_space=pltpu.SMEM)] + [in_hbm()] * 13,
-        out_specs=(in_hbm(),) * 2,
-        scratch_shapes=[HELD, SQUARES, TILE, TILE, TILE, DMA((8,)), DMA((7,))],
-        compiler_params=params(57),
-        cost_estimate=matmul_cost(),
-        name="slope",
-    )(where, *grads, *weights, gates)
-
-
-def weight_call(where, grads, gates, mixed, slope):
+def products_call(where, grads, weights, gates, mixed):
+    tile = jax.ShapeDtypeStruct((CH, TOK), BF)
     eight = jax.ShapeDtypeStruct((8, 256, 256), BF)
     return pl.pallas_call(
-        weight_kernel,
-        out_shape=(jax.ShapeDtypeStruct((CH, TOK), BF), eight, eight),
-        in_specs=[pl.BlockSpec(memory_space=pltpu.SMEM)] + [in_hbm()] * 11,
-        out_specs=(in_hbm(),) * 3,
-        scratch_shapes=[HELD, TILE, TILE, TILE, TILE, SQUARES, DMA((8,)), DMA((6,))],
-        compiler_params=params(57),
-        cost_estimate=matmul_cost(),
-        name="weight",
-    )(where, *grads, gates, mixed, slope)
+        products_kernel,
+        out_shape=(tile, tile, eight, eight),
+        in_specs=[pl.BlockSpec(memory_space=pltpu.SMEM)] + [in_hbm()] * 14,
+        out_specs=(in_hbm(),) * 4,
+        scratch_shapes=[HELD, SQUARES, TILE, TILE, TILE, TILE, SQUARES, DMA((8,)), DMA((6,)), DMA((10,))],
+        compiler_params=params(60),
+        cost_estimate=pl.CostEstimate(flops=4 * CH * TOK * 4096, bytes_accessed=9 << 20, transcendentals=0),
+        name="products",
+    )(where, *grads, *weights, gates, mixed)
 
 
 def exchange(value):
@@ -399,7 +363,7 @@
     up, down = send(out_grad, "tp", 4, 4, 1), send(out_grad, "tp", 4, 4, 3)
     up, w_line, own = lax.optimization_barrier((up, w_line, out_grad))
     near = [up, send(own, "tp", 4, 4, 2), down]
-    rest, near, w_line, inputs, filters = lax.optimization_barrier((rest, near, w_line, inputs, filters))
+    rest, near, w_line = lax.optimization_barrier((rest, near, w_line))
     rests = [send(rest, "tp", 4, 4, dy) for dy in (1, 2, 3)]
     grads = [out_grad, rest]
     for n, r in zip(near, rests):
@@ -412,17 +376,17 @@
     mixed_rows, spec = conv_call(exchange(both))
     mixed = exchange(mixed_rows).reshape(CH, TOK)
 
-    slope, product = slope_call(where, grads, weights, gates)
+    product, gate_grad, part_other, part_same = products_call(where, grads, weights, gates, mixed)
     product_rows = exchange(product.reshape(16, FEW, TOK))
-    gate_grad, part_same, part_other = weight_call(where, grads, gates, mixed, slope)
-    product_rows, part_same = lax.optimization_barrier((product_rows, part_same))
-    chip = add(part_same, send(part_other, "ctx", 1, 2, 1)).reshape(4, 2, 256, 256)
+    received = send(part_other, "ctx", 1, 2, 1)
+    chips = [add(part_same[2 * dx : 2 * dx + 2], received[2 * dx : 2 * dx + 2]) for dx in range(4)]
+    product_rows, chips = lax.optimization_barrier((product_rows, chips))
     grad_rows = grads_call(product_rows, spec)
     both_grads = exchange(grad_rows)
     input_grad = both_grads[:, :FEW].reshape(CH, TOK)
     filter_grad = both_grads[:, FEW:].reshape(CH, TOK)
 
-    line = add(chip[0], *[send(chip[dx], "ctx", 4, 4, dx) for dx in (1, 2, 3)])
+    line = add(chips[0], *[send(chips[dx], "ctx", 4, 4, dx) for dx in (1, 2, 3)])
     weight_grad = add(line[0], send(line[1], "ctx", 2, 2, 1))
     return (input_grad, gate_grad, filter_grad, weight_grad)
 

time: 172 us -> 161 us (0.936)
  the two profiles are of different devices: /device:TPU:33 before, /device:TPU:67 now
where the time goes in v3:
time: 161 us; the launch traced here: 160 us
  starting transfers between devices  61.6 us (38%)
  waiting for transfers between devices  57.9 us (36%)
  Pallas kernels  19 us (12%)
  blocking collectives  11.3 us (7%)
  other arithmetic  6.44 us (4%)
  local copies, waits for them, and re-layouts  3.24 us (2%)
    ppermute x17, waiting for transfers between devices, send(): return lax.ppermute(value, axis, shift_pairs(stride, size, by))  38.5 us
    all_to_all x4, starting transfers between devices, exchange(): return lax.all_to_all(value, 'ctx', split_axis=0, concat_axis=0, tiled=True)  30.9 us
    ppermute x17, starting transfers between devices, send(): return lax.ppermute(value, axis, shift_pairs(stride, size, by))  30.6 us
    all_to_all x4, waiting for transfers between devices, exchange(): return lax.all_to_all(value, 'ctx', split_axis=0, concat_axis=0, tiled=True)  19.5 us
    all_gather x1, blocking collectives, on_device(): w_line = lax.all_gather(out_weight.T, 'ctx', axis_index_groups=LINES_X)  11.3 us
    pallas_call x1, Pallas kernels, conv_call(): pl.pallas_call(conv_kernel, out_shape=(jax.ShapeDtypeStruct((16, FEW, TOK...  6.66 us
    pallas_call x1, Pallas kernels, products_call(): pl.pallas_call(products_kernel, out_shape=(tile, tile, eight, eight), in_...  6.63 us
    pallas_call x1, Pallas kernels, grads_call(): pl.pallas_call(grads_kernel, out_shape=jax.ShapeDtypeStruct((16, 2 * FEW,...  5.75 us
  transfers between devices with their start and end apart: 21, of which 7 were waited for; matrix products, arithmetic and copies ran while one was open for 5% of the time, Pallas kernels for 8%

profile of v3, /device:TPU:67, one launch (start us, length us, event | category | flops | bytes accessed | tf_op | source)
XLA Modules:
  0.0 160.5 jit_solution(10088512619099245052)
XLA Ops:
  0.6 0.0 copy-start.13
  0.7 1.4 collective-permute-start.3
  2.0 0.0 collective-permute-start.2
  2.0 3.7 %collective-permute-start.1 = (bf16[256,512]{1,0:T(8,128)(2,1)}, bf16[256,512]{1,0:T(8,128)(2,1)S(1)}, u32[]{:S(2)}, u32[]{:S(2)}) collective-permute-start(bf16[256,512]{1,0:T(8,128)(2,1)} %refs_0_.2), channel_id=1, source_target_pairs={{0,2},{1,3},{2,0},{3,1},{4,6},{5,7},{6,4},{7,5},{8,10},{9,11},{10,... | collective-permute-start | bytes 786440 | tf_op jit(solution)/shard_map/ppermute | solution.py:32
  5.7 0.0 collective-permute-start
  5.7 1.5 collective-permute-start.5
  7.3 1.9 %pad_maximum_fusion.1 = bf16[16,32,512]{2,1,0:T(8,128)(2,1)} fusion(bf16[16,16,512]{2,1,0:T(8,128)(2,1)} %bitcast.28, bf16[16,16,512]{2,1,0:T(8,128)(2,1)} %bitcast.29), kind=kLoop, calls=%fused_computation.1 | loop fusion | flops 1048576 | bytes 1048576 | tf_op jit(solution)/shard_map/concatenate | solution.py:375
  9.1 10.2 %all-to-all-start = ((bf16[16,32,512]{2,1,0:T(8,128)(2,1)}), bf16[16,32,512]{2,1,0:T(8,128)(2,1)S(1)}, u32[]{:S(2)}, u32[]{:S(2)}) async-start(bf16[16,32,512]{2,1,0:T(8,128)(2,1)} %pad_maximum_fusion.1), calls=%async_computation | async-start | bytes 1048576 | tf_op jit(solution)/shard_map/all_to_all | solution.py:345
  19.3 11.3 %all-gather = bf16[1024,256]{0,1:T(8,128)(2,1)S(1)} all-gather(bf16[256,256]{0,1:T(8,128)(2,1)S(1)} %bitcast.35), channel_id=2, replica_groups={{0,64,128,192},{16,80,144,208},{32,96,160,224},{48,112,176,240},{1,65,1..., dimensions={0}, use_global_device_ids=true | all-gather | bytes 655360 | tf_op jit(solution)/shard_map/all_gather | solution.py:360
  30.7 0.2 copy.14
  30.9 0.0 copy-start.7
  30.9 0.0 collective-permute-done.3.refs_2_
  30.9 0.0 copy-start.14
  30.9 1.8 %collective-permute-start.4 = (bf16[256,512]{1,0:T(8,128)(2,1)S(1)}, bf16[256,512]{1,0:T(8,128)(2,1)S(1)}, u32[]{:S(2)}, u32[]{:S(2)}) collective-permute-start(bf16[256,512]{1,0:T(8,128)(2,1)S(1)} %copy-done.13), channel_id=1, source_target_pairs={{0,8},{1,9},{2,10},{3,11},{4,12},{5,13},{6,14},{7,15},{8,0},{9,1},... | collective-permute-start | bytes 786440 | tf_op jit(solution)/shard_map/ppermute | solution.py:32
  32.7 0.0 collective-permute-done.2
  32.7 0.0 collective-permute-done.1
  32.7 3.3 %collective-permute-done = bf16[256,512]{1,0:T(8,128)(2,1)S(1)} collective-permute-done((bf16[256,512]{1,0:T(8,128)(2,1)}, bf16[256,512]{1,0:T(8,128)(2,1)S(1)}, u32[]{:S(2)}, u32[]{:S(2)}) %collective-permute-start) | collective-permute-done | bytes 262176 | tf_op jit(solution)/shard_map/ppermute | solution.py:32
  36.0 0.1 pad_maximum_fusion.refs_1_
  36.1 0.0 collective-permute-done.5.refs_6_
  36.1 1.9 %collective-permute-done.4.refs_4_ = bf16[256,512]{1,0:T(8,128)(2,1)S(1)} collective-permute-done((bf16[256,512]{1,0:T(8,128)(2,1)S(1)}, bf16[256,512]{1,0:T(8,128)(2,1)S(1)}, u32[]{:S(2)}, u32[]{:S(2)}) %collective-permute-start.4) | collective-permute-done | bytes 262176 | tf_op jit(solution)/shard_map/ppermute | solution.py:32
  38.0 9.0 %collective-permute-start.9 = (bf16[4,256,256]{2,1,0:T(8,128)(2,1)S(1)}, bf16[4,256,256]{2,1,0:T(8,128)(2,1)}, u32[]{:S(2)}, u32[]{:S(2)}) collective-permute-start(bf16[4,256,256]{2,1,0:T(8,128)(2,1)S(1)} %bitcast.23), channel_id=1, source_target_pairs={{0,32},{16,48},{32,0},{48,16},{64,96},{80,112},{96,64},{112,80},{1... | collective-permute-start | bytes 1572872 | tf_op jit(solution)/shard_map/ppermute | solution.py:32
  47.0 0.0 collective-permute-start.8
  47.0 1.0 collective-permute-start.7
  48.0 0.5 collective-permute-start.6
  48.5 3.3 %collective-permute-start.10 = (bf16[4,256,256]{2,1,0:T(8,128)(2,1)S(1)}, bf16[4,256,256]{2,1,0:T(8,128)(2,1)}, u32[]{:S(2)}, u32[]{:S(2)}) collective-permute-start(bf16[4,256,256]{2,1,0:T(8,128)(2,1)S(1)} %bitcast.24), channel_id=1, source_target_pairs={{0,16},{16,0},{32,48},{48,32},{64,80},{80,64},{96,112},{112,96},{1... | collective-permute-start | bytes 1572872 | tf_op jit(solution)/shard_map/ppermute | solution.py:32
  51.8 17.6 %collective-permute-done.9.refs_9_ = bf16[4,256,256]{2,1,0:T(8,128)(2,1)} collective-permute-done((bf16[4,256,256]{2,1,0:T(8,128)(2,1)S(1)}, bf16[4,256,256]{2,1,0:T(8,128)(2,1)}, u32[]{:S(2)}, u32[]{:S(2)}) %collective-permute-start.9) | collective-permute-done | bytes 524320 | tf_op jit(solution)/shard_map/ppermute | solution.py:32
  69.5 0.6 collective-permute-start.11
  70.0 0.0 all-to-all-done.xf_ref
  70.1 0.8 copy-done.8
  70.8 6.7 %conv.1 = (bf16[16,16,512]{2,1,0:T(8,128)(2,1)}, f32[4,1024,128]{2,1,0:T(8,128)}) custom-call(bf16[16,32,512]{2,1,0:T(8,128)(2,1)} %copy-done.8, bf16[128,128]{1,0:T(8,128)(2,1)} %constant.70.clone.refs_0_.first_ref, bf16[768,256]{1,0:T(8,128)(2,1)} %constant.71.clone.refs_1_.second_ref, bf16[768,256]{1,0:T(8,128)(2,1)} %constant.72.clone.refs_2_.back_ref, ...), custom_call_target="tpu_custom_call" | custom-call | flops 1000000000 | bytes 4194304 | tf_op jit(solution)/shard_map/conv/pallas_call | solution.py:228
  77.5 8.7 %all-to-all-start.1 = ((bf16[16,16,512]{2,1,0:T(8,128)(2,1)}), bf16[16,16,512]{2,1,0:T(8,128)(2,1)S(1)}, u32[]{:S(2)}, u32[]{:S(2)}) async-start(bf16[16,16,512]{2,1,0:T(8,128)(2,1)} %get-tuple-element.31), calls=%async_computation.1 | async-start | bytes 524288 | tf_op jit(solution)/shard_map/all_to_all | solution.py:345
  86.2 0.6 stack.35.where_ref
  86.8 0.0 collective-permute-done.10.refs_10_
  86.8 0.0 collective-permute-done.8.refs_7_
  86.8 0.0 collective-permute-done.7.refs_5_
  86.9 0.0 collective-permute-done.6.refs_3_
  86.9 11.9 %all-to-all-done.1 = bf16[16,16,512]{2,1,0:T(8,128)(2,1)S(1)} async-done(((bf16[16,16,512]{2,1,0:T(8,128)(2,1)}), bf16[16,16,512]{2,1,0:T(8,128)(2,1)S(1)}, u32[]{:S(2)}, u32[]{:S(2)}) %all-to-all-start.1) | async-done | bytes 262176 | tf_op jit(solution)/shard_map/all_to_all | solution.py:345
  98.8 0.0 collective-permute-done.11.refs_11_
  98.8 0.7 copy-done.9
  99.5 6.6 %products.1 = (bf16[256,512]{1,0:T(8,128)(2,1)}, bf16[256,512]{1,0:T(8,128)(2,1)}, bf16[8,256,256]{2,1,0:T(8,128)(2,1)}, bf16[8,256,256]{2,1,0:T(8,128)(2,1)}) custom-call(s32[5]{0:T(128)} %stack.35.where_ref, bf16[256,512]{1,0:T(8,128)(2,1)} %refs_0_.2, bf16[3,256,512]{2,1,0:T(8,128)(2,1)} %copy-done.6, bf16[256,512]{1,0:T(8,128)(2,1)} %copy-done.14, ...), custom_call_target="tpu_custom_call" | custom-call | flops 2147483648 | bytes 9437184 | tf_op jit(solution)/shard_map/products/pallas_call | solution.py:332
  106.2 0.0 copy-start
  106.2 0.0 copy-start.1
  106.2 0.0 copy-start.2
  106.2 0.0 copy-start.3
  106.2 0.0 copy-start.4
  106.2 0.2 collective-permute-start.12
  106.4 5.6 %all-to-all-start.2 = ((bf16[16,16,512]{2,1,0:T(8,128)(2,1)}), bf16[16,16,512]{2,1,0:T(8,128)(2,1)S(1)}, u32[]{:S(2)}, u32[]{:S(2)}) async-start(bf16[16,16,512]{2,1,0:T(8,128)(2,1)} %bitcast.27), calls=%async_computation.2 | async-start | bytes 524288 | tf_op jit(solution)/shard_map/all_to_all | solution.py:345
  112.1 0.0 collective-permute-done.12
  112.1 2.6 %add_convert_fusion.1 = (bf16[2,256,256]{2,1,0:T(8,128)(2,1)}, bf16[2,256,256]{2,1,0:T(8,128)(2,1)}, bf16[2,256,256]{2,1,0:T(8,128)(2,1)}, bf16[2,256,256]{2,1,0:T(8,128)(2,1)S(1)}) fusion(bf16[8,256,256]{2,1,0:T(8,128)(2,1)} %collective-permute-done.12, bf16[8,256,256]{2,1,0:T(8,128)(2,1)} %get-tuple-element.33), kind=kLoop, calls=%fused_computation.3 | loop fusion | flops 2097152 | bytes 3145728 | tf_op jit(solution)/shard_map/convert_element_type | solution.py:352
  114.7 7.5 %all-to-all-done.2.p_ref = bf16[16,16,512]{2,1,0:T(8,128)(2,1)S(1)} async-done(((bf16[16,16,512]{2,1,0:T(8,128)(2,1)}), bf16[16,16,512]{2,1,0:T(8,128)(2,1)S(1)}, u32[]{:S(2)}, u32[]{:S(2)}) %all-to-all-start.2) | async-done | bytes 262176 | tf_op jit(solution)/shard_map/all_to_all | solution.py:345
  122.2 0.7 collective-permute-start.13
  122.9 2.5 %collective-permute-start.14 = (bf16[2,256,256]{2,1,0:T(8,128)(2,1)}, bf16[2,256,256]{2,1,0:T(8,128)(2,1)}, u32[]{:S(2)}, u32[]{:S(2)}) collective-permute-start(bf16[2,256,256]{2,1,0:T(8,128)(2,1)} %get-tuple-element.40), channel_id=1, source_target_pairs={{0,128},{16,144},{32,160},{48,176},{64,192},{80,208},{96,224},{112... | collective-permute-start | bytes 786440 | tf_op jit(solution)/shard_map/ppermute | solution.py:32
  125.4 0.1 collective-permute-start.15
  125.5 5.7 %grads.1 = bf16[16,32,512]{2,1,0:T(8,128)(2,1)} custom-call(bf16[16,16,512]{2,1,0:T(8,128)(2,1)S(1)} %all-to-all-done.2.p_ref, bf16[128,128]{1,0:T(8,128)(2,1)S(1)} %copy-done.4, bf16[768,256]{1,0:T(8,128)(2,1)S(1)} %copy-done.1, bf16[768,256]{1,0:T(8,128)(2,1)S(1)} %copy-done, bf16[64,384]{1,0:T(8,128)(2,1)S(1)} %copy-done.3, f32[2,64,128]{2,1,0:T(8,128)S(1)} %copy-done.2, ...), custom_call_target="tpu_custom_call" | custom-call | flops 10000000000 | bytes 4194304 | tf_op jit(solution)/shard_map/grads/pallas_call | solution.py:244
  131.3 6.5 %all-to-all-start.3 = ((bf16[16,32,512]{2,1,0:T(8,128)(2,1)}), bf16[16,32,512]{2,1,0:T(8,128)(2,1)S(1)}, u32[]{:S(2)}, u32[]{:S(2)}) async-start(bf16[16,32,512]{2,1,0:T(8,128)(2,1)} %grads.1), calls=%async_computation.3 | async-start | bytes 1048576 | tf_op jit(solution)/shard_map/all_to_all | solution.py:345
  137.7 0.0 collective-permute-done.13
  137.7 0.0 collective-permute-done.14
  137.7 0.8 collective-permute-done.15
  138.6 1.2 add_convert_fusion
  139.8 4.4 %collective-permute-start.16 = (bf16[256,256]{1,0:T(8,128)(2,1)S(1)}, bf16[256,256]{1,0:T(8,128)(2,1)S(1)}, u32[]{:S(2)}, u32[]{:S(2)}) collective-permute-start(bf16[256,256]{1,0:T(8,128)(2,1)S(1)} %slice_bitcast_fusion), channel_id=1, source_target_pairs={{0,32},{16,48},{32,0},{48,16},{64,96},{80,112},{96,64},{112,80},{1... | collective-permute-start | bytes 393224 | tf_op jit(solution)/shard_map/ppermute | solution.py:32
  144.2 14.8 %collective-permute-done.16 = bf16[256,256]{1,0:T(8,128)(2,1)S(1)} collective-permute-done((bf16[256,256]{1,0:T(8,128)(2,1)S(1)}, bf16[256,256]{1,0:T(8,128)(2,1)S(1)}, u32[]{:S(2)}, u32[]{:S(2)}) %collective-permute-start.16) | collective-permute-done | bytes 131104 | tf_op jit(solution)/shard_map/ppermute | solution.py:32
  159.0 0.7 fusion
  159.7 0.0 all-to-all-done.3
  159.7 0.8 fusion.1
  (25 shorter events, 0.1 us)
Async XLA Ops:
  0.6 30.3 %copy-start.13 = (bf16[256,512]{1,0:T(8,128)(2,1)S(1)}, bf16[256,512]{1,0:T(8,128)(2,1)}, u32[]{:S(2)}) copy-start(bf16[256,512]{1,0:T(8,128)(2,1)} %refs_0_.2) | copy-start | bytes 786436
  0.6 18.7 %copy-start.10 = (bf16[256,256]{1,0:T(8,128)(2,1)S(1)}, bf16[256,256]{1,0:T(8,128)(2,1)}, u32[]{:S(2)}) copy-start(bf16[256,256]{1,0:T(8,128)(2,1)} %param.14) | copy-start | bytes 393220
  0.7 30.2 %collective-permute-start.3 = (bf16[256,512]{1,0:T(8,128)(2,1)}, bf16[256,512]{1,0:T(8,128)(2,1)S(1)}, u32[]{:S(2)}, u32[]{:S(2)}) collective-permute-start(bf16[256,512]{1,0:T(8,128)(2,1)} %refs_0_.2), channel_id=1, source_target_pairs={{0,4},{1,5},{2,6},{3,7},{4,8},{5,9},{6,10},{7,11},{8,12},{9,13},{1... | collective-permute-start | bytes 786440 | tf_op jit(solution)/shard_map/ppermute | solution.py:32
  2.0 30.7 %collective-permute-start.2 = (bf16[256,512]{1,0:T(8,128)(2,1)}, bf16[256,512]{1,0:T(8,128)(2,1)S(1)}, u32[]{:S(2)}, u32[]{:S(2)}) collective-permute-start(bf16[256,512]{1,0:T(8,128)(2,1)} %refs_0_.2), channel_id=1, source_target_pairs={{0,3},{1,0},{2,1},{3,2},{4,7},{5,4},{6,5},{7,6},{8,11},{9,8},{10,9... | collective-permute-start | bytes 786440 | tf_op jit(solution)/shard_map/ppermute | solution.py:32
  2.0 30.7 %collective-permute-start.1 = (bf16[256,512]{1,0:T(8,128)(2,1)}, bf16[256,512]{1,0:T(8,128)(2,1)S(1)}, u32[]{:S(2)}, u32[]{:S(2)}) collective-permute-start(bf16[256,512]{1,0:T(8,128)(2,1)} %refs_0_.2), channel_id=1, source_target_pairs={{0,2},{1,3},{2,0},{3,1},{4,6},{5,7},{6,4},{7,5},{8,10},{9,11},{10,... | collective-permute-start | bytes 786440 | tf_op jit(solution)/shard_map/ppermute | solution.py:32
  5.7 30.3 %collective-permute-start = (bf16[256,512]{1,0:T(8,128)(2,1)}, bf16[256,512]{1,0:T(8,128)(2,1)S(1)}, u32[]{:S(2)}, u32[]{:S(2)}) collective-permute-start(bf16[256,512]{1,0:T(8,128)(2,1)} %refs_0_.2), channel_id=1, source_target_pairs={{0,1},{1,2},{2,3},{3,0},{4,5},{5,6},{6,7},{7,4},{8,9},{9,10},{10,1... | collective-permute-start | bytes 786440 | tf_op jit(solution)/shard_map/ppermute | solution.py:32
  5.7 30.4 %collective-permute-start.5 = (bf16[256,512]{1,0:T(8,128)(2,1)}, bf16[256,512]{1,0:T(8,128)(2,1)S(1)}, u32[]{:S(2)}, u32[]{:S(2)}) collective-permute-start(bf16[256,512]{1,0:T(8,128)(2,1)} %refs_0_.2), channel_id=1, source_target_pairs={{0,12},{1,13},{2,14},{3,15},{4,0},{5,1},{6,2},{7,3},{8,4},{9,5},{1... | collective-permute-start | bytes 786440 | tf_op jit(solution)/shard_map/ppermute | solution.py:32
  9.1 60.9 %all-to-all-start = ((bf16[16,32,512]{2,1,0:T(8,128)(2,1)}), bf16[16,32,512]{2,1,0:T(8,128)(2,1)S(1)}, u32[]{:S(2)}, u32[]{:S(2)}) async-start(bf16[16,32,512]{2,1,0:T(8,128)(2,1)} %pad_maximum_fusion.1), calls=%async_computation | async-start | bytes 1048576 | tf_op jit(solution)/shard_map/all_to_all | solution.py:345
  30.9 46.7 %copy-start.7 = (bf16[1024,256]{1,0:T(8,128)(2,1)}, bf16[1024,256]{1,0:T(8,128)(2,1)S(1)}, u32[]{:S(2)}) copy-start(bf16[1024,256]{1,0:T(8,128)(2,1)S(1)} %copy.14) | copy-start | bytes 1572868
  30.9 16.1 %copy-start.14 = (bf16[256,512]{1,0:T(8,128)(2,1)}, bf16[256,512]{1,0:T(8,128)(2,1)S(1)}, u32[]{:S(2)}) copy-start(bf16[256,512]{1,0:T(8,128)(2,1)S(1)} %collective-permute-done.3.refs_2_) | copy-start | bytes 786436
  30.9 7.1 %collective-permute-start.4 = (bf16[256,512]{1,0:T(8,128)(2,1)S(1)}, bf16[256,512]{1,0:T(8,128)(2,1)S(1)}, u32[]{:S(2)}, u32[]{:S(2)}) collective-permute-start(bf16[256,512]{1,0:T(8,128)(2,1)S(1)} %copy-done.13), channel_id=1, source_target_pairs={{0,8},{1,9},{2,10},{3,11},{4,12},{5,13},{6,14},{7,15},{8,0},{9,1},... | collective-permute-start | bytes 786440 | tf_op jit(solution)/shard_map/ppermute | solution.py:32
  36.1 41.4 %copy-start.6 = (bf16[3,256,512]{2,1,0:T(8,128)(2,1)}, bf16[3,256,512]{2,1,0:T(8,128)(2,1)S(1)}, u32[]{:S(2)}) copy-start(bf16[3,256,512]{2,1,0:T(8,128)(2,1)S(1)} %pad_maximum_fusion.refs_1_) | copy-start | bytes 2359300
  36.1 10.9 %copy-start.15 = (bf16[256,512]{1,0:T(8,128)(2,1)}, bf16[256,512]{1,0:T(8,128)(2,1)S(1)}, u32[]{:S(2)}) copy-start(bf16[256,512]{1,0:T(8,128)(2,1)S(1)} %collective-permute-done.5.refs_6_) | copy-start | bytes 786436
  38.0 31.4 %copy-start.16 = (bf16[256,512]{1,0:T(8,128)(2,1)}, bf16[256,512]{1,0:T(8,128)(2,1)S(1)}, u32[]{:S(2)}) copy-start(bf16[256,512]{1,0:T(8,128)(2,1)S(1)} %collective-permute-done.4.refs_4_) | copy-start | bytes 786436
  38.0 31.4 %collective-permute-start.9 = (bf16[4,256,256]{2,1,0:T(8,128)(2,1)S(1)}, bf16[4,256,256]{2,1,0:T(8,128)(2,1)}, u32[]{:S(2)}, u32[]{:S(2)}) collective-permute-start(bf16[4,256,256]{2,1,0:T(8,128)(2,1)S(1)} %bitcast.23), channel_id=1, source_target_pairs={{0,32},{16,48},{32,0},{48,16},{64,96},{80,112},{96,64},{112,80},{1... | collective-permute-start | bytes 1572872 | tf_op jit(solution)/shard_map/ppermute | solution.py:32
  47.0 39.8 %collective-permute-start.8 = (bf16[3,256,512]{2,1,0:T(8,128)(2,1)S(1)}, bf16[3,256,512]{2,1,0:T(8,128)(2,1)S(1)}, u32[]{:S(2)}, u32[]{:S(2)}) collective-permute-start(bf16[3,256,512]{2,1,0:T(8,128)(2,1)S(1)} %pad_maximum_fusion.refs_1_), channel_id=1, source_target_pairs={{0,12},{1,13},{2,14},{3,15},{4,0},{5,1},{6,2},{7,3},{8,4},{9,5},{1... | collective-permute-start | bytes 2359304 | tf_op jit(solution)/shard_map/ppermute | solution.py:32
  47.0 39.8 %collective-permute-start.7 = (bf16[3,256,512]{2,1,0:T(8,128)(2,1)S(1)}, bf16[3,256,512]{2,1,0:T(8,128)(2,1)S(1)}, u32[]{:S(2)}, u32[]{:S(2)}) collective-permute-start(bf16[3,256,512]{2,1,0:T(8,128)(2,1)S(1)} %pad_maximum_fusion.refs_1_), channel_id=1, source_target_pairs={{0,8},{1,9},{2,10},{3,11},{4,12},{5,13},{6,14},{7,15},{8,0},{9,1},... | collective-permute-start | bytes 2359304 | tf_op jit(solution)/shard_map/ppermute | solution.py:32
  48.0 38.8 %collective-permute-start.6 = (bf16[3,256,512]{2,1,0:T(8,128)(2,1)S(1)}, bf16[3,256,512]{2,1,0:T(8,128)(2,1)}, u32[]{:S(2)}, u32[]{:S(2)}) collective-permute-start(bf16[3,256,512]{2,1,0:T(8,128)(2,1)S(1)} %pad_maximum_fusion.refs_1_), channel_id=1, source_target_pairs={{0,4},{1,5},{2,6},{3,7},{4,8},{5,9},{6,10},{7,11},{8,12},{9,13},{1... | collective-permute-start | bytes 2359304 | tf_op jit(solution)/shard_map/ppermute | solution.py:32
  48.5 38.3 %collective-permute-start.10 = (bf16[4,256,256]{2,1,0:T(8,128)(2,1)S(1)}, bf16[4,256,256]{2,1,0:T(8,128)(2,1)}, u32[]{:S(2)}, u32[]{:S(2)}) collective-permute-start(bf16[4,256,256]{2,1,0:T(8,128)(2,1)S(1)} %bitcast.24), channel_id=1, source_target_pairs={{0,16},{16,0},{32,48},{48,32},{64,80},{80,64},{96,112},{112,96},{1... | collective-permute-start | bytes 1572872 | tf_op jit(solution)/shard_map/ppermute | solution.py:32
  69.5 29.4 %collective-permute-start.11 = (bf16[4,256,256]{2,1,0:T(8,128)(2,1)}, bf16[4,256,256]{2,1,0:T(8,128)(2,1)}, u32[]{:S(2)}, u32[]{:S(2)}) collective-permute-start(bf16[4,256,256]{2,1,0:T(8,128)(2,1)} %collective-permute-done.9.refs_9_), channel_id=1, source_target_pairs={{0,16},{16,0},{32,48},{48,32},{64,80},{80,64},{96,112},{112,96},{1... | collective-permute-start | bytes 1572872 | tf_op jit(solution)/shard_map/ppermute | solution.py:32
  70.0 0.8 copy-start.8
  77.5 21.3 %all-to-all-start.1 = ((bf16[16,16,512]{2,1,0:T(8,128)(2,1)}), bf16[16,16,512]{2,1,0:T(8,128)(2,1)S(1)}, u32[]{:S(2)}, u32[]{:S(2)}) async-start(bf16[16,16,512]{2,1,0:T(8,128)(2,1)} %get-tuple-element.31), calls=%async_computation.1 | async-start | bytes 524288 | tf_op jit(solution)/shard_map/all_to_all | solution.py:345
  86.8 12.0 %copy-start.11 = (bf16[3,256,512]{2,1,0:T(8,128)(2,1)}, bf16[3,256,512]{2,1,0:T(8,128)(2,1)S(1)}, u32[]{:S(2)}) copy-start(bf16[3,256,512]{2,1,0:T(8,128)(2,1)S(1)} %collective-permute-done.8.refs_7_) | copy-start | bytes 2359300
  86.9 12.0 %copy-start.12 = (bf16[3,256,512]{2,1,0:T(8,128)(2,1)}, bf16[3,256,512]{2,1,0:T(8,128)(2,1)S(1)}, u32[]{:S(2)}) copy-start(bf16[3,256,512]{2,1,0:T(8,128)(2,1)S(1)} %collective-permute-done.7.refs_5_) | copy-start | bytes 2359300
  98.8 0.7 copy-start.9
  106.2 19.3 %copy-start = (bf16[768,256]{1,0:T(8,128)(2,1)S(1)}, bf16[768,256]{1,0:T(8,128)(2,1)}, u32[]{:S(2)}) copy-start(bf16[768,256]{1,0:T(8,128)(2,1)} %constant.72.clone.refs_2_.back_ref) | copy-start | bytes 1179652
  106.2 19.3 %copy-start.1 = (bf16[768,256]{1,0:T(8,128)(2,1)S(1)}, bf16[768,256]{1,0:T(8,128)(2,1)}, u32[]{:S(2)}) copy-start(bf16[768,256]{1,0:T(8,128)(2,1)} %constant.71.clone.refs_1_.second_ref) | copy-start | bytes 1179652
  106.2 19.3 %copy-start.2 = (f32[2,64,128]{2,1,0:T(8,128)S(1)}, f32[2,64,128]{2,1,0:T(8,128)}, u32[]{:S(2)}) copy-start(f32[2,64,128]{2,1,0:T(8,128)} %constant.74.clone.refs_4_.turn_ref) | copy-start | bytes 196612
  106.2 19.3 %copy-start.3 = (bf16[64,384]{1,0:T(8,128)(2,1)S(1)}, bf16[64,384]{1,0:T(8,128)(2,1)}, u32[]{:S(2)}) copy-start(bf16[64,384]{1,0:T(8,128)(2,1)} %constant.73.clone.refs_3_.last_ref) | copy-start | bytes 147460
  106.2 19.3 %copy-start.4 = (bf16[128,128]{1,0:T(8,128)(2,1)S(1)}, bf16[128,128]{1,0:T(8,128)(2,1)}, u32[]{:S(2)}) copy-start(bf16[128,128]{1,0:T(8,128)(2,1)} %constant.70.clone.refs_0_.first_ref) | copy-start | bytes 98308
  106.2 19.3 %copy-start.5 = (f32[4,1024,128]{2,1,0:T(8,128)S(1)}, f32[4,1024,128]{2,1,0:T(8,128)}, u32[]{:S(2)}) copy-start(f32[4,1024,128]{2,1,0:T(8,128)} %get-tuple-element.36.spec_ref) | copy-start | bytes 6291460
  106.2 5.9 %collective-permute-start.12 = (bf16[8,256,256]{2,1,0:T(8,128)(2,1)}, bf16[8,256,256]{2,1,0:T(8,128)(2,1)}, u32[]{:S(2)}, u32[]{:S(2)}) collective-permute-start(bf16[8,256,256]{2,1,0:T(8,128)(2,1)} %get-tuple-element.34), channel_id=1, source_target_pairs={{0,16},{16,0},{32,48},{48,32},{64,80},{80,64},{96,112},{112,96},{1... | collective-permute-start | bytes 3145736 | tf_op jit(solution)/shard_map/ppermute | solution.py:32
  106.4 15.8 %all-to-all-start.2 = ((bf16[16,16,512]{2,1,0:T(8,128)(2,1)}), bf16[16,16,512]{2,1,0:T(8,128)(2,1)S(1)}, u32[]{:S(2)}, u32[]{:S(2)}) async-start(bf16[16,16,512]{2,1,0:T(8,128)(2,1)} %bitcast.27), calls=%async_computation.2 | async-start | bytes 524288 | tf_op jit(solution)/shard_map/all_to_all | solution.py:345
  122.2 15.5 %collective-permute-start.13 = (bf16[2,256,256]{2,1,0:T(8,128)(2,1)}, bf16[2,256,256]{2,1,0:T(8,128)(2,1)}, u32[]{:S(2)}, u32[]{:S(2)}) collective-permute-start(bf16[2,256,256]{2,1,0:T(8,128)(2,1)} %get-tuple-element.39), channel_id=1, source_target_pairs={{0,64},{16,80},{32,96},{48,112},{64,128},{80,144},{96,160},{112,17... | collective-permute-start | bytes 786440 | tf_op jit(solution)/shard_map/ppermute | solution.py:32
  122.9 14.8 %collective-permute-start.14 = (bf16[2,256,256]{2,1,0:T(8,128)(2,1)}, bf16[2,256,256]{2,1,0:T(8,128)(2,1)}, u32[]{:S(2)}, u32[]{:S(2)}) collective-permute-start(bf16[2,256,256]{2,1,0:T(8,128)(2,1)} %get-tuple-element.40), channel_id=1, source_target_pairs={{0,128},{16,144},{32,160},{48,176},{64,192},{80,208},{96,224},{112... | collective-permute-start | bytes 786440 | tf_op jit(solution)/shard_map/ppermute | solution.py:32
  125.4 13.2 %collective-permute-start.15 = (bf16[2,256,256]{2,1,0:T(8,128)(2,1)}, bf16[2,256,256]{2,1,0:T(8,128)(2,1)}, u32[]{:S(2)}, u32[]{:S(2)}) collective-permute-start(bf16[2,256,256]{2,1,0:T(8,128)(2,1)} %get-tuple-element.41), channel_id=1, source_target_pairs={{0,192},{16,208},{32,224},{48,240},{64,0},{80,16},{96,32},{112,48}... | collective-permute-start | bytes 786440 | tf_op jit(solution)/shard_map/ppermute | solution.py:32
  131.3 28.4 %all-to-all-start.3 = ((bf16[16,32,512]{2,1,0:T(8,128)(2,1)}), bf16[16,32,512]{2,1,0:T(8,128)(2,1)S(1)}, u32[]{:S(2)}, u32[]{:S(2)}) async-start(bf16[16,32,512]{2,1,0:T(8,128)(2,1)} %grads.1), calls=%async_computation.3 | async-start | bytes 1048576 | tf_op jit(solution)/shard_map/all_to_all | solution.py:345
  139.8 19.1 %collective-permute-start.16 = (bf16[256,256]{1,0:T(8,128)(2,1)S(1)}, bf16[256,256]{1,0:T(8,128)(2,1)S(1)}, u32[]{:S(2)}, u32[]{:S(2)}) collective-permute-start(bf16[256,256]{1,0:T(8,128)(2,1)S(1)} %slice_bitcast_fusion), channel_id=1, source_target_pairs={{0,32},{16,48},{32,0},{48,16},{64,96},{80,112},{96,64},{112,80},{1... | collective-permute-start | bytes 393224 | tf_op jit(solution)/shard_map/ppermute | solution.py:32

commit v4 on v3

--- a/solution.py
+++ b/solution.py
@@ -33,6 +33,7 @@
 
 
 LINES_X = [[4 * x + i for x in range(4)] for i in range(4)]
+PLANES_X_CORE = [[4 * x + 2 * zh + core for x in range(4) for core in range(2)] for zh in range(2)]
 
 
 def split_hi_lo(matrix):
@@ -253,68 +254,71 @@
     )(product, *constants(), spec)
 
 
+GRAD_SLOTS = ((0, 1), (1, 3), (4, 1), (5, 3), (8, 1), (9, 1), (10, 1), (11, 1), (12, 1), (13, 3))
+GRAD_COUNTS = (2, 2, 4, 2)
+GRADS = len(GRAD_SLOTS)
+
+
 def fetch_grads(grads, held, sems):
     copies = []
-    for dy in range(4):
-        for part, target in enumerate((held.at[4 * dy], held.at[pl.ds(4 * dy + 1, 3)])):
-            copies.append(pltpu.make_async_copy(grads[2 * dy + part], target, sems.at[2 * dy + part]))
+    for i, (at, count) in enumerate(GRAD_SLOTS):
+        target = held.at[at] if count == 1 else held.at[pl.ds(at, count)]
+        copies.append(pltpu.make_async_copy(grads[i], target, sems.at[i]))
     for copy in copies:
         copy.start()
     return copies
 
 
 def weight_slot(where_ref, dy, dz):
-    zh, core, y, zl = (where_ref[i] for i in range(1, 5))
+    zh, _, y, zl = (where_ref[i] for i in range(1, 5))
     x_from = jnp.bitwise_and(y + 4 - dy, 3)
     zl_from = jnp.bitwise_and(zl + 4 - dz, 3)
     zh_from = jnp.right_shift(zl_from, 1)
     core_from = jnp.bitwise_and(zl_from, 1)
-    return jnp.bitwise_xor(core, core_from) * 8 + jnp.bitwise_xor(zh, zh_from) * 4 + x_from
-
-
-def grad_slot(where_ref, other, dx, dzh):
-    x, zh, core, y, zl = (where_ref[i] for i in range(5))
-    y_from = jnp.bitwise_and(x + dx, 3)
+    return x_from * 4 + core_from * 2 + jnp.bitwise_xor(zh, zh_from)
+
+
+def grad_slot(where_ref, other, x_to, dzh):
+    zh, core, y, zl = (where_ref[i] for i in range(1, 5))
     zl_from = jnp.bitwise_xor(zh, dzh) * 2 + jnp.bitwise_xor(core, other)
-    return jnp.bitwise_and(y + 4 - y_from, 3) * 4 + jnp.bitwise_and(zl + 4 - zl_from, 3)
+    return jnp.bitwise_and(y + 4 - x_to, 3) * 4 + jnp.bitwise_and(zl + 4 - zl_from, 3)
 
 
 def products_kernel(where_ref, *refs):
-    grads, ins_hbm = refs[:8], refs[8:14]
-    product_hbm, gate_grad_hbm, other_hbm, same_hbm = refs[14:18]
-    held, weights, gates_ref, mixed_ref, product_ref, gate_grad_ref, sums, grad_sems, sems, out_sems = refs[18:]
-    targets = [weights.at[pl.ds(4 * i, 4)] for i in range(4)] + [gates_ref, mixed_ref]
+    grads, refs = refs[:GRADS], refs[GRADS:]
+    ins_hbm, (product_hbm, gate_grad_hbm, other_hbm, same_hbm) = refs[:3], refs[3:7]
+    held, weights, gates_ref, mixed_ref, product_ref, gate_grad_ref, sums, grad_sems, sems, out_sems = refs[7:]
+    targets = [weights, gates_ref, mixed_ref]
     ins = fetch(ins_hbm, targets, sems)
     copies = fetch_grads(grads, held, grad_sems)
-    for copy in ins[:4]:
-        copy.wait()
+    ins[0].wait()
     total = None
     for dy in range(4):
-        copies[2 * dy].wait()
-        copies[2 * dy + 1].wait()
+        for _ in range(GRAD_COUNTS[dy]):
+            copies.pop(0).wait()
         weight = jnp.concatenate([weights[weight_slot(where_ref, dy, dz)] for dz in range(4)], axis=1)
         part = dot(weight, held[4 * dy : 4 * dy + 4].reshape(4 * CH, TOK))
         total = part if total is None else total + part
     slope = total.astype(BF).astype(F32)
-    ins[4].wait()
+    ins[1].wait()
     gates = gates_ref[...].astype(F32)
     product_ref[...] = (slope * gates).astype(BF)
     outs = [pltpu.make_async_copy(product_ref, product_hbm, out_sems.at[0])]
     outs[0].start()
-    ins[5].wait()
+    ins[2].wait()
     mixed = mixed_ref[...].astype(F32)
     gate_grad_ref[...] = (slope * mixed).astype(BF)
     outs.append(pltpu.make_async_copy(gate_grad_ref, gate_grad_hbm, out_sems.at[1]))
     outs[1].start()
     gated = (gates * mixed).astype(BF).T
     for other, target in ((1, other_hbm), (0, same_hbm)):
-        for dx in range(4):
-            at = other * 8 + 2 * dx
+        for x_to in range(4):
+            at = other * 8 + 2 * x_to
             for dzh in range(2):
-                part = dot(held[grad_slot(where_ref, other, dx, dzh)], gated)
+                part = dot(held[grad_slot(where_ref, other, x_to, dzh)], gated)
                 sums[at + dzh] = (part * (SEQ**-0.5)).astype(BF)
-            sem = out_sems.at[2 + other * 4 + dx]
-            out = pltpu.make_async_copy(sums.at[pl.ds(at, 2)], target.at[pl.ds(2 * dx, 2)], sem)
+            sem = out_sems.at[2 + other * 4 + x_to]
+            out = pltpu.make_async_copy(sums.at[pl.ds(at, 2)], target.at[pl.ds(2 * x_to, 2)], sem)
             out.start()
             outs.append(out)
     for out in outs:
@@ -332,13 +336,13 @@
     return pl.pallas_call(
         products_kernel,
         out_shape=(tile, tile, eight, eight),
-        in_specs=[pl.BlockSpec(memory_space=pltpu.SMEM)] + [in_hbm()] * 14,
+        in_specs=[pl.BlockSpec(memory_space=pltpu.SMEM)] + [in_hbm()] * (GRADS + 3),
         out_specs=(in_hbm(),) * 4,
-        scratch_shapes=[HELD, SQUARES, TILE, TILE, TILE, TILE, SQUARES, DMA((8,)), DMA((6,)), DMA((10,))],
+        scratch_shapes=[HELD, SQUARES, TILE, TILE, TILE, TILE, SQUARES, DMA((GRADS,)), DMA((3,)), DMA((10,))],
         compiler_params=params(60),
         cost_estimate=pl.CostEstimate(flops=4 * CH * TOK * 4096, bytes_accessed=9 << 20, transcendentals=0),
         name="products",
-    )(where, *grads, *weights, gates, mixed)
+    )(where, *grads, weights, gates, mixed)
 
 
 def exchange(value):
@@ -357,36 +361,33 @@
     tp = lax.axis_index("tp")
     where = jnp.stack([ctx // 4, (ctx // 2) % 2, ctx % 2, tp // 4, tp % 4]).astype(jnp.int32)
 
-    w_line = lax.all_gather(out_weight.T, "ctx", axis_index_groups=LINES_X)
-
-    rest = jnp.stack([send(out_grad, "tp", 1, 4, dz) for dz in (1, 2, 3)])
-    up, down = send(out_grad, "tp", 4, 4, 1), send(out_grad, "tp", 4, 4, 3)
-    up, w_line, own = lax.optimization_barrier((up, w_line, out_grad))
-    near = [up, send(own, "tp", 4, 4, 2), down]
-    rest, near, w_line = lax.optimization_barrier((rest, near, w_line))
-    rests = [send(rest, "tp", 4, 4, dy) for dy in (1, 2, 3)]
-    grads = [out_grad, rest]
-    for n, r in zip(near, rests):
-        grads += [n, r]
-
-    w_far = send(w_line, "ctx", 2, 2, 1)
-    weights = [w_line, w_far, send(w_line, "ctx", 1, 2, 1), send(w_far, "ctx", 1, 2, 1)]
+    w_own = out_weight.T
+    w_pair = jnp.stack([w_own, send(w_own, "ctx", 2, 2, 1)])
+    weights = lax.all_gather(w_pair, "ctx", axis_index_groups=PLANES_X_CORE, tiled=True)
 
     both = jnp.concatenate([inputs.reshape(16, FEW, TOK), filters.reshape(16, FEW, TOK)], axis=1)
     mixed_rows, spec = conv_call(exchange(both))
     mixed = exchange(mixed_rows).reshape(CH, TOK)
 
+    lines = [send(out_grad, "tp", 1, 4, dz) for dz in (1, 2, 3)]
+    up, down = send(out_grad, "tp", 4, 4, 1), send(out_grad, "tp", 4, 4, 3)
+    up, own = lax.optimization_barrier((up, out_grad))
+    far = send(own, "tp", 4, 4, 2)
+    lines, up, far, down, _ = lax.optimization_barrier((lines, up, far, down, mixed_rows))
+    rest = jnp.stack(lines)
+    grads = [out_grad, rest, up, send(rest, "tp", 4, 4, 1), far]
+    grads += [send(far, "tp", 1, 4, dz) for dz in (1, 2, 3)]
+    grads += [down, send(rest, "tp", 4, 4, 3)]
+
     product, gate_grad, part_other, part_same = products_call(where, grads, weights, gates, mixed)
     product_rows = exchange(product.reshape(16, FEW, TOK))
-    received = send(part_other, "ctx", 1, 2, 1)
-    chips = [add(part_same[2 * dx : 2 * dx + 2], received[2 * dx : 2 * dx + 2]) for dx in range(4)]
-    product_rows, chips = lax.optimization_barrier((product_rows, chips))
+    chip = add(part_same, send(part_other, "ctx", 1, 2, 1))
+    line = lax.psum_scatter(chip, "ctx", scatter_dimension=0, axis_index_groups=LINES_X, tiled=True)
     grad_rows = grads_call(product_rows, spec)
     both_grads = exchange(grad_rows)
     input_grad = both_grads[:, :FEW].reshape(CH, TOK)
     filter_grad = both_grads[:, FEW:].reshape(CH, TOK)
 
-    line = add(chips[0], *[send(chips[dx], "ctx", 4, 4, dx) for dx in (1, 2, 3)])
     weight_grad = add(line[0], send(line[1], "ctx", 2, 2, 1))
     return (input_grad, gate_grad, filter_grad, weight_grad)
 

time: 161 us -> 186 us (1.16); the launches traced: 160 us -> 183 us
  waiting for transfers between devices: 57.9 us -> 76.4 us
  between operations: 0.9 us -> 14.3 us
  blocking collectives: 11.3 us -> 0 us
  local copies, waits for them, and re-layouts: 3.24 us -> 7.15 us
  starting transfers between devices: 61.6 us -> 58.4 us
    all_gather x1 -> x0, blocking collectives: 11.3 us -> none  [on_device(): w_line = lax.all_gather(out_weight.T, 'ctx', axis_index_groups=LINES_X)]
    reduce_scatter x0 -> x1, waiting for transfers between devices: none -> 10.1 us  [on_device(): lax.psum_scatter(chip, 'ctx', scatter_dimension=0, axis_index_groups=LINE...]
    ppermute x17 -> x14, waiting for transfers between devices: 38.5 us -> 47.8 us  [send(): return lax.ppermute(value, axis, shift_pairs(stride, size, by))]
    ppermute x17 -> x14, starting transfers between devices: 30.6 us -> 24.1 us  [send(): return lax.ppermute(value, axis, shift_pairs(stride, size, by))]
    all_to_all x4, starting transfers between devices: 30.9 us -> 34.3 us  [exchange(): return lax.all_to_all(value, 'ctx', split_axis=0, concat_axis=0, tiled=True)]
    unnamed x34 -> x35, local copies, waits for them, and re-layouts: 1.57 us -> 4.79 us
    convert_element_type x3 -> x2, other arithmetic: 4.48 us -> 4.52 us  [add(): return total.astype(BF)]
  transfers between devices with their start and end apart: 21 -> 20, of which waited for: 7 -> 11; matrix products, arithmetic and copies ran while one was open for 5% -> 4% of each run, Pallas kernels for 8% -> 7%
where the time goes in v4:
time: 186 us; the launch traced here: 183 us
  waiting for transfers between devices  76.4 us (41%)
  starting transfers between devices  58.4 us (31%)
  Pallas kernels  19.3 us (10%)
  between operations  14.3 us (8%)
  other arithmetic  7.2 us (4%)
  local copies, waits for them, and re-layouts  7.15 us (4%)
    ppermute x14, waiting for transfers between devices, send(): return lax.ppermute(value, axis, shift_pairs(stride, size, by))  47.8 us
    all_to_all x4, starting transfers between devices, exchange(): return lax.all_to_all(value, 'ctx', split_axis=0, concat_axis=0, tiled=True)  34.3 us
    ppermute x14, starting transfers between devices, send(): return lax.ppermute(value, axis, shift_pairs(stride, size, by))  24.1 us
    all_to_all x4, waiting for transfers between devices, exchange(): return lax.all_to_all(value, 'ctx', split_axis=0, concat_axis=0, tiled=True)  18.5 us
    reduce_scatter x1, waiting for transfers between devices, on_device(): lax.psum_scatter(chip, 'ctx', scatter_dimension=0, axis_index_groups=LINE...  10.1 us
    pallas_call x1, Pallas kernels, products_call(): pl.pallas_call(products_kernel, out_shape=(tile, tile, eight, eight), in_...  6.89 us
    pallas_call x1, Pallas kernels, conv_call(): pl.pallas_call(conv_kernel, out_shape=(jax.ShapeDtypeStruct((16, FEW, TOK...  6.67 us
    pallas_call x1, Pallas kernels, grads_call(): pl.pallas_call(grads_kernel, out_shape=jax.ShapeDtypeStruct((16, 2 * FEW,...  5.75 us
  transfers between devices with their start and end apart: 20, of which 11 were waited for; matrix products, arithmetic and copies ran while one was open for 4% of the time, Pallas kernels for 7%

profile of v4, /device:TPU:67, one launch (start us, length us, event | category | flops | bytes accessed | tf_op | source)
XLA Modules:
  0.0 182.8 jit_solution(5887118640644465834)
XLA Ops:
  7.2 0.0 copy-start.12
  7.2 0.0 all-gather.2.cloned.1.call-start
  7.2 1.0 copy.15
  8.3 5.2 %collective-permute-start.11 = (bf16[256,256]{1,0:T(8,128)(2,1)S(1)}, bf16[256,256]{1,0:T(8,128)(2,1)S(1)}, u32[]{:S(2)}, u32[]{:S(2)}) collective-permute-start(bf16[256,256]{1,0:T(8,128)(2,1)S(1)} %bitcast.25), channel_id=1, source_target_pairs={{0,32},{16,48},{32,0},{48,16},{64,96},{80,112},{96,64},{112,80},{1... | collective-permute-start | bytes 393224 | tf_op jit(solution)/shard_map/ppermute | solution.py:32
  13.5 6.4 %collective-permute-done.11 = bf16[256,256]{1,0:T(8,128)(2,1)S(1)} collective-permute-done((bf16[256,256]{1,0:T(8,128)(2,1)S(1)}, bf16[256,256]{1,0:T(8,128)(2,1)S(1)}, u32[]{:S(2)}, u32[]{:S(2)}) %collective-permute-start.11) | collective-permute-done | bytes 131104 | tf_op jit(solution)/shard_map/ppermute | solution.py:32
  19.8 0.7 pad_maximum_fusion.2
  20.6 0.0 all-gather.2.cloned.1.call-update
  20.6 1.9 %pad_maximum_fusion.1 = bf16[16,32,512]{2,1,0:T(8,128)(2,1)} fusion(bf16[16,16,512]{2,1,0:T(8,128)(2,1)} %bitcast.29, bf16[16,16,512]{2,1,0:T(8,128)(2,1)} %bitcast.30), kind=kLoop, calls=%fused_computation.2 | loop fusion | flops 1048576 | bytes 1048576 | tf_op jit(solution)/shard_map/concatenate | solution.py:368
  22.5 10.4 %all-to-all-start = ((bf16[16,32,512]{2,1,0:T(8,128)(2,1)}), bf16[16,32,512]{2,1,0:T(8,128)(2,1)S(1)}, u32[]{:S(2)}, u32[]{:S(2)}) async-start(bf16[16,32,512]{2,1,0:T(8,128)(2,1)} %pad_maximum_fusion.1), calls=%async_computation | async-start | bytes 1048576 | tf_op jit(solution)/shard_map/all_to_all | solution.py:349
  32.8 1.4 collective-permute-start.3
  34.2 0.8 collective-permute-start.2
  35.0 0.4 collective-permute-start.1
  35.4 0.9 collective-permute-start
  36.2 1.6 collective-permute-start.5
  37.8 4.0 %collective-permute-done.3.refs_2_ = bf16[256,512]{1,0:T(8,128)(2,1)S(1)} collective-permute-done((bf16[256,512]{1,0:T(8,128)(2,1)S(1)}, bf16[256,512]{1,0:T(8,128)(2,1)S(1)}, u32[]{:S(2)}, u32[]{:S(2)}) %collective-permute-start.3) | collective-permute-done | bytes 262176 | tf_op jit(solution)/shard_map/ppermute | solution.py:32
  41.8 1.7 collective-permute-start.4
  43.5 12.5 %all-to-all-done.xf_ref = bf16[16,32,512]{2,1,0:T(8,128)(2,1)S(1)} async-done(((bf16[16,32,512]{2,1,0:T(8,128)(2,1)}), bf16[16,32,512]{2,1,0:T(8,128)(2,1)S(1)}, u32[]{:S(2)}, u32[]{:S(2)}) %all-to-all-start) | async-done | bytes 524320 | tf_op jit(solution)/shard_map/all_to_all | solution.py:349
  56.0 0.8 copy-done.8
  56.8 6.7 %conv.1 = (bf16[16,16,512]{2,1,0:T(8,128)(2,1)}, f32[4,1024,128]{2,1,0:T(8,128)}) custom-call(bf16[16,32,512]{2,1,0:T(8,128)(2,1)} %copy-done.8, bf16[128,128]{1,0:T(8,128)(2,1)} %constant.70.clone.refs_0_.first_ref, bf16[768,256]{1,0:T(8,128)(2,1)} %constant.71.clone.refs_1_.second_ref, bf16[768,256]{1,0:T(8,128)(2,1)} %constant.72.clone.refs_2_.back_ref, ...), custom_call_target="tpu_custom_call" | custom-call | flops 1000000000 | bytes 4194304 | tf_op jit(solution)/shard_map/conv/pallas_call | solution.py:229
  63.5 0.0 collective-permute-done.2
  63.5 2.5 %collective-permute-done.1 = bf16[256,512]{1,0:T(8,128)(2,1)S(1)} collective-permute-done((bf16[256,512]{1,0:T(8,128)(2,1)S(1)}, bf16[256,512]{1,0:T(8,128)(2,1)S(1)}, u32[]{:S(2)}, u32[]{:S(2)}) %collective-permute-start.1) | collective-permute-done | bytes 262176 | tf_op jit(solution)/shard_map/ppermute | solution.py:32
  66.0 2.5 %collective-permute-done = bf16[256,512]{1,0:T(8,128)(2,1)S(1)} collective-permute-done((bf16[256,512]{1,0:T(8,128)(2,1)S(1)}, bf16[256,512]{1,0:T(8,128)(2,1)S(1)}, u32[]{:S(2)}, u32[]{:S(2)}) %collective-permute-start) | collective-permute-done | bytes 262176 | tf_op jit(solution)/shard_map/ppermute | solution.py:32
  68.5 0.0 collective-permute-done.5.refs_8_
  68.5 0.0 collective-permute-done.4.refs_4_
  68.5 0.0 copy-start.15
  68.5 0.7 copy-done.15
  69.2 0.1 pad_maximum_fusion.refs_1_
  69.3 0.0 copy-start.7
  69.3 2.8 %collective-permute-start.10 = (bf16[3,256,512]{2,1,0:T(8,128)(2,1)S(1)}, bf16[3,256,512]{2,1,0:T(8,128)(2,1)S(1)}, u32[]{:S(2)}, u32[]{:S(2)}) collective-permute-start(bf16[3,256,512]{2,1,0:T(8,128)(2,1)S(1)} %pad_maximum_fusion.refs_1_), channel_id=1, source_target_pairs={{0,12},{1,13},{2,14},{3,15},{4,0},{5,1},{6,2},{7,3},{8,4},{9,5},{1... | collective-permute-start | bytes 2359304 | tf_op jit(solution)/shard_map/ppermute | solution.py:32
  72.2 0.0 collective-permute-start.6
  72.2 9.7 %all-to-all-start.1 = ((bf16[16,16,512]{2,1,0:T(8,128)(2,1)}), bf16[16,16,512]{2,1,0:T(8,128)(2,1)S(1)}, u32[]{:S(2)}, u32[]{:S(2)}) async-start(bf16[16,16,512]{2,1,0:T(8,128)(2,1)} %get-tuple-element.20), calls=%async_computation.1 | async-start | bytes 524288 | tf_op jit(solution)/shard_map/all_to_all | solution.py:349
  81.9 0.0 collective-permute-start.9
  81.9 1.0 collective-permute-start.8
  82.9 1.4 collective-permute-start.7
  84.3 0.6 stack.44.where_ref
  84.9 7.6 %collective-permute-done.9.refs_7_ = bf16[256,512]{1,0:T(8,128)(2,1)S(1)} collective-permute-done((bf16[256,512]{1,0:T(8,128)(2,1)}, bf16[256,512]{1,0:T(8,128)(2,1)S(1)}, u32[]{:S(2)}, u32[]{:S(2)}) %collective-permute-start.9) | collective-permute-done | bytes 262176 | tf_op jit(solution)/shard_map/ppermute | solution.py:32
  92.4 15.1 %collective-permute-done.8.refs_6_ = bf16[256,512]{1,0:T(8,128)(2,1)} collective-permute-done((bf16[256,512]{1,0:T(8,128)(2,1)}, bf16[256,512]{1,0:T(8,128)(2,1)}, u32[]{:S(2)}, u32[]{:S(2)}) %collective-permute-start.8) | collective-permute-done | bytes 262176 | tf_op jit(solution)/shard_map/ppermute | solution.py:32
  107.5 4.9 %collective-permute-done.7.refs_5_ = bf16[256,512]{1,0:T(8,128)(2,1)} collective-permute-done((bf16[256,512]{1,0:T(8,128)(2,1)}, bf16[256,512]{1,0:T(8,128)(2,1)}, u32[]{:S(2)}, u32[]{:S(2)}) %collective-permute-start.7) | collective-permute-done | bytes 262176 | tf_op jit(solution)/shard_map/ppermute | solution.py:32
  112.4 0.0 all-to-all-done.1
  112.4 0.0 collective-permute-done.10.refs_9_
  112.4 0.0 collective-permute-done.6.refs_3_
  112.5 0.0 all-gather.2.cloned.1.call-done.refs_10_
  112.5 0.6 copy-done.9
  113.1 0.3 copy-done.10
  113.5 0.3 copy-done.11
  113.7 6.9 %products.1 = (bf16[256,512]{1,0:T(8,128)(2,1)}, bf16[256,512]{1,0:T(8,128)(2,1)}, bf16[8,256,256]{2,1,0:T(8,128)(2,1)}, bf16[8,256,256]{2,1,0:T(8,128)(2,1)}) custom-call(s32[5]{0:T(128)} %stack.44.where_ref, bf16[256,512]{1,0:T(8,128)(2,1)} %refs_0_.2, bf16[3,256,512]{2,1,0:T(8,128)(2,1)} %copy-done.7, bf16[256,512]{1,0:T(8,128)(2,1)} %copy-done.13, ...), custom_call_target="tpu_custom_call" | custom-call | flops 2147483648 | bytes 9437184 | tf_op jit(solution)/shard_map/products/pallas_call | solution.py:336
  120.6 0.6 collective-permute-start.12
  121.2 8.7 %all-to-all-start.2 = ((bf16[16,16,512]{2,1,0:T(8,128)(2,1)}), bf16[16,16,512]{2,1,0:T(8,128)(2,1)S(1)}, u32[]{:S(2)}, u32[]{:S(2)}) async-start(bf16[16,16,512]{2,1,0:T(8,128)(2,1)} %bitcast.28), calls=%async_computation.2 | async-start | bytes 524288 | tf_op jit(solution)/shard_map/all_to_all | solution.py:349
  129.9 0.0 reduce-scatter.2.cloned.1.call-start
  130.0 0.0 collective-permute-done.12
  130.0 1.0 copy-done.6
  131.0 0.0 copy-start.4
  131.0 2.9 %add_convert_fusion = bf16[8,256,256]{2,1,0:T(8,128)(2,1)} fusion(bf16[8,256,256]{2,1,0:T(8,128)(2,1)} %copy-done.6, bf16[8,256,256]{2,1,0:T(8,128)(2,1)} %get-tuple-element.30), kind=kLoop, calls=%fused_computation | loop fusion | flops 2097152 | bytes 3145728 | tf_op jit(solution)/shard_map/convert_element_type | solution.py:356
  133.9 0.0 reduce-scatter.2.cloned.1.call-update
  133.9 6.0 %all-to-all-done.2.p_ref = bf16[16,16,512]{2,1,0:T(8,128)(2,1)S(1)} async-done(((bf16[16,16,512]{2,1,0:T(8,128)(2,1)}), bf16[16,16,512]{2,1,0:T(8,128)(2,1)S(1)}, u32[]{:S(2)}, u32[]{:S(2)}) %all-to-all-start.2) | async-done | bytes 262176 | tf_op jit(solution)/shard_map/all_to_all | solution.py:349
  139.9 5.7 %grads.1 = bf16[16,32,512]{2,1,0:T(8,128)(2,1)} custom-call(bf16[16,16,512]{2,1,0:T(8,128)(2,1)S(1)} %all-to-all-done.2.p_ref, bf16[128,128]{1,0:T(8,128)(2,1)S(1)} %copy-done.4, bf16[768,256]{1,0:T(8,128)(2,1)S(1)} %copy-done.1, bf16[768,256]{1,0:T(8,128)(2,1)S(1)} %copy-done, bf16[64,384]{1,0:T(8,128)(2,1)S(1)} %copy-done.3, f32[2,64,128]{2,1,0:T(8,128)S(1)} %copy-done.2, ...), custom_call_target="tpu_custom_call" | custom-call | flops 10000000000 | bytes 4194304 | tf_op jit(solution)/shard_map/grads/pallas_call | solution.py:245
  145.7 5.5 %all-to-all-start.3 = ((bf16[16,32,512]{2,1,0:T(8,128)(2,1)}), bf16[16,32,512]{2,1,0:T(8,128)(2,1)S(1)}, u32[]{:S(2)}, u32[]{:S(2)}) async-start(bf16[16,32,512]{2,1,0:T(8,128)(2,1)} %grads.1), calls=%async_computation.3 | async-start | bytes 1048576 | tf_op jit(solution)/shard_map/all_to_all | solution.py:349
  151.1 10.1 %reduce-scatter.2.cloned.1.call-done = bf16[2,256,256]{2,1,0:T(8,128)(2,1)} async-done(((bf16[8,256,256]{2,1,0:T(8,128)(2,1)}), bf16[2,256,256]{2,1,0:T(8,128)(2,1)}) %reduce-scatter.2.cloned.1.call-update) | async-done | bytes 262160 | tf_op jit(solution)/shard_map/reduce_scatter | solution.py:385
  161.2 0.9 slice_bitcast_fusion
  162.1 6.5 %collective-permute-start.13 = (bf16[256,256]{1,0:T(8,128)(2,1)S(1)}, bf16[256,256]{1,0:T(8,128)(2,1)S(1)}, u32[]{:S(2)}, u32[]{:S(2)}) collective-permute-start(bf16[256,256]{1,0:T(8,128)(2,1)S(1)} %slice_bitcast_fusion), channel_id=1, source_target_pairs={{0,32},{16,48},{32,0},{48,16},{64,96},{80,112},{96,64},{112,80},{1... | collective-permute-start | bytes 393224 | tf_op jit(solution)/shard_map/ppermute | solution.py:32
  168.6 0.0 all-to-all-done.3
  168.6 0.8 fusion.1
  169.4 4.9 %collective-permute-done.13 = bf16[256,256]{1,0:T(8,128)(2,1)S(1)} collective-permute-done((bf16[256,256]{1,0:T(8,128)(2,1)S(1)}, bf16[256,256]{1,0:T(8,128)(2,1)S(1)}, u32[]{:S(2)}, u32[]{:S(2)}) %collective-permute-start.13) | collective-permute-done | bytes 131104 | tf_op jit(solution)/shard_map/ppermute | solution.py:32
  174.3 1.6 fusion
  (24 shorter events, 0.0 us)
Async XLA Ops:
  7.2 25.7 %copy-start.12 = (bf16[256,512]{1,0:T(8,128)(2,1)S(1)}, bf16[256,512]{1,0:T(8,128)(2,1)}, u32[]{:S(2)}) copy-start(bf16[256,512]{1,0:T(8,128)(2,1)} %refs_0_.2) | copy-start | bytes 786436
  7.2 105.3 %all-gather.2.cloned.1.call-start = ((), (), s32[]{:S(2)}) async-start(), calls=%async_computation.5 | async-start | bytes 2359296 | tf_op jit(solution)/shard_map/all_gather | solution.py:366
  8.3 11.6 %collective-permute-start.11 = (bf16[256,256]{1,0:T(8,128)(2,1)S(1)}, bf16[256,256]{1,0:T(8,128)(2,1)S(1)}, u32[]{:S(2)}, u32[]{:S(2)}) collective-permute-start(bf16[256,256]{1,0:T(8,128)(2,1)S(1)} %bitcast.25), channel_id=1, source_target_pairs={{0,32},{16,48},{32,0},{48,16},{64,96},{80,112},{96,64},{112,80},{1... | collective-permute-start | bytes 393224 | tf_op jit(solution)/shard_map/ppermute | solution.py:32
  22.5 33.6 %all-to-all-start = ((bf16[16,32,512]{2,1,0:T(8,128)(2,1)}), bf16[16,32,512]{2,1,0:T(8,128)(2,1)S(1)}, u32[]{:S(2)}, u32[]{:S(2)}) async-start(bf16[16,32,512]{2,1,0:T(8,128)(2,1)} %pad_maximum_fusion.1), calls=%async_computation | async-start | bytes 1048576 | tf_op jit(solution)/shard_map/all_to_all | solution.py:349
  32.8 9.0 %collective-permute-start.3 = (bf16[256,512]{1,0:T(8,128)(2,1)S(1)}, bf16[256,512]{1,0:T(8,128)(2,1)S(1)}, u32[]{:S(2)}, u32[]{:S(2)}) collective-permute-start(bf16[256,512]{1,0:T(8,128)(2,1)S(1)} %copy-done.12), channel_id=1, source_target_pairs={{0,4},{1,5},{2,6},{3,7},{4,8},{5,9},{6,10},{7,11},{8,12},{9,13},{1... | collective-permute-start | bytes 786440 | tf_op jit(solution)/shard_map/ppermute | solution.py:32
  34.2 29.3 %collective-permute-start.2 = (bf16[256,512]{1,0:T(8,128)(2,1)S(1)}, bf16[256,512]{1,0:T(8,128)(2,1)S(1)}, u32[]{:S(2)}, u32[]{:S(2)}) collective-permute-start(bf16[256,512]{1,0:T(8,128)(2,1)S(1)} %copy-done.12), channel_id=1, source_target_pairs={{0,3},{1,0},{2,1},{3,2},{4,7},{5,4},{6,5},{7,6},{8,11},{9,8},{10,9... | collective-permute-start | bytes 786440 | tf_op jit(solution)/shard_map/ppermute | solution.py:32
  35.0 31.0 %collective-permute-start.1 = (bf16[256,512]{1,0:T(8,128)(2,1)S(1)}, bf16[256,512]{1,0:T(8,128)(2,1)S(1)}, u32[]{:S(2)}, u32[]{:S(2)}) collective-permute-start(bf16[256,512]{1,0:T(8,128)(2,1)S(1)} %copy-done.12), channel_id=1, source_target_pairs={{0,2},{1,3},{2,0},{3,1},{4,6},{5,7},{6,4},{7,5},{8,10},{9,11},{10,... | collective-permute-start | bytes 786440 | tf_op jit(solution)/shard_map/ppermute | solution.py:32
  35.4 33.1 %collective-permute-start = (bf16[256,512]{1,0:T(8,128)(2,1)S(1)}, bf16[256,512]{1,0:T(8,128)(2,1)S(1)}, u32[]{:S(2)}, u32[]{:S(2)}) collective-permute-start(bf16[256,512]{1,0:T(8,128)(2,1)S(1)} %copy-done.12), channel_id=1, source_target_pairs={{0,1},{1,2},{2,3},{3,0},{4,5},{5,6},{6,7},{7,4},{8,9},{9,10},{10,1... | collective-permute-start | bytes 786440 | tf_op jit(solution)/shard_map/ppermute | solution.py:32
  36.2 32.3 %collective-permute-start.5 = (bf16[256,512]{1,0:T(8,128)(2,1)S(1)}, bf16[256,512]{1,0:T(8,128)(2,1)S(1)}, u32[]{:S(2)}, u32[]{:S(2)}) collective-permute-start(bf16[256,512]{1,0:T(8,128)(2,1)S(1)} %copy-done.12), channel_id=1, source_target_pairs={{0,12},{1,13},{2,14},{3,15},{4,0},{5,1},{6,2},{7,3},{8,4},{9,5},{1... | collective-permute-start | bytes 786440 | tf_op jit(solution)/shard_map/ppermute | solution.py:32
  41.8 70.7 %copy-start.13 = (bf16[256,512]{1,0:T(8,128)(2,1)}, bf16[256,512]{1,0:T(8,128)(2,1)S(1)}, u32[]{:S(2)}) copy-start(bf16[256,512]{1,0:T(8,128)(2,1)S(1)} %collective-permute-done.3.refs_2_) | copy-start | bytes 786436
  41.8 26.7 %collective-permute-start.4 = (bf16[256,512]{1,0:T(8,128)(2,1)S(1)}, bf16[256,512]{1,0:T(8,128)(2,1)S(1)}, u32[]{:S(2)}, u32[]{:S(2)}) collective-permute-start(bf16[256,512]{1,0:T(8,128)(2,1)S(1)} %copy-done.12), channel_id=1, source_target_pairs={{0,8},{1,9},{2,10},{3,11},{4,12},{5,13},{6,14},{7,15},{8,0},{9,1},... | collective-permute-start | bytes 786440 | tf_op jit(solution)/shard_map/ppermute | solution.py:32
  56.0 0.8 copy-start.8
  68.5 44.0 %copy-start.14 = (bf16[256,512]{1,0:T(8,128)(2,1)}, bf16[256,512]{1,0:T(8,128)(2,1)S(1)}, u32[]{:S(2)}) copy-start(bf16[256,512]{1,0:T(8,128)(2,1)S(1)} %collective-permute-done.5.refs_8_) | copy-start | bytes 786436
  68.5 0.7 copy-start.15
  69.3 43.2 %copy-start.7 = (bf16[3,256,512]{2,1,0:T(8,128)(2,1)}, bf16[3,256,512]{2,1,0:T(8,128)(2,1)S(1)}, u32[]{:S(2)}) copy-start(bf16[3,256,512]{2,1,0:T(8,128)(2,1)S(1)} %pad_maximum_fusion.refs_1_) | copy-start | bytes 2359300
  69.3 43.1 %collective-permute-start.10 = (bf16[3,256,512]{2,1,0:T(8,128)(2,1)S(1)}, bf16[3,256,512]{2,1,0:T(8,128)(2,1)S(1)}, u32[]{:S(2)}, u32[]{:S(2)}) collective-permute-start(bf16[3,256,512]{2,1,0:T(8,128)(2,1)S(1)} %pad_maximum_fusion.refs_1_), channel_id=1, source_target_pairs={{0,12},{1,13},{2,14},{3,15},{4,0},{5,1},{6,2},{7,3},{8,4},{9,5},{1... | collective-permute-start | bytes 2359304 | tf_op jit(solution)/shard_map/ppermute | solution.py:32
  72.2 40.3 %collective-permute-start.6 = (bf16[3,256,512]{2,1,0:T(8,128)(2,1)S(1)}, bf16[3,256,512]{2,1,0:T(8,128)(2,1)S(1)}, u32[]{:S(2)}, u32[]{:S(2)}) collective-permute-start(bf16[3,256,512]{2,1,0:T(8,128)(2,1)S(1)} %pad_maximum_fusion.refs_1_), channel_id=1, source_target_pairs={{0,4},{1,5},{2,6},{3,7},{4,8},{5,9},{6,10},{7,11},{8,12},{9,13},{1... | collective-permute-start | bytes 2359304 | tf_op jit(solution)/shard_map/ppermute | solution.py:32
  72.2 40.3 %all-to-all-start.1 = ((bf16[16,16,512]{2,1,0:T(8,128)(2,1)}), bf16[16,16,512]{2,1,0:T(8,128)(2,1)S(1)}, u32[]{:S(2)}, u32[]{:S(2)}) async-start(bf16[16,16,512]{2,1,0:T(8,128)(2,1)} %get-tuple-element.20), calls=%async_computation.1 | async-start | bytes 524288 | tf_op jit(solution)/shard_map/all_to_all | solution.py:349
  81.9 10.6 %collective-permute-start.9 = (bf16[256,512]{1,0:T(8,128)(2,1)}, bf16[256,512]{1,0:T(8,128)(2,1)S(1)}, u32[]{:S(2)}, u32[]{:S(2)}) collective-permute-start(bf16[256,512]{1,0:T(8,128)(2,1)} %copy-done.15), channel_id=1, source_target_pairs={{0,3},{1,0},{2,1},{3,2},{4,7},{5,4},{6,5},{7,6},{8,11},{9,8},{10,9... | collective-permute-start | bytes 786440 | tf_op jit(solution)/shard_map/ppermute | solution.py:32
  81.9 25.6 %collective-permute-start.8 = (bf16[256,512]{1,0:T(8,128)(2,1)}, bf16[256,512]{1,0:T(8,128)(2,1)}, u32[]{:S(2)}, u32[]{:S(2)}) collective-permute-start(bf16[256,512]{1,0:T(8,128)(2,1)} %copy-done.15), channel_id=1, source_target_pairs={{0,2},{1,3},{2,0},{3,1},{4,6},{5,7},{6,4},{7,5},{8,10},{9,11},{10,... | collective-permute-start | bytes 786440 | tf_op jit(solution)/shard_map/ppermute | solution.py:32
  82.9 29.5 %collective-permute-start.7 = (bf16[256,512]{1,0:T(8,128)(2,1)}, bf16[256,512]{1,0:T(8,128)(2,1)}, u32[]{:S(2)}, u32[]{:S(2)}) collective-permute-start(bf16[256,512]{1,0:T(8,128)(2,1)} %copy-done.15), channel_id=1, source_target_pairs={{0,1},{1,2},{2,3},{3,0},{4,5},{5,6},{6,7},{7,4},{8,9},{9,10},{10,1... | collective-permute-start | bytes 786440 | tf_op jit(solution)/shard_map/ppermute | solution.py:32
  92.4 20.1 %copy-start.16 = (bf16[256,512]{1,0:T(8,128)(2,1)}, bf16[256,512]{1,0:T(8,128)(2,1)S(1)}, u32[]{:S(2)}) copy-start(bf16[256,512]{1,0:T(8,128)(2,1)S(1)} %collective-permute-done.9.refs_7_) | copy-start | bytes 786436
  112.4 0.7 copy-start.9
  112.4 1.0 copy-start.10
  112.4 1.3 copy-start.11
  120.6 9.3 %collective-permute-start.12 = (bf16[8,256,256]{2,1,0:T(8,128)(2,1)}, bf16[8,256,256]{2,1,0:T(8,128)(2,1)S(1)}, u32[]{:S(2)}, u32[]{:S(2)}) collective-permute-start(bf16[8,256,256]{2,1,0:T(8,128)(2,1)} %get-tuple-element.31), channel_id=1, source_target_pairs={{0,16},{16,0},{32,48},{48,32},{64,80},{80,64},{96,112},{112,96},{1... | collective-permute-start | bytes 3145736 | tf_op jit(solution)/shard_map/ppermute | solution.py:32
  121.2 18.7 %all-to-all-start.2 = ((bf16[16,16,512]{2,1,0:T(8,128)(2,1)}), bf16[16,16,512]{2,1,0:T(8,128)(2,1)S(1)}, u32[]{:S(2)}, u32[]{:S(2)}) async-start(bf16[16,16,512]{2,1,0:T(8,128)(2,1)} %bitcast.28), calls=%async_computation.2 | async-start | bytes 524288 | tf_op jit(solution)/shard_map/all_to_all | solution.py:349
  129.9 31.3 %reduce-scatter.2.cloned.1.call-start = ((), (), s32[]{:S(2)}) async-start(), calls=%async_computation.6 | async-start | bytes 1310720 | tf_op jit(solution)/shard_map/reduce_scatter | solution.py:385
  130.0 1.0 copy-start.6
  131.0 8.9 %copy-start = (bf16[768,256]{1,0:T(8,128)(2,1)S(1)}, bf16[768,256]{1,0:T(8,128)(2,1)}, u32[]{:S(2)}) copy-start(bf16[768,256]{1,0:T(8,128)(2,1)} %constant.72.clone.refs_2_.back_ref) | copy-start | bytes 1179652
  131.0 8.9 %copy-start.1 = (bf16[768,256]{1,0:T(8,128)(2,1)S(1)}, bf16[768,256]{1,0:T(8,128)(2,1)}, u32[]{:S(2)}) copy-start(bf16[768,256]{1,0:T(8,128)(2,1)} %constant.71.clone.refs_1_.second_ref) | copy-start | bytes 1179652
  131.0 8.9 %copy-start.2 = (f32[2,64,128]{2,1,0:T(8,128)S(1)}, f32[2,64,128]{2,1,0:T(8,128)}, u32[]{:S(2)}) copy-start(f32[2,64,128]{2,1,0:T(8,128)} %constant.74.clone.refs_4_.turn_ref) | copy-start | bytes 196612
  131.0 9.0 %copy-start.3 = (bf16[64,384]{1,0:T(8,128)(2,1)S(1)}, bf16[64,384]{1,0:T(8,128)(2,1)}, u32[]{:S(2)}) copy-start(bf16[64,384]{1,0:T(8,128)(2,1)} %constant.73.clone.refs_3_.last_ref) | copy-start | bytes 147460
  131.0 9.0 %copy-start.4 = (bf16[128,128]{1,0:T(8,128)(2,1)S(1)}, bf16[128,128]{1,0:T(8,128)(2,1)}, u32[]{:S(2)}) copy-start(bf16[128,128]{1,0:T(8,128)(2,1)} %constant.70.clone.refs_0_.first_ref) | copy-start | bytes 98308
  131.0 9.0 %copy-start.5 = (f32[4,1024,128]{2,1,0:T(8,128)S(1)}, f32[4,1024,128]{2,1,0:T(8,128)}, u32[]{:S(2)}) copy-start(f32[4,1024,128]{2,1,0:T(8,128)} %get-tuple-element.28.spec_ref) | copy-start | bytes 6291460
  145.7 22.9 %all-to-all-start.3 = ((bf16[16,32,512]{2,1,0:T(8,128)(2,1)}), bf16[16,32,512]{2,1,0:T(8,128)(2,1)S(1)}, u32[]{:S(2)}, u32[]{:S(2)}) async-start(bf16[16,32,512]{2,1,0:T(8,128)(2,1)} %grads.1), calls=%async_computation.3 | async-start | bytes 1048576 | tf_op jit(solution)/shard_map/all_to_all | solution.py:349
  162.1 12.2 %collective-permute-start.13 = (bf16[256,256]{1,0:T(8,128)(2,1)S(1)}, bf16[256,256]{1,0:T(8,128)(2,1)S(1)}, u32[]{:S(2)}, u32[]{:S(2)}) collective-permute-start(bf16[256,256]{1,0:T(8,128)(2,1)S(1)} %slice_bitcast_fusion), channel_id=1, source_target_pairs={{0,32},{16,48},{32,0},{48,16},{64,96},{80,112},{96,64},{112,80},{1... | collective-permute-start | bytes 393224 | tf_op jit(solution)/shard_map/ppermute | solution.py:32
Sparse Core Ops, SparseCore 0:
  20.7 29.8 all-gather.1
  134.1 27.1 reduce-scatter.1

commit v5 on v3

--- a/solution.py
+++ b/solution.py
@@ -280,13 +280,14 @@
 
 
 def products_kernel(where_ref, *refs):
-    grads, ins_hbm = refs[:8], refs[8:14]
-    product_hbm, gate_grad_hbm, other_hbm, same_hbm = refs[14:18]
-    held, weights, gates_ref, mixed_ref, product_ref, gate_grad_ref, sums, grad_sems, sems, out_sems = refs[18:]
-    targets = [weights.at[pl.ds(4 * i, 4)] for i in range(4)] + [gates_ref, mixed_ref]
+    grads, ins_hbm = refs[:8], refs[8:15]
+    product_hbm, gate_grad_hbm, other_hbm, same_hbm = refs[15:19]
+    held, weights, gates_ref, mixed_ref, product_ref, gate_grad_ref, sums, grad_sems, sems, out_sems = refs[19:]
+    targets = [weights.at[pl.ds(4 * i, 4)] for i in range(3)] + [weights.at[pl.ds(12 + i, 2)] for i in (0, 2)]
+    targets += [gates_ref, mixed_ref]
     ins = fetch(ins_hbm, targets, sems)
     copies = fetch_grads(grads, held, grad_sems)
-    for copy in ins[:4]:
+    for copy in ins[:5]:
         copy.wait()
     total = None
     for dy in range(4):
@@ -296,12 +297,12 @@
         part = dot(weight, held[4 * dy : 4 * dy + 4].reshape(4 * CH, TOK))
         total = part if total is None else total + part
     slope = total.astype(BF).astype(F32)
-    ins[4].wait()
+    ins[5].wait()
     gates = gates_ref[...].astype(F32)
     product_ref[...] = (slope * gates).astype(BF)
     outs = [pltpu.make_async_copy(product_ref, product_hbm, out_sems.at[0])]
     outs[0].start()
-    ins[5].wait()
+    ins[6].wait()
     mixed = mixed_ref[...].astype(F32)
     gate_grad_ref[...] = (slope * mixed).astype(BF)
     outs.append(pltpu.make_async_copy(gate_grad_ref, gate_grad_hbm, out_sems.at[1]))
@@ -321,6 +322,25 @@
         out.wait()
 
 
+def stack_kernel(*refs):
+    ins, out, sems = refs[:-2], refs[-2], refs[-1]
+    for copy in fetch(ins, [out.at[i] for i in range(len(ins))], sems):
+        copy.wait()
+
+
+def stack_call(parts):
+    return pl.pallas_call(
+        stack_kernel,
+        out_shape=jax.ShapeDtypeStruct((len(parts),) + parts[0].shape, BF),
+        in_specs=[in_hbm()] * len(parts),
+        out_specs=in_hbm(),
+        scratch_shapes=[DMA((len(parts),))],
+        compiler_params=params(60),
+        cost_estimate=pl.CostEstimate(flops=3 * 10**10, bytes_accessed=2 << 20, transcendentals=0),
+        name="stack",
+    )(*parts)
+
+
 HELD = pltpu.VMEM((16, CH, TOK), BF)
 SQUARES = pltpu.VMEM((16, 256, 256), BF)
 TILE = pltpu.VMEM((CH, TOK), BF)
@@ -332,9 +352,9 @@
     return pl.pallas_call(
         products_kernel,
         out_shape=(tile, tile, eight, eight),
-        in_specs=[pl.BlockSpec(memory_space=pltpu.SMEM)] + [in_hbm()] * 14,
+        in_specs=[pl.BlockSpec(memory_space=pltpu.SMEM)] + [in_hbm()] * 15,
         out_specs=(in_hbm(),) * 4,
-        scratch_shapes=[HELD, SQUARES, TILE, TILE, TILE, TILE, SQUARES, DMA((8,)), DMA((6,)), DMA((10,))],
+        scratch_shapes=[HELD, SQUARES, TILE, TILE, TILE, TILE, SQUARES, DMA((8,)), DMA((7,)), DMA((10,))],
         compiler_params=params(60),
         cost_estimate=pl.CostEstimate(flops=4 * CH * TOK * 4096, bytes_accessed=9 << 20, transcendentals=0),
         name="products",
@@ -359,10 +379,14 @@
 
     w_line = lax.all_gather(out_weight.T, "ctx", axis_index_groups=LINES_X)
 
-    rest = jnp.stack([send(out_grad, "tp", 1, 4, dz) for dz in (1, 2, 3)])
-    up, down = send(out_grad, "tp", 4, 4, 1), send(out_grad, "tp", 4, 4, 3)
-    up, w_line, own = lax.optimization_barrier((up, w_line, out_grad))
-    near = [up, send(own, "tp", 4, 4, 2), down]
+    both = jnp.concatenate([inputs.reshape(16, FEW, TOK), filters.reshape(16, FEW, TOK)], axis=1)
+    mixed_rows, spec = conv_call(exchange(both))
+    mixed = exchange(mixed_rows).reshape(CH, TOK)
+
+    rest = stack_call([send(out_grad, "tp", 1, 4, dz) for dz in (1, 2, 3)])
+    up, far = send(out_grad, "tp", 4, 4, 1), send(out_grad, "tp", 4, 4, 2)
+    up, own = lax.optimization_barrier((up, out_grad))
+    near = [up, far, send(own, "tp", 4, 4, 3)]
     rest, near, w_line = lax.optimization_barrier((rest, near, w_line))
     rests = [send(rest, "tp", 4, 4, dy) for dy in (1, 2, 3)]
     grads = [out_grad, rest]
@@ -370,11 +394,9 @@
         grads += [n, r]
 
     w_far = send(w_line, "ctx", 2, 2, 1)
-    weights = [w_line, w_far, send(w_line, "ctx", 1, 2, 1), send(w_far, "ctx", 1, 2, 1)]
-
-    both = jnp.concatenate([inputs.reshape(16, FEW, TOK), filters.reshape(16, FEW, TOK)], axis=1)
-    mixed_rows, spec = conv_call(exchange(both))
-    mixed = exchange(mixed_rows).reshape(CH, TOK)
+    w_line, w_far, _ = lax.optimization_barrier((w_line, w_far, mixed_rows))
+    weights = [w_line, w_far, send(w_line, "ctx", 1, 2, 1)]
+    weights += [send(w_far[i : i + 2], "ctx", 1, 2, 1) for i in (0, 2)]
 
     product, gate_grad, part_other, part_same = products_call(where, grads, weights, gates, mixed)
     product_rows = exchange(product.reshape(16, FEW, TOK))

time: 161 us -> 179 us (1.11)
  Pallas kernels: 19 us -> 44 us
  waiting for transfers between devices: 57.9 us -> 43.2 us
  starting transfers between devices: 61.6 us -> 66.3 us
    pallas_call x0 -> x1, Pallas kernels: none -> 24.9 us  [stack_call(): pl.pallas_call(stack_kernel, out_shape=jax.ShapeDtypeStruct((len(parts),)...]
    all_to_all x4, waiting for transfers between devices: 19.5 us -> 12 us  [exchange(): return lax.all_to_all(value, 'ctx', split_axis=0, concat_axis=0, tiled=True)]
    ppermute x17 -> x18, waiting for transfers between devices: 38.5 us -> 31.2 us  [send(): return lax.ppermute(value, axis, shift_pairs(stride, size, by))]
    ppermute x17 -> x18, starting transfers between devices: 30.6 us -> 34.5 us  [send(): return lax.ppermute(value, axis, shift_pairs(stride, size, by))]
  transfers between devices with their start and end apart: 21 -> 22, of which waited for: 7 -> 7; matrix products, arithmetic and copies ran while one was open for 5% -> 4% of each run, Pallas kernels for 8% -> 21%
where the time goes in v5:
time: 179 us; the launch traced here: 177 us
  starting transfers between devices  66.3 us (37%)
  Pallas kernels  44 us (25%)
  waiting for transfers between devices  43.2 us (24%)
  blocking collectives  11.5 us (6%)
  other arithmetic  6.34 us (4%)
  local copies, waits for them, and re-layouts  4.65 us (3%)
    ppermute x18, starting transfers between devices, send(): return lax.ppermute(value, axis, shift_pairs(stride, size, by))  34.5 us
    all_to_all x4, starting transfers between devices, exchange(): return lax.all_to_all(value, 'ctx', split_axis=0, concat_axis=0, tiled=True)  31.8 us
    ppermute x18, waiting for transfers between devices, send(): return lax.ppermute(value, axis, shift_pairs(stride, size, by))  31.2 us
    pallas_call x1, Pallas kernels, stack_call(): pl.pallas_call(stack_kernel, out_shape=jax.ShapeDtypeStruct((len(parts),)...  24.9 us
    all_to_all x4, waiting for transfers between devices, exchange(): return lax.all_to_all(value, 'ctx', split_axis=0, concat_axis=0, tiled=True)  12 us
    all_gather x1, blocking collectives, on_device(): w_line = lax.all_gather(out_weight.T, 'ctx', axis_index_groups=LINES_X)  11.5 us
    pallas_call x1, Pallas kernels, conv_call(): pl.pallas_call(conv_kernel, out_shape=(jax.ShapeDtypeStruct((16, FEW, TOK...  6.66 us
    pallas_call x1, Pallas kernels, products_call(): pl.pallas_call(products_kernel, out_shape=(tile, tile, eight, eight), in_...  6.65 us
  transfers between devices with their start and end apart: 22, of which 7 were waited for; matrix products, arithmetic and copies ran while one was open for 4% of the time, Pallas kernels for 21%

profile of v5, /device:TPU:67, one launch (start us, length us, event | category | flops | bytes accessed | tf_op | source)
XLA Modules:
  0.0 176.9 jit_solution(6208810285718397031)
XLA Ops:
  0.6 0.0 copy-start.13
  0.7 1.4 collective-permute-start.3
  2.0 0.0 collective-permute-start.2
  2.0 3.7 %collective-permute-start.1 = (bf16[256,512]{1,0:T(8,128)(2,1)}, bf16[256,512]{1,0:T(8,128)(2,1)S(1)}, u32[]{:S(2)}, u32[]{:S(2)}) collective-permute-start(bf16[256,512]{1,0:T(8,128)(2,1)} %refs_0_.2), channel_id=1, source_target_pairs={{0,2},{1,3},{2,0},{3,1},{4,6},{5,7},{6,4},{7,5},{8,10},{9,11},{10,... | collective-permute-start | bytes 786440 | tf_op jit(solution)/shard_map/ppermute | solution.py:32
  5.7 0.0 collective-permute-start
  5.7 2.6 %collective-permute-start.4 = (bf16[256,512]{1,0:T(8,128)(2,1)}, bf16[256,512]{1,0:T(8,128)(2,1)S(1)}, u32[]{:S(2)}, u32[]{:S(2)}) collective-permute-start(bf16[256,512]{1,0:T(8,128)(2,1)} %refs_0_.2), channel_id=1, source_target_pairs={{0,8},{1,9},{2,10},{3,11},{4,12},{5,13},{6,14},{7,15},{8,0},{9,1},... | collective-permute-start | bytes 786440 | tf_op jit(solution)/shard_map/ppermute | solution.py:32
  8.4 1.9 %pad_maximum_fusion = bf16[16,32,512]{2,1,0:T(8,128)(2,1)} fusion(bf16[16,16,512]{2,1,0:T(8,128)(2,1)} %bitcast.25, bf16[16,16,512]{2,1,0:T(8,128)(2,1)} %bitcast.26), kind=kLoop, calls=%fused_computation | loop fusion | flops 1048576 | bytes 1048576 | tf_op jit(solution)/shard_map/concatenate | solution.py:382
  10.2 10.3 %all-to-all-start = ((bf16[16,32,512]{2,1,0:T(8,128)(2,1)}), bf16[16,32,512]{2,1,0:T(8,128)(2,1)S(1)}, u32[]{:S(2)}, u32[]{:S(2)}) async-start(bf16[16,32,512]{2,1,0:T(8,128)(2,1)} %pad_maximum_fusion), calls=%async_computation | async-start | bytes 1048576 | tf_op jit(solution)/shard_map/all_to_all | solution.py:365
  20.6 11.5 %all-gather = bf16[1024,256]{0,1:T(8,128)(2,1)S(1)} all-gather(bf16[256,256]{0,1:T(8,128)(2,1)S(1)} %bitcast.29), channel_id=2, replica_groups={{0,64,128,192},{16,80,144,208},{32,96,160,224},{48,112,176,240},{1,65,1..., dimensions={0}, use_global_device_ids=true | all-gather | bytes 655360 | tf_op jit(solution)/shard_map/all_gather | solution.py:380
  32.1 0.2 copy.14
  32.3 0.0 collective-permute-done.3.refs_2_
  32.3 1.1 collective-permute-start.5
  33.4 0.0 collective-permute-done.2.refs_2_
  33.4 0.0 collective-permute-done.1.refs_1_
  33.4 0.0 copy-start.18
  33.4 2.4 %collective-permute-done.refs_0_ = bf16[256,512]{1,0:T(8,128)(2,1)S(1)} collective-permute-done((bf16[256,512]{1,0:T(8,128)(2,1)}, bf16[256,512]{1,0:T(8,128)(2,1)S(1)}, u32[]{:S(2)}, u32[]{:S(2)}) %collective-permute-start) | collective-permute-done | bytes 262176 | tf_op jit(solution)/shard_map/ppermute | solution.py:32
  35.8 0.7 copy-done.19
  36.5 24.9 %stack.25.refs_1_ = bf16[3,256,512]{2,1,0:T(8,128)(2,1)} custom-call(bf16[256,512]{1,0:T(8,128)(2,1)} %copy-done.19, bf16[256,512]{1,0:T(8,128)(2,1)} %copy-done.18, bf16[256,512]{1,0:T(8,128)(2,1)} %copy-done.17), custom_call_target="tpu_custom_call" | custom-call | flops 30000001024 | bytes 2097152 | tf_op jit(solution)/shard_map/stack/pallas_call | solution.py:332
  61.5 0.0 collective-permute-done.4.refs_4_
  61.5 0.0 copy-start.15
  61.5 0.0 collective-permute-done.5.refs_6_
  61.5 0.0 copy-start.16
  61.6 0.7 copy-done.15
  62.2 8.9 %collective-permute-start.9 = (bf16[4,256,256]{2,1,0:T(8,128)(2,1)S(1)}, bf16[4,256,256]{2,1,0:T(8,128)(2,1)S(1)}, u32[]{:S(2)}, u32[]{:S(2)}) collective-permute-start(bf16[4,256,256]{2,1,0:T(8,128)(2,1)S(1)} %bitcast.20), channel_id=1, source_target_pairs={{0,32},{16,48},{32,0},{48,16},{64,96},{80,112},{96,64},{112,80},{1... | collective-permute-start | bytes 1572872 | tf_op jit(solution)/shard_map/ppermute | solution.py:32
  71.1 1.5 collective-permute-start.8
  72.6 1.5 collective-permute-start.7
  74.2 0.4 collective-permute-start.6
  74.6 0.0 all-to-all-done.xf_ref
  74.6 0.8 copy-done.8
  75.4 6.7 %conv.1 = (bf16[16,16,512]{2,1,0:T(8,128)(2,1)}, f32[4,1024,128]{2,1,0:T(8,128)}) custom-call(bf16[16,32,512]{2,1,0:T(8,128)(2,1)} %copy-done.8, bf16[128,128]{1,0:T(8,128)(2,1)} %constant.70.clone.refs_0_.first_ref, bf16[768,256]{1,0:T(8,128)(2,1)} %constant.71.clone.refs_1_.second_ref, bf16[768,256]{1,0:T(8,128)(2,1)} %constant.72.clone.refs_2_.back_ref, ...), custom_call_target="tpu_custom_call" | custom-call | flops 1000000000 | bytes 4194304 | tf_op jit(solution)/shard_map/conv/pallas_call | solution.py:228
  82.1 10.6 %collective-permute-done.9.refs_9_ = bf16[4,256,256]{2,1,0:T(8,128)(2,1)S(1)} collective-permute-done((bf16[4,256,256]{2,1,0:T(8,128)(2,1)S(1)}, bf16[4,256,256]{2,1,0:T(8,128)(2,1)S(1)}, u32[]{:S(2)}, u32[]{:S(2)}) %collective-permute-start.9) | collective-permute-done | bytes 524320 | tf_op jit(solution)/shard_map/ppermute | solution.py:32
  92.7 0.6 collective-permute-start.10
  93.3 9.4 %all-to-all-start.1 = ((bf16[16,16,512]{2,1,0:T(8,128)(2,1)}), bf16[16,16,512]{2,1,0:T(8,128)(2,1)S(1)}, u32[]{:S(2)}, u32[]{:S(2)}) async-start(bf16[16,16,512]{2,1,0:T(8,128)(2,1)} %get-tuple-element.31), calls=%async_computation.1 | async-start | bytes 524288 | tf_op jit(solution)/shard_map/all_to_all | solution.py:365
  102.7 0.4 collective-permute-start.12
  103.1 4.5 %collective-permute-start.11 = (bf16[2,256,256]{2,1,0:T(8,128)(2,1)S(1)}, bf16[2,256,256]{2,1,0:T(8,128)(2,1)}, u32[]{:S(2)}, u32[]{:S(2)}) collective-permute-start(bf16[2,256,256]{2,1,0:T(8,128)(2,1)S(1)} %get-tuple-element.51), channel_id=1, source_target_pairs={{0,16},{16,0},{32,48},{48,32},{64,80},{80,64},{96,112},{112,96},{1... | collective-permute-start | bytes 786440 | tf_op jit(solution)/shard_map/ppermute | solution.py:32
  107.6 0.6 stack.24.where_ref
  108.2 2.5 %collective-permute-done.6.refs_3_ = bf16[3,256,512]{2,1,0:T(8,128)(2,1)} collective-permute-done((bf16[3,256,512]{2,1,0:T(8,128)(2,1)}, bf16[3,256,512]{2,1,0:T(8,128)(2,1)}, u32[]{:S(2)}, u32[]{:S(2)}) %collective-permute-start.6) | collective-permute-done | bytes 786464 | tf_op jit(solution)/shard_map/ppermute | solution.py:32
  110.8 0.0 collective-permute-done.11.refs_11_
  110.8 4.4 %all-to-all-done.1 = bf16[16,16,512]{2,1,0:T(8,128)(2,1)S(1)} async-done(((bf16[16,16,512]{2,1,0:T(8,128)(2,1)}), bf16[16,16,512]{2,1,0:T(8,128)(2,1)S(1)}, u32[]{:S(2)}, u32[]{:S(2)}) %all-to-all-start.1) | async-done | bytes 262176 | tf_op jit(solution)/shard_map/all_to_all | solution.py:365
  115.2 0.0 collective-permute-done.10.refs_10_
  115.2 0.7 copy-done.9
  115.9 6.6 %products.1 = (bf16[256,512]{1,0:T(8,128)(2,1)}, bf16[256,512]{1,0:T(8,128)(2,1)}, bf16[8,256,256]{2,1,0:T(8,128)(2,1)}, bf16[8,256,256]{2,1,0:T(8,128)(2,1)}) custom-call(s32[5]{0:T(128)} %stack.24.where_ref, bf16[256,512]{1,0:T(8,128)(2,1)} %refs_0_.2, bf16[3,256,512]{2,1,0:T(8,128)(2,1)} %stack.25.refs_1_, bf16[256,512]{1,0:T(8,128)(2,1)} %copy-done.14, ...), custom_call_target="tpu_custom_call" | custom-call | flops 2147483648 | bytes 9437184 | tf_op jit(solution)/shard_map/products/pallas_call | solution.py:352
  122.6 0.0 copy-start
  122.6 0.0 copy-start.1
  122.6 0.0 copy-start.2
  122.6 0.0 copy-start.3
  122.6 0.0 copy-start.4
  122.7 0.2 collective-permute-start.13
  122.9 5.6 %all-to-all-start.2 = ((bf16[16,16,512]{2,1,0:T(8,128)(2,1)}), bf16[16,16,512]{2,1,0:T(8,128)(2,1)S(1)}, u32[]{:S(2)}, u32[]{:S(2)}) async-start(bf16[16,16,512]{2,1,0:T(8,128)(2,1)} %bitcast.24), calls=%async_computation.2 | async-start | bytes 524288 | tf_op jit(solution)/shard_map/all_to_all | solution.py:365
  128.5 2.5 %add_convert_fusion.1 = (bf16[2,256,256]{2,1,0:T(8,128)(2,1)}, bf16[2,256,256]{2,1,0:T(8,128)(2,1)}, bf16[2,256,256]{2,1,0:T(8,128)(2,1)}, bf16[2,256,256]{2,1,0:T(8,128)(2,1)S(1)}) fusion(bf16[8,256,256]{2,1,0:T(8,128)(2,1)} %collective-permute-done.13, bf16[8,256,256]{2,1,0:T(8,128)(2,1)} %get-tuple-element.35), kind=kLoop, calls=%fused_computation.2 | loop fusion | flops 2097152 | bytes 3145728 | tf_op jit(solution)/shard_map/convert_element_type | solution.py:372
  131.1 7.6 %all-to-all-done.2.p_ref = bf16[16,16,512]{2,1,0:T(8,128)(2,1)S(1)} async-done(((bf16[16,16,512]{2,1,0:T(8,128)(2,1)}), bf16[16,16,512]{2,1,0:T(8,128)(2,1)S(1)}, u32[]{:S(2)}, u32[]{:S(2)}) %all-to-all-start.2) | async-done | bytes 262176 | tf_op jit(solution)/shard_map/all_to_all | solution.py:365
  138.6 0.7 collective-permute-start.14
  139.3 2.5 %collective-permute-start.15 = (bf16[2,256,256]{2,1,0:T(8,128)(2,1)}, bf16[2,256,256]{2,1,0:T(8,128)(2,1)}, u32[]{:S(2)}, u32[]{:S(2)}) collective-permute-start(bf16[2,256,256]{2,1,0:T(8,128)(2,1)} %get-tuple-element.42), channel_id=1, source_target_pairs={{0,128},{16,144},{32,160},{48,176},{64,192},{80,208},{96,224},{112... | collective-permute-start | bytes 786440 | tf_op jit(solution)/shard_map/ppermute | solution.py:32
  141.8 0.1 collective-permute-start.16
  141.9 5.8 %grads.1 = bf16[16,32,512]{2,1,0:T(8,128)(2,1)} custom-call(bf16[16,16,512]{2,1,0:T(8,128)(2,1)S(1)} %all-to-all-done.2.p_ref, bf16[128,128]{1,0:T(8,128)(2,1)S(1)} %copy-done.4, bf16[768,256]{1,0:T(8,128)(2,1)S(1)} %copy-done.1, bf16[768,256]{1,0:T(8,128)(2,1)S(1)} %copy-done, bf16[64,384]{1,0:T(8,128)(2,1)S(1)} %copy-done.3, f32[2,64,128]{2,1,0:T(8,128)S(1)} %copy-done.2, ...), custom_call_target="tpu_custom_call" | custom-call | flops 10000000000 | bytes 4194304 | tf_op jit(solution)/shard_map/grads/pallas_call | solution.py:244
  147.7 6.5 %all-to-all-start.3 = ((bf16[16,32,512]{2,1,0:T(8,128)(2,1)}), bf16[16,32,512]{2,1,0:T(8,128)(2,1)S(1)}, u32[]{:S(2)}, u32[]{:S(2)}) async-start(bf16[16,32,512]{2,1,0:T(8,128)(2,1)} %grads.1), calls=%async_computation.3 | async-start | bytes 1048576 | tf_op jit(solution)/shard_map/all_to_all | solution.py:365
  154.2 0.0 collective-permute-done.14
  154.2 0.8 collective-permute-done.16
  155.0 1.2 add_convert_fusion
  156.3 4.4 %collective-permute-start.17 = (bf16[256,256]{1,0:T(8,128)(2,1)S(1)}, bf16[256,256]{1,0:T(8,128)(2,1)S(1)}, u32[]{:S(2)}, u32[]{:S(2)}) collective-permute-start(bf16[256,256]{1,0:T(8,128)(2,1)S(1)} %slice_bitcast_fusion), channel_id=1, source_target_pairs={{0,32},{16,48},{32,0},{48,16},{64,96},{80,112},{96,64},{112,80},{1... | collective-permute-start | bytes 393224 | tf_op jit(solution)/shard_map/ppermute | solution.py:32
  160.6 14.8 %collective-permute-done.17 = bf16[256,256]{1,0:T(8,128)(2,1)S(1)} collective-permute-done((bf16[256,256]{1,0:T(8,128)(2,1)S(1)}, bf16[256,256]{1,0:T(8,128)(2,1)S(1)}, u32[]{:S(2)}, u32[]{:S(2)}) %collective-permute-start.17) | collective-permute-done | bytes 131104 | tf_op jit(solution)/shard_map/ppermute | solution.py:32
  175.4 0.7 fusion
  176.1 0.0 all-to-all-done.3
  176.1 0.8 fusion.1
  (34 shorter events, 0.1 us)
Async XLA Ops:
  0.6 31.7 %copy-start.13 = (bf16[256,512]{1,0:T(8,128)(2,1)S(1)}, bf16[256,512]{1,0:T(8,128)(2,1)}, u32[]{:S(2)}) copy-start(bf16[256,512]{1,0:T(8,128)(2,1)} %refs_0_.2) | copy-start | bytes 786436
  0.6 19.9 %copy-start.10 = (bf16[256,256]{1,0:T(8,128)(2,1)S(1)}, bf16[256,256]{1,0:T(8,128)(2,1)}, u32[]{:S(2)}) copy-start(bf16[256,256]{1,0:T(8,128)(2,1)} %param.14) | copy-start | bytes 393220
  0.7 31.6 %collective-permute-start.3 = (bf16[256,512]{1,0:T(8,128)(2,1)}, bf16[256,512]{1,0:T(8,128)(2,1)S(1)}, u32[]{:S(2)}, u32[]{:S(2)}) collective-permute-start(bf16[256,512]{1,0:T(8,128)(2,1)} %refs_0_.2), channel_id=1, source_target_pairs={{0,4},{1,5},{2,6},{3,7},{4,8},{5,9},{6,10},{7,11},{8,12},{9,13},{1... | collective-permute-start | bytes 786440 | tf_op jit(solution)/shard_map/ppermute | solution.py:32
  2.0 31.3 %collective-permute-start.2 = (bf16[256,512]{1,0:T(8,128)(2,1)}, bf16[256,512]{1,0:T(8,128)(2,1)S(1)}, u32[]{:S(2)}, u32[]{:S(2)}) collective-permute-start(bf16[256,512]{1,0:T(8,128)(2,1)} %refs_0_.2), channel_id=1, source_target_pairs={{0,3},{1,0},{2,1},{3,2},{4,7},{5,4},{6,5},{7,6},{8,11},{9,8},{10,9... | collective-permute-start | bytes 786440 | tf_op jit(solution)/shard_map/ppermute | solution.py:32
  2.0 31.3 %collective-permute-start.1 = (bf16[256,512]{1,0:T(8,128)(2,1)}, bf16[256,512]{1,0:T(8,128)(2,1)S(1)}, u32[]{:S(2)}, u32[]{:S(2)}) collective-permute-start(bf16[256,512]{1,0:T(8,128)(2,1)} %refs_0_.2), channel_id=1, source_target_pairs={{0,2},{1,3},{2,0},{3,1},{4,6},{5,7},{6,4},{7,5},{8,10},{9,11},{10,... | collective-permute-start | bytes 786440 | tf_op jit(solution)/shard_map/ppermute | solution.py:32
  5.7 30.1 %collective-permute-start = (bf16[256,512]{1,0:T(8,128)(2,1)}, bf16[256,512]{1,0:T(8,128)(2,1)S(1)}, u32[]{:S(2)}, u32[]{:S(2)}) collective-permute-start(bf16[256,512]{1,0:T(8,128)(2,1)} %refs_0_.2), channel_id=1, source_target_pairs={{0,1},{1,2},{2,3},{3,0},{4,5},{5,6},{6,7},{7,4},{8,9},{9,10},{10,1... | collective-permute-start | bytes 786440 | tf_op jit(solution)/shard_map/ppermute | solution.py:32
  5.7 55.8 %collective-permute-start.4 = (bf16[256,512]{1,0:T(8,128)(2,1)}, bf16[256,512]{1,0:T(8,128)(2,1)S(1)}, u32[]{:S(2)}, u32[]{:S(2)}) collective-permute-start(bf16[256,512]{1,0:T(8,128)(2,1)} %refs_0_.2), channel_id=1, source_target_pairs={{0,8},{1,9},{2,10},{3,11},{4,12},{5,13},{6,14},{7,15},{8,0},{9,1},... | collective-permute-start | bytes 786440 | tf_op jit(solution)/shard_map/ppermute | solution.py:32
  10.2 64.4 %all-to-all-start = ((bf16[16,32,512]{2,1,0:T(8,128)(2,1)}), bf16[16,32,512]{2,1,0:T(8,128)(2,1)S(1)}, u32[]{:S(2)}, u32[]{:S(2)}) async-start(bf16[16,32,512]{2,1,0:T(8,128)(2,1)} %pad_maximum_fusion), calls=%async_computation | async-start | bytes 1048576 | tf_op jit(solution)/shard_map/all_to_all | solution.py:365
  32.3 60.4 %copy-start.6 = (bf16[1024,256]{1,0:T(8,128)(2,1)}, bf16[1024,256]{1,0:T(8,128)(2,1)S(1)}, u32[]{:S(2)}) copy-start(bf16[1024,256]{1,0:T(8,128)(2,1)S(1)} %copy.14) | copy-start | bytes 1572868
  32.3 29.2 %copy-start.14 = (bf16[256,512]{1,0:T(8,128)(2,1)}, bf16[256,512]{1,0:T(8,128)(2,1)S(1)}, u32[]{:S(2)}) copy-start(bf16[256,512]{1,0:T(8,128)(2,1)S(1)} %collective-permute-done.3.refs_2_) | copy-start | bytes 786436
  32.3 29.2 %collective-permute-start.5 = (bf16[256,512]{1,0:T(8,128)(2,1)S(1)}, bf16[256,512]{1,0:T(8,128)(2,1)S(1)}, u32[]{:S(2)}, u32[]{:S(2)}) collective-permute-start(bf16[256,512]{1,0:T(8,128)(2,1)S(1)} %copy-done.13), channel_id=1, source_target_pairs={{0,12},{1,13},{2,14},{3,15},{4,0},{5,1},{6,2},{7,3},{8,4},{9,5},{1... | collective-permute-start | bytes 786440 | tf_op jit(solution)/shard_map/ppermute | solution.py:32
  33.4 2.5 %copy-start.17 = (bf16[256,512]{1,0:T(8,128)(2,1)}, bf16[256,512]{1,0:T(8,128)(2,1)S(1)}, u32[]{:S(2)}) copy-start(bf16[256,512]{1,0:T(8,128)(2,1)S(1)} %collective-permute-done.2.refs_2_) | copy-start | bytes 786436
  33.4 2.5 %copy-start.18 = (bf16[256,512]{1,0:T(8,128)(2,1)}, bf16[256,512]{1,0:T(8,128)(2,1)S(1)}, u32[]{:S(2)}) copy-start(bf16[256,512]{1,0:T(8,128)(2,1)S(1)} %collective-permute-done.1.refs_1_) | copy-start | bytes 786436
  35.8 0.7 copy-start.19
  61.5 0.7 copy-start.15
  61.5 12.6 %copy-start.16 = (bf16[256,512]{1,0:T(8,128)(2,1)}, bf16[256,512]{1,0:T(8,128)(2,1)S(1)}, u32[]{:S(2)}) copy-start(bf16[256,512]{1,0:T(8,128)(2,1)S(1)} %collective-permute-done.5.refs_6_) | copy-start | bytes 786436
  62.2 30.4 %collective-permute-start.9 = (bf16[4,256,256]{2,1,0:T(8,128)(2,1)S(1)}, bf16[4,256,256]{2,1,0:T(8,128)(2,1)S(1)}, u32[]{:S(2)}, u32[]{:S(2)}) collective-permute-start(bf16[4,256,256]{2,1,0:T(8,128)(2,1)S(1)} %bitcast.20), channel_id=1, source_target_pairs={{0,32},{16,48},{32,0},{48,16},{64,96},{80,112},{96,64},{112,80},{1... | collective-permute-start | bytes 1572872 | tf_op jit(solution)/shard_map/ppermute | solution.py:32
  71.1 32.0 %collective-permute-start.8 = (bf16[3,256,512]{2,1,0:T(8,128)(2,1)}, bf16[3,256,512]{2,1,0:T(8,128)(2,1)S(1)}, u32[]{:S(2)}, u32[]{:S(2)}) collective-permute-start(bf16[3,256,512]{2,1,0:T(8,128)(2,1)} %stack.25.refs_1_), channel_id=1, source_target_pairs={{0,12},{1,13},{2,14},{3,15},{4,0},{5,1},{6,2},{7,3},{8,4},{9,5},{1... | collective-permute-start | bytes 2359304 | tf_op jit(solution)/shard_map/ppermute | solution.py:32
  72.6 35.6 %collective-permute-start.7 = (bf16[3,256,512]{2,1,0:T(8,128)(2,1)}, bf16[3,256,512]{2,1,0:T(8,128)(2,1)S(1)}, u32[]{:S(2)}, u32[]{:S(2)}) collective-permute-start(bf16[3,256,512]{2,1,0:T(8,128)(2,1)} %stack.25.refs_1_), channel_id=1, source_target_pairs={{0,8},{1,9},{2,10},{3,11},{4,12},{5,13},{6,14},{7,15},{8,0},{9,1},... | collective-permute-start | bytes 2359304 | tf_op jit(solution)/shard_map/ppermute | solution.py:32
  74.2 36.6 %collective-permute-start.6 = (bf16[3,256,512]{2,1,0:T(8,128)(2,1)}, bf16[3,256,512]{2,1,0:T(8,128)(2,1)}, u32[]{:S(2)}, u32[]{:S(2)}) collective-permute-start(bf16[3,256,512]{2,1,0:T(8,128)(2,1)} %stack.25.refs_1_), channel_id=1, source_target_pairs={{0,4},{1,5},{2,6},{3,7},{4,8},{5,9},{6,10},{7,11},{8,12},{9,13},{1... | collective-permute-start | bytes 2359304 | tf_op jit(solution)/shard_map/ppermute | solution.py:32
  74.6 0.8 copy-start.8
  92.7 22.6 %copy-start.7 = (bf16[4,256,256]{2,1,0:T(8,128)(2,1)}, bf16[4,256,256]{2,1,0:T(8,128)(2,1)S(1)}, u32[]{:S(2)}) copy-start(bf16[4,256,256]{2,1,0:T(8,128)(2,1)S(1)} %collective-permute-done.9.refs_9_) | copy-start | bytes 1572868
  92.7 22.5 %collective-permute-start.10 = (bf16[4,256,256]{2,1,0:T(8,128)(2,1)S(1)}, bf16[4,256,256]{2,1,0:T(8,128)(2,1)}, u32[]{:S(2)}, u32[]{:S(2)}) collective-permute-start(bf16[4,256,256]{2,1,0:T(8,128)(2,1)S(1)} %bitcast.21), channel_id=1, source_target_pairs={{0,16},{16,0},{32,48},{48,32},{64,80},{80,64},{96,112},{112,96},{1... | collective-permute-start | bytes 1572872 | tf_op jit(solution)/shard_map/ppermute | solution.py:32
  93.3 21.9 %all-to-all-start.1 = ((bf16[16,16,512]{2,1,0:T(8,128)(2,1)}), bf16[16,16,512]{2,1,0:T(8,128)(2,1)S(1)}, u32[]{:S(2)}, u32[]{:S(2)}) async-start(bf16[16,16,512]{2,1,0:T(8,128)(2,1)} %get-tuple-element.31), calls=%async_computation.1 | async-start | bytes 524288 | tf_op jit(solution)/shard_map/all_to_all | solution.py:365
  102.7 8.1 %collective-permute-start.12 = (bf16[2,256,256]{2,1,0:T(8,128)(2,1)S(1)}, bf16[2,256,256]{2,1,0:T(8,128)(2,1)}, u32[]{:S(2)}, u32[]{:S(2)}) collective-permute-start(bf16[2,256,256]{2,1,0:T(8,128)(2,1)S(1)} %get-tuple-element.50), channel_id=1, source_target_pairs={{0,16},{16,0},{32,48},{48,32},{64,80},{80,64},{96,112},{112,96},{1... | collective-permute-start | bytes 786440 | tf_op jit(solution)/shard_map/ppermute | solution.py:32
  103.1 12.1 %copy-start.11 = (bf16[3,256,512]{2,1,0:T(8,128)(2,1)}, bf16[3,256,512]{2,1,0:T(8,128)(2,1)S(1)}, u32[]{:S(2)}) copy-start(bf16[3,256,512]{2,1,0:T(8,128)(2,1)S(1)} %collective-permute-done.8.refs_7_) | copy-start | bytes 2359300
  103.1 7.7 %collective-permute-start.11 = (bf16[2,256,256]{2,1,0:T(8,128)(2,1)S(1)}, bf16[2,256,256]{2,1,0:T(8,128)(2,1)}, u32[]{:S(2)}, u32[]{:S(2)}) collective-permute-start(bf16[2,256,256]{2,1,0:T(8,128)(2,1)S(1)} %get-tuple-element.51), channel_id=1, source_target_pairs={{0,16},{16,0},{32,48},{48,32},{64,80},{80,64},{96,112},{112,96},{1... | collective-permute-start | bytes 786440 | tf_op jit(solution)/shard_map/ppermute | solution.py:32
  108.2 7.0 %copy-start.12 = (bf16[3,256,512]{2,1,0:T(8,128)(2,1)}, bf16[3,256,512]{2,1,0:T(8,128)(2,1)S(1)}, u32[]{:S(2)}) copy-start(bf16[3,256,512]{2,1,0:T(8,128)(2,1)S(1)} %collective-permute-done.7.refs_5_) | copy-start | bytes 2359300
  115.2 0.7 copy-start.9
  122.6 19.3 %copy-start = (bf16[768,256]{1,0:T(8,128)(2,1)S(1)}, bf16[768,256]{1,0:T(8,128)(2,1)}, u32[]{:S(2)}) copy-start(bf16[768,256]{1,0:T(8,128)(2,1)} %constant.72.clone.refs_2_.back_ref) | copy-start | bytes 1179652
  122.6 19.3 %copy-start.1 = (bf16[768,256]{1,0:T(8,128)(2,1)S(1)}, bf16[768,256]{1,0:T(8,128)(2,1)}, u32[]{:S(2)}) copy-start(bf16[768,256]{1,0:T(8,128)(2,1)} %constant.71.clone.refs_1_.second_ref) | copy-start | bytes 1179652
  122.6 19.3 %copy-start.2 = (f32[2,64,128]{2,1,0:T(8,128)S(1)}, f32[2,64,128]{2,1,0:T(8,128)}, u32[]{:S(2)}) copy-start(f32[2,64,128]{2,1,0:T(8,128)} %constant.74.clone.refs_4_.turn_ref) | copy-start | bytes 196612
  122.6 19.3 %copy-start.3 = (bf16[64,384]{1,0:T(8,128)(2,1)S(1)}, bf16[64,384]{1,0:T(8,128)(2,1)}, u32[]{:S(2)}) copy-start(bf16[64,384]{1,0:T(8,128)(2,1)} %constant.73.clone.refs_3_.last_ref) | copy-start | bytes 147460
  122.6 19.3 %copy-start.4 = (bf16[128,128]{1,0:T(8,128)(2,1)S(1)}, bf16[128,128]{1,0:T(8,128)(2,1)}, u32[]{:S(2)}) copy-start(bf16[128,128]{1,0:T(8,128)(2,1)} %constant.70.clone.refs_0_.first_ref) | copy-start | bytes 98308
  122.6 19.3 %copy-start.5 = (f32[4,1024,128]{2,1,0:T(8,128)S(1)}, f32[4,1024,128]{2,1,0:T(8,128)}, u32[]{:S(2)}) copy-start(f32[4,1024,128]{2,1,0:T(8,128)} %get-tuple-element.38.spec_ref) | copy-start | bytes 6291460
  122.7 5.9 %collective-permute-start.13 = (bf16[8,256,256]{2,1,0:T(8,128)(2,1)}, bf16[8,256,256]{2,1,0:T(8,128)(2,1)}, u32[]{:S(2)}, u32[]{:S(2)}) collective-permute-start(bf16[8,256,256]{2,1,0:T(8,128)(2,1)} %get-tuple-element.36), channel_id=1, source_target_pairs={{0,16},{16,0},{32,48},{48,32},{64,80},{80,64},{96,112},{112,96},{1... | collective-permute-start | bytes 3145736 | tf_op jit(solution)/shard_map/ppermute | solution.py:32
  122.9 15.7 %all-to-all-start.2 = ((bf16[16,16,512]{2,1,0:T(8,128)(2,1)}), bf16[16,16,512]{2,1,0:T(8,128)(2,1)S(1)}, u32[]{:S(2)}, u32[]{:S(2)}) async-start(bf16[16,16,512]{2,1,0:T(8,128)(2,1)} %bitcast.24), calls=%async_computation.2 | async-start | bytes 524288 | tf_op jit(solution)/shard_map/all_to_all | solution.py:365
  138.6 15.5 %collective-permute-start.14 = (bf16[2,256,256]{2,1,0:T(8,128)(2,1)}, bf16[2,256,256]{2,1,0:T(8,128)(2,1)}, u32[]{:S(2)}, u32[]{:S(2)}) collective-permute-start(bf16[2,256,256]{2,1,0:T(8,128)(2,1)} %get-tuple-element.41), channel_id=1, source_target_pairs={{0,64},{16,80},{32,96},{48,112},{64,128},{80,144},{96,160},{112,17... | collective-permute-start | bytes 786440 | tf_op jit(solution)/shard_map/ppermute | solution.py:32
  139.3 14.8 %collective-permute-start.15 = (bf16[2,256,256]{2,1,0:T(8,128)(2,1)}, bf16[2,256,256]{2,1,0:T(8,128)(2,1)}, u32[]{:S(2)}, u32[]{:S(2)}) collective-permute-start(bf16[2,256,256]{2,1,0:T(8,128)(2,1)} %get-tuple-element.42), channel_id=1, source_target_pairs={{0,128},{16,144},{32,160},{48,176},{64,192},{80,208},{96,224},{112... | collective-permute-start | bytes 786440 | tf_op jit(solution)/shard_map/ppermute | solution.py:32
  141.8 13.2 %collective-permute-start.16 = (bf16[2,256,256]{2,1,0:T(8,128)(2,1)}, bf16[2,256,256]{2,1,0:T(8,128)(2,1)}, u32[]{:S(2)}, u32[]{:S(2)}) collective-permute-start(bf16[2,256,256]{2,1,0:T(8,128)(2,1)} %get-tuple-element.43), channel_id=1, source_target_pairs={{0,192},{16,208},{32,224},{48,240},{64,0},{80,16},{96,32},{112,48}... | collective-permute-start | bytes 786440 | tf_op jit(solution)/shard_map/ppermute | solution.py:32
  147.7 28.4 %all-to-all-start.3 = ((bf16[16,32,512]{2,1,0:T(8,128)(2,1)}), bf16[16,32,512]{2,1,0:T(8,128)(2,1)S(1)}, u32[]{:S(2)}, u32[]{:S(2)}) async-start(bf16[16,32,512]{2,1,0:T(8,128)(2,1)} %grads.1), calls=%async_computation.3 | async-start | bytes 1048576 | tf_op jit(solution)/shard_map/all_to_all | solution.py:365
  156.3 19.1 %collective-permute-start.17 = (bf16[256,256]{1,0:T(8,128)(2,1)S(1)}, bf16[256,256]{1,0:T(8,128)(2,1)S(1)}, u32[]{:S(2)}, u32[]{:S(2)}) collective-permute-start(bf16[256,256]{1,0:T(8,128)(2,1)S(1)} %slice_bitcast_fusion), channel_id=1, source_target_pairs={{0,32},{16,48},{32,0},{48,16},{64,96},{80,112},{96,64},{112,80},{1... | collective-permute-start | bytes 393224 | tf_op jit(solution)/shard_map/ppermute | solution.py:32

commit v6 on v5

--- a/solution.py
+++ b/solution.py
@@ -248,7 +248,7 @@
         out_specs=whole_vmem(),
         scratch_shapes=[ROWS_SCRATCH] * 3,
         compiler_params=params(24),
-        cost_estimate=pl.CostEstimate(flops=10**10, bytes_accessed=4 << 20, transcendentals=0),
+        cost_estimate=pl.CostEstimate(flops=1 * 10**10, bytes_accessed=4 << 20, transcendentals=0),
         name="grads",
     )(product, *constants(), spec)
 
@@ -323,19 +323,17 @@
 
 
 def stack_kernel(*refs):
-    ins, out, sems = refs[:-2], refs[-2], refs[-1]
-    for copy in fetch(ins, [out.at[i] for i in range(len(ins))], sems):
-        copy.wait()
+    for i, ref in enumerate(refs[:-1]):
+        refs[-1][i] = ref[...]
 
 
 def stack_call(parts):
     return pl.pallas_call(
         stack_kernel,
         out_shape=jax.ShapeDtypeStruct((len(parts),) + parts[0].shape, BF),
-        in_specs=[in_hbm()] * len(parts),
-        out_specs=in_hbm(),
-        scratch_shapes=[DMA((len(parts),))],
-        compiler_params=params(60),
+        in_specs=[whole_vmem()] * len(parts),
+        out_specs=whole_vmem(),
+        compiler_params=params(8),
         cost_estimate=pl.CostEstimate(flops=3 * 10**10, bytes_accessed=2 << 20, transcendentals=0),
         name="stack",
     )(*parts)
@@ -402,7 +400,7 @@
     product_rows = exchange(product.reshape(16, FEW, TOK))
     received = send(part_other, "ctx", 1, 2, 1)
     chips = [add(part_same[2 * dx : 2 * dx + 2], received[2 * dx : 2 * dx + 2]) for dx in range(4)]
-    product_rows, chips = lax.optimization_barrier((product_rows, chips))
+
     grad_rows = grads_call(product_rows, spec)
     both_grads = exchange(grad_rows)
     input_grad = both_grads[:, :FEW].reshape(CH, TOK)

time: 179 us -> 150 us (0.84); the launches traced: 177 us -> 150 us
  Pallas kernels: 44 us -> 19.2 us
    pallas_call x1, Pallas kernels: 24.9 us -> 0.05 us  [stack_call(): pl.pallas_call(stack_kernel, out_shape=jax.ShapeDtypeStruct((len(parts),)...]
  transfers between devices with their start and end apart: 22 -> 22, of which waited for: 7 -> 7; matrix products, arithmetic and copies ran while one was open for 4% -> 5% of each run, Pallas kernels for 21% -> 8%
where the time goes in v6:
time: 150 us
  starting transfers between devices  65.4 us (44%)
  waiting for transfers between devices  43.3 us (29%)
  Pallas kernels  19.2 us (13%)
  blocking collectives  11.5 us (8%)
  other arithmetic  6.3 us (4%)
  local copies, waits for them, and re-layouts  3.21 us (2%)
    ppermute x18, starting transfers between devices, send(): return lax.ppermute(value, axis, shift_pairs(stride, size, by))  34.1 us
    ppermute x18, waiting for transfers between devices, send(): return lax.ppermute(value, axis, shift_pairs(stride, size, by))  32.6 us
    all_to_all x4, starting transfers between devices, exchange(): return lax.all_to_all(value, 'ctx', split_axis=0, concat_axis=0, tiled=True)  31.4 us
    all_gather x1, blocking collectives, on_device(): w_line = lax.all_gather(out_weight.T, 'ctx', axis_index_groups=LINES_X)  11.5 us
    all_to_all x4, waiting for transfers between devices, exchange(): return lax.all_to_all(value, 'ctx', split_axis=0, concat_axis=0, tiled=True)  10.6 us
    pallas_call x1, Pallas kernels, products_call(): pl.pallas_call(products_kernel, out_shape=(tile, tile, eight, eight), in_...  6.76 us
    pallas_call x1, Pallas kernels, conv_call(): pl.pallas_call(conv_kernel, out_shape=(jax.ShapeDtypeStruct((16, FEW, TOK...  6.66 us
    pallas_call x1, Pallas kernels, grads_call(): pl.pallas_call(grads_kernel, out_shape=jax.ShapeDtypeStruct((16, 2 * FEW,...  5.75 us
  transfers between devices with their start and end apart: 22, of which 7 were waited for; matrix products, arithmetic and copies ran while one was open for 5% of the time, Pallas kernels for 8%

profile of v6, /device:TPU:67, one launch (start us, length us, event | category | flops | bytes accessed | tf_op | source)
XLA Modules:
  0.0 149.8 jit_solution(17812373684472154114)
XLA Ops:
  0.6 0.0 copy-start.13
  0.7 1.4 collective-permute-start.3
  2.0 0.0 collective-permute-start.2
  2.0 3.7 %collective-permute-start.1 = (bf16[256,512]{1,0:T(8,128)(2,1)}, bf16[256,512]{1,0:T(8,128)(2,1)S(1)}, u32[]{:S(2)}, u32[]{:S(2)}) collective-permute-start(bf16[256,512]{1,0:T(8,128)(2,1)} %refs_0_.2), channel_id=1, source_target_pairs={{0,2},{1,3},{2,0},{3,1},{4,6},{5,7},{6,4},{7,5},{8,10},{9,11},{10,... | collective-permute-start | bytes 786440 | tf_op jit(solution)/shard_map/ppermute | solution.py:32
  5.7 0.0 collective-permute-start
  5.7 2.6 %collective-permute-start.4 = (bf16[256,512]{1,0:T(8,128)(2,1)}, bf16[256,512]{1,0:T(8,128)(2,1)S(1)}, u32[]{:S(2)}, u32[]{:S(2)}) collective-permute-start(bf16[256,512]{1,0:T(8,128)(2,1)} %refs_0_.2), channel_id=1, source_target_pairs={{0,8},{1,9},{2,10},{3,11},{4,12},{5,13},{6,14},{7,15},{8,0},{9,1},... | collective-permute-start | bytes 786440 | tf_op jit(solution)/shard_map/ppermute | solution.py:32
  8.4 1.9 %pad_maximum_fusion = bf16[16,32,512]{2,1,0:T(8,128)(2,1)} fusion(bf16[16,16,512]{2,1,0:T(8,128)(2,1)} %bitcast.25, bf16[16,16,512]{2,1,0:T(8,128)(2,1)} %bitcast.26), kind=kLoop, calls=%fused_computation | loop fusion | flops 1048576 | bytes 1048576 | tf_op jit(solution)/shard_map/concatenate | solution.py:380
  10.2 10.3 %all-to-all-start = ((bf16[16,32,512]{2,1,0:T(8,128)(2,1)}), bf16[16,32,512]{2,1,0:T(8,128)(2,1)S(1)}, u32[]{:S(2)}, u32[]{:S(2)}) async-start(bf16[16,32,512]{2,1,0:T(8,128)(2,1)} %pad_maximum_fusion), calls=%async_computation | async-start | bytes 1048576 | tf_op jit(solution)/shard_map/all_to_all | solution.py:363
  20.5 11.5 %all-gather = bf16[1024,256]{0,1:T(8,128)(2,1)S(1)} all-gather(bf16[256,256]{0,1:T(8,128)(2,1)S(1)} %bitcast.29), channel_id=2, replica_groups={{0,64,128,192},{16,80,144,208},{32,96,160,224},{48,112,176,240},{1,65,1..., dimensions={0}, use_global_device_ids=true | all-gather | bytes 655360 | tf_op jit(solution)/shard_map/all_gather | solution.py:378
  32.0 0.2 copy.14
  32.3 0.0 collective-permute-done.3.refs_2_
  32.3 0.0 copy-start.14
  32.3 1.1 collective-permute-start.5
  33.4 0.0 collective-permute-done.2.refs_2_
  33.4 0.0 collective-permute-done.1.refs_1_
  33.4 2.5 %collective-permute-done.refs_0_ = bf16[256,512]{1,0:T(8,128)(2,1)S(1)} collective-permute-done((bf16[256,512]{1,0:T(8,128)(2,1)}, bf16[256,512]{1,0:T(8,128)(2,1)S(1)}, u32[]{:S(2)}, u32[]{:S(2)}) %collective-permute-start) | collective-permute-done | bytes 262176 | tf_op jit(solution)/shard_map/ppermute | solution.py:32
  35.9 0.1 stack.25.refs_1_
  35.9 0.0 collective-permute-done.4.refs_4_
  35.9 0.0 copy-start.15
  35.9 2.2 %collective-permute-done.5.refs_6_ = bf16[256,512]{1,0:T(8,128)(2,1)S(1)} collective-permute-done((bf16[256,512]{1,0:T(8,128)(2,1)S(1)}, bf16[256,512]{1,0:T(8,128)(2,1)S(1)}, u32[]{:S(2)}, u32[]{:S(2)}) %collective-permute-start.5) | collective-permute-done | bytes 262176 | tf_op jit(solution)/shard_map/ppermute | solution.py:32
  38.1 7.8 %collective-permute-start.9 = (bf16[4,256,256]{2,1,0:T(8,128)(2,1)S(1)}, bf16[4,256,256]{2,1,0:T(8,128)(2,1)S(1)}, u32[]{:S(2)}, u32[]{:S(2)}) collective-permute-start(bf16[4,256,256]{2,1,0:T(8,128)(2,1)S(1)} %bitcast.20), channel_id=1, source_target_pairs={{0,32},{16,48},{32,0},{48,16},{64,96},{80,112},{96,64},{112,80},{1... | collective-permute-start | bytes 1572872 | tf_op jit(solution)/shard_map/ppermute | solution.py:32
  45.9 3.2 %collective-permute-start.8 = (bf16[3,256,512]{2,1,0:T(8,128)(2,1)S(1)}, bf16[3,256,512]{2,1,0:T(8,128)(2,1)S(1)}, u32[]{:S(2)}, u32[]{:S(2)}) collective-permute-start(bf16[3,256,512]{2,1,0:T(8,128)(2,1)S(1)} %stack.25.refs_1_), channel_id=1, source_target_pairs={{0,12},{1,13},{2,14},{3,15},{4,0},{5,1},{6,2},{7,3},{8,4},{9,5},{1... | collective-permute-start | bytes 2359304 | tf_op jit(solution)/shard_map/ppermute | solution.py:32
  49.1 0.0 collective-permute-start.7
  49.1 0.6 collective-permute-start.6
  49.7 0.0 all-to-all-done.xf_ref
  49.7 0.8 copy-done.9
  50.5 6.7 %conv.1 = (bf16[16,16,512]{2,1,0:T(8,128)(2,1)}, f32[4,1024,128]{2,1,0:T(8,128)}) custom-call(bf16[16,32,512]{2,1,0:T(8,128)(2,1)} %copy-done.9, bf16[128,128]{1,0:T(8,128)(2,1)} %constant.70.clone.refs_0_.first_ref, bf16[768,256]{1,0:T(8,128)(2,1)} %constant.71.clone.refs_1_.second_ref, bf16[768,256]{1,0:T(8,128)(2,1)} %constant.72.clone.refs_2_.back_ref, ...), custom_call_target="tpu_custom_call" | custom-call | flops 1000000000 | bytes 4194304 | tf_op jit(solution)/shard_map/conv/pallas_call | solution.py:228
  57.1 11.8 %collective-permute-done.9.refs_9_ = bf16[4,256,256]{2,1,0:T(8,128)(2,1)S(1)} collective-permute-done((bf16[4,256,256]{2,1,0:T(8,128)(2,1)S(1)}, bf16[4,256,256]{2,1,0:T(8,128)(2,1)S(1)}, u32[]{:S(2)}, u32[]{:S(2)}) %collective-permute-start.9) | collective-permute-done | bytes 524320 | tf_op jit(solution)/shard_map/ppermute | solution.py:32
  68.9 1.3 collective-permute-start.10
  70.2 9.7 %all-to-all-start.1 = ((bf16[16,16,512]{2,1,0:T(8,128)(2,1)}), bf16[16,16,512]{2,1,0:T(8,128)(2,1)S(1)}, u32[]{:S(2)}, u32[]{:S(2)}) async-start(bf16[16,16,512]{2,1,0:T(8,128)(2,1)} %get-tuple-element.26), calls=%async_computation.1 | async-start | bytes 524288 | tf_op jit(solution)/shard_map/all_to_all | solution.py:363
  80.0 0.4 collective-permute-start.12
  80.4 0.0 collective-permute-done.8.refs_7_
  80.4 3.3 %collective-permute-start.11 = (bf16[2,256,256]{2,1,0:T(8,128)(2,1)S(1)}, bf16[2,256,256]{2,1,0:T(8,128)(2,1)}, u32[]{:S(2)}, u32[]{:S(2)}) collective-permute-start(bf16[2,256,256]{2,1,0:T(8,128)(2,1)S(1)} %get-tuple-element.40), channel_id=1, source_target_pairs={{0,16},{16,0},{32,48},{48,32},{64,80},{80,64},{96,112},{112,96},{1... | collective-permute-start | bytes 786440 | tf_op jit(solution)/shard_map/ppermute | solution.py:32
  83.7 0.6 stack.24.where_ref
  84.3 0.0 collective-permute-done.7.refs_5_
  84.3 2.1 %collective-permute-done.6.refs_3_ = bf16[3,256,512]{2,1,0:T(8,128)(2,1)} collective-permute-done((bf16[3,256,512]{2,1,0:T(8,128)(2,1)S(1)}, bf16[3,256,512]{2,1,0:T(8,128)(2,1)}, u32[]{:S(2)}, u32[]{:S(2)}) %collective-permute-start.6) | collective-permute-done | bytes 786464 | tf_op jit(solution)/shard_map/ppermute | solution.py:32
  86.4 0.0 collective-permute-done.12.refs_12_
  86.4 0.0 collective-permute-done.11.refs_11_
  86.4 6.1 %all-to-all-done.1 = bf16[16,16,512]{2,1,0:T(8,128)(2,1)S(1)} async-done(((bf16[16,16,512]{2,1,0:T(8,128)(2,1)}), bf16[16,16,512]{2,1,0:T(8,128)(2,1)S(1)}, u32[]{:S(2)}, u32[]{:S(2)}) %all-to-all-start.1) | async-done | bytes 262176 | tf_op jit(solution)/shard_map/all_to_all | solution.py:363
  92.5 0.7 copy-done.10
  93.2 6.8 %products.1 = (bf16[256,512]{1,0:T(8,128)(2,1)}, bf16[256,512]{1,0:T(8,128)(2,1)}, bf16[8,256,256]{2,1,0:T(8,128)(2,1)}, bf16[8,256,256]{2,1,0:T(8,128)(2,1)}) custom-call(s32[5]{0:T(128)} %stack.24.where_ref, bf16[256,512]{1,0:T(8,128)(2,1)} %refs_0_.2, bf16[3,256,512]{2,1,0:T(8,128)(2,1)} %copy-done, bf16[256,512]{1,0:T(8,128)(2,1)} %copy-done.14, ...), custom_call_target="tpu_custom_call" | custom-call | flops 2147483648 | bytes 9437184 | tf_op jit(solution)/shard_map/products/pallas_call | solution.py:350
  100.0 0.0 copy-start.1
  100.0 0.0 copy-start.2
  100.0 0.0 copy-start.3
  100.0 0.0 copy-start.4
  100.1 0.0 copy-start.5
  100.1 0.2 collective-permute-start.13
  100.3 5.6 %all-to-all-start.2 = ((bf16[16,16,512]{2,1,0:T(8,128)(2,1)}), bf16[16,16,512]{2,1,0:T(8,128)(2,1)S(1)}, u32[]{:S(2)}, u32[]{:S(2)}) async-start(bf16[16,16,512]{2,1,0:T(8,128)(2,1)} %bitcast.24), calls=%async_computation.2 | async-start | bytes 524288 | tf_op jit(solution)/shard_map/all_to_all | solution.py:363
  105.9 0.0 collective-permute-done.13
  105.9 2.3 %add_convert_fusion.3 = (bf16[2,256,256]{2,1,0:T(8,128)(2,1)}, bf16[2,256,256]{2,1,0:T(8,128)(2,1)}, bf16[2,256,256]{2,1,0:T(8,128)(2,1)S(1)}) fusion(bf16[8,256,256]{2,1,0:T(8,128)(2,1)} %collective-permute-done.13, bf16[8,256,256]{2,1,0:T(8,128)(2,1)} %get-tuple-element.32), kind=kLoop, calls=%fused_computation.4 | loop fusion | flops 1572864 | bytes 2359296 | tf_op jit(solution)/shard_map/convert_element_type | solution.py:370
  108.2 1.2 collective-permute-start.14
  109.5 0.3 collective-permute-start.16
  109.7 1.8 %collective-permute-start.15 = (bf16[2,256,256]{2,1,0:T(8,128)(2,1)S(1)}, bf16[2,256,256]{2,1,0:T(8,128)(2,1)}, u32[]{:S(2)}, u32[]{:S(2)}) collective-permute-start(bf16[2,256,256]{2,1,0:T(8,128)(2,1)S(1)} %get-tuple-element.36), channel_id=1, source_target_pairs={{0,128},{16,144},{32,160},{48,176},{64,192},{80,208},{96,224},{112... | collective-permute-start | bytes 786440 | tf_op jit(solution)/shard_map/ppermute | solution.py:32
  111.6 4.5 %all-to-all-done.2.p_ref = bf16[16,16,512]{2,1,0:T(8,128)(2,1)S(1)} async-done(((bf16[16,16,512]{2,1,0:T(8,128)(2,1)}), bf16[16,16,512]{2,1,0:T(8,128)(2,1)S(1)}, u32[]{:S(2)}, u32[]{:S(2)}) %all-to-all-start.2) | async-done | bytes 262176 | tf_op jit(solution)/shard_map/all_to_all | solution.py:363
  116.1 5.8 %grads.1 = bf16[16,32,512]{2,1,0:T(8,128)(2,1)} custom-call(bf16[16,16,512]{2,1,0:T(8,128)(2,1)S(1)} %all-to-all-done.2.p_ref, bf16[128,128]{1,0:T(8,128)(2,1)S(1)} %copy-done.5, bf16[768,256]{1,0:T(8,128)(2,1)S(1)} %copy-done.2, bf16[768,256]{1,0:T(8,128)(2,1)S(1)} %copy-done.1, bf16[64,384]{1,0:T(8,128)(2,1)S(1)} %copy-done.4, ...), custom_call_target="tpu_custom_call" | custom-call | flops 10000000000 | bytes 4194304 | tf_op jit(solution)/shard_map/grads/pallas_call | solution.py:244
  121.8 5.7 %all-to-all-start.3 = ((bf16[16,32,512]{2,1,0:T(8,128)(2,1)}), bf16[16,32,512]{2,1,0:T(8,128)(2,1)S(1)}, u32[]{:S(2)}, u32[]{:S(2)}) async-start(bf16[16,32,512]{2,1,0:T(8,128)(2,1)} %grads.1), calls=%async_computation.3 | async-start | bytes 1048576 | tf_op jit(solution)/shard_map/all_to_all | solution.py:363
  127.5 0.0 collective-permute-done.14
  127.5 0.0 collective-permute-done.15
  127.5 1.4 add_convert_fusion
  129.0 5.2 %collective-permute-start.17 = (bf16[256,256]{1,0:T(8,128)(2,1)S(1)}, bf16[256,256]{1,0:T(8,128)(2,1)S(1)}, u32[]{:S(2)}, u32[]{:S(2)}) collective-permute-start(bf16[256,256]{1,0:T(8,128)(2,1)S(1)} %slice_bitcast_fusion), channel_id=1, source_target_pairs={{0,32},{16,48},{32,0},{48,16},{64,96},{80,112},{96,64},{112,80},{1... | collective-permute-start | bytes 393224 | tf_op jit(solution)/shard_map/ppermute | solution.py:32
  134.2 14.1 %collective-permute-done.17 = bf16[256,256]{1,0:T(8,128)(2,1)S(1)} collective-permute-done((bf16[256,256]{1,0:T(8,128)(2,1)S(1)}, bf16[256,256]{1,0:T(8,128)(2,1)S(1)}, u32[]{:S(2)}, u32[]{:S(2)}) %collective-permute-start.17) | collective-permute-done | bytes 131104 | tf_op jit(solution)/shard_map/ppermute | solution.py:32
  148.3 0.7 fusion
  149.0 0.0 all-to-all-done.3
  149.0 0.8 fusion.1
  (28 shorter events, 0.1 us)
Async XLA Ops:
  0.6 31.6 %copy-start.13 = (bf16[256,512]{1,0:T(8,128)(2,1)S(1)}, bf16[256,512]{1,0:T(8,128)(2,1)}, u32[]{:S(2)}) copy-start(bf16[256,512]{1,0:T(8,128)(2,1)} %refs_0_.2) | copy-start | bytes 786436
  0.6 19.9 %copy-start.11 = (bf16[256,256]{1,0:T(8,128)(2,1)S(1)}, bf16[256,256]{1,0:T(8,128)(2,1)}, u32[]{:S(2)}) copy-start(bf16[256,256]{1,0:T(8,128)(2,1)} %param.14) | copy-start | bytes 393220
  0.7 31.6 %collective-permute-start.3 = (bf16[256,512]{1,0:T(8,128)(2,1)}, bf16[256,512]{1,0:T(8,128)(2,1)S(1)}, u32[]{:S(2)}, u32[]{:S(2)}) collective-permute-start(bf16[256,512]{1,0:T(8,128)(2,1)} %refs_0_.2), channel_id=1, source_target_pairs={{0,4},{1,5},{2,6},{3,7},{4,8},{5,9},{6,10},{7,11},{8,12},{9,13},{1... | collective-permute-start | bytes 786440 | tf_op jit(solution)/shard_map/ppermute | solution.py:32
  2.0 31.3 %collective-permute-start.2 = (bf16[256,512]{1,0:T(8,128)(2,1)}, bf16[256,512]{1,0:T(8,128)(2,1)S(1)}, u32[]{:S(2)}, u32[]{:S(2)}) collective-permute-start(bf16[256,512]{1,0:T(8,128)(2,1)} %refs_0_.2), channel_id=1, source_target_pairs={{0,3},{1,0},{2,1},{3,2},{4,7},{5,4},{6,5},{7,6},{8,11},{9,8},{10,9... | collective-permute-start | bytes 786440 | tf_op jit(solution)/shard_map/ppermute | solution.py:32
  2.0 31.3 %collective-permute-start.1 = (bf16[256,512]{1,0:T(8,128)(2,1)}, bf16[256,512]{1,0:T(8,128)(2,1)S(1)}, u32[]{:S(2)}, u32[]{:S(2)}) collective-permute-start(bf16[256,512]{1,0:T(8,128)(2,1)} %refs_0_.2), channel_id=1, source_target_pairs={{0,2},{1,3},{2,0},{3,1},{4,6},{5,7},{6,4},{7,5},{8,10},{9,11},{10,... | collective-permute-start | bytes 786440 | tf_op jit(solution)/shard_map/ppermute | solution.py:32
  5.7 30.1 %collective-permute-start = (bf16[256,512]{1,0:T(8,128)(2,1)}, bf16[256,512]{1,0:T(8,128)(2,1)S(1)}, u32[]{:S(2)}, u32[]{:S(2)}) collective-permute-start(bf16[256,512]{1,0:T(8,128)(2,1)} %refs_0_.2), channel_id=1, source_target_pairs={{0,1},{1,2},{2,3},{3,0},{4,5},{5,6},{6,7},{7,4},{8,9},{9,10},{10,1... | collective-permute-start | bytes 786440 | tf_op jit(solution)/shard_map/ppermute | solution.py:32
  5.7 30.2 %collective-permute-start.4 = (bf16[256,512]{1,0:T(8,128)(2,1)}, bf16[256,512]{1,0:T(8,128)(2,1)S(1)}, u32[]{:S(2)}, u32[]{:S(2)}) collective-permute-start(bf16[256,512]{1,0:T(8,128)(2,1)} %refs_0_.2), channel_id=1, source_target_pairs={{0,8},{1,9},{2,10},{3,11},{4,12},{5,13},{6,14},{7,15},{8,0},{9,1},... | collective-permute-start | bytes 786440 | tf_op jit(solution)/shard_map/ppermute | solution.py:32
  10.2 39.5 %all-to-all-start = ((bf16[16,32,512]{2,1,0:T(8,128)(2,1)}), bf16[16,32,512]{2,1,0:T(8,128)(2,1)S(1)}, u32[]{:S(2)}, u32[]{:S(2)}) async-start(bf16[16,32,512]{2,1,0:T(8,128)(2,1)} %pad_maximum_fusion), calls=%async_computation | async-start | bytes 1048576 | tf_op jit(solution)/shard_map/all_to_all | solution.py:363
  32.2 36.7 %copy-start.7 = (bf16[1024,256]{1,0:T(8,128)(2,1)}, bf16[1024,256]{1,0:T(8,128)(2,1)S(1)}, u32[]{:S(2)}) copy-start(bf16[1024,256]{1,0:T(8,128)(2,1)S(1)} %copy.14) | copy-start | bytes 1572868
  32.3 1.1 copy-start.14
  32.3 5.8 %collective-permute-start.5 = (bf16[256,512]{1,0:T(8,128)(2,1)S(1)}, bf16[256,512]{1,0:T(8,128)(2,1)S(1)}, u32[]{:S(2)}, u32[]{:S(2)}) collective-permute-start(bf16[256,512]{1,0:T(8,128)(2,1)S(1)} %copy-done.13), channel_id=1, source_target_pairs={{0,12},{1,13},{2,14},{3,15},{4,0},{5,1},{6,2},{7,3},{8,4},{9,5},{1... | collective-permute-start | bytes 786440 | tf_op jit(solution)/shard_map/ppermute | solution.py:32
  35.9 34.3 %copy-start = (bf16[3,256,512]{2,1,0:T(8,128)(2,1)}, bf16[3,256,512]{2,1,0:T(8,128)(2,1)S(1)}, u32[]{:S(2)}) copy-start(bf16[3,256,512]{2,1,0:T(8,128)(2,1)S(1)} %stack.25.refs_1_) | copy-start | bytes 2359300
  35.9 2.2 %copy-start.15 = (bf16[256,512]{1,0:T(8,128)(2,1)}, bf16[256,512]{1,0:T(8,128)(2,1)S(1)}, u32[]{:S(2)}) copy-start(bf16[256,512]{1,0:T(8,128)(2,1)S(1)} %collective-permute-done.4.refs_4_) | copy-start | bytes 786436
  38.1 11.0 %copy-start.16 = (bf16[256,512]{1,0:T(8,128)(2,1)}, bf16[256,512]{1,0:T(8,128)(2,1)S(1)}, u32[]{:S(2)}) copy-start(bf16[256,512]{1,0:T(8,128)(2,1)S(1)} %collective-permute-done.5.refs_6_) | copy-start | bytes 786436
  38.1 30.8 %collective-permute-start.9 = (bf16[4,256,256]{2,1,0:T(8,128)(2,1)S(1)}, bf16[4,256,256]{2,1,0:T(8,128)(2,1)S(1)}, u32[]{:S(2)}, u32[]{:S(2)}) collective-permute-start(bf16[4,256,256]{2,1,0:T(8,128)(2,1)S(1)} %bitcast.20), channel_id=1, source_target_pairs={{0,32},{16,48},{32,0},{48,16},{64,96},{80,112},{96,64},{112,80},{1... | collective-permute-start | bytes 1572872 | tf_op jit(solution)/shard_map/ppermute | solution.py:32
  45.9 34.5 %collective-permute-start.8 = (bf16[3,256,512]{2,1,0:T(8,128)(2,1)S(1)}, bf16[3,256,512]{2,1,0:T(8,128)(2,1)S(1)}, u32[]{:S(2)}, u32[]{:S(2)}) collective-permute-start(bf16[3,256,512]{2,1,0:T(8,128)(2,1)S(1)} %stack.25.refs_1_), channel_id=1, source_target_pairs={{0,12},{1,13},{2,14},{3,15},{4,0},{5,1},{6,2},{7,3},{8,4},{9,5},{1... | collective-permute-start | bytes 2359304 | tf_op jit(solution)/shard_map/ppermute | solution.py:32
  49.1 35.2 %collective-permute-start.7 = (bf16[3,256,512]{2,1,0:T(8,128)(2,1)S(1)}, bf16[3,256,512]{2,1,0:T(8,128)(2,1)}, u32[]{:S(2)}, u32[]{:S(2)}) collective-permute-start(bf16[3,256,512]{2,1,0:T(8,128)(2,1)S(1)} %stack.25.refs_1_), channel_id=1, source_target_pairs={{0,8},{1,9},{2,10},{3,11},{4,12},{5,13},{6,14},{7,15},{8,0},{9,1},... | collective-permute-start | bytes 2359304 | tf_op jit(solution)/shard_map/ppermute | solution.py:32
  49.1 37.3 %collective-permute-start.6 = (bf16[3,256,512]{2,1,0:T(8,128)(2,1)S(1)}, bf16[3,256,512]{2,1,0:T(8,128)(2,1)}, u32[]{:S(2)}, u32[]{:S(2)}) collective-permute-start(bf16[3,256,512]{2,1,0:T(8,128)(2,1)S(1)} %stack.25.refs_1_), channel_id=1, source_target_pairs={{0,4},{1,5},{2,6},{3,7},{4,8},{5,9},{6,10},{7,11},{8,12},{9,13},{1... | collective-permute-start | bytes 2359304 | tf_op jit(solution)/shard_map/ppermute | solution.py:32
  49.7 0.8 copy-start.9
  68.9 23.6 %copy-start.8 = (bf16[4,256,256]{2,1,0:T(8,128)(2,1)}, bf16[4,256,256]{2,1,0:T(8,128)(2,1)S(1)}, u32[]{:S(2)}) copy-start(bf16[4,256,256]{2,1,0:T(8,128)(2,1)S(1)} %collective-permute-done.9.refs_9_) | copy-start | bytes 1572868
  68.9 23.6 %collective-permute-start.10 = (bf16[4,256,256]{2,1,0:T(8,128)(2,1)S(1)}, bf16[4,256,256]{2,1,0:T(8,128)(2,1)}, u32[]{:S(2)}, u32[]{:S(2)}) collective-permute-start(bf16[4,256,256]{2,1,0:T(8,128)(2,1)S(1)} %bitcast.21), channel_id=1, source_target_pairs={{0,16},{16,0},{32,48},{48,32},{64,80},{80,64},{96,112},{112,96},{1... | collective-permute-start | bytes 1572872 | tf_op jit(solution)/shard_map/ppermute | solution.py:32
  70.2 22.3 %all-to-all-start.1 = ((bf16[16,16,512]{2,1,0:T(8,128)(2,1)}), bf16[16,16,512]{2,1,0:T(8,128)(2,1)S(1)}, u32[]{:S(2)}, u32[]{:S(2)}) async-start(bf16[16,16,512]{2,1,0:T(8,128)(2,1)} %get-tuple-element.26), calls=%async_computation.1 | async-start | bytes 524288 | tf_op jit(solution)/shard_map/all_to_all | solution.py:363
  80.0 6.4 %collective-permute-start.12 = (bf16[2,256,256]{2,1,0:T(8,128)(2,1)S(1)}, bf16[2,256,256]{2,1,0:T(8,128)(2,1)}, u32[]{:S(2)}, u32[]{:S(2)}) collective-permute-start(bf16[2,256,256]{2,1,0:T(8,128)(2,1)S(1)} %get-tuple-element.39), channel_id=1, source_target_pairs={{0,16},{16,0},{32,48},{48,32},{64,80},{80,64},{96,112},{112,96},{1... | collective-permute-start | bytes 786440 | tf_op jit(solution)/shard_map/ppermute | solution.py:32
  80.4 12.8 %copy-start.12 = (bf16[3,256,512]{2,1,0:T(8,128)(2,1)}, bf16[3,256,512]{2,1,0:T(8,128)(2,1)S(1)}, u32[]{:S(2)}) copy-start(bf16[3,256,512]{2,1,0:T(8,128)(2,1)S(1)} %collective-permute-done.8.refs_7_) | copy-start | bytes 2359300
  80.4 6.0 %collective-permute-start.11 = (bf16[2,256,256]{2,1,0:T(8,128)(2,1)S(1)}, bf16[2,256,256]{2,1,0:T(8,128)(2,1)}, u32[]{:S(2)}, u32[]{:S(2)}) collective-permute-start(bf16[2,256,256]{2,1,0:T(8,128)(2,1)S(1)} %get-tuple-element.40), channel_id=1, source_target_pairs={{0,16},{16,0},{32,48},{48,32},{64,80},{80,64},{96,112},{112,96},{1... | collective-permute-start | bytes 786440 | tf_op jit(solution)/shard_map/ppermute | solution.py:32
  92.5 0.7 copy-start.10
  93.2 22.8 %copy-start.6 = (f32[4,1024,128]{2,1,0:T(8,128)S(1)}, f32[4,1024,128]{2,1,0:T(8,128)}, u32[]{:S(2)}) copy-start(f32[4,1024,128]{2,1,0:T(8,128)} %get-tuple-element.30.spec_ref) | copy-start | bytes 6291460
  100.0 16.0 %copy-start.1 = (bf16[768,256]{1,0:T(8,128)(2,1)S(1)}, bf16[768,256]{1,0:T(8,128)(2,1)}, u32[]{:S(2)}) copy-start(bf16[768,256]{1,0:T(8,128)(2,1)} %constant.72.clone.refs_2_.back_ref) | copy-start | bytes 1179652
  100.0 16.0 %copy-start.2 = (bf16[768,256]{1,0:T(8,128)(2,1)S(1)}, bf16[768,256]{1,0:T(8,128)(2,1)}, u32[]{:S(2)}) copy-start(bf16[768,256]{1,0:T(8,128)(2,1)} %constant.71.clone.refs_1_.second_ref) | copy-start | bytes 1179652
  100.0 16.0 %copy-start.3 = (f32[2,64,128]{2,1,0:T(8,128)S(1)}, f32[2,64,128]{2,1,0:T(8,128)}, u32[]{:S(2)}) copy-start(f32[2,64,128]{2,1,0:T(8,128)} %constant.74.clone.refs_4_.turn_ref) | copy-start | bytes 196612
  100.0 16.0 %copy-start.4 = (bf16[64,384]{1,0:T(8,128)(2,1)S(1)}, bf16[64,384]{1,0:T(8,128)(2,1)}, u32[]{:S(2)}) copy-start(bf16[64,384]{1,0:T(8,128)(2,1)} %constant.73.clone.refs_3_.last_ref) | copy-start | bytes 147460
  100.1 16.0 %copy-start.5 = (bf16[128,128]{1,0:T(8,128)(2,1)S(1)}, bf16[128,128]{1,0:T(8,128)(2,1)}, u32[]{:S(2)}) copy-start(bf16[128,128]{1,0:T(8,128)(2,1)} %constant.70.clone.refs_0_.first_ref) | copy-start | bytes 98308
  100.1 5.9 %collective-permute-start.13 = (bf16[8,256,256]{2,1,0:T(8,128)(2,1)}, bf16[8,256,256]{2,1,0:T(8,128)(2,1)}, u32[]{:S(2)}, u32[]{:S(2)}) collective-permute-start(bf16[8,256,256]{2,1,0:T(8,128)(2,1)} %get-tuple-element.33), channel_id=1, source_target_pairs={{0,16},{16,0},{32,48},{48,32},{64,80},{80,64},{96,112},{112,96},{1... | collective-permute-start | bytes 3145736 | tf_op jit(solution)/shard_map/ppermute | solution.py:32
  100.3 15.8 %all-to-all-start.2 = ((bf16[16,16,512]{2,1,0:T(8,128)(2,1)}), bf16[16,16,512]{2,1,0:T(8,128)(2,1)S(1)}, u32[]{:S(2)}, u32[]{:S(2)}) async-start(bf16[16,16,512]{2,1,0:T(8,128)(2,1)} %bitcast.24), calls=%async_computation.2 | async-start | bytes 524288 | tf_op jit(solution)/shard_map/all_to_all | solution.py:363
  108.2 19.3 %collective-permute-start.14 = (bf16[2,256,256]{2,1,0:T(8,128)(2,1)}, bf16[2,256,256]{2,1,0:T(8,128)(2,1)}, u32[]{:S(2)}, u32[]{:S(2)}) collective-permute-start(bf16[2,256,256]{2,1,0:T(8,128)(2,1)} %get-tuple-element.34), channel_id=1, source_target_pairs={{0,64},{16,80},{32,96},{48,112},{64,128},{80,144},{96,160},{112,17... | collective-permute-start | bytes 786440 | tf_op jit(solution)/shard_map/ppermute | solution.py:32
  109.5 18.1 %collective-permute-start.16 = (bf16[2,256,256]{2,1,0:T(8,128)(2,1)}, bf16[2,256,256]{2,1,0:T(8,128)(2,1)}, u32[]{:S(2)}, u32[]{:S(2)}) collective-permute-start(bf16[2,256,256]{2,1,0:T(8,128)(2,1)} %get-tuple-element.35), channel_id=1, source_target_pairs={{0,192},{16,208},{32,224},{48,240},{64,0},{80,16},{96,32},{112,48}... | collective-permute-start | bytes 786440 | tf_op jit(solution)/shard_map/ppermute | solution.py:32
  109.7 17.8 %collective-permute-start.15 = (bf16[2,256,256]{2,1,0:T(8,128)(2,1)S(1)}, bf16[2,256,256]{2,1,0:T(8,128)(2,1)}, u32[]{:S(2)}, u32[]{:S(2)}) collective-permute-start(bf16[2,256,256]{2,1,0:T(8,128)(2,1)S(1)} %get-tuple-element.36), channel_id=1, source_target_pairs={{0,128},{16,144},{32,160},{48,176},{64,192},{80,208},{96,224},{112... | collective-permute-start | bytes 786440 | tf_op jit(solution)/shard_map/ppermute | solution.py:32
  121.8 27.1 %all-to-all-start.3 = ((bf16[16,32,512]{2,1,0:T(8,128)(2,1)}), bf16[16,32,512]{2,1,0:T(8,128)(2,1)S(1)}, u32[]{:S(2)}, u32[]{:S(2)}) async-start(bf16[16,32,512]{2,1,0:T(8,128)(2,1)} %grads.1), calls=%async_computation.3 | async-start | bytes 1048576 | tf_op jit(solution)/shard_map/all_to_all | solution.py:363
  129.0 19.3 %collective-permute-start.17 = (bf16[256,256]{1,0:T(8,128)(2,1)S(1)}, bf16[256,256]{1,0:T(8,128)(2,1)S(1)}, u32[]{:S(2)}, u32[]{:S(2)}) collective-permute-start(bf16[256,256]{1,0:T(8,128)(2,1)S(1)} %slice_bitcast_fusion), channel_id=1, source_target_pairs={{0,32},{16,48},{32,0},{48,16},{64,96},{80,112},{96,64},{112,80},{1... | collective-permute-start | bytes 393224 | tf_op jit(solution)/shard_map/ppermute | solution.py:32

commit v7 on v6

--- a/solution.py
+++ b/solution.py
@@ -378,7 +378,8 @@
     w_line = lax.all_gather(out_weight.T, "ctx", axis_index_groups=LINES_X)
 
     both = jnp.concatenate([inputs.reshape(16, FEW, TOK), filters.reshape(16, FEW, TOK)], axis=1)
-    mixed_rows, spec = conv_call(exchange(both))
+    arrived = exchange(both)
+    mixed_rows, spec = conv_call(arrived)
     mixed = exchange(mixed_rows).reshape(CH, TOK)
 
     rest = stack_call([send(out_grad, "tp", 1, 4, dz) for dz in (1, 2, 3)])
@@ -391,8 +392,8 @@
     for n, r in zip(near, rests):
         grads += [n, r]
 
+    w_line, _ = lax.optimization_barrier((w_line, arrived))
     w_far = send(w_line, "ctx", 2, 2, 1)
-    w_line, w_far, _ = lax.optimization_barrier((w_line, w_far, mixed_rows))
     weights = [w_line, w_far, send(w_line, "ctx", 1, 2, 1)]
     weights += [send(w_far[i : i + 2], "ctx", 1, 2, 1) for i in (0, 2)]
 

time: 150 us -> 147 us (0.980)
  starting transfers between devices: 65.4 us -> 59 us
  waiting for transfers between devices: 43.3 us -> 46.7 us
    all_to_all x4, starting transfers between devices: 31.4 us -> 23.6 us  [exchange(): return lax.all_to_all(value, 'ctx', split_axis=0, concat_axis=0, tiled=True)]
    ppermute x18, waiting for transfers between devices: 32.6 us -> 39.4 us  [send(): return lax.ppermute(value, axis, shift_pairs(stride, size, by))]
    all_to_all x4, waiting for transfers between devices: 10.6 us -> 7.26 us  [exchange(): return lax.all_to_all(value, 'ctx', split_axis=0, concat_axis=0, tiled=True)]
  transfers between devices with their start and end apart: 22 -> 22, of which waited for: 7 -> 6; matrix products, arithmetic and copies ran while one was open for 5% -> 5% of each run, Pallas kernels for 8% -> 8%
where the time goes in v7:
time: 147 us
  starting transfers between devices  59 us (40%)
  waiting for transfers between devices  46.7 us (32%)
  Pallas kernels  19.2 us (13%)
  blocking collectives  11.5 us (8%)
  other arithmetic  6.33 us (4%)
  local copies, waits for them, and re-layouts  3.12 us (2%)
    ppermute x18, waiting for transfers between devices, send(): return lax.ppermute(value, axis, shift_pairs(stride, size, by))  39.4 us
    ppermute x18, starting transfers between devices, send(): return lax.ppermute(value, axis, shift_pairs(stride, size, by))  35.4 us
    all_to_all x4, starting transfers between devices, exchange(): return lax.all_to_all(value, 'ctx', split_axis=0, concat_axis=0, tiled=True)  23.6 us
    all_gather x1, blocking collectives, on_device(): w_line = lax.all_gather(out_weight.T, 'ctx', axis_index_groups=LINES_X)  11.5 us
    all_to_all x4, waiting for transfers between devices, exchange(): return lax.all_to_all(value, 'ctx', split_axis=0, concat_axis=0, tiled=True)  7.26 us
    pallas_call x1, Pallas kernels, products_call(): pl.pallas_call(products_kernel, out_shape=(tile, tile, eight, eight), in_...  6.76 us
    pallas_call x1, Pallas kernels, conv_call(): pl.pallas_call(conv_kernel, out_shape=(jax.ShapeDtypeStruct((16, FEW, TOK...  6.66 us
    pallas_call x1, Pallas kernels, grads_call(): pl.pallas_call(grads_kernel, out_shape=jax.ShapeDtypeStruct((16, 2 * FEW,...  5.75 us
  transfers between devices with their start and end apart: 22, of which 6 were waited for; matrix products, arithmetic and copies ran while one was open for 5% of the time, Pallas kernels for 8%

profile of v7, /device:TPU:67, one launch (start us, length us, event | category | flops | bytes accessed | tf_op | source)
XLA Modules:
  0.0 146.8 jit_solution(5124951399251418152)
XLA Ops:
  0.6 0.0 copy-start.13
  0.7 1.4 collective-permute-start.3
  2.0 0.0 collective-permute-start.2
  2.0 3.7 %collective-permute-start.1 = (bf16[256,512]{1,0:T(8,128)(2,1)}, bf16[256,512]{1,0:T(8,128)(2,1)S(1)}, u32[]{:S(2)}, u32[]{:S(2)}) collective-permute-start(bf16[256,512]{1,0:T(8,128)(2,1)} %refs_0_.2), channel_id=1, source_target_pairs={{0,2},{1,3},{2,0},{3,1},{4,6},{5,7},{6,4},{7,5},{8,10},{9,11},{10,... | collective-permute-start | bytes 786440 | tf_op jit(solution)/shard_map/ppermute | solution.py:32
  5.7 0.0 collective-permute-start
  5.7 2.6 %collective-permute-start.4 = (bf16[256,512]{1,0:T(8,128)(2,1)}, bf16[256,512]{1,0:T(8,128)(2,1)S(1)}, u32[]{:S(2)}, u32[]{:S(2)}) collective-permute-start(bf16[256,512]{1,0:T(8,128)(2,1)} %refs_0_.2), channel_id=1, source_target_pairs={{0,8},{1,9},{2,10},{3,11},{4,12},{5,13},{6,14},{7,15},{8,0},{9,1},... | collective-permute-start | bytes 786440 | tf_op jit(solution)/shard_map/ppermute | solution.py:32
  8.4 1.9 %pad_maximum_fusion = bf16[16,32,512]{2,1,0:T(8,128)(2,1)} fusion(bf16[16,16,512]{2,1,0:T(8,128)(2,1)} %bitcast.25, bf16[16,16,512]{2,1,0:T(8,128)(2,1)} %bitcast.26), kind=kLoop, calls=%fused_computation | loop fusion | flops 1048576 | bytes 1048576 | tf_op jit(solution)/shard_map/concatenate | solution.py:380
  10.2 10.3 %all-to-all-start = ((bf16[16,32,512]{2,1,0:T(8,128)(2,1)}), bf16[16,32,512]{2,1,0:T(8,128)(2,1)S(1)}, u32[]{:S(2)}, u32[]{:S(2)}) async-start(bf16[16,32,512]{2,1,0:T(8,128)(2,1)} %pad_maximum_fusion), calls=%async_computation | async-start | bytes 1048576 | tf_op jit(solution)/shard_map/all_to_all | solution.py:363
  20.6 11.5 %all-gather = bf16[1024,256]{0,1:T(8,128)(2,1)S(1)} all-gather(bf16[256,256]{0,1:T(8,128)(2,1)S(1)} %bitcast.29), channel_id=2, replica_groups={{0,64,128,192},{16,80,144,208},{32,96,160,224},{48,112,176,240},{1,65,1..., dimensions={0}, use_global_device_ids=true | all-gather | bytes 655360 | tf_op jit(solution)/shard_map/all_gather | solution.py:378
  32.1 0.2 copy.14
  32.3 0.0 collective-permute-done.3.refs_2_
  32.3 0.0 copy-start.14
  32.3 1.1 collective-permute-start.5
  33.4 0.0 collective-permute-done.2.refs_2_
  33.4 0.0 collective-permute-done.1.refs_1_
  33.4 2.4 %collective-permute-done.refs_0_ = bf16[256,512]{1,0:T(8,128)(2,1)S(1)} collective-permute-done((bf16[256,512]{1,0:T(8,128)(2,1)}, bf16[256,512]{1,0:T(8,128)(2,1)S(1)}, u32[]{:S(2)}, u32[]{:S(2)}) %collective-permute-start) | collective-permute-done | bytes 262176 | tf_op jit(solution)/shard_map/ppermute | solution.py:32
  35.8 0.1 stack.25.refs_1_
  35.9 0.0 collective-permute-done.4.refs_4_
  35.9 0.0 copy-start.15
  35.9 2.2 %collective-permute-done.5.refs_6_ = bf16[256,512]{1,0:T(8,128)(2,1)S(1)} collective-permute-done((bf16[256,512]{1,0:T(8,128)(2,1)S(1)}, bf16[256,512]{1,0:T(8,128)(2,1)S(1)}, u32[]{:S(2)}, u32[]{:S(2)}) %collective-permute-start.5) | collective-permute-done | bytes 262176 | tf_op jit(solution)/shard_map/ppermute | solution.py:32
  38.2 0.7 copy-done.16
  38.9 3.4 %collective-permute-start.8 = (bf16[3,256,512]{2,1,0:T(8,128)(2,1)S(1)}, bf16[3,256,512]{2,1,0:T(8,128)(2,1)S(1)}, u32[]{:S(2)}, u32[]{:S(2)}) collective-permute-start(bf16[3,256,512]{2,1,0:T(8,128)(2,1)S(1)} %stack.25.refs_1_), channel_id=1, source_target_pairs={{0,12},{1,13},{2,14},{3,15},{4,0},{5,1},{6,2},{7,3},{8,4},{9,5},{1... | collective-permute-start | bytes 2359304 | tf_op jit(solution)/shard_map/ppermute | solution.py:32
  42.3 0.0 all-to-all-done.xf_ref
  42.3 7.6 %collective-permute-start.9 = (bf16[4,256,256]{2,1,0:T(8,128)(2,1)S(1)}, bf16[4,256,256]{2,1,0:T(8,128)(2,1)S(1)}, u32[]{:S(2)}, u32[]{:S(2)}) collective-permute-start(bf16[4,256,256]{2,1,0:T(8,128)(2,1)S(1)} %bitcast.20), channel_id=1, source_target_pairs={{0,32},{16,48},{32,0},{48,16},{64,96},{80,112},{96,64},{112,80},{1... | collective-permute-start | bytes 1572872 | tf_op jit(solution)/shard_map/ppermute | solution.py:32
  50.0 0.0 collective-permute-start.7
  50.0 0.7 collective-permute-start.6
  50.6 2.4 %collective-permute-start.10 = (bf16[4,256,256]{2,1,0:T(8,128)(2,1)S(1)}, bf16[4,256,256]{2,1,0:T(8,128)(2,1)}, u32[]{:S(2)}, u32[]{:S(2)}) collective-permute-start(bf16[4,256,256]{2,1,0:T(8,128)(2,1)S(1)} %bitcast.21), channel_id=1, source_target_pairs={{0,16},{16,0},{32,48},{48,32},{64,80},{80,64},{96,112},{112,96},{1... | collective-permute-start | bytes 1572872 | tf_op jit(solution)/shard_map/ppermute | solution.py:32
  53.1 6.7 %conv.1 = (bf16[16,16,512]{2,1,0:T(8,128)(2,1)}, f32[4,1024,128]{2,1,0:T(8,128)}) custom-call(bf16[16,32,512]{2,1,0:T(8,128)(2,1)} %copy-done.9, bf16[128,128]{1,0:T(8,128)(2,1)} %constant.70.clone.refs_0_.first_ref, bf16[768,256]{1,0:T(8,128)(2,1)} %constant.71.clone.refs_1_.second_ref, bf16[768,256]{1,0:T(8,128)(2,1)} %constant.72.clone.refs_2_.back_ref, ...), custom_call_target="tpu_custom_call" | custom-call | flops 1000000000 | bytes 4194304 | tf_op jit(solution)/shard_map/conv/pallas_call | solution.py:228
  59.8 4.4 %all-to-all-start.1 = ((bf16[16,16,512]{2,1,0:T(8,128)(2,1)}), bf16[16,16,512]{2,1,0:T(8,128)(2,1)S(1)}, u32[]{:S(2)}, u32[]{:S(2)}) async-start(bf16[16,16,512]{2,1,0:T(8,128)(2,1)} %get-tuple-element.26), calls=%async_computation.1 | async-start | bytes 524288 | tf_op jit(solution)/shard_map/all_to_all | solution.py:363
  64.1 9.5 %collective-permute-done.9.refs_9_ = bf16[4,256,256]{2,1,0:T(8,128)(2,1)S(1)} collective-permute-done((bf16[4,256,256]{2,1,0:T(8,128)(2,1)S(1)}, bf16[4,256,256]{2,1,0:T(8,128)(2,1)S(1)}, u32[]{:S(2)}, u32[]{:S(2)}) %collective-permute-start.9) | collective-permute-done | bytes 524320 | tf_op jit(solution)/shard_map/ppermute | solution.py:32
  73.7 0.8 collective-permute-start.12
  74.5 2.4 %collective-permute-start.11 = (bf16[2,256,256]{2,1,0:T(8,128)(2,1)S(1)}, bf16[2,256,256]{2,1,0:T(8,128)(2,1)}, u32[]{:S(2)}, u32[]{:S(2)}) collective-permute-start(bf16[2,256,256]{2,1,0:T(8,128)(2,1)S(1)} %get-tuple-element.38), channel_id=1, source_target_pairs={{0,16},{16,0},{32,48},{48,32},{64,80},{80,64},{96,112},{112,96},{1... | collective-permute-start | bytes 786440 | tf_op jit(solution)/shard_map/ppermute | solution.py:32
  76.9 0.6 stack.24.where_ref
  77.5 0.0 collective-permute-done.7.refs_5_
  77.5 9.7 %collective-permute-done.6.refs_3_ = bf16[3,256,512]{2,1,0:T(8,128)(2,1)} collective-permute-done((bf16[3,256,512]{2,1,0:T(8,128)(2,1)S(1)}, bf16[3,256,512]{2,1,0:T(8,128)(2,1)}, u32[]{:S(2)}, u32[]{:S(2)}) %collective-permute-start.6) | collective-permute-done | bytes 786464 | tf_op jit(solution)/shard_map/ppermute | solution.py:32
  87.2 0.0 all-to-all-done.1
  87.2 0.0 collective-permute-done.10.refs_10_
  87.2 0.0 collective-permute-done.12.refs_12_
  87.3 0.0 collective-permute-done.11.refs_11_
  87.3 0.7 copy-done.10
  88.0 6.8 %products.1 = (bf16[256,512]{1,0:T(8,128)(2,1)}, bf16[256,512]{1,0:T(8,128)(2,1)}, bf16[8,256,256]{2,1,0:T(8,128)(2,1)}, bf16[8,256,256]{2,1,0:T(8,128)(2,1)}) custom-call(s32[5]{0:T(128)} %stack.24.where_ref, bf16[256,512]{1,0:T(8,128)(2,1)} %refs_0_.2, bf16[3,256,512]{2,1,0:T(8,128)(2,1)} %copy-done, bf16[256,512]{1,0:T(8,128)(2,1)} %copy-done.14, ...), custom_call_target="tpu_custom_call" | custom-call | flops 2147483648 | bytes 9437184 | tf_op jit(solution)/shard_map/products/pallas_call | solution.py:350
  94.7 0.0 copy-start.1
  94.7 0.0 copy-start.2
  94.8 0.0 copy-start.3
  94.8 0.0 copy-start.4
  94.8 0.0 copy-start.5
  94.8 0.9 collective-permute-start.13
  95.7 3.4 %all-to-all-start.2 = ((bf16[16,16,512]{2,1,0:T(8,128)(2,1)}), bf16[16,16,512]{2,1,0:T(8,128)(2,1)S(1)}, u32[]{:S(2)}, u32[]{:S(2)}) async-start(bf16[16,16,512]{2,1,0:T(8,128)(2,1)} %bitcast.24), calls=%async_computation.2 | async-start | bytes 524288 | tf_op jit(solution)/shard_map/all_to_all | solution.py:363
  99.2 0.0 collective-permute-done.13
  99.2 2.3 %add_convert_fusion.3 = (bf16[2,256,256]{2,1,0:T(8,128)(2,1)}, bf16[2,256,256]{2,1,0:T(8,128)(2,1)}, bf16[2,256,256]{2,1,0:T(8,128)(2,1)S(1)}) fusion(bf16[8,256,256]{2,1,0:T(8,128)(2,1)} %collective-permute-done.13, bf16[8,256,256]{2,1,0:T(8,128)(2,1)} %get-tuple-element.30), kind=kLoop, calls=%fused_computation.4 | loop fusion | flops 1572864 | bytes 2359296 | tf_op jit(solution)/shard_map/convert_element_type | solution.py:370
  101.5 1.0 collective-permute-start.14
  102.5 0.5 collective-permute-start.16
  103.0 1.6 %collective-permute-start.15 = (bf16[2,256,256]{2,1,0:T(8,128)(2,1)S(1)}, bf16[2,256,256]{2,1,0:T(8,128)(2,1)}, u32[]{:S(2)}, u32[]{:S(2)}) collective-permute-start(bf16[2,256,256]{2,1,0:T(8,128)(2,1)S(1)} %get-tuple-element.34), channel_id=1, source_target_pairs={{0,128},{16,144},{32,160},{48,176},{64,192},{80,208},{96,224},{112... | collective-permute-start | bytes 786440 | tf_op jit(solution)/shard_map/ppermute | solution.py:32
  104.6 7.3 %all-to-all-done.2.p_ref = bf16[16,16,512]{2,1,0:T(8,128)(2,1)S(1)} async-done(((bf16[16,16,512]{2,1,0:T(8,128)(2,1)}), bf16[16,16,512]{2,1,0:T(8,128)(2,1)S(1)}, u32[]{:S(2)}, u32[]{:S(2)}) %all-to-all-start.2) | async-done | bytes 262176 | tf_op jit(solution)/shard_map/all_to_all | solution.py:363
  111.9 5.8 %grads.1 = bf16[16,32,512]{2,1,0:T(8,128)(2,1)} custom-call(bf16[16,16,512]{2,1,0:T(8,128)(2,1)S(1)} %all-to-all-done.2.p_ref, bf16[128,128]{1,0:T(8,128)(2,1)S(1)} %copy-done.5, bf16[768,256]{1,0:T(8,128)(2,1)S(1)} %copy-done.2, bf16[768,256]{1,0:T(8,128)(2,1)S(1)} %copy-done.1, bf16[64,384]{1,0:T(8,128)(2,1)S(1)} %copy-done.4, ...), custom_call_target="tpu_custom_call" | custom-call | flops 10000000000 | bytes 4194304 | tf_op jit(solution)/shard_map/grads/pallas_call | solution.py:244
  117.7 5.5 %all-to-all-start.3 = ((bf16[16,32,512]{2,1,0:T(8,128)(2,1)}), bf16[16,32,512]{2,1,0:T(8,128)(2,1)S(1)}, u32[]{:S(2)}, u32[]{:S(2)}) async-start(bf16[16,32,512]{2,1,0:T(8,128)(2,1)} %grads.1), calls=%async_computation.3 | async-start | bytes 1048576 | tf_op jit(solution)/shard_map/all_to_all | solution.py:363
  123.2 0.0 collective-permute-done.14
  123.2 0.0 collective-permute-done.15
  123.2 1.4 add_convert_fusion
  124.6 5.2 %collective-permute-start.17 = (bf16[256,256]{1,0:T(8,128)(2,1)S(1)}, bf16[256,256]{1,0:T(8,128)(2,1)S(1)}, u32[]{:S(2)}, u32[]{:S(2)}) collective-permute-start(bf16[256,256]{1,0:T(8,128)(2,1)S(1)} %slice_bitcast_fusion), channel_id=1, source_target_pairs={{0,32},{16,48},{32,0},{48,16},{64,96},{80,112},{96,64},{112,80},{1... | collective-permute-start | bytes 393224 | tf_op jit(solution)/shard_map/ppermute | solution.py:32
  129.8 15.5 %collective-permute-done.17 = bf16[256,256]{1,0:T(8,128)(2,1)S(1)} collective-permute-done((bf16[256,256]{1,0:T(8,128)(2,1)S(1)}, bf16[256,256]{1,0:T(8,128)(2,1)S(1)}, u32[]{:S(2)}, u32[]{:S(2)}) %collective-permute-start.17) | collective-permute-done | bytes 131104 | tf_op jit(solution)/shard_map/ppermute | solution.py:32
  145.3 0.7 fusion
  146.0 0.0 all-to-all-done.3
  146.0 0.8 fusion.1
  (28 shorter events, 0.1 us)
Async XLA Ops:
  0.6 31.7 %copy-start.13 = (bf16[256,512]{1,0:T(8,128)(2,1)S(1)}, bf16[256,512]{1,0:T(8,128)(2,1)}, u32[]{:S(2)}) copy-start(bf16[256,512]{1,0:T(8,128)(2,1)} %refs_0_.2) | copy-start | bytes 786436
  0.6 19.9 %copy-start.11 = (bf16[256,256]{1,0:T(8,128)(2,1)S(1)}, bf16[256,256]{1,0:T(8,128)(2,1)}, u32[]{:S(2)}) copy-start(bf16[256,256]{1,0:T(8,128)(2,1)} %param.14) | copy-start | bytes 393220
  0.7 31.6 %collective-permute-start.3 = (bf16[256,512]{1,0:T(8,128)(2,1)}, bf16[256,512]{1,0:T(8,128)(2,1)S(1)}, u32[]{:S(2)}, u32[]{:S(2)}) collective-permute-start(bf16[256,512]{1,0:T(8,128)(2,1)} %refs_0_.2), channel_id=1, source_target_pairs={{0,4},{1,5},{2,6},{3,7},{4,8},{5,9},{6,10},{7,11},{8,12},{9,13},{1... | collective-permute-start | bytes 786440 | tf_op jit(solution)/shard_map/ppermute | solution.py:32
  2.0 31.4 %collective-permute-start.2 = (bf16[256,512]{1,0:T(8,128)(2,1)}, bf16[256,512]{1,0:T(8,128)(2,1)S(1)}, u32[]{:S(2)}, u32[]{:S(2)}) collective-permute-start(bf16[256,512]{1,0:T(8,128)(2,1)} %refs_0_.2), channel_id=1, source_target_pairs={{0,3},{1,0},{2,1},{3,2},{4,7},{5,4},{6,5},{7,6},{8,11},{9,8},{10,9... | collective-permute-start | bytes 786440 | tf_op jit(solution)/shard_map/ppermute | solution.py:32
  2.0 31.4 %collective-permute-start.1 = (bf16[256,512]{1,0:T(8,128)(2,1)}, bf16[256,512]{1,0:T(8,128)(2,1)S(1)}, u32[]{:S(2)}, u32[]{:S(2)}) collective-permute-start(bf16[256,512]{1,0:T(8,128)(2,1)} %refs_0_.2), channel_id=1, source_target_pairs={{0,2},{1,3},{2,0},{3,1},{4,6},{5,7},{6,4},{7,5},{8,10},{9,11},{10,... | collective-permute-start | bytes 786440 | tf_op jit(solution)/shard_map/ppermute | solution.py:32
  5.7 30.1 %collective-permute-start = (bf16[256,512]{1,0:T(8,128)(2,1)}, bf16[256,512]{1,0:T(8,128)(2,1)S(1)}, u32[]{:S(2)}, u32[]{:S(2)}) collective-permute-start(bf16[256,512]{1,0:T(8,128)(2,1)} %refs_0_.2), channel_id=1, source_target_pairs={{0,1},{1,2},{2,3},{3,0},{4,5},{5,6},{6,7},{7,4},{8,9},{9,10},{10,1... | collective-permute-start | bytes 786440 | tf_op jit(solution)/shard_map/ppermute | solution.py:32
  5.7 30.2 %collective-permute-start.4 = (bf16[256,512]{1,0:T(8,128)(2,1)}, bf16[256,512]{1,0:T(8,128)(2,1)S(1)}, u32[]{:S(2)}, u32[]{:S(2)}) collective-permute-start(bf16[256,512]{1,0:T(8,128)(2,1)} %refs_0_.2), channel_id=1, source_target_pairs={{0,8},{1,9},{2,10},{3,11},{4,12},{5,13},{6,14},{7,15},{8,0},{9,1},... | collective-permute-start | bytes 786440 | tf_op jit(solution)/shard_map/ppermute | solution.py:32
  10.2 32.1 %all-to-all-start = ((bf16[16,32,512]{2,1,0:T(8,128)(2,1)}), bf16[16,32,512]{2,1,0:T(8,128)(2,1)S(1)}, u32[]{:S(2)}, u32[]{:S(2)}) async-start(bf16[16,32,512]{2,1,0:T(8,128)(2,1)} %pad_maximum_fusion), calls=%async_computation | async-start | bytes 1048576 | tf_op jit(solution)/shard_map/all_to_all | solution.py:363
  32.3 18.4 %copy-start.7 = (bf16[1024,256]{1,0:T(8,128)(2,1)}, bf16[1024,256]{1,0:T(8,128)(2,1)S(1)}, u32[]{:S(2)}) copy-start(bf16[1024,256]{1,0:T(8,128)(2,1)S(1)} %copy.14) | copy-start | bytes 1572868
  32.3 3.6 %copy-start.14 = (bf16[256,512]{1,0:T(8,128)(2,1)}, bf16[256,512]{1,0:T(8,128)(2,1)S(1)}, u32[]{:S(2)}) copy-start(bf16[256,512]{1,0:T(8,128)(2,1)S(1)} %collective-permute-done.3.refs_2_) | copy-start | bytes 786436
  32.3 5.8 %collective-permute-start.5 = (bf16[256,512]{1,0:T(8,128)(2,1)S(1)}, bf16[256,512]{1,0:T(8,128)(2,1)S(1)}, u32[]{:S(2)}, u32[]{:S(2)}) collective-permute-start(bf16[256,512]{1,0:T(8,128)(2,1)S(1)} %copy-done.13), channel_id=1, source_target_pairs={{0,12},{1,13},{2,14},{3,15},{4,0},{5,1},{6,2},{7,3},{8,4},{9,5},{1... | collective-permute-start | bytes 786440 | tf_op jit(solution)/shard_map/ppermute | solution.py:32
  35.9 23.9 %copy-start = (bf16[3,256,512]{2,1,0:T(8,128)(2,1)}, bf16[3,256,512]{2,1,0:T(8,128)(2,1)S(1)}, u32[]{:S(2)}) copy-start(bf16[3,256,512]{2,1,0:T(8,128)(2,1)S(1)} %stack.25.refs_1_) | copy-start | bytes 2359300
  35.9 2.2 %copy-start.15 = (bf16[256,512]{1,0:T(8,128)(2,1)}, bf16[256,512]{1,0:T(8,128)(2,1)S(1)}, u32[]{:S(2)}) copy-start(bf16[256,512]{1,0:T(8,128)(2,1)S(1)} %collective-permute-done.4.refs_4_) | copy-start | bytes 786436
  38.1 0.7 copy-start.16
  38.9 35.6 %collective-permute-start.8 = (bf16[3,256,512]{2,1,0:T(8,128)(2,1)S(1)}, bf16[3,256,512]{2,1,0:T(8,128)(2,1)S(1)}, u32[]{:S(2)}, u32[]{:S(2)}) collective-permute-start(bf16[3,256,512]{2,1,0:T(8,128)(2,1)S(1)} %stack.25.refs_1_), channel_id=1, source_target_pairs={{0,12},{1,13},{2,14},{3,15},{4,0},{5,1},{6,2},{7,3},{8,4},{9,5},{1... | collective-permute-start | bytes 2359304 | tf_op jit(solution)/shard_map/ppermute | solution.py:32
  42.3 10.8 %copy-start.9 = (bf16[16,32,512]{2,1,0:T(8,128)(2,1)}, bf16[16,32,512]{2,1,0:T(8,128)(2,1)S(1)}, u32[]{:S(2)}) copy-start(bf16[16,32,512]{2,1,0:T(8,128)(2,1)S(1)} %all-to-all-done.xf_ref) | copy-start | bytes 1572868
  42.3 31.3 %collective-permute-start.9 = (bf16[4,256,256]{2,1,0:T(8,128)(2,1)S(1)}, bf16[4,256,256]{2,1,0:T(8,128)(2,1)S(1)}, u32[]{:S(2)}, u32[]{:S(2)}) collective-permute-start(bf16[4,256,256]{2,1,0:T(8,128)(2,1)S(1)} %bitcast.20), channel_id=1, source_target_pairs={{0,32},{16,48},{32,0},{48,16},{64,96},{80,112},{96,64},{112,80},{1... | collective-permute-start | bytes 1572872 | tf_op jit(solution)/shard_map/ppermute | solution.py:32
  50.0 27.5 %collective-permute-start.7 = (bf16[3,256,512]{2,1,0:T(8,128)(2,1)S(1)}, bf16[3,256,512]{2,1,0:T(8,128)(2,1)}, u32[]{:S(2)}, u32[]{:S(2)}) collective-permute-start(bf16[3,256,512]{2,1,0:T(8,128)(2,1)S(1)} %stack.25.refs_1_), channel_id=1, source_target_pairs={{0,8},{1,9},{2,10},{3,11},{4,12},{5,13},{6,14},{7,15},{8,0},{9,1},... | collective-permute-start | bytes 2359304 | tf_op jit(solution)/shard_map/ppermute | solution.py:32
  50.0 37.3 %collective-permute-start.6 = (bf16[3,256,512]{2,1,0:T(8,128)(2,1)S(1)}, bf16[3,256,512]{2,1,0:T(8,128)(2,1)}, u32[]{:S(2)}, u32[]{:S(2)}) collective-permute-start(bf16[3,256,512]{2,1,0:T(8,128)(2,1)S(1)} %stack.25.refs_1_), channel_id=1, source_target_pairs={{0,4},{1,5},{2,6},{3,7},{4,8},{5,9},{6,10},{7,11},{8,12},{9,13},{1... | collective-permute-start | bytes 2359304 | tf_op jit(solution)/shard_map/ppermute | solution.py:32
  50.6 36.6 %collective-permute-start.10 = (bf16[4,256,256]{2,1,0:T(8,128)(2,1)S(1)}, bf16[4,256,256]{2,1,0:T(8,128)(2,1)}, u32[]{:S(2)}, u32[]{:S(2)}) collective-permute-start(bf16[4,256,256]{2,1,0:T(8,128)(2,1)S(1)} %bitcast.21), channel_id=1, source_target_pairs={{0,16},{16,0},{32,48},{48,32},{64,80},{80,64},{96,112},{112,96},{1... | collective-permute-start | bytes 1572872 | tf_op jit(solution)/shard_map/ppermute | solution.py:32
  59.8 27.5 %all-to-all-start.1 = ((bf16[16,16,512]{2,1,0:T(8,128)(2,1)}), bf16[16,16,512]{2,1,0:T(8,128)(2,1)S(1)}, u32[]{:S(2)}, u32[]{:S(2)}) async-start(bf16[16,16,512]{2,1,0:T(8,128)(2,1)} %get-tuple-element.26), calls=%async_computation.1 | async-start | bytes 524288 | tf_op jit(solution)/shard_map/all_to_all | solution.py:363
  73.7 13.6 %copy-start.8 = (bf16[4,256,256]{2,1,0:T(8,128)(2,1)}, bf16[4,256,256]{2,1,0:T(8,128)(2,1)S(1)}, u32[]{:S(2)}) copy-start(bf16[4,256,256]{2,1,0:T(8,128)(2,1)S(1)} %collective-permute-done.9.refs_9_) | copy-start | bytes 1572868
  73.7 13.6 %collective-permute-start.12 = (bf16[2,256,256]{2,1,0:T(8,128)(2,1)S(1)}, bf16[2,256,256]{2,1,0:T(8,128)(2,1)}, u32[]{:S(2)}, u32[]{:S(2)}) collective-permute-start(bf16[2,256,256]{2,1,0:T(8,128)(2,1)S(1)} %get-tuple-element.37), channel_id=1, source_target_pairs={{0,16},{16,0},{32,48},{48,32},{64,80},{80,64},{96,112},{112,96},{1... | collective-permute-start | bytes 786440 | tf_op jit(solution)/shard_map/ppermute | solution.py:32
  74.5 13.5 %copy-start.12 = (bf16[3,256,512]{2,1,0:T(8,128)(2,1)}, bf16[3,256,512]{2,1,0:T(8,128)(2,1)S(1)}, u32[]{:S(2)}) copy-start(bf16[3,256,512]{2,1,0:T(8,128)(2,1)S(1)} %collective-permute-done.8.refs_7_) | copy-start | bytes 2359300
  74.5 12.8 %collective-permute-start.11 = (bf16[2,256,256]{2,1,0:T(8,128)(2,1)S(1)}, bf16[2,256,256]{2,1,0:T(8,128)(2,1)}, u32[]{:S(2)}, u32[]{:S(2)}) collective-permute-start(bf16[2,256,256]{2,1,0:T(8,128)(2,1)S(1)} %get-tuple-element.38), channel_id=1, source_target_pairs={{0,16},{16,0},{32,48},{48,32},{64,80},{80,64},{96,112},{112,96},{1... | collective-permute-start | bytes 786440 | tf_op jit(solution)/shard_map/ppermute | solution.py:32
  87.2 0.7 copy-start.10
  88.0 23.9 %copy-start.6 = (f32[4,1024,128]{2,1,0:T(8,128)S(1)}, f32[4,1024,128]{2,1,0:T(8,128)}, u32[]{:S(2)}) copy-start(f32[4,1024,128]{2,1,0:T(8,128)} %get-tuple-element.28.spec_ref) | copy-start | bytes 6291460
  94.7 17.1 %copy-start.1 = (bf16[768,256]{1,0:T(8,128)(2,1)S(1)}, bf16[768,256]{1,0:T(8,128)(2,1)}, u32[]{:S(2)}) copy-start(bf16[768,256]{1,0:T(8,128)(2,1)} %constant.72.clone.refs_2_.back_ref) | copy-start | bytes 1179652
  94.7 17.1 %copy-start.2 = (bf16[768,256]{1,0:T(8,128)(2,1)S(1)}, bf16[768,256]{1,0:T(8,128)(2,1)}, u32[]{:S(2)}) copy-start(bf16[768,256]{1,0:T(8,128)(2,1)} %constant.71.clone.refs_1_.second_ref) | copy-start | bytes 1179652
  94.8 17.1 %copy-start.3 = (f32[2,64,128]{2,1,0:T(8,128)S(1)}, f32[2,64,128]{2,1,0:T(8,128)}, u32[]{:S(2)}) copy-start(f32[2,64,128]{2,1,0:T(8,128)} %constant.74.clone.refs_4_.turn_ref) | copy-start | bytes 196612
  94.8 17.1 %copy-start.4 = (bf16[64,384]{1,0:T(8,128)(2,1)S(1)}, bf16[64,384]{1,0:T(8,128)(2,1)}, u32[]{:S(2)}) copy-start(bf16[64,384]{1,0:T(8,128)(2,1)} %constant.73.clone.refs_3_.last_ref) | copy-start | bytes 147460
  94.8 17.1 %copy-start.5 = (bf16[128,128]{1,0:T(8,128)(2,1)S(1)}, bf16[128,128]{1,0:T(8,128)(2,1)}, u32[]{:S(2)}) copy-start(bf16[128,128]{1,0:T(8,128)(2,1)} %constant.70.clone.refs_0_.first_ref) | copy-start | bytes 98308
  94.8 4.4 %collective-permute-start.13 = (bf16[8,256,256]{2,1,0:T(8,128)(2,1)}, bf16[8,256,256]{2,1,0:T(8,128)(2,1)}, u32[]{:S(2)}, u32[]{:S(2)}) collective-permute-start(bf16[8,256,256]{2,1,0:T(8,128)(2,1)} %get-tuple-element.31), channel_id=1, source_target_pairs={{0,16},{16,0},{32,48},{48,32},{64,80},{80,64},{96,112},{112,96},{1... | collective-permute-start | bytes 3145736 | tf_op jit(solution)/shard_map/ppermute | solution.py:32
  95.7 16.1 %all-to-all-start.2 = ((bf16[16,16,512]{2,1,0:T(8,128)(2,1)}), bf16[16,16,512]{2,1,0:T(8,128)(2,1)S(1)}, u32[]{:S(2)}, u32[]{:S(2)}) async-start(bf16[16,16,512]{2,1,0:T(8,128)(2,1)} %bitcast.24), calls=%async_computation.2 | async-start | bytes 524288 | tf_op jit(solution)/shard_map/all_to_all | solution.py:363
  101.5 21.7 %collective-permute-start.14 = (bf16[2,256,256]{2,1,0:T(8,128)(2,1)}, bf16[2,256,256]{2,1,0:T(8,128)(2,1)}, u32[]{:S(2)}, u32[]{:S(2)}) collective-permute-start(bf16[2,256,256]{2,1,0:T(8,128)(2,1)} %get-tuple-element.32), channel_id=1, source_target_pairs={{0,64},{16,80},{32,96},{48,112},{64,128},{80,144},{96,160},{112,17... | collective-permute-start | bytes 786440 | tf_op jit(solution)/shard_map/ppermute | solution.py:32
  102.5 20.7 %collective-permute-start.16 = (bf16[2,256,256]{2,1,0:T(8,128)(2,1)}, bf16[2,256,256]{2,1,0:T(8,128)(2,1)}, u32[]{:S(2)}, u32[]{:S(2)}) collective-permute-start(bf16[2,256,256]{2,1,0:T(8,128)(2,1)} %get-tuple-element.33), channel_id=1, source_target_pairs={{0,192},{16,208},{32,224},{48,240},{64,0},{80,16},{96,32},{112,48}... | collective-permute-start | bytes 786440 | tf_op jit(solution)/shard_map/ppermute | solution.py:32
  103.0 20.2 %collective-permute-start.15 = (bf16[2,256,256]{2,1,0:T(8,128)(2,1)S(1)}, bf16[2,256,256]{2,1,0:T(8,128)(2,1)}, u32[]{:S(2)}, u32[]{:S(2)}) collective-permute-start(bf16[2,256,256]{2,1,0:T(8,128)(2,1)S(1)} %get-tuple-element.34), channel_id=1, source_target_pairs={{0,128},{16,144},{32,160},{48,176},{64,192},{80,208},{96,224},{112... | collective-permute-start | bytes 786440 | tf_op jit(solution)/shard_map/ppermute | solution.py:32
  117.7 28.3 %all-to-all-start.3 = ((bf16[16,32,512]{2,1,0:T(8,128)(2,1)}), bf16[16,32,512]{2,1,0:T(8,128)(2,1)S(1)}, u32[]{:S(2)}, u32[]{:S(2)}) async-start(bf16[16,32,512]{2,1,0:T(8,128)(2,1)} %grads.1), calls=%async_computation.3 | async-start | bytes 1048576 | tf_op jit(solution)/shard_map/all_to_all | solution.py:363
  124.6 20.7 %collective-permute-start.17 = (bf16[256,256]{1,0:T(8,128)(2,1)S(1)}, bf16[256,256]{1,0:T(8,128)(2,1)S(1)}, u32[]{:S(2)}, u32[]{:S(2)}) collective-permute-start(bf16[256,256]{1,0:T(8,128)(2,1)S(1)} %slice_bitcast_fusion), channel_id=1, source_target_pairs={{0,32},{16,48},{32,0},{48,16},{64,96},{80,112},{96,64},{112,80},{1... | collective-permute-start | bytes 393224 | tf_op jit(solution)/shard_map/ppermute | solution.py:32

commit v8 on v7

--- a/solution.py
+++ b/solution.py
@@ -280,7 +280,7 @@
 
 
 def products_kernel(where_ref, *refs):
-    grads, ins_hbm = refs[:8], refs[8:15]
+    grads, ins_hbm = [refs[i] for i in (0, 1, 2, 3, 6, 7, 4, 5)], refs[8:15]
     product_hbm, gate_grad_hbm, other_hbm, same_hbm = refs[15:19]
     held, weights, gates_ref, mixed_ref, product_ref, gate_grad_ref, sums, grad_sems, sems, out_sems = refs[19:]
     targets = [weights.at[pl.ds(4 * i, 4)] for i in range(3)] + [weights.at[pl.ds(12 + i, 2)] for i in (0, 2)]
@@ -375,22 +375,23 @@
     tp = lax.axis_index("tp")
     where = jnp.stack([ctx // 4, (ctx // 2) % 2, ctx % 2, tp // 4, tp % 4]).astype(jnp.int32)
 
-    w_line = lax.all_gather(out_weight.T, "ctx", axis_index_groups=LINES_X)
 
     both = jnp.concatenate([inputs.reshape(16, FEW, TOK), filters.reshape(16, FEW, TOK)], axis=1)
     arrived = exchange(both)
     mixed_rows, spec = conv_call(arrived)
     mixed = exchange(mixed_rows).reshape(CH, TOK)
 
-    rest = stack_call([send(out_grad, "tp", 1, 4, dz) for dz in (1, 2, 3)])
+    lines = [send(out_grad, "tp", 1, 4, dz) for dz in (1, 2, 3)]
     up, far = send(out_grad, "tp", 4, 4, 1), send(out_grad, "tp", 4, 4, 2)
-    up, own = lax.optimization_barrier((up, out_grad))
+    up, own, w_own = lax.optimization_barrier((up, out_grad, out_weight))
+    w_line = lax.all_gather(w_own.T, "ctx", axis_index_groups=LINES_X)
     near = [up, far, send(own, "tp", 4, 4, 3)]
-    rest, near, w_line = lax.optimization_barrier((rest, near, w_line))
+    lines, w_line = lax.optimization_barrier((lines, w_line))
+    rest, near = lax.optimization_barrier((stack_call(lines), near))
     rests = [send(rest, "tp", 4, 4, dy) for dy in (1, 2, 3)]
     grads = [out_grad, rest]
-    for n, r in zip(near, rests):
-        grads += [n, r]
+    for dy in (1, 3, 2):
+        grads += [near[dy - 1], rests[dy - 1]]
 
     w_line, _ = lax.optimization_barrier((w_line, arrived))
     w_far = send(w_line, "ctx", 2, 2, 1)

time: 147 us -> 145 us (0.986)
  waiting for transfers between devices: 46.7 us -> 23.8 us
  starting transfers between devices: 59 us -> 80.1 us
    ppermute x18, waiting for transfers between devices: 39.4 us -> 14.8 us  [send(): return lax.ppermute(value, axis, shift_pairs(stride, size, by))]
    all_to_all x4, starting transfers between devices: 23.6 us -> 36 us  [exchange(): return lax.all_to_all(value, 'ctx', split_axis=0, concat_axis=0, tiled=True)]
    ppermute x18, starting transfers between devices: 35.4 us -> 44.2 us  [send(): return lax.ppermute(value, axis, shift_pairs(stride, size, by))]
    all_to_all x4, waiting for transfers between devices: 7.26 us -> 9.03 us  [exchange(): return lax.all_to_all(value, 'ctx', split_axis=0, concat_axis=0, tiled=True)]
  transfers between devices with their start and end apart: 22 -> 22, of which waited for: 6 -> 6; matrix products, arithmetic and copies ran while one was open for 5% -> 5% of each run, Pallas kernels for 8% -> 9%
where the time goes in v8:
time: 145 us; the launch traced here: 144 us
  starting transfers between devices  80.1 us (55%)
  waiting for transfers between devices  23.8 us (16%)
  Pallas kernels  19.2 us (13%)
  blocking collectives  10.9 us (8%)
  other arithmetic  6.31 us (4%)
  local copies, waits for them, and re-layouts  3.18 us (2%)
    ppermute x18, starting transfers between devices, send(): return lax.ppermute(value, axis, shift_pairs(stride, size, by))  44.2 us
    all_to_all x4, starting transfers between devices, exchange(): return lax.all_to_all(value, 'ctx', split_axis=0, concat_axis=0, tiled=True)  36 us
    ppermute x18, waiting for transfers between devices, send(): return lax.ppermute(value, axis, shift_pairs(stride, size, by))  14.8 us
    all_gather x1, blocking collectives, on_device(): w_line = lax.all_gather(w_own.T, 'ctx', axis_index_groups=LINES_X)  10.9 us
    all_to_all x4, waiting for transfers between devices, exchange(): return lax.all_to_all(value, 'ctx', split_axis=0, concat_axis=0, tiled=True)  9.03 us
    pallas_call x1, Pallas kernels, products_call(): pl.pallas_call(products_kernel, out_shape=(tile, tile, eight, eight), in_...  6.75 us
    pallas_call x1, Pallas kernels, conv_call(): pl.pallas_call(conv_kernel, out_shape=(jax.ShapeDtypeStruct((16, FEW, TOK...  6.67 us
    pallas_call x1, Pallas kernels, grads_call(): pl.pallas_call(grads_kernel, out_shape=jax.ShapeDtypeStruct((16, 2 * FEW,...  5.75 us
  transfers between devices with their start and end apart: 22, of which 6 were waited for; matrix products, arithmetic and copies ran while one was open for 5% of the time, Pallas kernels for 9%

profile of v8, /device:TPU:67, one launch (start us, length us, event | category | flops | bytes accessed | tf_op | source)
XLA Modules:
  0.0 144.4 jit_solution(9199919776118095014)
XLA Ops:
  0.6 0.0 copy-start.13
  0.7 1.4 collective-permute-start.3
  2.0 0.0 collective-permute-start.2
  2.0 3.7 %collective-permute-start.1 = (bf16[256,512]{1,0:T(8,128)(2,1)}, bf16[256,512]{1,0:T(8,128)(2,1)S(1)}, u32[]{:S(2)}, u32[]{:S(2)}) collective-permute-start(bf16[256,512]{1,0:T(8,128)(2,1)} %refs_0_.2), channel_id=1, source_target_pairs={{0,2},{1,3},{2,0},{3,1},{4,6},{5,7},{6,4},{7,5},{8,10},{9,11},{10,... | collective-permute-start | bytes 786440 | tf_op jit(solution)/shard_map/ppermute | solution.py:32
  5.7 0.0 collective-permute-start
  5.7 2.6 %collective-permute-start.4 = (bf16[256,512]{1,0:T(8,128)(2,1)}, bf16[256,512]{1,0:T(8,128)(2,1)S(1)}, u32[]{:S(2)}, u32[]{:S(2)}) collective-permute-start(bf16[256,512]{1,0:T(8,128)(2,1)} %refs_0_.2), channel_id=1, source_target_pairs={{0,8},{1,9},{2,10},{3,11},{4,12},{5,13},{6,14},{7,15},{8,0},{9,1},... | collective-permute-start | bytes 786440 | tf_op jit(solution)/shard_map/ppermute | solution.py:32
  8.4 1.9 %pad_maximum_fusion = bf16[16,32,512]{2,1,0:T(8,128)(2,1)} fusion(bf16[16,16,512]{2,1,0:T(8,128)(2,1)} %bitcast.25, bf16[16,16,512]{2,1,0:T(8,128)(2,1)} %bitcast.26), kind=kLoop, calls=%fused_computation | loop fusion | flops 1048576 | bytes 1048576 | tf_op jit(solution)/shard_map/concatenate | solution.py:379
  10.2 10.3 %all-to-all-start = ((bf16[16,32,512]{2,1,0:T(8,128)(2,1)}), bf16[16,32,512]{2,1,0:T(8,128)(2,1)S(1)}, u32[]{:S(2)}, u32[]{:S(2)}) async-start(bf16[16,32,512]{2,1,0:T(8,128)(2,1)} %pad_maximum_fusion), calls=%async_computation | async-start | bytes 1048576 | tf_op jit(solution)/shard_map/all_to_all | solution.py:363
  20.5 0.0 collective-permute-done.3.refs_2_
  20.6 0.0 copy-start.14
  20.6 1.1 collective-permute-start.5
  21.7 10.9 %all-gather = bf16[1024,256]{0,1:T(8,128)(2,1)S(1)} all-gather(bf16[256,256]{0,1:T(8,128)(2,1)S(1)} %bitcast.29), channel_id=2, replica_groups={{0,64,128,192},{16,80,144,208},{32,96,160,224},{48,112,176,240},{1,65,1..., dimensions={0}, use_global_device_ids=true | all-gather | bytes 655360 | tf_op jit(solution)/shard_map/all_gather | solution.py:387
  32.6 0.2 copy.14
  32.8 0.0 collective-permute-done.2.refs_2_
  32.8 0.0 collective-permute-done.1.refs_1_
  32.9 3.0 %collective-permute-done.refs_0_ = bf16[256,512]{1,0:T(8,128)(2,1)S(1)} collective-permute-done((bf16[256,512]{1,0:T(8,128)(2,1)}, bf16[256,512]{1,0:T(8,128)(2,1)S(1)}, u32[]{:S(2)}, u32[]{:S(2)}) %collective-permute-start) | collective-permute-done | bytes 262176 | tf_op jit(solution)/shard_map/ppermute | solution.py:32
  35.8 0.1 stack.25.refs_1_
  35.9 0.0 collective-permute-done.4.refs_6_
  35.9 0.0 copy-start.15
  35.9 0.7 copy-done.15
  36.7 0.0 collective-permute-done.5.refs_4_
  36.7 2.9 %collective-permute-start.8 = (bf16[3,256,512]{2,1,0:T(8,128)(2,1)S(1)}, bf16[3,256,512]{2,1,0:T(8,128)(2,1)S(1)}, u32[]{:S(2)}, u32[]{:S(2)}) collective-permute-start(bf16[3,256,512]{2,1,0:T(8,128)(2,1)S(1)} %stack.25.refs_1_), channel_id=1, source_target_pairs={{0,8},{1,9},{2,10},{3,11},{4,12},{5,13},{6,14},{7,15},{8,0},{9,1},... | collective-permute-start | bytes 2359304 | tf_op jit(solution)/shard_map/ppermute | solution.py:32
  39.6 0.0 all-to-all-done.xf_ref
  39.6 19.8 %collective-permute-start.9 = (bf16[4,256,256]{2,1,0:T(8,128)(2,1)S(1)}, bf16[4,256,256]{2,1,0:T(8,128)(2,1)S(1)}, u32[]{:S(2)}, u32[]{:S(2)}) collective-permute-start(bf16[4,256,256]{2,1,0:T(8,128)(2,1)S(1)} %bitcast.20), channel_id=1, source_target_pairs={{0,32},{16,48},{32,0},{48,16},{64,96},{80,112},{96,64},{112,80},{1... | collective-permute-start | bytes 1572872 | tf_op jit(solution)/shard_map/ppermute | solution.py:32
  59.4 1.1 collective-permute-start.7
  60.5 0.4 collective-permute-start.6
  60.9 1.8 %collective-permute-start.10 = (bf16[4,256,256]{2,1,0:T(8,128)(2,1)S(1)}, bf16[4,256,256]{2,1,0:T(8,128)(2,1)}, u32[]{:S(2)}, u32[]{:S(2)}) collective-permute-start(bf16[4,256,256]{2,1,0:T(8,128)(2,1)S(1)} %bitcast.21), channel_id=1, source_target_pairs={{0,16},{16,0},{32,48},{48,32},{64,80},{80,64},{96,112},{112,96},{1... | collective-permute-start | bytes 1572872 | tf_op jit(solution)/shard_map/ppermute | solution.py:32
  62.7 6.7 %conv.1 = (bf16[16,16,512]{2,1,0:T(8,128)(2,1)}, f32[4,1024,128]{2,1,0:T(8,128)}) custom-call(bf16[16,32,512]{2,1,0:T(8,128)(2,1)} %copy-done.9, bf16[128,128]{1,0:T(8,128)(2,1)} %constant.70.clone.refs_0_.first_ref, bf16[768,256]{1,0:T(8,128)(2,1)} %constant.71.clone.refs_1_.second_ref, bf16[768,256]{1,0:T(8,128)(2,1)} %constant.72.clone.refs_2_.back_ref, ...), custom_call_target="tpu_custom_call" | custom-call | flops 1000000000 | bytes 4194304 | tf_op jit(solution)/shard_map/conv/pallas_call | solution.py:228
  69.4 4.6 %all-to-all-start.1 = ((bf16[16,16,512]{2,1,0:T(8,128)(2,1)}), bf16[16,16,512]{2,1,0:T(8,128)(2,1)S(1)}, u32[]{:S(2)}, u32[]{:S(2)}) async-start(bf16[16,16,512]{2,1,0:T(8,128)(2,1)} %get-tuple-element.34), calls=%async_computation.1 | async-start | bytes 524288 | tf_op jit(solution)/shard_map/all_to_all | solution.py:363
  74.0 0.0 collective-permute-done.9.refs_9_
  74.0 0.5 collective-permute-start.12
  74.5 0.0 collective-permute-done.8.refs_7_
  74.5 0.3 collective-permute-start.11
  74.8 0.6 stack.24.where_ref
  75.4 1.9 %collective-permute-done.7.refs_5_ = bf16[3,256,512]{2,1,0:T(8,128)(2,1)} collective-permute-done((bf16[3,256,512]{2,1,0:T(8,128)(2,1)S(1)}, bf16[3,256,512]{2,1,0:T(8,128)(2,1)}, u32[]{:S(2)}, u32[]{:S(2)}) %collective-permute-start.7) | collective-permute-done | bytes 786464 | tf_op jit(solution)/shard_map/ppermute | solution.py:32
  77.3 2.0 %collective-permute-done.6.refs_3_ = bf16[3,256,512]{2,1,0:T(8,128)(2,1)} collective-permute-done((bf16[3,256,512]{2,1,0:T(8,128)(2,1)S(1)}, bf16[3,256,512]{2,1,0:T(8,128)(2,1)}, u32[]{:S(2)}, u32[]{:S(2)}) %collective-permute-start.6) | collective-permute-done | bytes 786464 | tf_op jit(solution)/shard_map/ppermute | solution.py:32
  79.3 4.6 %all-to-all-done.1 = bf16[16,16,512]{2,1,0:T(8,128)(2,1)S(1)} async-done(((bf16[16,16,512]{2,1,0:T(8,128)(2,1)}), bf16[16,16,512]{2,1,0:T(8,128)(2,1)S(1)}, u32[]{:S(2)}, u32[]{:S(2)}) %all-to-all-start.1) | async-done | bytes 262176 | tf_op jit(solution)/shard_map/all_to_all | solution.py:363
  83.9 0.0 collective-permute-done.10.refs_10_
  83.9 0.0 collective-permute-done.12.refs_12_
  84.0 0.0 collective-permute-done.11.refs_11_
  84.0 0.7 copy-done.10
  84.7 6.8 %products.1 = (bf16[256,512]{1,0:T(8,128)(2,1)}, bf16[256,512]{1,0:T(8,128)(2,1)}, bf16[8,256,256]{2,1,0:T(8,128)(2,1)}, bf16[8,256,256]{2,1,0:T(8,128)(2,1)}) custom-call(s32[5]{0:T(128)} %stack.24.where_ref, bf16[256,512]{1,0:T(8,128)(2,1)} %refs_0_.2, bf16[3,256,512]{2,1,0:T(8,128)(2,1)} %copy-done, bf16[256,512]{1,0:T(8,128)(2,1)} %copy-done.14, ...), custom_call_target="tpu_custom_call" | custom-call | flops 2147483648 | bytes 9437184 | tf_op jit(solution)/shard_map/products/pallas_call | solution.py:350
  91.4 0.0 copy-start.1
  91.4 0.0 copy-start.2
  91.5 0.0 copy-start.3
  91.5 0.0 copy-start.4
  91.5 0.0 copy-start.5
  91.5 0.1 collective-permute-start.13
  91.6 15.3 %all-to-all-start.2 = ((bf16[16,16,512]{2,1,0:T(8,128)(2,1)}), bf16[16,16,512]{2,1,0:T(8,128)(2,1)S(1)}, u32[]{:S(2)}, u32[]{:S(2)}) async-start(bf16[16,16,512]{2,1,0:T(8,128)(2,1)} %bitcast.24), calls=%async_computation.2 | async-start | bytes 524288 | tf_op jit(solution)/shard_map/all_to_all | solution.py:363
  106.9 0.0 collective-permute-done.13
  106.9 2.3 %add_convert_fusion.3 = (bf16[2,256,256]{2,1,0:T(8,128)(2,1)}, bf16[2,256,256]{2,1,0:T(8,128)(2,1)}, bf16[2,256,256]{2,1,0:T(8,128)(2,1)S(1)}) fusion(bf16[8,256,256]{2,1,0:T(8,128)(2,1)} %collective-permute-done.13, bf16[8,256,256]{2,1,0:T(8,128)(2,1)} %get-tuple-element.38), kind=kLoop, calls=%fused_computation.4 | loop fusion | flops 1572864 | bytes 2359296 | tf_op jit(solution)/shard_map/convert_element_type | solution.py:370
  109.2 1.2 collective-permute-start.14
  110.4 0.3 collective-permute-start.16
  110.7 1.8 %collective-permute-start.15 = (bf16[2,256,256]{2,1,0:T(8,128)(2,1)S(1)}, bf16[2,256,256]{2,1,0:T(8,128)(2,1)}, u32[]{:S(2)}, u32[]{:S(2)}) collective-permute-start(bf16[2,256,256]{2,1,0:T(8,128)(2,1)S(1)} %get-tuple-element.42), channel_id=1, source_target_pairs={{0,128},{16,144},{32,160},{48,176},{64,192},{80,208},{96,224},{112... | collective-permute-start | bytes 786440 | tf_op jit(solution)/shard_map/ppermute | solution.py:32
  112.4 4.4 %all-to-all-done.2.p_ref = bf16[16,16,512]{2,1,0:T(8,128)(2,1)S(1)} async-done(((bf16[16,16,512]{2,1,0:T(8,128)(2,1)}), bf16[16,16,512]{2,1,0:T(8,128)(2,1)S(1)}, u32[]{:S(2)}, u32[]{:S(2)}) %all-to-all-start.2) | async-done | bytes 262176 | tf_op jit(solution)/shard_map/all_to_all | solution.py:363
  116.9 5.7 %grads.1 = bf16[16,32,512]{2,1,0:T(8,128)(2,1)} custom-call(bf16[16,16,512]{2,1,0:T(8,128)(2,1)S(1)} %all-to-all-done.2.p_ref, bf16[128,128]{1,0:T(8,128)(2,1)S(1)} %copy-done.5, bf16[768,256]{1,0:T(8,128)(2,1)S(1)} %copy-done.2, bf16[768,256]{1,0:T(8,128)(2,1)S(1)} %copy-done.1, bf16[64,384]{1,0:T(8,128)(2,1)S(1)} %copy-done.4, ...), custom_call_target="tpu_custom_call" | custom-call | flops 10000000000 | bytes 4194304 | tf_op jit(solution)/shard_map/grads/pallas_call | solution.py:244
  122.6 5.8 %all-to-all-start.3 = ((bf16[16,32,512]{2,1,0:T(8,128)(2,1)}), bf16[16,32,512]{2,1,0:T(8,128)(2,1)S(1)}, u32[]{:S(2)}, u32[]{:S(2)}) async-start(bf16[16,32,512]{2,1,0:T(8,128)(2,1)} %grads.1), calls=%async_computation.3 | async-start | bytes 1048576 | tf_op jit(solution)/shard_map/all_to_all | solution.py:363
  128.4 0.0 collective-permute-done.16
  128.4 0.0 collective-permute-done.15
  128.4 1.4 add_convert_fusion
  129.9 5.2 %collective-permute-start.17 = (bf16[256,256]{1,0:T(8,128)(2,1)S(1)}, bf16[256,256]{1,0:T(8,128)(2,1)S(1)}, u32[]{:S(2)}, u32[]{:S(2)}) collective-permute-start(bf16[256,256]{1,0:T(8,128)(2,1)S(1)} %slice_bitcast_fusion), channel_id=1, source_target_pairs={{0,32},{16,48},{32,0},{48,16},{64,96},{80,112},{96,64},{112,80},{1... | collective-permute-start | bytes 393224 | tf_op jit(solution)/shard_map/ppermute | solution.py:32
  135.1 7.8 %collective-permute-done.17 = bf16[256,256]{1,0:T(8,128)(2,1)S(1)} collective-permute-done((bf16[256,256]{1,0:T(8,128)(2,1)S(1)}, bf16[256,256]{1,0:T(8,128)(2,1)S(1)}, u32[]{:S(2)}, u32[]{:S(2)}) %collective-permute-start.17) | collective-permute-done | bytes 131104 | tf_op jit(solution)/shard_map/ppermute | solution.py:32
  142.9 0.7 fusion
  143.6 0.8 fusion.1
  (26 shorter events, 0.1 us)
Async XLA Ops:
  0.6 19.9 %copy-start.13 = (bf16[256,512]{1,0:T(8,128)(2,1)S(1)}, bf16[256,512]{1,0:T(8,128)(2,1)}, u32[]{:S(2)}) copy-start(bf16[256,512]{1,0:T(8,128)(2,1)} %refs_0_.2) | copy-start | bytes 786436
  0.6 21.1 %copy-start.11 = (bf16[256,256]{1,0:T(8,128)(2,1)S(1)}, bf16[256,256]{1,0:T(8,128)(2,1)}, u32[]{:S(2)}) copy-start(bf16[256,256]{1,0:T(8,128)(2,1)} %param.14) | copy-start | bytes 393220
  0.7 19.9 %collective-permute-start.3 = (bf16[256,512]{1,0:T(8,128)(2,1)}, bf16[256,512]{1,0:T(8,128)(2,1)S(1)}, u32[]{:S(2)}, u32[]{:S(2)}) collective-permute-start(bf16[256,512]{1,0:T(8,128)(2,1)} %refs_0_.2), channel_id=1, source_target_pairs={{0,4},{1,5},{2,6},{3,7},{4,8},{5,9},{6,10},{7,11},{8,12},{9,13},{1... | collective-permute-start | bytes 786440 | tf_op jit(solution)/shard_map/ppermute | solution.py:32
  2.0 30.8 %collective-permute-start.2 = (bf16[256,512]{1,0:T(8,128)(2,1)}, bf16[256,512]{1,0:T(8,128)(2,1)S(1)}, u32[]{:S(2)}, u32[]{:S(2)}) collective-permute-start(bf16[256,512]{1,0:T(8,128)(2,1)} %refs_0_.2), channel_id=1, source_target_pairs={{0,3},{1,0},{2,1},{3,2},{4,7},{5,4},{6,5},{7,6},{8,11},{9,8},{10,9... | collective-permute-start | bytes 786440 | tf_op jit(solution)/shard_map/ppermute | solution.py:32
  2.0 30.8 %collective-permute-start.1 = (bf16[256,512]{1,0:T(8,128)(2,1)}, bf16[256,512]{1,0:T(8,128)(2,1)S(1)}, u32[]{:S(2)}, u32[]{:S(2)}) collective-permute-start(bf16[256,512]{1,0:T(8,128)(2,1)} %refs_0_.2), channel_id=1, source_target_pairs={{0,2},{1,3},{2,0},{3,1},{4,6},{5,7},{6,4},{7,5},{8,10},{9,11},{10,... | collective-permute-start | bytes 786440 | tf_op jit(solution)/shard_map/ppermute | solution.py:32
  5.7 30.1 %collective-permute-start = (bf16[256,512]{1,0:T(8,128)(2,1)}, bf16[256,512]{1,0:T(8,128)(2,1)S(1)}, u32[]{:S(2)}, u32[]{:S(2)}) collective-permute-start(bf16[256,512]{1,0:T(8,128)(2,1)} %refs_0_.2), channel_id=1, source_target_pairs={{0,1},{1,2},{2,3},{3,0},{4,5},{5,6},{6,7},{7,4},{8,9},{9,10},{10,1... | collective-permute-start | bytes 786440 | tf_op jit(solution)/shard_map/ppermute | solution.py:32
  5.7 30.2 %collective-permute-start.4 = (bf16[256,512]{1,0:T(8,128)(2,1)}, bf16[256,512]{1,0:T(8,128)(2,1)S(1)}, u32[]{:S(2)}, u32[]{:S(2)}) collective-permute-start(bf16[256,512]{1,0:T(8,128)(2,1)} %refs_0_.2), channel_id=1, source_target_pairs={{0,8},{1,9},{2,10},{3,11},{4,12},{5,13},{6,14},{7,15},{8,0},{9,1},... | collective-permute-start | bytes 786440 | tf_op jit(solution)/shard_map/ppermute | solution.py:32
  10.2 29.4 %all-to-all-start = ((bf16[16,32,512]{2,1,0:T(8,128)(2,1)}), bf16[16,32,512]{2,1,0:T(8,128)(2,1)S(1)}, u32[]{:S(2)}, u32[]{:S(2)}) async-start(bf16[16,32,512]{2,1,0:T(8,128)(2,1)} %pad_maximum_fusion), calls=%async_computation | async-start | bytes 1048576 | tf_op jit(solution)/shard_map/all_to_all | solution.py:363
  20.6 1.2 copy-start.14
  20.6 16.1 %collective-permute-start.5 = (bf16[256,512]{1,0:T(8,128)(2,1)S(1)}, bf16[256,512]{1,0:T(8,128)(2,1)}, u32[]{:S(2)}, u32[]{:S(2)}) collective-permute-start(bf16[256,512]{1,0:T(8,128)(2,1)S(1)} %copy-done.13), channel_id=1, source_target_pairs={{0,12},{1,13},{2,14},{3,15},{4,0},{5,1},{6,2},{7,3},{8,4},{9,5},{1... | collective-permute-start | bytes 786440 | tf_op jit(solution)/shard_map/ppermute | solution.py:32
  32.8 28.1 %copy-start.7 = (bf16[1024,256]{1,0:T(8,128)(2,1)}, bf16[1024,256]{1,0:T(8,128)(2,1)S(1)}, u32[]{:S(2)}) copy-start(bf16[1024,256]{1,0:T(8,128)(2,1)S(1)} %copy.14) | copy-start | bytes 1572868
  35.9 33.5 %copy-start = (bf16[3,256,512]{2,1,0:T(8,128)(2,1)}, bf16[3,256,512]{2,1,0:T(8,128)(2,1)S(1)}, u32[]{:S(2)}) copy-start(bf16[3,256,512]{2,1,0:T(8,128)(2,1)S(1)} %stack.25.refs_1_) | copy-start | bytes 2359300
  35.9 0.7 copy-start.15
  36.7 37.8 %collective-permute-start.8 = (bf16[3,256,512]{2,1,0:T(8,128)(2,1)S(1)}, bf16[3,256,512]{2,1,0:T(8,128)(2,1)S(1)}, u32[]{:S(2)}, u32[]{:S(2)}) collective-permute-start(bf16[3,256,512]{2,1,0:T(8,128)(2,1)S(1)} %stack.25.refs_1_), channel_id=1, source_target_pairs={{0,8},{1,9},{2,10},{3,11},{4,12},{5,13},{6,14},{7,15},{8,0},{9,1},... | collective-permute-start | bytes 2359304 | tf_op jit(solution)/shard_map/ppermute | solution.py:32
  39.6 23.1 %copy-start.9 = (bf16[16,32,512]{2,1,0:T(8,128)(2,1)}, bf16[16,32,512]{2,1,0:T(8,128)(2,1)S(1)}, u32[]{:S(2)}) copy-start(bf16[16,32,512]{2,1,0:T(8,128)(2,1)S(1)} %all-to-all-done.xf_ref) | copy-start | bytes 1572868
  39.6 34.4 %collective-permute-start.9 = (bf16[4,256,256]{2,1,0:T(8,128)(2,1)S(1)}, bf16[4,256,256]{2,1,0:T(8,128)(2,1)S(1)}, u32[]{:S(2)}, u32[]{:S(2)}) collective-permute-start(bf16[4,256,256]{2,1,0:T(8,128)(2,1)S(1)} %bitcast.20), channel_id=1, source_target_pairs={{0,32},{16,48},{32,0},{48,16},{64,96},{80,112},{96,64},{112,80},{1... | collective-permute-start | bytes 1572872 | tf_op jit(solution)/shard_map/ppermute | solution.py:32
  59.4 17.9 %collective-permute-start.7 = (bf16[3,256,512]{2,1,0:T(8,128)(2,1)S(1)}, bf16[3,256,512]{2,1,0:T(8,128)(2,1)}, u32[]{:S(2)}, u32[]{:S(2)}) collective-permute-start(bf16[3,256,512]{2,1,0:T(8,128)(2,1)S(1)} %stack.25.refs_1_), channel_id=1, source_target_pairs={{0,12},{1,13},{2,14},{3,15},{4,0},{5,1},{6,2},{7,3},{8,4},{9,5},{1... | collective-permute-start | bytes 2359304 | tf_op jit(solution)/shard_map/ppermute | solution.py:32
  60.5 18.8 %collective-permute-start.6 = (bf16[3,256,512]{2,1,0:T(8,128)(2,1)S(1)}, bf16[3,256,512]{2,1,0:T(8,128)(2,1)}, u32[]{:S(2)}, u32[]{:S(2)}) collective-permute-start(bf16[3,256,512]{2,1,0:T(8,128)(2,1)S(1)} %stack.25.refs_1_), channel_id=1, source_target_pairs={{0,4},{1,5},{2,6},{3,7},{4,8},{5,9},{6,10},{7,11},{8,12},{9,13},{1... | collective-permute-start | bytes 2359304 | tf_op jit(solution)/shard_map/ppermute | solution.py:32
  60.9 23.1 %collective-permute-start.10 = (bf16[4,256,256]{2,1,0:T(8,128)(2,1)S(1)}, bf16[4,256,256]{2,1,0:T(8,128)(2,1)}, u32[]{:S(2)}, u32[]{:S(2)}) collective-permute-start(bf16[4,256,256]{2,1,0:T(8,128)(2,1)S(1)} %bitcast.21), channel_id=1, source_target_pairs={{0,16},{16,0},{32,48},{48,32},{64,80},{80,64},{96,112},{112,96},{1... | collective-permute-start | bytes 1572872 | tf_op jit(solution)/shard_map/ppermute | solution.py:32
  69.4 14.6 %all-to-all-start.1 = ((bf16[16,16,512]{2,1,0:T(8,128)(2,1)}), bf16[16,16,512]{2,1,0:T(8,128)(2,1)S(1)}, u32[]{:S(2)}, u32[]{:S(2)}) async-start(bf16[16,16,512]{2,1,0:T(8,128)(2,1)} %get-tuple-element.34), calls=%async_computation.1 | async-start | bytes 524288 | tf_op jit(solution)/shard_map/all_to_all | solution.py:363
  74.0 10.0 %copy-start.8 = (bf16[4,256,256]{2,1,0:T(8,128)(2,1)}, bf16[4,256,256]{2,1,0:T(8,128)(2,1)S(1)}, u32[]{:S(2)}) copy-start(bf16[4,256,256]{2,1,0:T(8,128)(2,1)S(1)} %collective-permute-done.9.refs_9_) | copy-start | bytes 1572868
  74.0 9.9 %collective-permute-start.12 = (bf16[2,256,256]{2,1,0:T(8,128)(2,1)S(1)}, bf16[2,256,256]{2,1,0:T(8,128)(2,1)}, u32[]{:S(2)}, u32[]{:S(2)}) collective-permute-start(bf16[2,256,256]{2,1,0:T(8,128)(2,1)S(1)} %get-tuple-element.45), channel_id=1, source_target_pairs={{0,16},{16,0},{32,48},{48,32},{64,80},{80,64},{96,112},{112,96},{1... | collective-permute-start | bytes 786440 | tf_op jit(solution)/shard_map/ppermute | solution.py:32
  74.5 10.2 %copy-start.12 = (bf16[3,256,512]{2,1,0:T(8,128)(2,1)}, bf16[3,256,512]{2,1,0:T(8,128)(2,1)S(1)}, u32[]{:S(2)}) copy-start(bf16[3,256,512]{2,1,0:T(8,128)(2,1)S(1)} %collective-permute-done.8.refs_7_) | copy-start | bytes 2359300
  74.5 9.4 %collective-permute-start.11 = (bf16[2,256,256]{2,1,0:T(8,128)(2,1)S(1)}, bf16[2,256,256]{2,1,0:T(8,128)(2,1)}, u32[]{:S(2)}, u32[]{:S(2)}) collective-permute-start(bf16[2,256,256]{2,1,0:T(8,128)(2,1)S(1)} %get-tuple-element.46), channel_id=1, source_target_pairs={{0,16},{16,0},{32,48},{48,32},{64,80},{80,64},{96,112},{112,96},{1... | collective-permute-start | bytes 786440 | tf_op jit(solution)/shard_map/ppermute | solution.py:32
  83.9 0.7 copy-start.10
  84.7 32.2 %copy-start.6 = (f32[4,1024,128]{2,1,0:T(8,128)S(1)}, f32[4,1024,128]{2,1,0:T(8,128)}, u32[]{:S(2)}) copy-start(f32[4,1024,128]{2,1,0:T(8,128)} %get-tuple-element.36.spec_ref) | copy-start | bytes 6291460
  91.4 25.4 %copy-start.1 = (bf16[768,256]{1,0:T(8,128)(2,1)S(1)}, bf16[768,256]{1,0:T(8,128)(2,1)}, u32[]{:S(2)}) copy-start(bf16[768,256]{1,0:T(8,128)(2,1)} %constant.72.clone.refs_2_.back_ref) | copy-start | bytes 1179652
  91.4 25.4 %copy-start.2 = (bf16[768,256]{1,0:T(8,128)(2,1)S(1)}, bf16[768,256]{1,0:T(8,128)(2,1)}, u32[]{:S(2)}) copy-start(bf16[768,256]{1,0:T(8,128)(2,1)} %constant.71.clone.refs_1_.second_ref) | copy-start | bytes 1179652
  91.5 25.4 %copy-start.3 = (f32[2,64,128]{2,1,0:T(8,128)S(1)}, f32[2,64,128]{2,1,0:T(8,128)}, u32[]{:S(2)}) copy-start(f32[2,64,128]{2,1,0:T(8,128)} %constant.74.clone.refs_4_.turn_ref) | copy-start | bytes 196612
  91.5 25.4 %copy-start.4 = (bf16[64,384]{1,0:T(8,128)(2,1)S(1)}, bf16[64,384]{1,0:T(8,128)(2,1)}, u32[]{:S(2)}) copy-start(bf16[64,384]{1,0:T(8,128)(2,1)} %constant.73.clone.refs_3_.last_ref) | copy-start | bytes 147460
  91.5 25.4 %copy-start.5 = (bf16[128,128]{1,0:T(8,128)(2,1)S(1)}, bf16[128,128]{1,0:T(8,128)(2,1)}, u32[]{:S(2)}) copy-start(bf16[128,128]{1,0:T(8,128)(2,1)} %constant.70.clone.refs_0_.first_ref) | copy-start | bytes 98308
  91.5 15.4 %collective-permute-start.13 = (bf16[8,256,256]{2,1,0:T(8,128)(2,1)}, bf16[8,256,256]{2,1,0:T(8,128)(2,1)}, u32[]{:S(2)}, u32[]{:S(2)}) collective-permute-start(bf16[8,256,256]{2,1,0:T(8,128)(2,1)} %get-tuple-element.39), channel_id=1, source_target_pairs={{0,16},{16,0},{32,48},{48,32},{64,80},{80,64},{96,112},{112,96},{1... | collective-permute-start | bytes 3145736 | tf_op jit(solution)/shard_map/ppermute | solution.py:32
  91.6 25.2 %all-to-all-start.2 = ((bf16[16,16,512]{2,1,0:T(8,128)(2,1)}), bf16[16,16,512]{2,1,0:T(8,128)(2,1)S(1)}, u32[]{:S(2)}, u32[]{:S(2)}) async-start(bf16[16,16,512]{2,1,0:T(8,128)(2,1)} %bitcast.24), calls=%async_computation.2 | async-start | bytes 524288 | tf_op jit(solution)/shard_map/all_to_all | solution.py:363
  109.2 19.2 %collective-permute-start.14 = (bf16[2,256,256]{2,1,0:T(8,128)(2,1)}, bf16[2,256,256]{2,1,0:T(8,128)(2,1)}, u32[]{:S(2)}, u32[]{:S(2)}) collective-permute-start(bf16[2,256,256]{2,1,0:T(8,128)(2,1)} %get-tuple-element.40), channel_id=1, source_target_pairs={{0,64},{16,80},{32,96},{48,112},{64,128},{80,144},{96,160},{112,17... | collective-permute-start | bytes 786440 | tf_op jit(solution)/shard_map/ppermute | solution.py:32
  110.4 18.0 %collective-permute-start.16 = (bf16[2,256,256]{2,1,0:T(8,128)(2,1)}, bf16[2,256,256]{2,1,0:T(8,128)(2,1)}, u32[]{:S(2)}, u32[]{:S(2)}) collective-permute-start(bf16[2,256,256]{2,1,0:T(8,128)(2,1)} %get-tuple-element.41), channel_id=1, source_target_pairs={{0,192},{16,208},{32,224},{48,240},{64,0},{80,16},{96,32},{112,48}... | collective-permute-start | bytes 786440 | tf_op jit(solution)/shard_map/ppermute | solution.py:32
  110.7 17.8 %collective-permute-start.15 = (bf16[2,256,256]{2,1,0:T(8,128)(2,1)S(1)}, bf16[2,256,256]{2,1,0:T(8,128)(2,1)}, u32[]{:S(2)}, u32[]{:S(2)}) collective-permute-start(bf16[2,256,256]{2,1,0:T(8,128)(2,1)S(1)} %get-tuple-element.42), channel_id=1, source_target_pairs={{0,128},{16,144},{32,160},{48,176},{64,192},{80,208},{96,224},{112... | collective-permute-start | bytes 786440 | tf_op jit(solution)/shard_map/ppermute | solution.py:32
  122.6 21.0 %all-to-all-start.3 = ((bf16[16,32,512]{2,1,0:T(8,128)(2,1)}), bf16[16,32,512]{2,1,0:T(8,128)(2,1)S(1)}, u32[]{:S(2)}, u32[]{:S(2)}) async-start(bf16[16,32,512]{2,1,0:T(8,128)(2,1)} %grads.1), calls=%async_computation.3 | async-start | bytes 1048576 | tf_op jit(solution)/shard_map/all_to_all | solution.py:363
  129.9 13.0 %collective-permute-start.17 = (bf16[256,256]{1,0:T(8,128)(2,1)S(1)}, bf16[256,256]{1,0:T(8,128)(2,1)S(1)}, u32[]{:S(2)}, u32[]{:S(2)}) collective-permute-start(bf16[256,256]{1,0:T(8,128)(2,1)S(1)} %slice_bitcast_fusion), channel_id=1, source_target_pairs={{0,32},{16,48},{32,0},{48,16},{64,96},{80,112},{96,64},{112,80},{1... | collective-permute-start | bytes 393224 | tf_op jit(solution)/shard_map/ppermute | solution.py:32

commit v9 on v8

--- a/solution.py
+++ b/solution.py
@@ -383,18 +383,19 @@
 
     lines = [send(out_grad, "tp", 1, 4, dz) for dz in (1, 2, 3)]
     up, far = send(out_grad, "tp", 4, 4, 1), send(out_grad, "tp", 4, 4, 2)
+    w_swap = send(out_weight, "ctx", 2, 2, 1)
     up, own, w_own = lax.optimization_barrier((up, out_grad, out_weight))
     w_line = lax.all_gather(w_own.T, "ctx", axis_index_groups=LINES_X)
     near = [up, far, send(own, "tp", 4, 4, 3)]
     lines, w_line = lax.optimization_barrier((lines, w_line))
-    rest, near = lax.optimization_barrier((stack_call(lines), near))
+    rest, near[0], near[1], w_swap = lax.optimization_barrier((stack_call(lines), near[0], near[1], w_swap))
+    w_swap, _ = lax.optimization_barrier((w_swap, mixed_rows))
     rests = [send(rest, "tp", 4, 4, dy) for dy in (1, 2, 3)]
     grads = [out_grad, rest]
     for dy in (1, 3, 2):
         grads += [near[dy - 1], rests[dy - 1]]
 
-    w_line, _ = lax.optimization_barrier((w_line, arrived))
-    w_far = send(w_line, "ctx", 2, 2, 1)
+    w_far = lax.all_gather(w_swap.T, "ctx", axis_index_groups=LINES_X)
     weights = [w_line, w_far, send(w_line, "ctx", 1, 2, 1)]
     weights += [send(w_far[i : i + 2], "ctx", 1, 2, 1) for i in (0, 2)]
 

time: 145 us -> 151 us (1.041)
  starting transfers between devices: 80.1 us -> 68.1 us
  blocking collectives: 10.9 us -> 22.6 us
  waiting for transfers between devices: 23.8 us -> 29 us
    all_gather x0 -> x1, blocking collectives: none -> 11.8 us  [on_device(): w_far = lax.all_gather(w_swap.T, 'ctx', axis_index_groups=LINES_X)]
    ppermute x18, starting transfers between devices: 44.2 us -> 32.8 us  [send(): return lax.ppermute(value, axis, shift_pairs(stride, size, by))]
    ppermute x18, waiting for transfers between devices: 14.8 us -> 24.6 us  [send(): return lax.ppermute(value, axis, shift_pairs(stride, size, by))]
    all_to_all x4, waiting for transfers between devices: 9.03 us -> 4.4 us  [exchange(): return lax.all_to_all(value, 'ctx', split_axis=0, concat_axis=0, tiled=True)]
  transfers between devices with their start and end apart: 22 -> 22, of which waited for: 6 -> 5; matrix products, arithmetic and copies ran while one was open for 5% -> 6% of each run, Pallas kernels for 9% -> 8%
where the time goes in v9:
time: 151 us
  starting transfers between devices  68.1 us (45%)
  waiting for transfers between devices  29 us (19%)
  blocking collectives  22.6 us (15%)
  Pallas kernels  19.3 us (13%)
  other arithmetic  6.32 us (4%)
  local copies, waits for them, and re-layouts  4.68 us (3%)
    all_to_all x4, starting transfers between devices, exchange(): return lax.all_to_all(value, 'ctx', split_axis=0, concat_axis=0, tiled=True)  35.3 us
    ppermute x18, starting transfers between devices, send(): return lax.ppermute(value, axis, shift_pairs(stride, size, by))  32.8 us
    ppermute x18, waiting for transfers between devices, send(): return lax.ppermute(value, axis, shift_pairs(stride, size, by))  24.6 us
    all_gather x1, blocking collectives, on_device(): w_far = lax.all_gather(w_swap.T, 'ctx', axis_index_groups=LINES_X)  11.8 us
    all_gather x1, blocking collectives, on_device(): w_line = lax.all_gather(w_own.T, 'ctx', axis_index_groups=LINES_X)  10.8 us
    pallas_call x1, Pallas kernels, products_call(): pl.pallas_call(products_kernel, out_shape=(tile, tile, eight, eight), in_...  6.78 us
    pallas_call x1, Pallas kernels, conv_call(): pl.pallas_call(conv_kernel, out_shape=(jax.ShapeDtypeStruct((16, FEW, TOK...  6.67 us
    pallas_call x1, Pallas kernels, grads_call(): pl.pallas_call(grads_kernel, out_shape=jax.ShapeDtypeStruct((16, 2 * FEW,...  5.75 us
  transfers between devices with their start and end apart: 22, of which 5 were waited for; matrix products, arithmetic and copies ran while one was open for 6% of the time, Pallas kernels for 8%

profile of v9, /device:TPU:67, one launch (start us, length us, event | category | flops | bytes accessed | tf_op | source)
XLA Modules:
  0.0 150.8 jit_solution(16959725631789344886)
XLA Ops:
  0.6 1.4 collective-permute-start.3
  2.0 0.0 collective-permute-start.2
  2.0 3.7 %collective-permute-start.1 = (bf16[256,512]{1,0:T(8,128)(2,1)}, bf16[256,512]{1,0:T(8,128)(2,1)S(1)}, u32[]{:S(2)}, u32[]{:S(2)}) collective-permute-start(bf16[256,512]{1,0:T(8,128)(2,1)} %refs_0_.2), channel_id=1, source_target_pairs={{0,2},{1,3},{2,0},{3,1},{4,6},{5,7},{6,4},{7,5},{8,10},{9,11},{10,... | collective-permute-start | bytes 786440 | tf_op jit(solution)/shard_map/ppermute | solution.py:32
  5.7 0.0 collective-permute-start
  5.7 2.6 %collective-permute-start.4 = (bf16[256,512]{1,0:T(8,128)(2,1)}, bf16[256,512]{1,0:T(8,128)(2,1)S(1)}, u32[]{:S(2)}, u32[]{:S(2)}) collective-permute-start(bf16[256,512]{1,0:T(8,128)(2,1)} %refs_0_.2), channel_id=1, source_target_pairs={{0,8},{1,9},{2,10},{3,11},{4,12},{5,13},{6,14},{7,15},{8,0},{9,1},... | collective-permute-start | bytes 786440 | tf_op jit(solution)/shard_map/ppermute | solution.py:32
  8.4 1.9 %pad_maximum_fusion = bf16[16,32,512]{2,1,0:T(8,128)(2,1)} fusion(bf16[16,16,512]{2,1,0:T(8,128)(2,1)} %bitcast.31, bf16[16,16,512]{2,1,0:T(8,128)(2,1)} %bitcast.32), kind=kLoop, calls=%fused_computation | loop fusion | flops 1048576 | bytes 1048576 | tf_op jit(solution)/shard_map/concatenate | solution.py:379
  10.2 10.3 %all-to-all-start = ((bf16[16,32,512]{2,1,0:T(8,128)(2,1)}), bf16[16,32,512]{2,1,0:T(8,128)(2,1)S(1)}, u32[]{:S(2)}, u32[]{:S(2)}) async-start(bf16[16,32,512]{2,1,0:T(8,128)(2,1)} %pad_maximum_fusion), calls=%async_computation | async-start | bytes 1048576 | tf_op jit(solution)/shard_map/all_to_all | solution.py:363
  20.5 0.0 collective-permute-done.3.refs_2_
  20.6 0.0 copy-start.12
  20.6 5.2 %collective-permute-start.5 = (bf16[256,256]{1,0:T(8,128)(2,1)S(1)}, bf16[256,256]{1,0:T(8,128)(2,1)S(1)}, u32[]{:S(2)}, u32[]{:S(2)}) collective-permute-start(bf16[256,256]{1,0:T(8,128)(2,1)S(1)} %copy-done.10), channel_id=1, source_target_pairs={{0,32},{16,48},{32,0},{48,16},{64,96},{80,112},{96,64},{112,80},{1... | collective-permute-start | bytes 393224 | tf_op jit(solution)/shard_map/ppermute | solution.py:32
  25.7 10.8 %all-gather = bf16[1024,256]{0,1:T(8,128)(2,1)S(1)} all-gather(bf16[256,256]{0,1:T(8,128)(2,1)S(1)} %bitcast.35), channel_id=2, replica_groups={{0,64,128,192},{16,80,144,208},{32,96,160,224},{48,112,176,240},{1,65,1..., dimensions={0}, use_global_device_ids=true | all-gather | bytes 655360 | tf_op jit(solution)/shard_map/all_gather | solution.py:388
  36.5 0.2 copy.14
  36.7 0.0 collective-permute-done.2.refs_2_
  36.7 0.0 collective-permute-done.1.refs_1_
  36.8 3.1 %collective-permute-done.refs_0_ = bf16[256,512]{1,0:T(8,128)(2,1)S(1)} collective-permute-done((bf16[256,512]{1,0:T(8,128)(2,1)}, bf16[256,512]{1,0:T(8,128)(2,1)S(1)}, u32[]{:S(2)}, u32[]{:S(2)}) %collective-permute-start) | collective-permute-done | bytes 262176 | tf_op jit(solution)/shard_map/ppermute | solution.py:32
  39.9 0.1 stack.25.refs_1_
  39.9 4.5 %collective-permute-done.5 = bf16[256,256]{1,0:T(8,128)(2,1)S(1)} collective-permute-done((bf16[256,256]{1,0:T(8,128)(2,1)S(1)}, bf16[256,256]{1,0:T(8,128)(2,1)S(1)}, u32[]{:S(2)}, u32[]{:S(2)}) %collective-permute-start.5) | collective-permute-done | bytes 131104 | tf_op jit(solution)/shard_map/ppermute | solution.py:32
  44.4 0.0 collective-permute-done.4.refs_6_
  44.4 2.8 %collective-permute-start.9 = (bf16[3,256,512]{2,1,0:T(8,128)(2,1)S(1)}, bf16[3,256,512]{2,1,0:T(8,128)(2,1)}, u32[]{:S(2)}, u32[]{:S(2)}) collective-permute-start(bf16[3,256,512]{2,1,0:T(8,128)(2,1)S(1)} %stack.25.refs_1_), channel_id=1, source_target_pairs={{0,8},{1,9},{2,10},{3,11},{4,12},{5,13},{6,14},{7,15},{8,0},{9,1},... | collective-permute-start | bytes 2359304 | tf_op jit(solution)/shard_map/ppermute | solution.py:32
  47.2 1.1 collective-permute-start.8
  48.2 0.4 collective-permute-start.6
  48.6 2.3 %collective-permute-start.7 = (bf16[256,512]{1,0:T(8,128)(2,1)}, bf16[256,512]{1,0:T(8,128)(2,1)}, u32[]{:S(2)}, u32[]{:S(2)}) collective-permute-start(bf16[256,512]{1,0:T(8,128)(2,1)} %refs_0_.2), channel_id=1, source_target_pairs={{0,12},{1,13},{2,14},{3,15},{4,0},{5,1},{6,2},{7,3},{8,4},{9,5},{1... | collective-permute-start | bytes 786440 | tf_op jit(solution)/shard_map/ppermute | solution.py:32
  50.9 2.8 %collective-permute-start.10 = (bf16[4,256,256]{2,1,0:T(8,128)(2,1)S(1)}, bf16[4,256,256]{2,1,0:T(8,128)(2,1)S(1)}, u32[]{:S(2)}, u32[]{:S(2)}) collective-permute-start(bf16[4,256,256]{2,1,0:T(8,128)(2,1)S(1)} %bitcast.24), channel_id=1, source_target_pairs={{0,16},{16,0},{32,48},{48,32},{64,80},{80,64},{96,112},{112,96},{1... | collective-permute-start | bytes 1572872 | tf_op jit(solution)/shard_map/ppermute | solution.py:32
  53.8 0.0 all-to-all-done.xf_ref
  53.8 0.8 copy-done.8
  54.6 6.7 %conv.1 = (bf16[16,16,512]{2,1,0:T(8,128)(2,1)}, f32[4,1024,128]{2,1,0:T(8,128)}) custom-call(bf16[16,32,512]{2,1,0:T(8,128)(2,1)} %copy-done.8, bf16[128,128]{1,0:T(8,128)(2,1)} %constant.70.clone.refs_0_.first_ref, bf16[768,256]{1,0:T(8,128)(2,1)} %constant.71.clone.refs_1_.second_ref, bf16[768,256]{1,0:T(8,128)(2,1)} %constant.72.clone.refs_2_.back_ref, ...), custom_call_target="tpu_custom_call" | custom-call | flops 1000000000 | bytes 4194304 | tf_op jit(solution)/shard_map/conv/pallas_call | solution.py:228
  61.3 9.2 %all-to-all-start.1 = ((bf16[16,16,512]{2,1,0:T(8,128)(2,1)}), bf16[16,16,512]{2,1,0:T(8,128)(2,1)S(1)}, u32[]{:S(2)}, u32[]{:S(2)}) async-start(bf16[16,16,512]{2,1,0:T(8,128)(2,1)} %get-tuple-element.33), calls=%async_computation.1 | async-start | bytes 524288 | tf_op jit(solution)/shard_map/all_to_all | solution.py:363
  70.5 11.8 %all-gather.1 = bf16[1024,256]{0,1:T(8,128)(2,1)S(1)} all-gather(bf16[256,256]{0,1:T(8,128)(2,1)S(1)} %bitcast.36), channel_id=3, replica_groups={{0,64,128,192},{16,80,144,208},{32,96,160,224},{48,112,176,240},{1,65,1..., dimensions={0}, use_global_device_ids=true | all-gather | bytes 655360 | tf_op jit(solution)/shard_map/all_gather | solution.py:398
  82.3 0.1 copy.17
  82.5 0.1 copy.16
  82.6 4.1 %collective-permute-done.7.refs_4_ = bf16[256,512]{1,0:T(8,128)(2,1)} collective-permute-done((bf16[256,512]{1,0:T(8,128)(2,1)}, bf16[256,512]{1,0:T(8,128)(2,1)}, u32[]{:S(2)}, u32[]{:S(2)}) %collective-permute-start.7) | collective-permute-done | bytes 262176 | tf_op jit(solution)/shard_map/ppermute | solution.py:32
  86.7 1.6 %collective-permute-start.11 = (bf16[2,256,256]{2,1,0:T(8,128)(2,1)S(1)}, bf16[2,256,256]{2,1,0:T(8,128)(2,1)S(1)}, u32[]{:S(2)}, u32[]{:S(2)}) collective-permute-start(bf16[2,256,256]{2,1,0:T(8,128)(2,1)S(1)} %bitcast.29), channel_id=1, source_target_pairs={{0,16},{16,0},{32,48},{48,32},{64,80},{80,64},{96,112},{112,96},{1... | collective-permute-start | bytes 786440 | tf_op jit(solution)/shard_map/ppermute | solution.py:32
  88.2 0.3 collective-permute-start.12
  88.5 0.6 stack.24.where_ref
  89.1 1.0 copy.15
  90.1 0.0 collective-permute-done.9.refs_7_
  90.1 0.0 collective-permute-done.11.refs_11_
  90.2 0.7 copy-done.14
  90.9 0.1 copy-done.9
  91.0 0.1 copy-done.15
  91.1 6.8 %products.1 = (bf16[256,512]{1,0:T(8,128)(2,1)}, bf16[256,512]{1,0:T(8,128)(2,1)}, bf16[8,256,256]{2,1,0:T(8,128)(2,1)}, bf16[8,256,256]{2,1,0:T(8,128)(2,1)}) custom-call(s32[5]{0:T(128)} %stack.24.where_ref, bf16[256,512]{1,0:T(8,128)(2,1)} %refs_0_.2, bf16[3,256,512]{2,1,0:T(8,128)(2,1)} %copy-done, bf16[256,512]{1,0:T(8,128)(2,1)} %copy-done.12, ...), custom_call_target="tpu_custom_call" | custom-call | flops 2147483648 | bytes 9437184 | tf_op jit(solution)/shard_map/products/pallas_call | solution.py:350
  97.9 0.0 copy-start.1
  97.9 0.0 copy-start.2
  97.9 0.0 copy-start.3
  97.9 0.0 copy-start.4
  97.9 0.0 copy-start.5
  97.9 0.3 collective-permute-start.13
  98.2 10.0 %all-to-all-start.2 = ((bf16[16,16,512]{2,1,0:T(8,128)(2,1)}), bf16[16,16,512]{2,1,0:T(8,128)(2,1)S(1)}, u32[]{:S(2)}, u32[]{:S(2)}) async-start(bf16[16,16,512]{2,1,0:T(8,128)(2,1)} %bitcast.30), calls=%async_computation.2 | async-start | bytes 524288 | tf_op jit(solution)/shard_map/all_to_all | solution.py:363
  108.2 0.0 collective-permute-done.13
  108.2 2.3 %add_convert_fusion.3 = (bf16[2,256,256]{2,1,0:T(8,128)(2,1)}, bf16[2,256,256]{2,1,0:T(8,128)(2,1)}, bf16[2,256,256]{2,1,0:T(8,128)(2,1)S(1)}) fusion(bf16[8,256,256]{2,1,0:T(8,128)(2,1)} %collective-permute-done.13, bf16[8,256,256]{2,1,0:T(8,128)(2,1)} %get-tuple-element.38), kind=kLoop, calls=%fused_computation.4 | loop fusion | flops 1572864 | bytes 2359296 | tf_op jit(solution)/shard_map/convert_element_type | solution.py:370
  110.6 1.2 collective-permute-start.14
  111.7 0.3 collective-permute-start.16
  112.0 1.8 %collective-permute-start.15 = (bf16[2,256,256]{2,1,0:T(8,128)(2,1)S(1)}, bf16[2,256,256]{2,1,0:T(8,128)(2,1)}, u32[]{:S(2)}, u32[]{:S(2)}) collective-permute-start(bf16[2,256,256]{2,1,0:T(8,128)(2,1)S(1)} %get-tuple-element.42), channel_id=1, source_target_pairs={{0,128},{16,144},{32,160},{48,176},{64,192},{80,208},{96,224},{112... | collective-permute-start | bytes 786440 | tf_op jit(solution)/shard_map/ppermute | solution.py:32
  113.8 4.4 %all-to-all-done.2.p_ref = bf16[16,16,512]{2,1,0:T(8,128)(2,1)S(1)} async-done(((bf16[16,16,512]{2,1,0:T(8,128)(2,1)}), bf16[16,16,512]{2,1,0:T(8,128)(2,1)S(1)}, u32[]{:S(2)}, u32[]{:S(2)}) %all-to-all-start.2) | async-done | bytes 262176 | tf_op jit(solution)/shard_map/all_to_all | solution.py:363
  118.3 5.7 %grads.1 = bf16[16,32,512]{2,1,0:T(8,128)(2,1)} custom-call(bf16[16,16,512]{2,1,0:T(8,128)(2,1)S(1)} %all-to-all-done.2.p_ref, bf16[128,128]{1,0:T(8,128)(2,1)S(1)} %copy-done.5, bf16[768,256]{1,0:T(8,128)(2,1)S(1)} %copy-done.2, bf16[768,256]{1,0:T(8,128)(2,1)S(1)} %copy-done.1, bf16[64,384]{1,0:T(8,128)(2,1)S(1)} %copy-done.4, ...), custom_call_target="tpu_custom_call" | custom-call | flops 10000000000 | bytes 4194304 | tf_op jit(solution)/shard_map/grads/pallas_call | solution.py:244
  124.0 5.8 %all-to-all-start.3 = ((bf16[16,32,512]{2,1,0:T(8,128)(2,1)}), bf16[16,32,512]{2,1,0:T(8,128)(2,1)S(1)}, u32[]{:S(2)}, u32[]{:S(2)}) async-start(bf16[16,32,512]{2,1,0:T(8,128)(2,1)} %grads.1), calls=%async_computation.3 | async-start | bytes 1048576 | tf_op jit(solution)/shard_map/all_to_all | solution.py:363
  129.8 0.0 collective-permute-done.14
  129.8 0.0 collective-permute-done.15
  129.8 1.4 add_convert_fusion
  131.3 5.2 %collective-permute-start.17 = (bf16[256,256]{1,0:T(8,128)(2,1)S(1)}, bf16[256,256]{1,0:T(8,128)(2,1)S(1)}, u32[]{:S(2)}, u32[]{:S(2)}) collective-permute-start(bf16[256,256]{1,0:T(8,128)(2,1)S(1)} %slice_bitcast_fusion), channel_id=1, source_target_pairs={{0,32},{16,48},{32,0},{48,16},{64,96},{80,112},{96,64},{112,80},{1... | collective-permute-start | bytes 393224 | tf_op jit(solution)/shard_map/ppermute | solution.py:32
  136.4 12.9 %collective-permute-done.17 = bf16[256,256]{1,0:T(8,128)(2,1)S(1)} collective-permute-done((bf16[256,256]{1,0:T(8,128)(2,1)S(1)}, bf16[256,256]{1,0:T(8,128)(2,1)S(1)}, u32[]{:S(2)}, u32[]{:S(2)}) %collective-permute-start.17) | collective-permute-done | bytes 131104 | tf_op jit(solution)/shard_map/ppermute | solution.py:32
  149.3 0.7 fusion
  150.0 0.0 all-to-all-done.3
  150.0 0.8 fusion.1
  (30 shorter events, 0.1 us)
Async XLA Ops:
  0.6 19.9 %copy-start.10 = (bf16[256,256]{1,0:T(8,128)(2,1)S(1)}, bf16[256,256]{1,0:T(8,128)(2,1)}, u32[]{:S(2)}) copy-start(bf16[256,256]{1,0:T(8,128)(2,1)} %param.14) | copy-start | bytes 393220
  0.6 19.9 %collective-permute-start.3 = (bf16[256,512]{1,0:T(8,128)(2,1)}, bf16[256,512]{1,0:T(8,128)(2,1)S(1)}, u32[]{:S(2)}, u32[]{:S(2)}) collective-permute-start(bf16[256,512]{1,0:T(8,128)(2,1)} %refs_0_.2), channel_id=1, source_target_pairs={{0,4},{1,5},{2,6},{3,7},{4,8},{5,9},{6,10},{7,11},{8,12},{9,13},{1... | collective-permute-start | bytes 786440 | tf_op jit(solution)/shard_map/ppermute | solution.py:32
  2.0 34.7 %collective-permute-start.2 = (bf16[256,512]{1,0:T(8,128)(2,1)}, bf16[256,512]{1,0:T(8,128)(2,1)S(1)}, u32[]{:S(2)}, u32[]{:S(2)}) collective-permute-start(bf16[256,512]{1,0:T(8,128)(2,1)} %refs_0_.2), channel_id=1, source_target_pairs={{0,3},{1,0},{2,1},{3,2},{4,7},{5,4},{6,5},{7,6},{8,11},{9,8},{10,9... | collective-permute-start | bytes 786440 | tf_op jit(solution)/shard_map/ppermute | solution.py:32
  2.0 34.7 %collective-permute-start.1 = (bf16[256,512]{1,0:T(8,128)(2,1)}, bf16[256,512]{1,0:T(8,128)(2,1)S(1)}, u32[]{:S(2)}, u32[]{:S(2)}) collective-permute-start(bf16[256,512]{1,0:T(8,128)(2,1)} %refs_0_.2), channel_id=1, source_target_pairs={{0,2},{1,3},{2,0},{3,1},{4,6},{5,7},{6,4},{7,5},{8,10},{9,11},{10,... | collective-permute-start | bytes 786440 | tf_op jit(solution)/shard_map/ppermute | solution.py:32
  5.7 34.1 %collective-permute-start = (bf16[256,512]{1,0:T(8,128)(2,1)}, bf16[256,512]{1,0:T(8,128)(2,1)S(1)}, u32[]{:S(2)}, u32[]{:S(2)}) collective-permute-start(bf16[256,512]{1,0:T(8,128)(2,1)} %refs_0_.2), channel_id=1, source_target_pairs={{0,1},{1,2},{2,3},{3,0},{4,5},{5,6},{6,7},{7,4},{8,9},{9,10},{10,1... | collective-permute-start | bytes 786440 | tf_op jit(solution)/shard_map/ppermute | solution.py:32
  5.7 38.7 %collective-permute-start.4 = (bf16[256,512]{1,0:T(8,128)(2,1)}, bf16[256,512]{1,0:T(8,128)(2,1)S(1)}, u32[]{:S(2)}, u32[]{:S(2)}) collective-permute-start(bf16[256,512]{1,0:T(8,128)(2,1)} %refs_0_.2), channel_id=1, source_target_pairs={{0,8},{1,9},{2,10},{3,11},{4,12},{5,13},{6,14},{7,15},{8,0},{9,1},... | collective-permute-start | bytes 786440 | tf_op jit(solution)/shard_map/ppermute | solution.py:32
  10.2 43.5 %all-to-all-start = ((bf16[16,32,512]{2,1,0:T(8,128)(2,1)}), bf16[16,32,512]{2,1,0:T(8,128)(2,1)S(1)}, u32[]{:S(2)}, u32[]{:S(2)}) async-start(bf16[16,32,512]{2,1,0:T(8,128)(2,1)} %pad_maximum_fusion), calls=%async_computation | async-start | bytes 1048576 | tf_op jit(solution)/shard_map/all_to_all | solution.py:363
  20.6 5.2 %copy-start.12 = (bf16[256,512]{1,0:T(8,128)(2,1)}, bf16[256,512]{1,0:T(8,128)(2,1)S(1)}, u32[]{:S(2)}) copy-start(bf16[256,512]{1,0:T(8,128)(2,1)S(1)} %collective-permute-done.3.refs_2_) | copy-start | bytes 786436
  20.6 23.8 %collective-permute-start.5 = (bf16[256,256]{1,0:T(8,128)(2,1)S(1)}, bf16[256,256]{1,0:T(8,128)(2,1)S(1)}, u32[]{:S(2)}, u32[]{:S(2)}) collective-permute-start(bf16[256,256]{1,0:T(8,128)(2,1)S(1)} %copy-done.10), channel_id=1, source_target_pairs={{0,32},{16,48},{32,0},{48,16},{64,96},{80,112},{96,64},{112,80},{1... | collective-permute-start | bytes 393224 | tf_op jit(solution)/shard_map/ppermute | solution.py:32
  36.7 14.2 %copy-start.7 = (bf16[1024,256]{1,0:T(8,128)(2,1)}, bf16[1024,256]{1,0:T(8,128)(2,1)S(1)}, u32[]{:S(2)}) copy-start(bf16[1024,256]{1,0:T(8,128)(2,1)S(1)} %copy.14) | copy-start | bytes 1572868
  39.9 21.3 %copy-start = (bf16[3,256,512]{2,1,0:T(8,128)(2,1)}, bf16[3,256,512]{2,1,0:T(8,128)(2,1)S(1)}, u32[]{:S(2)}) copy-start(bf16[3,256,512]{2,1,0:T(8,128)(2,1)S(1)} %stack.25.refs_1_) | copy-start | bytes 2359300
  44.4 4.2 %copy-start.13 = (bf16[256,512]{1,0:T(8,128)(2,1)}, bf16[256,512]{1,0:T(8,128)(2,1)S(1)}, u32[]{:S(2)}) copy-start(bf16[256,512]{1,0:T(8,128)(2,1)S(1)} %collective-permute-done.4.refs_6_) | copy-start | bytes 786436
  44.4 45.7 %collective-permute-start.9 = (bf16[3,256,512]{2,1,0:T(8,128)(2,1)S(1)}, bf16[3,256,512]{2,1,0:T(8,128)(2,1)}, u32[]{:S(2)}, u32[]{:S(2)}) collective-permute-start(bf16[3,256,512]{2,1,0:T(8,128)(2,1)S(1)} %stack.25.refs_1_), channel_id=1, source_target_pairs={{0,8},{1,9},{2,10},{3,11},{4,12},{5,13},{6,14},{7,15},{8,0},{9,1},... | collective-permute-start | bytes 2359304 | tf_op jit(solution)/shard_map/ppermute | solution.py:32
  47.2 43.0 %collective-permute-start.8 = (bf16[3,256,512]{2,1,0:T(8,128)(2,1)S(1)}, bf16[3,256,512]{2,1,0:T(8,128)(2,1)}, u32[]{:S(2)}, u32[]{:S(2)}) collective-permute-start(bf16[3,256,512]{2,1,0:T(8,128)(2,1)S(1)} %stack.25.refs_1_), channel_id=1, source_target_pairs={{0,12},{1,13},{2,14},{3,15},{4,0},{5,1},{6,2},{7,3},{8,4},{9,5},{1... | collective-permute-start | bytes 2359304 | tf_op jit(solution)/shard_map/ppermute | solution.py:32
  48.2 41.9 %collective-permute-start.6 = (bf16[3,256,512]{2,1,0:T(8,128)(2,1)S(1)}, bf16[3,256,512]{2,1,0:T(8,128)(2,1)}, u32[]{:S(2)}, u32[]{:S(2)}) collective-permute-start(bf16[3,256,512]{2,1,0:T(8,128)(2,1)S(1)} %stack.25.refs_1_), channel_id=1, source_target_pairs={{0,4},{1,5},{2,6},{3,7},{4,8},{5,9},{6,10},{7,11},{8,12},{9,13},{1... | collective-permute-start | bytes 2359304 | tf_op jit(solution)/shard_map/ppermute | solution.py:32
  48.6 38.0 %collective-permute-start.7 = (bf16[256,512]{1,0:T(8,128)(2,1)}, bf16[256,512]{1,0:T(8,128)(2,1)}, u32[]{:S(2)}, u32[]{:S(2)}) collective-permute-start(bf16[256,512]{1,0:T(8,128)(2,1)} %refs_0_.2), channel_id=1, source_target_pairs={{0,12},{1,13},{2,14},{3,15},{4,0},{5,1},{6,2},{7,3},{8,4},{9,5},{1... | collective-permute-start | bytes 786440 | tf_op jit(solution)/shard_map/ppermute | solution.py:32
  50.9 37.3 %collective-permute-start.10 = (bf16[4,256,256]{2,1,0:T(8,128)(2,1)S(1)}, bf16[4,256,256]{2,1,0:T(8,128)(2,1)S(1)}, u32[]{:S(2)}, u32[]{:S(2)}) collective-permute-start(bf16[4,256,256]{2,1,0:T(8,128)(2,1)S(1)} %bitcast.24), channel_id=1, source_target_pairs={{0,16},{16,0},{32,48},{48,32},{64,80},{80,64},{96,112},{112,96},{1... | collective-permute-start | bytes 1572872 | tf_op jit(solution)/shard_map/ppermute | solution.py:32
  53.8 0.8 copy-start.8
  61.3 28.9 %all-to-all-start.1 = ((bf16[16,16,512]{2,1,0:T(8,128)(2,1)}), bf16[16,16,512]{2,1,0:T(8,128)(2,1)S(1)}, u32[]{:S(2)}, u32[]{:S(2)}) async-start(bf16[16,16,512]{2,1,0:T(8,128)(2,1)} %get-tuple-element.33), calls=%async_computation.1 | async-start | bytes 524288 | tf_op jit(solution)/shard_map/all_to_all | solution.py:363
  86.7 3.5 %collective-permute-start.11 = (bf16[2,256,256]{2,1,0:T(8,128)(2,1)S(1)}, bf16[2,256,256]{2,1,0:T(8,128)(2,1)S(1)}, u32[]{:S(2)}, u32[]{:S(2)}) collective-permute-start(bf16[2,256,256]{2,1,0:T(8,128)(2,1)S(1)} %bitcast.29), channel_id=1, source_target_pairs={{0,16},{16,0},{32,48},{48,32},{64,80},{80,64},{96,112},{112,96},{1... | collective-permute-start | bytes 786440 | tf_op jit(solution)/shard_map/ppermute | solution.py:32
  88.2 2.0 %copy-start.11 = (bf16[4,256,256]{2,1,0:T(8,128)(2,1)}, bf16[4,256,256]{2,1,0:T(8,128)(2,1)S(1)}, u32[]{:S(2)}) copy-start(bf16[4,256,256]{2,1,0:T(8,128)(2,1)S(1)} %collective-permute-done.10.refs_10_) | copy-start | bytes 1572868
  88.2 1.9 %collective-permute-start.12 = (bf16[2,256,256]{2,1,0:T(8,128)(2,1)S(1)}, bf16[2,256,256]{2,1,0:T(8,128)(2,1)S(1)}, u32[]{:S(2)}, u32[]{:S(2)}) collective-permute-start(bf16[2,256,256]{2,1,0:T(8,128)(2,1)S(1)} %bitcast.28), channel_id=1, source_target_pairs={{0,16},{16,0},{32,48},{48,32},{64,80},{80,64},{96,112},{112,96},{1... | collective-permute-start | bytes 786440 | tf_op jit(solution)/shard_map/ppermute | solution.py:32
  90.2 0.7 copy-start.14
  90.2 0.9 copy-start.15
  90.2 0.8 copy-start.9
  91.1 27.2 %copy-start.6 = (f32[4,1024,128]{2,1,0:T(8,128)S(1)}, f32[4,1024,128]{2,1,0:T(8,128)}, u32[]{:S(2)}) copy-start(f32[4,1024,128]{2,1,0:T(8,128)} %get-tuple-element.36.spec_ref) | copy-start | bytes 6291460
  97.9 20.4 %copy-start.1 = (bf16[768,256]{1,0:T(8,128)(2,1)S(1)}, bf16[768,256]{1,0:T(8,128)(2,1)}, u32[]{:S(2)}) copy-start(bf16[768,256]{1,0:T(8,128)(2,1)} %constant.72.clone.refs_2_.back_ref) | copy-start | bytes 1179652
  97.9 20.4 %copy-start.2 = (bf16[768,256]{1,0:T(8,128)(2,1)S(1)}, bf16[768,256]{1,0:T(8,128)(2,1)}, u32[]{:S(2)}) copy-start(bf16[768,256]{1,0:T(8,128)(2,1)} %constant.71.clone.refs_1_.second_ref) | copy-start | bytes 1179652
  97.9 20.3 %copy-start.3 = (f32[2,64,128]{2,1,0:T(8,128)S(1)}, f32[2,64,128]{2,1,0:T(8,128)}, u32[]{:S(2)}) copy-start(f32[2,64,128]{2,1,0:T(8,128)} %constant.74.clone.refs_4_.turn_ref) | copy-start | bytes 196612
  97.9 20.3 %copy-start.4 = (bf16[64,384]{1,0:T(8,128)(2,1)S(1)}, bf16[64,384]{1,0:T(8,128)(2,1)}, u32[]{:S(2)}) copy-start(bf16[64,384]{1,0:T(8,128)(2,1)} %constant.73.clone.refs_3_.last_ref) | copy-start | bytes 147460
  97.9 20.3 %copy-start.5 = (bf16[128,128]{1,0:T(8,128)(2,1)S(1)}, bf16[128,128]{1,0:T(8,128)(2,1)}, u32[]{:S(2)}) copy-start(bf16[128,128]{1,0:T(8,128)(2,1)} %constant.70.clone.refs_0_.first_ref) | copy-start | bytes 98308
  97.9 10.3 %collective-permute-start.13 = (bf16[8,256,256]{2,1,0:T(8,128)(2,1)}, bf16[8,256,256]{2,1,0:T(8,128)(2,1)}, u32[]{:S(2)}, u32[]{:S(2)}) collective-permute-start(bf16[8,256,256]{2,1,0:T(8,128)(2,1)} %get-tuple-element.39), channel_id=1, source_target_pairs={{0,16},{16,0},{32,48},{48,32},{64,80},{80,64},{96,112},{112,96},{1... | collective-permute-start | bytes 3145736 | tf_op jit(solution)/shard_map/ppermute | solution.py:32
  98.2 20.0 %all-to-all-start.2 = ((bf16[16,16,512]{2,1,0:T(8,128)(2,1)}), bf16[16,16,512]{2,1,0:T(8,128)(2,1)S(1)}, u32[]{:S(2)}, u32[]{:S(2)}) async-start(bf16[16,16,512]{2,1,0:T(8,128)(2,1)} %bitcast.30), calls=%async_computation.2 | async-start | bytes 524288 | tf_op jit(solution)/shard_map/all_to_all | solution.py:363
  110.6 19.2 %collective-permute-start.14 = (bf16[2,256,256]{2,1,0:T(8,128)(2,1)}, bf16[2,256,256]{2,1,0:T(8,128)(2,1)}, u32[]{:S(2)}, u32[]{:S(2)}) collective-permute-start(bf16[2,256,256]{2,1,0:T(8,128)(2,1)} %get-tuple-element.40), channel_id=1, source_target_pairs={{0,64},{16,80},{32,96},{48,112},{64,128},{80,144},{96,160},{112,17... | collective-permute-start | bytes 786440 | tf_op jit(solution)/shard_map/ppermute | solution.py:32
  111.7 18.0 %collective-permute-start.16 = (bf16[2,256,256]{2,1,0:T(8,128)(2,1)}, bf16[2,256,256]{2,1,0:T(8,128)(2,1)}, u32[]{:S(2)}, u32[]{:S(2)}) collective-permute-start(bf16[2,256,256]{2,1,0:T(8,128)(2,1)} %get-tuple-element.41), channel_id=1, source_target_pairs={{0,192},{16,208},{32,224},{48,240},{64,0},{80,16},{96,32},{112,48}... | collective-permute-start | bytes 786440 | tf_op jit(solution)/shard_map/ppermute | solution.py:32
  112.0 17.8 %collective-permute-start.15 = (bf16[2,256,256]{2,1,0:T(8,128)(2,1)S(1)}, bf16[2,256,256]{2,1,0:T(8,128)(2,1)}, u32[]{:S(2)}, u32[]{:S(2)}) collective-permute-start(bf16[2,256,256]{2,1,0:T(8,128)(2,1)S(1)} %get-tuple-element.42), channel_id=1, source_target_pairs={{0,128},{16,144},{32,160},{48,176},{64,192},{80,208},{96,224},{112... | collective-permute-start | bytes 786440 | tf_op jit(solution)/shard_map/ppermute | solution.py:32
  124.0 26.0 %all-to-all-start.3 = ((bf16[16,32,512]{2,1,0:T(8,128)(2,1)}), bf16[16,32,512]{2,1,0:T(8,128)(2,1)S(1)}, u32[]{:S(2)}, u32[]{:S(2)}) async-start(bf16[16,32,512]{2,1,0:T(8,128)(2,1)} %grads.1), calls=%async_computation.3 | async-start | bytes 1048576 | tf_op jit(solution)/shard_map/all_to_all | solution.py:363
  131.3 18.1 %collective-permute-start.17 = (bf16[256,256]{1,0:T(8,128)(2,1)S(1)}, bf16[256,256]{1,0:T(8,128)(2,1)S(1)}, u32[]{:S(2)}, u32[]{:S(2)}) collective-permute-start(bf16[256,256]{1,0:T(8,128)(2,1)S(1)} %slice_bitcast_fusion), channel_id=1, source_target_pairs={{0,32},{16,48},{32,0},{48,16},{64,96},{80,112},{96,64},{112,80},{1... | collective-permute-start | bytes 393224 | tf_op jit(solution)/shard_map/ppermute | solution.py:32

commit v10 on v8

--- a/solution.py
+++ b/solution.py
@@ -15,7 +15,7 @@
 SEQ = 8192
 ROWS = 64
 LANES = 128
-GROUP = 4
+GROUP = 8
 BF = jnp.bfloat16
 F32 = jnp.float32
 
@@ -280,14 +280,14 @@
 
 
 def products_kernel(where_ref, *refs):
-    grads, ins_hbm = [refs[i] for i in (0, 1, 2, 3, 6, 7, 4, 5)], refs[8:15]
-    product_hbm, gate_grad_hbm, other_hbm, same_hbm = refs[15:19]
-    held, weights, gates_ref, mixed_ref, product_ref, gate_grad_ref, sums, grad_sems, sems, out_sems = refs[19:]
-    targets = [weights.at[pl.ds(4 * i, 4)] for i in range(3)] + [weights.at[pl.ds(12 + i, 2)] for i in (0, 2)]
+    grads, ins_hbm = [refs[i] for i in (0, 1, 2, 3, 6, 7, 4, 5)], refs[8:17]
+    product_hbm, gate_grad_hbm, other_hbm, same_hbm = refs[17:21]
+    held, weights, gates_ref, mixed_ref, product_ref, gate_grad_ref, sums, grad_sems, sems, out_sems = refs[21:]
+    targets = [weights.at[pl.ds(4 * i, 4)] for i in range(3)] + [weights.at[pl.ds(12 + i, 1)] for i in range(4)]
     targets += [gates_ref, mixed_ref]
     ins = fetch(ins_hbm, targets, sems)
     copies = fetch_grads(grads, held, grad_sems)
-    for copy in ins[:5]:
+    for copy in ins[:7]:
         copy.wait()
     total = None
     for dy in range(4):
@@ -297,12 +297,12 @@
         part = dot(weight, held[4 * dy : 4 * dy + 4].reshape(4 * CH, TOK))
         total = part if total is None else total + part
     slope = total.astype(BF).astype(F32)
-    ins[5].wait()
+    ins[7].wait()
     gates = gates_ref[...].astype(F32)
     product_ref[...] = (slope * gates).astype(BF)
     outs = [pltpu.make_async_copy(product_ref, product_hbm, out_sems.at[0])]
     outs[0].start()
-    ins[6].wait()
+    ins[8].wait()
     mixed = mixed_ref[...].astype(F32)
     gate_grad_ref[...] = (slope * mixed).astype(BF)
     outs.append(pltpu.make_async_copy(gate_grad_ref, gate_grad_hbm, out_sems.at[1]))
@@ -350,9 +350,9 @@
     return pl.pallas_call(
         products_kernel,
         out_shape=(tile, tile, eight, eight),
-        in_specs=[pl.BlockSpec(memory_space=pltpu.SMEM)] + [in_hbm()] * 15,
+        in_specs=[pl.BlockSpec(memory_space=pltpu.SMEM)] + [in_hbm()] * 17,
         out_specs=(in_hbm(),) * 4,
-        scratch_shapes=[HELD, SQUARES, TILE, TILE, TILE, TILE, SQUARES, DMA((8,)), DMA((7,)), DMA((10,))],
+        scratch_shapes=[HELD, SQUARES, TILE, TILE, TILE, TILE, SQUARES, DMA((8,)), DMA((9,)), DMA((10,))],
         compiler_params=params(60),
         cost_estimate=pl.CostEstimate(flops=4 * CH * TOK * 4096, bytes_accessed=9 << 20, transcendentals=0),
         name="products",
@@ -396,7 +396,7 @@
     w_line, _ = lax.optimization_barrier((w_line, arrived))
     w_far = send(w_line, "ctx", 2, 2, 1)
     weights = [w_line, w_far, send(w_line, "ctx", 1, 2, 1)]
-    weights += [send(w_far[i : i + 2], "ctx", 1, 2, 1) for i in (0, 2)]
+    weights += [send(w_far[i : i + 1], "ctx", 1, 2, 1) for i in range(4)]
 
     product, gate_grad, part_other, part_same = products_call(where, grads, weights, gates, mixed)
     product_rows = exchange(product.reshape(16, FEW, TOK))

time: 145 us -> 141 us (0.972); the launches traced: 144 us -> 139 us
  Pallas kernels: 19.2 us -> 17 us
  waiting for transfers between devices: 23.8 us -> 21.9 us
  starting transfers between devices: 80.1 us -> 78.5 us
    all_to_all x4, starting transfers between devices: 36 us -> 32.3 us  [exchange(): return lax.all_to_all(value, 'ctx', split_axis=0, concat_axis=0, tiled=True)]
    ppermute x18 -> x20, waiting for transfers between devices: 14.8 us -> 12.6 us  [send(): return lax.ppermute(value, axis, shift_pairs(stride, size, by))]
    ppermute x18 -> x20, starting transfers between devices: 44.2 us -> 46.2 us  [send(): return lax.ppermute(value, axis, shift_pairs(stride, size, by))]
  transfers between devices with their start and end apart: 22 -> 24, of which waited for: 6 -> 5; matrix products, arithmetic and copies ran while one was open for 5% -> 5% of each run, Pallas kernels for 9% -> 7%
where the time goes in v10:
time: 141 us; the launch traced here: 139 us
  starting transfers between devices  78.5 us (56%)
  waiting for transfers between devices  21.9 us (16%)
  Pallas kernels  17 us (12%)
  blocking collectives  10.9 us (8%)
  other arithmetic  6.31 us (4%)
  local copies, waits for them, and re-layouts  3.1 us (2%)
    ppermute x20, starting transfers between devices, send(): return lax.ppermute(value, axis, shift_pairs(stride, size, by))  46.2 us
    all_to_all x4, starting transfers between devices, exchange(): return lax.all_to_all(value, 'ctx', split_axis=0, concat_axis=0, tiled=True)  32.3 us
    ppermute x20, waiting for transfers between devices, send(): return lax.ppermute(value, axis, shift_pairs(stride, size, by))  12.6 us
    all_gather x1, blocking collectives, on_device(): w_line = lax.all_gather(w_own.T, 'ctx', axis_index_groups=LINES_X)  10.9 us
    all_to_all x4, waiting for transfers between devices, exchange(): return lax.all_to_all(value, 'ctx', split_axis=0, concat_axis=0, tiled=True)  9.3 us
    pallas_call x1, Pallas kernels, products_call(): pl.pallas_call(products_kernel, out_shape=(tile, tile, eight, eight), in_...  6.67 us
    pallas_call x1, Pallas kernels, conv_call(): pl.pallas_call(conv_kernel, out_shape=(jax.ShapeDtypeStruct((16, FEW, TOK...  5.72 us
    pallas_call x1, Pallas kernels, grads_call(): pl.pallas_call(grads_kernel, out_shape=jax.ShapeDtypeStruct((16, 2 * FEW,...  4.53 us
  transfers between devices with their start and end apart: 24, of which 5 were waited for; matrix products, arithmetic and copies ran while one was open for 5% of the time, Pallas kernels for 7%

profile of v10, /device:TPU:67, one launch (start us, length us, event | category | flops | bytes accessed | tf_op | source)
XLA Modules:
  0.0 138.7 jit_solution(1652536238737760051)
XLA Ops:
  0.6 0.0 copy-start.12
  0.7 1.4 collective-permute-start.3
  2.0 0.0 collective-permute-start.2
  2.0 3.7 %collective-permute-start.1 = (bf16[256,512]{1,0:T(8,128)(2,1)}, bf16[256,512]{1,0:T(8,128)(2,1)S(1)}, u32[]{:S(2)}, u32[]{:S(2)}) collective-permute-start(bf16[256,512]{1,0:T(8,128)(2,1)} %refs_0_.2), channel_id=1, source_target_pairs={{0,2},{1,3},{2,0},{3,1},{4,6},{5,7},{6,4},{7,5},{8,10},{9,11},{10,... | collective-permute-start | bytes 786440 | tf_op jit(solution)/shard_map/ppermute | solution.py:32
  5.7 0.0 collective-permute-start
  5.7 2.6 %collective-permute-start.4 = (bf16[256,512]{1,0:T(8,128)(2,1)}, bf16[256,512]{1,0:T(8,128)(2,1)S(1)}, u32[]{:S(2)}, u32[]{:S(2)}) collective-permute-start(bf16[256,512]{1,0:T(8,128)(2,1)} %refs_0_.2), channel_id=1, source_target_pairs={{0,8},{1,9},{2,10},{3,11},{4,12},{5,13},{6,14},{7,15},{8,0},{9,1},... | collective-permute-start | bytes 786440 | tf_op jit(solution)/shard_map/ppermute | solution.py:32
  8.4 1.9 %pad_maximum_fusion = bf16[16,32,512]{2,1,0:T(8,128)(2,1)} fusion(bf16[16,16,512]{2,1,0:T(8,128)(2,1)} %bitcast.25, bf16[16,16,512]{2,1,0:T(8,128)(2,1)} %bitcast.26), kind=kLoop, calls=%fused_computation | loop fusion | flops 1048576 | bytes 1048576 | tf_op jit(solution)/shard_map/concatenate | solution.py:379
  10.2 10.3 %all-to-all-start = ((bf16[16,32,512]{2,1,0:T(8,128)(2,1)}), bf16[16,32,512]{2,1,0:T(8,128)(2,1)S(1)}, u32[]{:S(2)}, u32[]{:S(2)}) async-start(bf16[16,32,512]{2,1,0:T(8,128)(2,1)} %pad_maximum_fusion), calls=%async_computation | async-start | bytes 1048576 | tf_op jit(solution)/shard_map/all_to_all | solution.py:363
  20.5 0.0 collective-permute-done.3.refs_2_
  20.6 0.0 copy-start.13
  20.6 1.1 collective-permute-start.5
  21.7 10.9 %all-gather = bf16[1024,256]{0,1:T(8,128)(2,1)S(1)} all-gather(bf16[256,256]{0,1:T(8,128)(2,1)S(1)} %bitcast.29), channel_id=2, replica_groups={{0,64,128,192},{16,80,144,208},{32,96,160,224},{48,112,176,240},{1,65,1..., dimensions={0}, use_global_device_ids=true | all-gather | bytes 655360 | tf_op jit(solution)/shard_map/all_gather | solution.py:387
  32.6 0.2 copy.14
  32.8 0.0 collective-permute-done.2.refs_2_
  32.8 0.0 collective-permute-done.1.refs_1_
  32.9 3.0 %collective-permute-done.refs_0_ = bf16[256,512]{1,0:T(8,128)(2,1)S(1)} collective-permute-done((bf16[256,512]{1,0:T(8,128)(2,1)}, bf16[256,512]{1,0:T(8,128)(2,1)S(1)}, u32[]{:S(2)}, u32[]{:S(2)}) %collective-permute-start) | collective-permute-done | bytes 262176 | tf_op jit(solution)/shard_map/ppermute | solution.py:32
  35.8 0.1 stack.25.refs_1_
  35.9 0.0 collective-permute-done.5.refs_4_
  35.9 0.0 copy-start.15
  35.9 3.0 %collective-permute-start.8 = (bf16[3,256,512]{2,1,0:T(8,128)(2,1)S(1)}, bf16[3,256,512]{2,1,0:T(8,128)(2,1)}, u32[]{:S(2)}, u32[]{:S(2)}) collective-permute-start(bf16[3,256,512]{2,1,0:T(8,128)(2,1)S(1)} %stack.25.refs_1_), channel_id=1, source_target_pairs={{0,8},{1,9},{2,10},{3,11},{4,12},{5,13},{6,14},{7,15},{8,0},{9,1},... | collective-permute-start | bytes 2359304 | tf_op jit(solution)/shard_map/ppermute | solution.py:32
  39.0 2.1 %collective-permute-start.7 = (bf16[3,256,512]{2,1,0:T(8,128)(2,1)S(1)}, bf16[3,256,512]{2,1,0:T(8,128)(2,1)}, u32[]{:S(2)}, u32[]{:S(2)}) collective-permute-start(bf16[3,256,512]{2,1,0:T(8,128)(2,1)S(1)} %stack.25.refs_1_), channel_id=1, source_target_pairs={{0,12},{1,13},{2,14},{3,15},{4,0},{5,1},{6,2},{7,3},{8,4},{9,5},{1... | collective-permute-start | bytes 2359304 | tf_op jit(solution)/shard_map/ppermute | solution.py:32
  41.0 0.5 collective-permute-start.6
  41.5 0.0 all-to-all-done.xf_ref
  41.5 13.3 %collective-permute-start.9 = (bf16[4,256,256]{2,1,0:T(8,128)(2,1)S(1)}, bf16[4,256,256]{2,1,0:T(8,128)(2,1)S(1)}, u32[]{:S(2)}, u32[]{:S(2)}) collective-permute-start(bf16[4,256,256]{2,1,0:T(8,128)(2,1)S(1)} %bitcast.20), channel_id=1, source_target_pairs={{0,32},{16,48},{32,0},{48,16},{64,96},{80,112},{96,64},{112,80},{1... | collective-permute-start | bytes 1572872 | tf_op jit(solution)/shard_map/ppermute | solution.py:32
  54.8 7.3 %collective-permute-start.10 = (bf16[4,256,256]{2,1,0:T(8,128)(2,1)S(1)}, bf16[4,256,256]{2,1,0:T(8,128)(2,1)}, u32[]{:S(2)}, u32[]{:S(2)}) collective-permute-start(bf16[4,256,256]{2,1,0:T(8,128)(2,1)S(1)} %bitcast.21), channel_id=1, source_target_pairs={{0,16},{16,0},{32,48},{48,32},{64,80},{80,64},{96,112},{112,96},{1... | collective-permute-start | bytes 1572872 | tf_op jit(solution)/shard_map/ppermute | solution.py:32
  62.1 5.7 %conv.1 = (bf16[16,16,512]{2,1,0:T(8,128)(2,1)}, f32[4,1024,128]{2,1,0:T(8,128)}) custom-call(bf16[16,32,512]{2,1,0:T(8,128)(2,1)} %copy-done.9, bf16[128,128]{1,0:T(8,128)(2,1)} %constant.70.clone.refs_0_.first_ref, bf16[768,256]{1,0:T(8,128)(2,1)} %constant.71.clone.refs_1_.second_ref, bf16[768,256]{1,0:T(8,128)(2,1)} %constant.72.clone.refs_2_.back_ref, ...), custom_call_target="tpu_custom_call" | custom-call | flops 1000000000 | bytes 4194304 | tf_op jit(solution)/shard_map/conv/pallas_call | solution.py:228
  67.9 4.6 %all-to-all-start.1 = ((bf16[16,16,512]{2,1,0:T(8,128)(2,1)}), bf16[16,16,512]{2,1,0:T(8,128)(2,1)S(1)}, u32[]{:S(2)}, u32[]{:S(2)}) async-start(bf16[16,16,512]{2,1,0:T(8,128)(2,1)} %get-tuple-element.34), calls=%async_computation.1 | async-start | bytes 524288 | tf_op jit(solution)/shard_map/all_to_all | solution.py:363
  72.5 0.0 collective-permute-done.9.refs_9_
  72.6 0.4 collective-permute-start.14
  73.0 0.1 collective-permute-start.13
  73.2 1.8 %collective-permute-done.7.refs_5_ = bf16[3,256,512]{2,1,0:T(8,128)(2,1)} collective-permute-done((bf16[3,256,512]{2,1,0:T(8,128)(2,1)S(1)}, bf16[3,256,512]{2,1,0:T(8,128)(2,1)}, u32[]{:S(2)}, u32[]{:S(2)}) %collective-permute-start.7) | collective-permute-done | bytes 786464 | tf_op jit(solution)/shard_map/ppermute | solution.py:32
  74.9 2.1 %collective-permute-start.12 = (bf16[1,256,256]{2,1,0:T(8,128)(2,1)S(1)}, bf16[1,256,256]{2,1,0:T(8,128)(2,1)S(1)}, u32[]{:S(2)}, u32[]{:S(2)}) collective-permute-start(bf16[1,256,256]{2,1,0:T(8,128)(2,1)S(1)} %get-tuple-element.47), channel_id=1, source_target_pairs={{0,16},{16,0},{32,48},{48,32},{64,80},{80,64},{96,112},{112,96},{1... | collective-permute-start | bytes 393224 | tf_op jit(solution)/shard_map/ppermute | solution.py:32
  77.0 0.0 collective-permute-start.11
  77.0 0.6 stack.24.where_ref
  77.6 4.9 %all-to-all-done.1 = bf16[16,16,512]{2,1,0:T(8,128)(2,1)S(1)} async-done(((bf16[16,16,512]{2,1,0:T(8,128)(2,1)}), bf16[16,16,512]{2,1,0:T(8,128)(2,1)S(1)}, u32[]{:S(2)}, u32[]{:S(2)}) %all-to-all-start.1) | async-done | bytes 262176 | tf_op jit(solution)/shard_map/all_to_all | solution.py:363
  82.5 0.0 collective-permute-done.14.refs_14_
  82.5 0.0 collective-permute-done.12.refs_12_
  82.6 0.7 copy-done.17
  83.2 0.0 copy-done.18
  83.3 0.7 copy-done.19
  83.9 6.7 %products.1 = (bf16[256,512]{1,0:T(8,128)(2,1)}, bf16[256,512]{1,0:T(8,128)(2,1)}, bf16[8,256,256]{2,1,0:T(8,128)(2,1)}, bf16[8,256,256]{2,1,0:T(8,128)(2,1)}) custom-call(s32[5]{0:T(128)} %stack.24.where_ref, bf16[256,512]{1,0:T(8,128)(2,1)} %refs_0_.2, bf16[3,256,512]{2,1,0:T(8,128)(2,1)} %copy-done, bf16[256,512]{1,0:T(8,128)(2,1)} %copy-done.13, ...), custom_call_target="tpu_custom_call" | custom-call | flops 2147483648 | bytes 9437184 | tf_op jit(solution)/shard_map/products/pallas_call | solution.py:350
  90.6 0.0 copy-start.1
  90.6 0.0 copy-start.2
  90.6 0.0 copy-start.3
  90.6 0.0 copy-start.4
  90.7 0.0 copy-start.5
  90.7 0.1 collective-permute-start.15
  90.8 11.5 %all-to-all-start.2 = ((bf16[16,16,512]{2,1,0:T(8,128)(2,1)}), bf16[16,16,512]{2,1,0:T(8,128)(2,1)S(1)}, u32[]{:S(2)}, u32[]{:S(2)}) async-start(bf16[16,16,512]{2,1,0:T(8,128)(2,1)} %bitcast.24), calls=%async_computation.2 | async-start | bytes 524288 | tf_op jit(solution)/shard_map/all_to_all | solution.py:363
  102.3 0.0 collective-permute-done.15
  102.3 2.3 %add_convert_fusion.3 = (bf16[2,256,256]{2,1,0:T(8,128)(2,1)}, bf16[2,256,256]{2,1,0:T(8,128)(2,1)}, bf16[2,256,256]{2,1,0:T(8,128)(2,1)S(1)}) fusion(bf16[8,256,256]{2,1,0:T(8,128)(2,1)} %collective-permute-done.15, bf16[8,256,256]{2,1,0:T(8,128)(2,1)} %get-tuple-element.38), kind=kLoop, calls=%fused_computation.4 | loop fusion | flops 1572864 | bytes 2359296 | tf_op jit(solution)/shard_map/convert_element_type | solution.py:370
  104.6 1.2 collective-permute-start.16
  105.8 0.3 collective-permute-start.18
  106.1 1.8 %collective-permute-start.17 = (bf16[2,256,256]{2,1,0:T(8,128)(2,1)S(1)}, bf16[2,256,256]{2,1,0:T(8,128)(2,1)}, u32[]{:S(2)}, u32[]{:S(2)}) collective-permute-start(bf16[2,256,256]{2,1,0:T(8,128)(2,1)S(1)} %get-tuple-element.42), channel_id=1, source_target_pairs={{0,128},{16,144},{32,160},{48,176},{64,192},{80,208},{96,224},{112... | collective-permute-start | bytes 786440 | tf_op jit(solution)/shard_map/ppermute | solution.py:32
  107.9 4.4 %all-to-all-done.2.p_ref = bf16[16,16,512]{2,1,0:T(8,128)(2,1)S(1)} async-done(((bf16[16,16,512]{2,1,0:T(8,128)(2,1)}), bf16[16,16,512]{2,1,0:T(8,128)(2,1)S(1)}, u32[]{:S(2)}, u32[]{:S(2)}) %all-to-all-start.2) | async-done | bytes 262176 | tf_op jit(solution)/shard_map/all_to_all | solution.py:363
  112.3 4.5 %grads.1 = bf16[16,32,512]{2,1,0:T(8,128)(2,1)} custom-call(bf16[16,16,512]{2,1,0:T(8,128)(2,1)S(1)} %all-to-all-done.2.p_ref, bf16[128,128]{1,0:T(8,128)(2,1)S(1)} %copy-done.5, bf16[768,256]{1,0:T(8,128)(2,1)S(1)} %copy-done.2, bf16[768,256]{1,0:T(8,128)(2,1)S(1)} %copy-done.1, bf16[64,384]{1,0:T(8,128)(2,1)S(1)} %copy-done.4, ...), custom_call_target="tpu_custom_call" | custom-call | flops 10000000000 | bytes 4194304 | tf_op jit(solution)/shard_map/grads/pallas_call | solution.py:244
  116.9 5.8 %all-to-all-start.3 = ((bf16[16,32,512]{2,1,0:T(8,128)(2,1)}), bf16[16,32,512]{2,1,0:T(8,128)(2,1)S(1)}, u32[]{:S(2)}, u32[]{:S(2)}) async-start(bf16[16,32,512]{2,1,0:T(8,128)(2,1)} %grads.1), calls=%async_computation.3 | async-start | bytes 1048576 | tf_op jit(solution)/shard_map/all_to_all | solution.py:363
  122.6 0.0 collective-permute-done.16
  122.7 0.0 collective-permute-done.18
  122.7 1.4 %add_convert_fusion = bf16[2,256,256]{2,1,0:T(8,128)(2,1)S(1)} fusion(bf16[2,256,256]{2,1,0:T(8,128)(2,1)} %collective-permute-done.18, bf16[2,256,256]{2,1,0:T(8,128)(2,1)} %collective-permute-done.17, bf16[2,256,256]{2,1,0:T(8,128)(2,1)} %collective-permute-done.16, bf16[8,256,256]{2,1,0:T(8,128)(2,1)} %collective-permute-done.15, ...), kind=kLoop, calls=%fused_computation.1 | loop fusion | flops 1572864 | bytes 1572864 | tf_op jit(solution)/shard_map/convert_element_type | solution.py:370
  124.1 5.2 %collective-permute-start.19 = (bf16[256,256]{1,0:T(8,128)(2,1)S(1)}, bf16[256,256]{1,0:T(8,128)(2,1)S(1)}, u32[]{:S(2)}, u32[]{:S(2)}) collective-permute-start(bf16[256,256]{1,0:T(8,128)(2,1)S(1)} %slice_bitcast_fusion), channel_id=1, source_target_pairs={{0,32},{16,48},{32,0},{48,16},{64,96},{80,112},{96,64},{112,80},{1... | collective-permute-start | bytes 393224 | tf_op jit(solution)/shard_map/ppermute | solution.py:32
  129.3 7.8 %collective-permute-done.19 = bf16[256,256]{1,0:T(8,128)(2,1)S(1)} collective-permute-done((bf16[256,256]{1,0:T(8,128)(2,1)S(1)}, bf16[256,256]{1,0:T(8,128)(2,1)S(1)}, u32[]{:S(2)}, u32[]{:S(2)}) %collective-permute-start.19) | collective-permute-done | bytes 131104 | tf_op jit(solution)/shard_map/ppermute | solution.py:32
  137.1 0.7 fusion
  137.8 0.0 all-to-all-done.3
  137.8 0.8 fusion.1
  (38 shorter events, 0.1 us)
Async XLA Ops:
  0.6 19.9 %copy-start.12 = (bf16[256,512]{1,0:T(8,128)(2,1)S(1)}, bf16[256,512]{1,0:T(8,128)(2,1)}, u32[]{:S(2)}) copy-start(bf16[256,512]{1,0:T(8,128)(2,1)} %refs_0_.2) | copy-start | bytes 786436
  0.6 21.1 %copy-start.11 = (bf16[256,256]{1,0:T(8,128)(2,1)S(1)}, bf16[256,256]{1,0:T(8,128)(2,1)}, u32[]{:S(2)}) copy-start(bf16[256,256]{1,0:T(8,128)(2,1)} %param.14) | copy-start | bytes 393220
  0.7 19.9 %collective-permute-start.3 = (bf16[256,512]{1,0:T(8,128)(2,1)}, bf16[256,512]{1,0:T(8,128)(2,1)S(1)}, u32[]{:S(2)}, u32[]{:S(2)}) collective-permute-start(bf16[256,512]{1,0:T(8,128)(2,1)} %refs_0_.2), channel_id=1, source_target_pairs={{0,4},{1,5},{2,6},{3,7},{4,8},{5,9},{6,10},{7,11},{8,12},{9,13},{1... | collective-permute-start | bytes 786440 | tf_op jit(solution)/shard_map/ppermute | solution.py:32
  2.0 30.8 %collective-permute-start.2 = (bf16[256,512]{1,0:T(8,128)(2,1)}, bf16[256,512]{1,0:T(8,128)(2,1)S(1)}, u32[]{:S(2)}, u32[]{:S(2)}) collective-permute-start(bf16[256,512]{1,0:T(8,128)(2,1)} %refs_0_.2), channel_id=1, source_target_pairs={{0,3},{1,0},{2,1},{3,2},{4,7},{5,4},{6,5},{7,6},{8,11},{9,8},{10,9... | collective-permute-start | bytes 786440 | tf_op jit(solution)/shard_map/ppermute | solution.py:32
  2.0 30.8 %collective-permute-start.1 = (bf16[256,512]{1,0:T(8,128)(2,1)}, bf16[256,512]{1,0:T(8,128)(2,1)S(1)}, u32[]{:S(2)}, u32[]{:S(2)}) collective-permute-start(bf16[256,512]{1,0:T(8,128)(2,1)} %refs_0_.2), channel_id=1, source_target_pairs={{0,2},{1,3},{2,0},{3,1},{4,6},{5,7},{6,4},{7,5},{8,10},{9,11},{10,... | collective-permute-start | bytes 786440 | tf_op jit(solution)/shard_map/ppermute | solution.py:32
  5.7 30.1 %collective-permute-start = (bf16[256,512]{1,0:T(8,128)(2,1)}, bf16[256,512]{1,0:T(8,128)(2,1)S(1)}, u32[]{:S(2)}, u32[]{:S(2)}) collective-permute-start(bf16[256,512]{1,0:T(8,128)(2,1)} %refs_0_.2), channel_id=1, source_target_pairs={{0,1},{1,2},{2,3},{3,0},{4,5},{5,6},{6,7},{7,4},{8,9},{9,10},{10,1... | collective-permute-start | bytes 786440 | tf_op jit(solution)/shard_map/ppermute | solution.py:32
  5.7 30.2 %collective-permute-start.4 = (bf16[256,512]{1,0:T(8,128)(2,1)}, bf16[256,512]{1,0:T(8,128)(2,1)S(1)}, u32[]{:S(2)}, u32[]{:S(2)}) collective-permute-start(bf16[256,512]{1,0:T(8,128)(2,1)} %refs_0_.2), channel_id=1, source_target_pairs={{0,8},{1,9},{2,10},{3,11},{4,12},{5,13},{6,14},{7,15},{8,0},{9,1},... | collective-permute-start | bytes 786440 | tf_op jit(solution)/shard_map/ppermute | solution.py:32
  10.2 31.3 %all-to-all-start = ((bf16[16,32,512]{2,1,0:T(8,128)(2,1)}), bf16[16,32,512]{2,1,0:T(8,128)(2,1)S(1)}, u32[]{:S(2)}, u32[]{:S(2)}) async-start(bf16[16,32,512]{2,1,0:T(8,128)(2,1)} %pad_maximum_fusion), calls=%async_computation | async-start | bytes 1048576 | tf_op jit(solution)/shard_map/all_to_all | solution.py:363
  20.6 1.2 copy-start.13
  20.6 15.4 %collective-permute-start.5 = (bf16[256,512]{1,0:T(8,128)(2,1)S(1)}, bf16[256,512]{1,0:T(8,128)(2,1)S(1)}, u32[]{:S(2)}, u32[]{:S(2)}) collective-permute-start(bf16[256,512]{1,0:T(8,128)(2,1)S(1)} %copy-done.12), channel_id=1, source_target_pairs={{0,12},{1,13},{2,14},{3,15},{4,0},{5,1},{6,2},{7,3},{8,4},{9,5},{1... | collective-permute-start | bytes 786440 | tf_op jit(solution)/shard_map/ppermute | solution.py:32
  32.8 22.0 %copy-start.7 = (bf16[1024,256]{1,0:T(8,128)(2,1)}, bf16[1024,256]{1,0:T(8,128)(2,1)S(1)}, u32[]{:S(2)}) copy-start(bf16[1024,256]{1,0:T(8,128)(2,1)S(1)} %copy.14) | copy-start | bytes 1572868
  35.9 32.0 %copy-start = (bf16[3,256,512]{2,1,0:T(8,128)(2,1)}, bf16[3,256,512]{2,1,0:T(8,128)(2,1)S(1)}, u32[]{:S(2)}) copy-start(bf16[3,256,512]{2,1,0:T(8,128)(2,1)S(1)} %stack.25.refs_1_) | copy-start | bytes 2359300
  35.9 5.6 %copy-start.14 = (bf16[256,512]{1,0:T(8,128)(2,1)}, bf16[256,512]{1,0:T(8,128)(2,1)S(1)}, u32[]{:S(2)}) copy-start(bf16[256,512]{1,0:T(8,128)(2,1)S(1)} %collective-permute-done.4.refs_6_) | copy-start | bytes 786436
  35.9 31.9 %copy-start.15 = (bf16[256,512]{1,0:T(8,128)(2,1)}, bf16[256,512]{1,0:T(8,128)(2,1)S(1)}, u32[]{:S(2)}) copy-start(bf16[256,512]{1,0:T(8,128)(2,1)S(1)} %collective-permute-done.5.refs_4_) | copy-start | bytes 786436
  35.9 37.1 %collective-permute-start.8 = (bf16[3,256,512]{2,1,0:T(8,128)(2,1)S(1)}, bf16[3,256,512]{2,1,0:T(8,128)(2,1)}, u32[]{:S(2)}, u32[]{:S(2)}) collective-permute-start(bf16[3,256,512]{2,1,0:T(8,128)(2,1)S(1)} %stack.25.refs_1_), channel_id=1, source_target_pairs={{0,8},{1,9},{2,10},{3,11},{4,12},{5,13},{6,14},{7,15},{8,0},{9,1},... | collective-permute-start | bytes 2359304 | tf_op jit(solution)/shard_map/ppermute | solution.py:32
  39.0 36.0 %collective-permute-start.7 = (bf16[3,256,512]{2,1,0:T(8,128)(2,1)S(1)}, bf16[3,256,512]{2,1,0:T(8,128)(2,1)}, u32[]{:S(2)}, u32[]{:S(2)}) collective-permute-start(bf16[3,256,512]{2,1,0:T(8,128)(2,1)S(1)} %stack.25.refs_1_), channel_id=1, source_target_pairs={{0,12},{1,13},{2,14},{3,15},{4,0},{5,1},{6,2},{7,3},{8,4},{9,5},{1... | collective-permute-start | bytes 2359304 | tf_op jit(solution)/shard_map/ppermute | solution.py:32
  41.0 36.0 %collective-permute-start.6 = (bf16[3,256,512]{2,1,0:T(8,128)(2,1)S(1)}, bf16[3,256,512]{2,1,0:T(8,128)(2,1)}, u32[]{:S(2)}, u32[]{:S(2)}) collective-permute-start(bf16[3,256,512]{2,1,0:T(8,128)(2,1)S(1)} %stack.25.refs_1_), channel_id=1, source_target_pairs={{0,4},{1,5},{2,6},{3,7},{4,8},{5,9},{6,10},{7,11},{8,12},{9,13},{1... | collective-permute-start | bytes 2359304 | tf_op jit(solution)/shard_map/ppermute | solution.py:32
  41.5 20.6 %copy-start.9 = (bf16[16,32,512]{2,1,0:T(8,128)(2,1)}, bf16[16,32,512]{2,1,0:T(8,128)(2,1)S(1)}, u32[]{:S(2)}) copy-start(bf16[16,32,512]{2,1,0:T(8,128)(2,1)S(1)} %all-to-all-done.xf_ref) | copy-start | bytes 1572868
  41.5 31.0 %collective-permute-start.9 = (bf16[4,256,256]{2,1,0:T(8,128)(2,1)S(1)}, bf16[4,256,256]{2,1,0:T(8,128)(2,1)S(1)}, u32[]{:S(2)}, u32[]{:S(2)}) collective-permute-start(bf16[4,256,256]{2,1,0:T(8,128)(2,1)S(1)} %bitcast.20), channel_id=1, source_target_pairs={{0,32},{16,48},{32,0},{48,16},{64,96},{80,112},{96,64},{112,80},{1... | collective-permute-start | bytes 1572872 | tf_op jit(solution)/shard_map/ppermute | solution.py:32
  54.8 27.7 %collective-permute-start.10 = (bf16[4,256,256]{2,1,0:T(8,128)(2,1)S(1)}, bf16[4,256,256]{2,1,0:T(8,128)(2,1)}, u32[]{:S(2)}, u32[]{:S(2)}) collective-permute-start(bf16[4,256,256]{2,1,0:T(8,128)(2,1)S(1)} %bitcast.21), channel_id=1, source_target_pairs={{0,16},{16,0},{32,48},{48,32},{64,80},{80,64},{96,112},{112,96},{1... | collective-permute-start | bytes 1572872 | tf_op jit(solution)/shard_map/ppermute | solution.py:32
  67.9 14.6 %all-to-all-start.1 = ((bf16[16,16,512]{2,1,0:T(8,128)(2,1)}), bf16[16,16,512]{2,1,0:T(8,128)(2,1)S(1)}, u32[]{:S(2)}, u32[]{:S(2)}) async-start(bf16[16,16,512]{2,1,0:T(8,128)(2,1)} %get-tuple-element.34), calls=%async_computation.1 | async-start | bytes 524288 | tf_op jit(solution)/shard_map/all_to_all | solution.py:363
  72.5 11.4 %copy-start.8 = (bf16[4,256,256]{2,1,0:T(8,128)(2,1)}, bf16[4,256,256]{2,1,0:T(8,128)(2,1)S(1)}, u32[]{:S(2)}) copy-start(bf16[4,256,256]{2,1,0:T(8,128)(2,1)S(1)} %collective-permute-done.9.refs_9_) | copy-start | bytes 1572868
  72.6 9.9 %collective-permute-start.14 = (bf16[1,256,256]{2,1,0:T(8,128)(2,1)S(1)}, bf16[1,256,256]{2,1,0:T(8,128)(2,1)S(1)}, u32[]{:S(2)}, u32[]{:S(2)}) collective-permute-start(bf16[1,256,256]{2,1,0:T(8,128)(2,1)S(1)} %get-tuple-element.45), channel_id=1, source_target_pairs={{0,16},{16,0},{32,48},{48,32},{64,80},{80,64},{96,112},{112,96},{1... | collective-permute-start | bytes 393224 | tf_op jit(solution)/shard_map/ppermute | solution.py:32
  73.0 9.5 %collective-permute-start.13 = (bf16[1,256,256]{2,1,0:T(8,128)(2,1)S(1)}, bf16[1,256,256]{2,1,0:T(8,128)(2,1)S(1)}, u32[]{:S(2)}, u32[]{:S(2)}) collective-permute-start(bf16[1,256,256]{2,1,0:T(8,128)(2,1)S(1)} %get-tuple-element.46), channel_id=1, source_target_pairs={{0,16},{16,0},{32,48},{48,32},{64,80},{80,64},{96,112},{112,96},{1... | collective-permute-start | bytes 393224 | tf_op jit(solution)/shard_map/ppermute | solution.py:32
  74.9 7.6 %collective-permute-start.12 = (bf16[1,256,256]{2,1,0:T(8,128)(2,1)S(1)}, bf16[1,256,256]{2,1,0:T(8,128)(2,1)S(1)}, u32[]{:S(2)}, u32[]{:S(2)}) collective-permute-start(bf16[1,256,256]{2,1,0:T(8,128)(2,1)S(1)} %get-tuple-element.47), channel_id=1, source_target_pairs={{0,16},{16,0},{32,48},{48,32},{64,80},{80,64},{96,112},{112,96},{1... | collective-permute-start | bytes 393224 | tf_op jit(solution)/shard_map/ppermute | solution.py:32
  77.0 5.5 %collective-permute-start.11 = (bf16[1,256,256]{2,1,0:T(8,128)(2,1)S(1)}, bf16[1,256,256]{2,1,0:T(8,128)(2,1)S(1)}, u32[]{:S(2)}, u32[]{:S(2)}) collective-permute-start(bf16[1,256,256]{2,1,0:T(8,128)(2,1)S(1)} %get-tuple-element.48), channel_id=1, source_target_pairs={{0,16},{16,0},{32,48},{48,32},{64,80},{80,64},{96,112},{112,96},{1... | collective-permute-start | bytes 393224 | tf_op jit(solution)/shard_map/ppermute | solution.py:32
  82.5 1.4 %copy-start.10 = (bf16[16,16,512]{2,1,0:T(8,128)(2,1)}, bf16[16,16,512]{2,1,0:T(8,128)(2,1)S(1)}, u32[]{:S(2)}) copy-start(bf16[16,16,512]{2,1,0:T(8,128)(2,1)S(1)} %all-to-all-done.1) | copy-start | bytes 786436
  82.5 1.4 %copy-start.16 = (bf16[1,256,256]{2,1,0:T(8,128)(2,1)}, bf16[1,256,256]{2,1,0:T(8,128)(2,1)S(1)}, u32[]{:S(2)}) copy-start(bf16[1,256,256]{2,1,0:T(8,128)(2,1)S(1)} %collective-permute-done.14.refs_14_) | copy-start | bytes 393220
  82.5 0.7 copy-start.17
  82.5 0.7 copy-start.18
  83.3 0.7 copy-start.19
  83.9 28.4 %copy-start.6 = (f32[4,1024,128]{2,1,0:T(8,128)S(1)}, f32[4,1024,128]{2,1,0:T(8,128)}, u32[]{:S(2)}) copy-start(f32[4,1024,128]{2,1,0:T(8,128)} %get-tuple-element.36.spec_ref) | copy-start | bytes 6291460
  90.6 21.7 %copy-start.1 = (bf16[768,256]{1,0:T(8,128)(2,1)S(1)}, bf16[768,256]{1,0:T(8,128)(2,1)}, u32[]{:S(2)}) copy-start(bf16[768,256]{1,0:T(8,128)(2,1)} %constant.72.clone.refs_2_.back_ref) | copy-start | bytes 1179652
  90.6 21.7 %copy-start.2 = (bf16[768,256]{1,0:T(8,128)(2,1)S(1)}, bf16[768,256]{1,0:T(8,128)(2,1)}, u32[]{:S(2)}) copy-start(bf16[768,256]{1,0:T(8,128)(2,1)} %constant.71.clone.refs_1_.second_ref) | copy-start | bytes 1179652
  90.6 21.7 %copy-start.3 = (f32[2,64,128]{2,1,0:T(8,128)S(1)}, f32[2,64,128]{2,1,0:T(8,128)}, u32[]{:S(2)}) copy-start(f32[2,64,128]{2,1,0:T(8,128)} %constant.74.clone.refs_4_.turn_ref) | copy-start | bytes 196612
  90.6 21.7 %copy-start.4 = (bf16[64,384]{1,0:T(8,128)(2,1)S(1)}, bf16[64,384]{1,0:T(8,128)(2,1)}, u32[]{:S(2)}) copy-start(bf16[64,384]{1,0:T(8,128)(2,1)} %constant.73.clone.refs_3_.last_ref) | copy-start | bytes 147460
  90.7 21.7 %copy-start.5 = (bf16[128,128]{1,0:T(8,128)(2,1)S(1)}, bf16[128,128]{1,0:T(8,128)(2,1)}, u32[]{:S(2)}) copy-start(bf16[128,128]{1,0:T(8,128)(2,1)} %constant.70.clone.refs_0_.first_ref) | copy-start | bytes 98308
  90.7 11.6 %collective-permute-start.15 = (bf16[8,256,256]{2,1,0:T(8,128)(2,1)}, bf16[8,256,256]{2,1,0:T(8,128)(2,1)}, u32[]{:S(2)}, u32[]{:S(2)}) collective-permute-start(bf16[8,256,256]{2,1,0:T(8,128)(2,1)} %get-tuple-element.39), channel_id=1, source_target_pairs={{0,16},{16,0},{32,48},{48,32},{64,80},{80,64},{96,112},{112,96},{1... | collective-permute-start | bytes 3145736 | tf_op jit(solution)/shard_map/ppermute | solution.py:32
  90.8 21.5 %all-to-all-start.2 = ((bf16[16,16,512]{2,1,0:T(8,128)(2,1)}), bf16[16,16,512]{2,1,0:T(8,128)(2,1)S(1)}, u32[]{:S(2)}, u32[]{:S(2)}) async-start(bf16[16,16,512]{2,1,0:T(8,128)(2,1)} %bitcast.24), calls=%async_computation.2 | async-start | bytes 524288 | tf_op jit(solution)/shard_map/all_to_all | solution.py:363
  104.6 18.0 %collective-permute-start.16 = (bf16[2,256,256]{2,1,0:T(8,128)(2,1)}, bf16[2,256,256]{2,1,0:T(8,128)(2,1)}, u32[]{:S(2)}, u32[]{:S(2)}) collective-permute-start(bf16[2,256,256]{2,1,0:T(8,128)(2,1)} %get-tuple-element.40), channel_id=1, source_target_pairs={{0,64},{16,80},{32,96},{48,112},{64,128},{80,144},{96,160},{112,17... | collective-permute-start | bytes 786440 | tf_op jit(solution)/shard_map/ppermute | solution.py:32
  105.8 16.8 %collective-permute-start.18 = (bf16[2,256,256]{2,1,0:T(8,128)(2,1)}, bf16[2,256,256]{2,1,0:T(8,128)(2,1)}, u32[]{:S(2)}, u32[]{:S(2)}) collective-permute-start(bf16[2,256,256]{2,1,0:T(8,128)(2,1)} %get-tuple-element.41), channel_id=1, source_target_pairs={{0,192},{16,208},{32,224},{48,240},{64,0},{80,16},{96,32},{112,48}... | collective-permute-start | bytes 786440 | tf_op jit(solution)/shard_map/ppermute | solution.py:32
  106.1 16.6 %collective-permute-start.17 = (bf16[2,256,256]{2,1,0:T(8,128)(2,1)S(1)}, bf16[2,256,256]{2,1,0:T(8,128)(2,1)}, u32[]{:S(2)}, u32[]{:S(2)}) collective-permute-start(bf16[2,256,256]{2,1,0:T(8,128)(2,1)S(1)} %get-tuple-element.42), channel_id=1, source_target_pairs={{0,128},{16,144},{32,160},{48,176},{64,192},{80,208},{96,224},{112... | collective-permute-start | bytes 786440 | tf_op jit(solution)/shard_map/ppermute | solution.py:32
  116.9 21.0 %all-to-all-start.3 = ((bf16[16,32,512]{2,1,0:T(8,128)(2,1)}), bf16[16,32,512]{2,1,0:T(8,128)(2,1)S(1)}, u32[]{:S(2)}, u32[]{:S(2)}) async-start(bf16[16,32,512]{2,1,0:T(8,128)(2,1)} %grads.1), calls=%async_computation.3 | async-start | bytes 1048576 | tf_op jit(solution)/shard_map/all_to_all | solution.py:363
  124.1 13.0 %collective-permute-start.19 = (bf16[256,256]{1,0:T(8,128)(2,1)S(1)}, bf16[256,256]{1,0:T(8,128)(2,1)S(1)}, u32[]{:S(2)}, u32[]{:S(2)}) collective-permute-start(bf16[256,256]{1,0:T(8,128)(2,1)S(1)} %slice_bitcast_fusion), channel_id=1, source_target_pairs={{0,32},{16,48},{32,0},{48,16},{64,96},{80,112},{96,64},{112,80},{1... | collective-permute-start | bytes 393224 | tf_op jit(solution)/shard_map/ppermute | solution.py:32

commit v11 on v10

--- a/solution.py
+++ b/solution.py
@@ -15,7 +15,7 @@
 SEQ = 8192
 ROWS = 64
 LANES = 128
-GROUP = 8
+GROUP = 16
 BF = jnp.bfloat16
 F32 = jnp.float32
 

time: 141 us -> 141 us (level)
  no operation moved by 1% of the time
where the time goes in v11:
time: 141 us; the launch traced here: 138 us
  starting transfers between devices  78.6 us (56%)
  waiting for transfers between devices  21.9 us (16%)
  Pallas kernels  16.3 us (12%)
  blocking collectives  10.9 us (8%)
  other arithmetic  6.31 us (4%)
  local copies, waits for them, and re-layouts  3.1 us (2%)
    ppermute x20, starting transfers between devices, send(): return lax.ppermute(value, axis, shift_pairs(stride, size, by))  46.2 us
    all_to_all x4, starting transfers between devices, exchange(): return lax.all_to_all(value, 'ctx', split_axis=0, concat_axis=0, tiled=True)  32.3 us
    ppermute x20, waiting for transfers between devices, send(): return lax.ppermute(value, axis, shift_pairs(stride, size, by))  12.7 us
    all_gather x1, blocking collectives, on_device(): w_line = lax.all_gather(w_own.T, 'ctx', axis_index_groups=LINES_X)  10.9 us
    all_to_all x4, waiting for transfers between devices, exchange(): return lax.all_to_all(value, 'ctx', split_axis=0, concat_axis=0, tiled=True)  9.23 us
    pallas_call x1, Pallas kernels, products_call(): pl.pallas_call(products_kernel, out_shape=(tile, tile, eight, eight), in_...  6.67 us
    pallas_call x1, Pallas kernels, conv_call(): pl.pallas_call(conv_kernel, out_shape=(jax.ShapeDtypeStruct((16, FEW, TOK...  5.65 us
    convert_element_type x3, other arithmetic, add(): return total.astype(BF)  4.45 us
  transfers between devices with their start and end apart: 24, of which 5 were waited for; matrix products, arithmetic and copies ran while one was open for 5% of the time, Pallas kernels for 7%

profile of v11, /device:TPU:67, one launch (start us, length us, event | category | flops | bytes accessed | tf_op | source)
XLA Modules:
  0.0 138.1 jit_solution(16120851292759236340)
XLA Ops:
  0.6 0.0 copy-start.12
  0.7 1.4 collective-permute-start.3
  2.0 0.0 collective-permute-start.2
  2.0 3.7 %collective-permute-start.1 = (bf16[256,512]{1,0:T(8,128)(2,1)}, bf16[256,512]{1,0:T(8,128)(2,1)S(1)}, u32[]{:S(2)}, u32[]{:S(2)}) collective-permute-start(bf16[256,512]{1,0:T(8,128)(2,1)} %refs_0_.2), channel_id=1, source_target_pairs={{0,2},{1,3},{2,0},{3,1},{4,6},{5,7},{6,4},{7,5},{8,10},{9,11},{10,... | collective-permute-start | bytes 786440 | tf_op jit(solution)/shard_map/ppermute | solution.py:32
  5.7 0.0 collective-permute-start
  5.7 2.6 %collective-permute-start.4 = (bf16[256,512]{1,0:T(8,128)(2,1)}, bf16[256,512]{1,0:T(8,128)(2,1)S(1)}, u32[]{:S(2)}, u32[]{:S(2)}) collective-permute-start(bf16[256,512]{1,0:T(8,128)(2,1)} %refs_0_.2), channel_id=1, source_target_pairs={{0,8},{1,9},{2,10},{3,11},{4,12},{5,13},{6,14},{7,15},{8,0},{9,1},... | collective-permute-start | bytes 786440 | tf_op jit(solution)/shard_map/ppermute | solution.py:32
  8.4 1.9 %pad_maximum_fusion = bf16[16,32,512]{2,1,0:T(8,128)(2,1)} fusion(bf16[16,16,512]{2,1,0:T(8,128)(2,1)} %bitcast.25, bf16[16,16,512]{2,1,0:T(8,128)(2,1)} %bitcast.26), kind=kLoop, calls=%fused_computation | loop fusion | flops 1048576 | bytes 1048576 | tf_op jit(solution)/shard_map/concatenate | solution.py:379
  10.2 10.3 %all-to-all-start = ((bf16[16,32,512]{2,1,0:T(8,128)(2,1)}), bf16[16,32,512]{2,1,0:T(8,128)(2,1)S(1)}, u32[]{:S(2)}, u32[]{:S(2)}) async-start(bf16[16,32,512]{2,1,0:T(8,128)(2,1)} %pad_maximum_fusion), calls=%async_computation | async-start | bytes 1048576 | tf_op jit(solution)/shard_map/all_to_all | solution.py:363
  20.5 0.0 collective-permute-done.3.refs_2_
  20.6 0.0 copy-start.13
  20.6 1.1 collective-permute-start.5
  21.7 10.9 %all-gather = bf16[1024,256]{0,1:T(8,128)(2,1)S(1)} all-gather(bf16[256,256]{0,1:T(8,128)(2,1)S(1)} %bitcast.29), channel_id=2, replica_groups={{0,64,128,192},{16,80,144,208},{32,96,160,224},{48,112,176,240},{1,65,1..., dimensions={0}, use_global_device_ids=true | all-gather | bytes 655360 | tf_op jit(solution)/shard_map/all_gather | solution.py:387
  32.6 0.2 copy.14
  32.8 0.0 collective-permute-done.2.refs_2_
  32.8 0.0 collective-permute-done.1.refs_1_
  32.9 3.0 %collective-permute-done.refs_0_ = bf16[256,512]{1,0:T(8,128)(2,1)S(1)} collective-permute-done((bf16[256,512]{1,0:T(8,128)(2,1)}, bf16[256,512]{1,0:T(8,128)(2,1)S(1)}, u32[]{:S(2)}, u32[]{:S(2)}) %collective-permute-start) | collective-permute-done | bytes 262176 | tf_op jit(solution)/shard_map/ppermute | solution.py:32
  35.8 0.1 stack.25.refs_1_
  35.9 0.0 collective-permute-done.5.refs_4_
  35.9 0.0 copy-start.15
  35.9 3.0 %collective-permute-start.8 = (bf16[3,256,512]{2,1,0:T(8,128)(2,1)S(1)}, bf16[3,256,512]{2,1,0:T(8,128)(2,1)}, u32[]{:S(2)}, u32[]{:S(2)}) collective-permute-start(bf16[3,256,512]{2,1,0:T(8,128)(2,1)S(1)} %stack.25.refs_1_), channel_id=1, source_target_pairs={{0,8},{1,9},{2,10},{3,11},{4,12},{5,13},{6,14},{7,15},{8,0},{9,1},... | collective-permute-start | bytes 2359304 | tf_op jit(solution)/shard_map/ppermute | solution.py:32
  39.0 2.1 %collective-permute-start.7 = (bf16[3,256,512]{2,1,0:T(8,128)(2,1)S(1)}, bf16[3,256,512]{2,1,0:T(8,128)(2,1)}, u32[]{:S(2)}, u32[]{:S(2)}) collective-permute-start(bf16[3,256,512]{2,1,0:T(8,128)(2,1)S(1)} %stack.25.refs_1_), channel_id=1, source_target_pairs={{0,12},{1,13},{2,14},{3,15},{4,0},{5,1},{6,2},{7,3},{8,4},{9,5},{1... | collective-permute-start | bytes 2359304 | tf_op jit(solution)/shard_map/ppermute | solution.py:32
  41.0 0.5 collective-permute-start.6
  41.5 0.0 all-to-all-done.xf_ref
  41.5 13.3 %collective-permute-start.9 = (bf16[4,256,256]{2,1,0:T(8,128)(2,1)S(1)}, bf16[4,256,256]{2,1,0:T(8,128)(2,1)S(1)}, u32[]{:S(2)}, u32[]{:S(2)}) collective-permute-start(bf16[4,256,256]{2,1,0:T(8,128)(2,1)S(1)} %bitcast.20), channel_id=1, source_target_pairs={{0,32},{16,48},{32,0},{48,16},{64,96},{80,112},{96,64},{112,80},{1... | collective-permute-start | bytes 1572872 | tf_op jit(solution)/shard_map/ppermute | solution.py:32
  54.8 7.3 %collective-permute-start.10 = (bf16[4,256,256]{2,1,0:T(8,128)(2,1)S(1)}, bf16[4,256,256]{2,1,0:T(8,128)(2,1)}, u32[]{:S(2)}, u32[]{:S(2)}) collective-permute-start(bf16[4,256,256]{2,1,0:T(8,128)(2,1)S(1)} %bitcast.21), channel_id=1, source_target_pairs={{0,16},{16,0},{32,48},{48,32},{64,80},{80,64},{96,112},{112,96},{1... | collective-permute-start | bytes 1572872 | tf_op jit(solution)/shard_map/ppermute | solution.py:32
  62.1 5.6 %conv.1 = (bf16[16,16,512]{2,1,0:T(8,128)(2,1)}, f32[4,1024,128]{2,1,0:T(8,128)}) custom-call(bf16[16,32,512]{2,1,0:T(8,128)(2,1)} %copy-done.9, bf16[128,128]{1,0:T(8,128)(2,1)} %constant.70.clone.refs_0_.first_ref, bf16[768,256]{1,0:T(8,128)(2,1)} %constant.71.clone.refs_1_.second_ref, bf16[768,256]{1,0:T(8,128)(2,1)} %constant.72.clone.refs_2_.back_ref, ...), custom_call_target="tpu_custom_call" | custom-call | flops 1000000000 | bytes 4194304 | tf_op jit(solution)/shard_map/conv/pallas_call | solution.py:228
  67.8 4.6 %all-to-all-start.1 = ((bf16[16,16,512]{2,1,0:T(8,128)(2,1)}), bf16[16,16,512]{2,1,0:T(8,128)(2,1)S(1)}, u32[]{:S(2)}, u32[]{:S(2)}) async-start(bf16[16,16,512]{2,1,0:T(8,128)(2,1)} %get-tuple-element.34), calls=%async_computation.1 | async-start | bytes 524288 | tf_op jit(solution)/shard_map/all_to_all | solution.py:363
  72.4 0.0 collective-permute-done.9.refs_9_
  72.5 0.4 collective-permute-start.14
  72.9 0.0 collective-permute-done.8.refs_7_
  72.9 0.1 collective-permute-start.13
  73.1 1.8 %collective-permute-done.7.refs_5_ = bf16[3,256,512]{2,1,0:T(8,128)(2,1)} collective-permute-done((bf16[3,256,512]{2,1,0:T(8,128)(2,1)S(1)}, bf16[3,256,512]{2,1,0:T(8,128)(2,1)}, u32[]{:S(2)}, u32[]{:S(2)}) %collective-permute-start.7) | collective-permute-done | bytes 786464 | tf_op jit(solution)/shard_map/ppermute | solution.py:32
  74.9 2.1 %collective-permute-start.12 = (bf16[1,256,256]{2,1,0:T(8,128)(2,1)S(1)}, bf16[1,256,256]{2,1,0:T(8,128)(2,1)S(1)}, u32[]{:S(2)}, u32[]{:S(2)}) collective-permute-start(bf16[1,256,256]{2,1,0:T(8,128)(2,1)S(1)} %get-tuple-element.47), channel_id=1, source_target_pairs={{0,16},{16,0},{32,48},{48,32},{64,80},{80,64},{96,112},{112,96},{1... | collective-permute-start | bytes 393224 | tf_op jit(solution)/shard_map/ppermute | solution.py:32
  77.0 0.0 collective-permute-start.11
  77.0 0.6 stack.24.where_ref
  77.6 4.8 %all-to-all-done.1 = bf16[16,16,512]{2,1,0:T(8,128)(2,1)S(1)} async-done(((bf16[16,16,512]{2,1,0:T(8,128)(2,1)}), bf16[16,16,512]{2,1,0:T(8,128)(2,1)S(1)}, u32[]{:S(2)}, u32[]{:S(2)}) %all-to-all-start.1) | async-done | bytes 262176 | tf_op jit(solution)/shard_map/all_to_all | solution.py:363
  82.4 0.0 collective-permute-done.10.refs_10_
  82.4 0.0 collective-permute-done.14.refs_14_
  82.5 0.0 collective-permute-done.12.refs_12_
  82.5 0.0 collective-permute-done.11.refs_11_
  82.5 0.7 copy-done.17
  83.1 0.0 copy-done.18
  83.2 0.7 copy-done.19
  83.9 6.7 %products.1 = (bf16[256,512]{1,0:T(8,128)(2,1)}, bf16[256,512]{1,0:T(8,128)(2,1)}, bf16[8,256,256]{2,1,0:T(8,128)(2,1)}, bf16[8,256,256]{2,1,0:T(8,128)(2,1)}) custom-call(s32[5]{0:T(128)} %stack.24.where_ref, bf16[256,512]{1,0:T(8,128)(2,1)} %refs_0_.2, bf16[3,256,512]{2,1,0:T(8,128)(2,1)} %copy-done, bf16[256,512]{1,0:T(8,128)(2,1)} %copy-done.13, ...), custom_call_target="tpu_custom_call" | custom-call | flops 2147483648 | bytes 9437184 | tf_op jit(solution)/shard_map/products/pallas_call | solution.py:350
  90.5 0.0 copy-start.1
  90.5 0.0 copy-start.2
  90.6 0.0 copy-start.3
  90.6 0.0 copy-start.4
  90.6 0.0 copy-start.5
  90.6 0.1 collective-permute-start.15
  90.7 11.6 %all-to-all-start.2 = ((bf16[16,16,512]{2,1,0:T(8,128)(2,1)}), bf16[16,16,512]{2,1,0:T(8,128)(2,1)S(1)}, u32[]{:S(2)}, u32[]{:S(2)}) async-start(bf16[16,16,512]{2,1,0:T(8,128)(2,1)} %bitcast.24), calls=%async_computation.2 | async-start | bytes 524288 | tf_op jit(solution)/shard_map/all_to_all | solution.py:363
  102.3 2.3 %add_convert_fusion.3 = (bf16[2,256,256]{2,1,0:T(8,128)(2,1)}, bf16[2,256,256]{2,1,0:T(8,128)(2,1)}, bf16[2,256,256]{2,1,0:T(8,128)(2,1)S(1)}) fusion(bf16[8,256,256]{2,1,0:T(8,128)(2,1)} %collective-permute-done.15, bf16[8,256,256]{2,1,0:T(8,128)(2,1)} %get-tuple-element.38), kind=kLoop, calls=%fused_computation.4 | loop fusion | flops 1572864 | bytes 2359296 | tf_op jit(solution)/shard_map/convert_element_type | solution.py:370
  104.6 1.2 collective-permute-start.16
  105.8 0.3 collective-permute-start.18
  106.1 1.8 %collective-permute-start.17 = (bf16[2,256,256]{2,1,0:T(8,128)(2,1)S(1)}, bf16[2,256,256]{2,1,0:T(8,128)(2,1)}, u32[]{:S(2)}, u32[]{:S(2)}) collective-permute-start(bf16[2,256,256]{2,1,0:T(8,128)(2,1)S(1)} %get-tuple-element.42), channel_id=1, source_target_pairs={{0,128},{16,144},{32,160},{48,176},{64,192},{80,208},{96,224},{112... | collective-permute-start | bytes 786440 | tf_op jit(solution)/shard_map/ppermute | solution.py:32
  107.9 4.4 %all-to-all-done.2.p_ref = bf16[16,16,512]{2,1,0:T(8,128)(2,1)S(1)} async-done(((bf16[16,16,512]{2,1,0:T(8,128)(2,1)}), bf16[16,16,512]{2,1,0:T(8,128)(2,1)S(1)}, u32[]{:S(2)}, u32[]{:S(2)}) %all-to-all-start.2) | async-done | bytes 262176 | tf_op jit(solution)/shard_map/all_to_all | solution.py:363
  112.3 3.9 %grads.1 = bf16[16,32,512]{2,1,0:T(8,128)(2,1)} custom-call(bf16[16,16,512]{2,1,0:T(8,128)(2,1)S(1)} %all-to-all-done.2.p_ref, bf16[128,128]{1,0:T(8,128)(2,1)S(1)} %copy-done.5, bf16[768,256]{1,0:T(8,128)(2,1)S(1)} %copy-done.2, bf16[768,256]{1,0:T(8,128)(2,1)S(1)} %copy-done.1, bf16[64,384]{1,0:T(8,128)(2,1)S(1)} %copy-done.4, ...), custom_call_target="tpu_custom_call" | custom-call | flops 10000000000 | bytes 4194304 | tf_op jit(solution)/shard_map/grads/pallas_call | solution.py:244
  116.3 5.8 %all-to-all-start.3 = ((bf16[16,32,512]{2,1,0:T(8,128)(2,1)}), bf16[16,32,512]{2,1,0:T(8,128)(2,1)S(1)}, u32[]{:S(2)}, u32[]{:S(2)}) async-start(bf16[16,32,512]{2,1,0:T(8,128)(2,1)} %grads.1), calls=%async_computation.3 | async-start | bytes 1048576 | tf_op jit(solution)/shard_map/all_to_all | solution.py:363
  122.1 0.0 collective-permute-done.18
  122.1 1.4 %add_convert_fusion = bf16[2,256,256]{2,1,0:T(8,128)(2,1)S(1)} fusion(bf16[2,256,256]{2,1,0:T(8,128)(2,1)} %collective-permute-done.18, bf16[2,256,256]{2,1,0:T(8,128)(2,1)} %collective-permute-done.17, bf16[2,256,256]{2,1,0:T(8,128)(2,1)} %collective-permute-done.16, bf16[8,256,256]{2,1,0:T(8,128)(2,1)} %collective-permute-done.15, ...), kind=kLoop, calls=%fused_computation.1 | loop fusion | flops 1572864 | bytes 1572864 | tf_op jit(solution)/shard_map/convert_element_type | solution.py:370
  123.5 5.2 %collective-permute-start.19 = (bf16[256,256]{1,0:T(8,128)(2,1)S(1)}, bf16[256,256]{1,0:T(8,128)(2,1)S(1)}, u32[]{:S(2)}, u32[]{:S(2)}) collective-permute-start(bf16[256,256]{1,0:T(8,128)(2,1)S(1)} %slice_bitcast_fusion), channel_id=1, source_target_pairs={{0,32},{16,48},{32,0},{48,16},{64,96},{80,112},{96,64},{112,80},{1... | collective-permute-start | bytes 393224 | tf_op jit(solution)/shard_map/ppermute | solution.py:32
  128.7 7.8 %collective-permute-done.19 = bf16[256,256]{1,0:T(8,128)(2,1)S(1)} collective-permute-done((bf16[256,256]{1,0:T(8,128)(2,1)S(1)}, bf16[256,256]{1,0:T(8,128)(2,1)S(1)}, u32[]{:S(2)}, u32[]{:S(2)}) %collective-permute-start.19) | collective-permute-done | bytes 131104 | tf_op jit(solution)/shard_map/ppermute | solution.py:32
  136.5 0.7 fusion
  137.2 0.8 fusion.1
  (38 shorter events, 0.1 us)
Async XLA Ops:
  0.6 19.9 %copy-start.12 = (bf16[256,512]{1,0:T(8,128)(2,1)S(1)}, bf16[256,512]{1,0:T(8,128)(2,1)}, u32[]{:S(2)}) copy-start(bf16[256,512]{1,0:T(8,128)(2,1)} %refs_0_.2) | copy-start | bytes 786436
  0.6 21.1 %copy-start.11 = (bf16[256,256]{1,0:T(8,128)(2,1)S(1)}, bf16[256,256]{1,0:T(8,128)(2,1)}, u32[]{:S(2)}) copy-start(bf16[256,256]{1,0:T(8,128)(2,1)} %param.14) | copy-start | bytes 393220
  0.7 19.9 %collective-permute-start.3 = (bf16[256,512]{1,0:T(8,128)(2,1)}, bf16[256,512]{1,0:T(8,128)(2,1)S(1)}, u32[]{:S(2)}, u32[]{:S(2)}) collective-permute-start(bf16[256,512]{1,0:T(8,128)(2,1)} %refs_0_.2), channel_id=1, source_target_pairs={{0,4},{1,5},{2,6},{3,7},{4,8},{5,9},{6,10},{7,11},{8,12},{9,13},{1... | collective-permute-start | bytes 786440 | tf_op jit(solution)/shard_map/ppermute | solution.py:32
  2.0 30.8 %collective-permute-start.2 = (bf16[256,512]{1,0:T(8,128)(2,1)}, bf16[256,512]{1,0:T(8,128)(2,1)S(1)}, u32[]{:S(2)}, u32[]{:S(2)}) collective-permute-start(bf16[256,512]{1,0:T(8,128)(2,1)} %refs_0_.2), channel_id=1, source_target_pairs={{0,3},{1,0},{2,1},{3,2},{4,7},{5,4},{6,5},{7,6},{8,11},{9,8},{10,9... | collective-permute-start | bytes 786440 | tf_op jit(solution)/shard_map/ppermute | solution.py:32
  2.0 30.8 %collective-permute-start.1 = (bf16[256,512]{1,0:T(8,128)(2,1)}, bf16[256,512]{1,0:T(8,128)(2,1)S(1)}, u32[]{:S(2)}, u32[]{:S(2)}) collective-permute-start(bf16[256,512]{1,0:T(8,128)(2,1)} %refs_0_.2), channel_id=1, source_target_pairs={{0,2},{1,3},{2,0},{3,1},{4,6},{5,7},{6,4},{7,5},{8,10},{9,11},{10,... | collective-permute-start | bytes 786440 | tf_op jit(solution)/shard_map/ppermute | solution.py:32
  5.7 30.1 %collective-permute-start = (bf16[256,512]{1,0:T(8,128)(2,1)}, bf16[256,512]{1,0:T(8,128)(2,1)S(1)}, u32[]{:S(2)}, u32[]{:S(2)}) collective-permute-start(bf16[256,512]{1,0:T(8,128)(2,1)} %refs_0_.2), channel_id=1, source_target_pairs={{0,1},{1,2},{2,3},{3,0},{4,5},{5,6},{6,7},{7,4},{8,9},{9,10},{10,1... | collective-permute-start | bytes 786440 | tf_op jit(solution)/shard_map/ppermute | solution.py:32
  5.7 30.2 %collective-permute-start.4 = (bf16[256,512]{1,0:T(8,128)(2,1)}, bf16[256,512]{1,0:T(8,128)(2,1)S(1)}, u32[]{:S(2)}, u32[]{:S(2)}) collective-permute-start(bf16[256,512]{1,0:T(8,128)(2,1)} %refs_0_.2), channel_id=1, source_target_pairs={{0,8},{1,9},{2,10},{3,11},{4,12},{5,13},{6,14},{7,15},{8,0},{9,1},... | collective-permute-start | bytes 786440 | tf_op jit(solution)/shard_map/ppermute | solution.py:32
  10.2 31.3 %all-to-all-start = ((bf16[16,32,512]{2,1,0:T(8,128)(2,1)}), bf16[16,32,512]{2,1,0:T(8,128)(2,1)S(1)}, u32[]{:S(2)}, u32[]{:S(2)}) async-start(bf16[16,32,512]{2,1,0:T(8,128)(2,1)} %pad_maximum_fusion), calls=%async_computation | async-start | bytes 1048576 | tf_op jit(solution)/shard_map/all_to_all | solution.py:363
  20.6 1.2 copy-start.13
  20.6 15.4 %collective-permute-start.5 = (bf16[256,512]{1,0:T(8,128)(2,1)S(1)}, bf16[256,512]{1,0:T(8,128)(2,1)S(1)}, u32[]{:S(2)}, u32[]{:S(2)}) collective-permute-start(bf16[256,512]{1,0:T(8,128)(2,1)S(1)} %copy-done.12), channel_id=1, source_target_pairs={{0,12},{1,13},{2,14},{3,15},{4,0},{5,1},{6,2},{7,3},{8,4},{9,5},{1... | collective-permute-start | bytes 786440 | tf_op jit(solution)/shard_map/ppermute | solution.py:32
  32.8 22.0 %copy-start.7 = (bf16[1024,256]{1,0:T(8,128)(2,1)}, bf16[1024,256]{1,0:T(8,128)(2,1)S(1)}, u32[]{:S(2)}) copy-start(bf16[1024,256]{1,0:T(8,128)(2,1)S(1)} %copy.14) | copy-start | bytes 1572868
  35.9 31.9 %copy-start = (bf16[3,256,512]{2,1,0:T(8,128)(2,1)}, bf16[3,256,512]{2,1,0:T(8,128)(2,1)S(1)}, u32[]{:S(2)}) copy-start(bf16[3,256,512]{2,1,0:T(8,128)(2,1)S(1)} %stack.25.refs_1_) | copy-start | bytes 2359300
  35.9 5.6 %copy-start.14 = (bf16[256,512]{1,0:T(8,128)(2,1)}, bf16[256,512]{1,0:T(8,128)(2,1)S(1)}, u32[]{:S(2)}) copy-start(bf16[256,512]{1,0:T(8,128)(2,1)S(1)} %collective-permute-done.4.refs_6_) | copy-start | bytes 786436
  35.9 31.8 %copy-start.15 = (bf16[256,512]{1,0:T(8,128)(2,1)}, bf16[256,512]{1,0:T(8,128)(2,1)S(1)}, u32[]{:S(2)}) copy-start(bf16[256,512]{1,0:T(8,128)(2,1)S(1)} %collective-permute-done.5.refs_4_) | copy-start | bytes 786436
  35.9 37.0 %collective-permute-start.8 = (bf16[3,256,512]{2,1,0:T(8,128)(2,1)S(1)}, bf16[3,256,512]{2,1,0:T(8,128)(2,1)}, u32[]{:S(2)}, u32[]{:S(2)}) collective-permute-start(bf16[3,256,512]{2,1,0:T(8,128)(2,1)S(1)} %stack.25.refs_1_), channel_id=1, source_target_pairs={{0,8},{1,9},{2,10},{3,11},{4,12},{5,13},{6,14},{7,15},{8,0},{9,1},... | collective-permute-start | bytes 2359304 | tf_op jit(solution)/shard_map/ppermute | solution.py:32
  39.0 36.0 %collective-permute-start.7 = (bf16[3,256,512]{2,1,0:T(8,128)(2,1)S(1)}, bf16[3,256,512]{2,1,0:T(8,128)(2,1)}, u32[]{:S(2)}, u32[]{:S(2)}) collective-permute-start(bf16[3,256,512]{2,1,0:T(8,128)(2,1)S(1)} %stack.25.refs_1_), channel_id=1, source_target_pairs={{0,12},{1,13},{2,14},{3,15},{4,0},{5,1},{6,2},{7,3},{8,4},{9,5},{1... | collective-permute-start | bytes 2359304 | tf_op jit(solution)/shard_map/ppermute | solution.py:32
  41.0 36.0 %collective-permute-start.6 = (bf16[3,256,512]{2,1,0:T(8,128)(2,1)S(1)}, bf16[3,256,512]{2,1,0:T(8,128)(2,1)}, u32[]{:S(2)}, u32[]{:S(2)}) collective-permute-start(bf16[3,256,512]{2,1,0:T(8,128)(2,1)S(1)} %stack.25.refs_1_), channel_id=1, source_target_pairs={{0,4},{1,5},{2,6},{3,7},{4,8},{5,9},{6,10},{7,11},{8,12},{9,13},{1... | collective-permute-start | bytes 2359304 | tf_op jit(solution)/shard_map/ppermute | solution.py:32
  41.5 20.6 %copy-start.9 = (bf16[16,32,512]{2,1,0:T(8,128)(2,1)}, bf16[16,32,512]{2,1,0:T(8,128)(2,1)S(1)}, u32[]{:S(2)}) copy-start(bf16[16,32,512]{2,1,0:T(8,128)(2,1)S(1)} %all-to-all-done.xf_ref) | copy-start | bytes 1572868
  41.5 30.9 %collective-permute-start.9 = (bf16[4,256,256]{2,1,0:T(8,128)(2,1)S(1)}, bf16[4,256,256]{2,1,0:T(8,128)(2,1)S(1)}, u32[]{:S(2)}, u32[]{:S(2)}) collective-permute-start(bf16[4,256,256]{2,1,0:T(8,128)(2,1)S(1)} %bitcast.20), channel_id=1, source_target_pairs={{0,32},{16,48},{32,0},{48,16},{64,96},{80,112},{96,64},{112,80},{1... | collective-permute-start | bytes 1572872 | tf_op jit(solution)/shard_map/ppermute | solution.py:32
  54.8 27.6 %collective-permute-start.10 = (bf16[4,256,256]{2,1,0:T(8,128)(2,1)S(1)}, bf16[4,256,256]{2,1,0:T(8,128)(2,1)}, u32[]{:S(2)}, u32[]{:S(2)}) collective-permute-start(bf16[4,256,256]{2,1,0:T(8,128)(2,1)S(1)} %bitcast.21), channel_id=1, source_target_pairs={{0,16},{16,0},{32,48},{48,32},{64,80},{80,64},{96,112},{112,96},{1... | collective-permute-start | bytes 1572872 | tf_op jit(solution)/shard_map/ppermute | solution.py:32
  67.8 14.6 %all-to-all-start.1 = ((bf16[16,16,512]{2,1,0:T(8,128)(2,1)}), bf16[16,16,512]{2,1,0:T(8,128)(2,1)S(1)}, u32[]{:S(2)}, u32[]{:S(2)}) async-start(bf16[16,16,512]{2,1,0:T(8,128)(2,1)} %get-tuple-element.34), calls=%async_computation.1 | async-start | bytes 524288 | tf_op jit(solution)/shard_map/all_to_all | solution.py:363
  72.4 11.4 %copy-start.8 = (bf16[4,256,256]{2,1,0:T(8,128)(2,1)}, bf16[4,256,256]{2,1,0:T(8,128)(2,1)S(1)}, u32[]{:S(2)}) copy-start(bf16[4,256,256]{2,1,0:T(8,128)(2,1)S(1)} %collective-permute-done.9.refs_9_) | copy-start | bytes 1572868
  72.5 9.9 %collective-permute-start.14 = (bf16[1,256,256]{2,1,0:T(8,128)(2,1)S(1)}, bf16[1,256,256]{2,1,0:T(8,128)(2,1)S(1)}, u32[]{:S(2)}, u32[]{:S(2)}) collective-permute-start(bf16[1,256,256]{2,1,0:T(8,128)(2,1)S(1)} %get-tuple-element.45), channel_id=1, source_target_pairs={{0,16},{16,0},{32,48},{48,32},{64,80},{80,64},{96,112},{112,96},{1... | collective-permute-start | bytes 393224 | tf_op jit(solution)/shard_map/ppermute | solution.py:32
  72.9 9.5 %collective-permute-start.13 = (bf16[1,256,256]{2,1,0:T(8,128)(2,1)S(1)}, bf16[1,256,256]{2,1,0:T(8,128)(2,1)S(1)}, u32[]{:S(2)}, u32[]{:S(2)}) collective-permute-start(bf16[1,256,256]{2,1,0:T(8,128)(2,1)S(1)} %get-tuple-element.46), channel_id=1, source_target_pairs={{0,16},{16,0},{32,48},{48,32},{64,80},{80,64},{96,112},{112,96},{1... | collective-permute-start | bytes 393224 | tf_op jit(solution)/shard_map/ppermute | solution.py:32
  74.9 7.5 %collective-permute-start.12 = (bf16[1,256,256]{2,1,0:T(8,128)(2,1)S(1)}, bf16[1,256,256]{2,1,0:T(8,128)(2,1)S(1)}, u32[]{:S(2)}, u32[]{:S(2)}) collective-permute-start(bf16[1,256,256]{2,1,0:T(8,128)(2,1)S(1)} %get-tuple-element.47), channel_id=1, source_target_pairs={{0,16},{16,0},{32,48},{48,32},{64,80},{80,64},{96,112},{112,96},{1... | collective-permute-start | bytes 393224 | tf_op jit(solution)/shard_map/ppermute | solution.py:32
  77.0 5.5 %collective-permute-start.11 = (bf16[1,256,256]{2,1,0:T(8,128)(2,1)S(1)}, bf16[1,256,256]{2,1,0:T(8,128)(2,1)S(1)}, u32[]{:S(2)}, u32[]{:S(2)}) collective-permute-start(bf16[1,256,256]{2,1,0:T(8,128)(2,1)S(1)} %get-tuple-element.48), channel_id=1, source_target_pairs={{0,16},{16,0},{32,48},{48,32},{64,80},{80,64},{96,112},{112,96},{1... | collective-permute-start | bytes 393224 | tf_op jit(solution)/shard_map/ppermute | solution.py:32
  82.4 1.4 %copy-start.10 = (bf16[16,16,512]{2,1,0:T(8,128)(2,1)}, bf16[16,16,512]{2,1,0:T(8,128)(2,1)S(1)}, u32[]{:S(2)}) copy-start(bf16[16,16,512]{2,1,0:T(8,128)(2,1)S(1)} %all-to-all-done.1) | copy-start | bytes 786436
  82.4 1.4 %copy-start.16 = (bf16[1,256,256]{2,1,0:T(8,128)(2,1)}, bf16[1,256,256]{2,1,0:T(8,128)(2,1)S(1)}, u32[]{:S(2)}) copy-start(bf16[1,256,256]{2,1,0:T(8,128)(2,1)S(1)} %collective-permute-done.14.refs_14_) | copy-start | bytes 393220
  82.4 0.7 copy-start.17
  82.5 0.7 copy-start.18
  83.2 0.7 copy-start.19
  83.9 28.4 %copy-start.6 = (f32[4,1024,128]{2,1,0:T(8,128)S(1)}, f32[4,1024,128]{2,1,0:T(8,128)}, u32[]{:S(2)}) copy-start(f32[4,1024,128]{2,1,0:T(8,128)} %get-tuple-element.36.spec_ref) | copy-start | bytes 6291460
  90.5 21.8 %copy-start.1 = (bf16[768,256]{1,0:T(8,128)(2,1)S(1)}, bf16[768,256]{1,0:T(8,128)(2,1)}, u32[]{:S(2)}) copy-start(bf16[768,256]{1,0:T(8,128)(2,1)} %constant.72.clone.refs_2_.back_ref) | copy-start | bytes 1179652
  90.5 21.8 %copy-start.2 = (bf16[768,256]{1,0:T(8,128)(2,1)S(1)}, bf16[768,256]{1,0:T(8,128)(2,1)}, u32[]{:S(2)}) copy-start(bf16[768,256]{1,0:T(8,128)(2,1)} %constant.71.clone.refs_1_.second_ref) | copy-start | bytes 1179652
  90.6 21.7 %copy-start.3 = (f32[2,64,128]{2,1,0:T(8,128)S(1)}, f32[2,64,128]{2,1,0:T(8,128)}, u32[]{:S(2)}) copy-start(f32[2,64,128]{2,1,0:T(8,128)} %constant.74.clone.refs_4_.turn_ref) | copy-start | bytes 196612
  90.6 21.7 %copy-start.4 = (bf16[64,384]{1,0:T(8,128)(2,1)S(1)}, bf16[64,384]{1,0:T(8,128)(2,1)}, u32[]{:S(2)}) copy-start(bf16[64,384]{1,0:T(8,128)(2,1)} %constant.73.clone.refs_3_.last_ref) | copy-start | bytes 147460
  90.6 21.7 %copy-start.5 = (bf16[128,128]{1,0:T(8,128)(2,1)S(1)}, bf16[128,128]{1,0:T(8,128)(2,1)}, u32[]{:S(2)}) copy-start(bf16[128,128]{1,0:T(8,128)(2,1)} %constant.70.clone.refs_0_.first_ref) | copy-start | bytes 98308
  90.6 11.7 %collective-permute-start.15 = (bf16[8,256,256]{2,1,0:T(8,128)(2,1)}, bf16[8,256,256]{2,1,0:T(8,128)(2,1)}, u32[]{:S(2)}, u32[]{:S(2)}) collective-permute-start(bf16[8,256,256]{2,1,0:T(8,128)(2,1)} %get-tuple-element.39), channel_id=1, source_target_pairs={{0,16},{16,0},{32,48},{48,32},{64,80},{80,64},{96,112},{112,96},{1... | collective-permute-start | bytes 3145736 | tf_op jit(solution)/shard_map/ppermute | solution.py:32
  90.7 21.6 %all-to-all-start.2 = ((bf16[16,16,512]{2,1,0:T(8,128)(2,1)}), bf16[16,16,512]{2,1,0:T(8,128)(2,1)S(1)}, u32[]{:S(2)}, u32[]{:S(2)}) async-start(bf16[16,16,512]{2,1,0:T(8,128)(2,1)} %bitcast.24), calls=%async_computation.2 | async-start | bytes 524288 | tf_op jit(solution)/shard_map/all_to_all | solution.py:363
  104.6 17.4 %collective-permute-start.16 = (bf16[2,256,256]{2,1,0:T(8,128)(2,1)}, bf16[2,256,256]{2,1,0:T(8,128)(2,1)}, u32[]{:S(2)}, u32[]{:S(2)}) collective-permute-start(bf16[2,256,256]{2,1,0:T(8,128)(2,1)} %get-tuple-element.40), channel_id=1, source_target_pairs={{0,64},{16,80},{32,96},{48,112},{64,128},{80,144},{96,160},{112,17... | collective-permute-start | bytes 786440 | tf_op jit(solution)/shard_map/ppermute | solution.py:32
  105.8 16.2 %collective-permute-start.18 = (bf16[2,256,256]{2,1,0:T(8,128)(2,1)}, bf16[2,256,256]{2,1,0:T(8,128)(2,1)}, u32[]{:S(2)}, u32[]{:S(2)}) collective-permute-start(bf16[2,256,256]{2,1,0:T(8,128)(2,1)} %get-tuple-element.41), channel_id=1, source_target_pairs={{0,192},{16,208},{32,224},{48,240},{64,0},{80,16},{96,32},{112,48}... | collective-permute-start | bytes 786440 | tf_op jit(solution)/shard_map/ppermute | solution.py:32
  106.1 16.0 %collective-permute-start.17 = (bf16[2,256,256]{2,1,0:T(8,128)(2,1)S(1)}, bf16[2,256,256]{2,1,0:T(8,128)(2,1)}, u32[]{:S(2)}, u32[]{:S(2)}) collective-permute-start(bf16[2,256,256]{2,1,0:T(8,128)(2,1)S(1)} %get-tuple-element.42), channel_id=1, source_target_pairs={{0,128},{16,144},{32,160},{48,176},{64,192},{80,208},{96,224},{112... | collective-permute-start | bytes 786440 | tf_op jit(solution)/shard_map/ppermute | solution.py:32
  116.3 21.0 %all-to-all-start.3 = ((bf16[16,32,512]{2,1,0:T(8,128)(2,1)}), bf16[16,32,512]{2,1,0:T(8,128)(2,1)S(1)}, u32[]{:S(2)}, u32[]{:S(2)}) async-start(bf16[16,32,512]{2,1,0:T(8,128)(2,1)} %grads.1), calls=%async_computation.3 | async-start | bytes 1048576 | tf_op jit(solution)/shard_map/all_to_all | solution.py:363
  123.5 13.0 %collective-permute-start.19 = (bf16[256,256]{1,0:T(8,128)(2,1)S(1)}, bf16[256,256]{1,0:T(8,128)(2,1)S(1)}, u32[]{:S(2)}, u32[]{:S(2)}) collective-permute-start(bf16[256,256]{1,0:T(8,128)(2,1)S(1)} %slice_bitcast_fusion), channel_id=1, source_target_pairs={{0,32},{16,48},{32,0},{48,16},{64,96},{80,112},{96,64},{112,80},{1... | collective-permute-start | bytes 393224 | tf_op jit(solution)/shard_map/ppermute | solution.py:32

commit v12 on v11

--- a/solution.py
+++ b/solution.py
@@ -309,13 +309,14 @@
     outs[1].start()
     gated = (gates * mixed).astype(BF).T
     for other, target in ((1, other_hbm), (0, same_hbm)):
-        for dx in range(4):
-            at = other * 8 + 2 * dx
-            for dzh in range(2):
-                part = dot(held[grad_slot(where_ref, other, dx, dzh)], gated)
-                sums[at + dzh] = (part * (SEQ**-0.5)).astype(BF)
-            sem = out_sems.at[2 + other * 4 + dx]
-            out = pltpu.make_async_copy(sums.at[pl.ds(at, 2)], target.at[pl.ds(2 * dx, 2)], sem)
+        for half in range(2):
+            places = [(2 * half + i, dzh) for i in range(2) for dzh in range(2)]
+            blocks = [held[grad_slot(where_ref, other, dx, dzh)] for dx, dzh in places]
+            part = dot(jnp.concatenate(blocks, axis=0), gated)
+            at = other * 8 + 4 * half
+            sums[at : at + 4] = (part * (SEQ**-0.5)).astype(BF).reshape(4, 256, 256)
+            sem = out_sems.at[2 + other * 2 + half]
+            out = pltpu.make_async_copy(sums.at[pl.ds(at, 4)], target.at[pl.ds(4 * half, 4)], sem)
             out.start()
             outs.append(out)
     for out in outs:
@@ -352,7 +353,7 @@
         out_shape=(tile, tile, eight, eight),
         in_specs=[pl.BlockSpec(memory_space=pltpu.SMEM)] + [in_hbm()] * 17,
         out_specs=(in_hbm(),) * 4,
-        scratch_shapes=[HELD, SQUARES, TILE, TILE, TILE, TILE, SQUARES, DMA((8,)), DMA((9,)), DMA((10,))],
+        scratch_shapes=[HELD, SQUARES, TILE, TILE, TILE, TILE, SQUARES, DMA((8,)), DMA((9,)), DMA((6,))],
         compiler_params=params(60),
         cost_estimate=pl.CostEstimate(flops=4 * CH * TOK * 4096, bytes_accessed=9 << 20, transcendentals=0),
         name="products",

time: 141 us -> 141 us (level)
  no operation moved by 1% of the time
where the time goes in v12:
time: 141 us; the launch traced here: 138 us
  starting transfers between devices  78.5 us (56%)
  waiting for transfers between devices  21.9 us (16%)
  Pallas kernels  16.5 us (12%)
  blocking collectives  10.9 us (8%)
  other arithmetic  6.31 us (4%)
  local copies, waits for them, and re-layouts  3.1 us (2%)
    ppermute x20, starting transfers between devices, send(): return lax.ppermute(value, axis, shift_pairs(stride, size, by))  46.2 us
    all_to_all x4, starting transfers between devices, exchange(): return lax.all_to_all(value, 'ctx', split_axis=0, concat_axis=0, tiled=True)  32.3 us
    ppermute x20, waiting for transfers between devices, send(): return lax.ppermute(value, axis, shift_pairs(stride, size, by))  12.7 us
    all_gather x1, blocking collectives, on_device(): w_line = lax.all_gather(w_own.T, 'ctx', axis_index_groups=LINES_X)  10.9 us
    all_to_all x4, waiting for transfers between devices, exchange(): return lax.all_to_all(value, 'ctx', split_axis=0, concat_axis=0, tiled=True)  9.23 us
    pallas_call x1, Pallas kernels, products_call(): pl.pallas_call(products_kernel, out_shape=(tile, tile, eight, eight), in_...  6.9 us
    pallas_call x1, Pallas kernels, conv_call(): pl.pallas_call(conv_kernel, out_shape=(jax.ShapeDtypeStruct((16, FEW, TOK...  5.65 us
    convert_element_type x3, other arithmetic, add(): return total.astype(BF)  4.45 us
  transfers between devices with their start and end apart: 24, of which 5 were waited for; matrix products, arithmetic and copies ran while one was open for 5% of the time, Pallas kernels for 7%

profile of v12, /device:TPU:67, one launch (start us, length us, event | category | flops | bytes accessed | tf_op | source)
XLA Modules:
  0.0 138.3 jit_solution(8151967695820475217)
XLA Ops:
  0.6 0.0 copy-start.12
  0.7 1.4 collective-permute-start.3
  2.0 0.0 collective-permute-start.2
  2.0 3.7 %collective-permute-start.1 = (bf16[256,512]{1,0:T(8,128)(2,1)}, bf16[256,512]{1,0:T(8,128)(2,1)S(1)}, u32[]{:S(2)}, u32[]{:S(2)}) collective-permute-start(bf16[256,512]{1,0:T(8,128)(2,1)} %refs_0_.2), channel_id=1, source_target_pairs={{0,2},{1,3},{2,0},{3,1},{4,6},{5,7},{6,4},{7,5},{8,10},{9,11},{10,... | collective-permute-start | bytes 786440 | tf_op jit(solution)/shard_map/ppermute | solution.py:32
  5.7 2.6 %collective-permute-start.4 = (bf16[256,512]{1,0:T(8,128)(2,1)}, bf16[256,512]{1,0:T(8,128)(2,1)S(1)}, u32[]{:S(2)}, u32[]{:S(2)}) collective-permute-start(bf16[256,512]{1,0:T(8,128)(2,1)} %refs_0_.2), channel_id=1, source_target_pairs={{0,8},{1,9},{2,10},{3,11},{4,12},{5,13},{6,14},{7,15},{8,0},{9,1},... | collective-permute-start | bytes 786440 | tf_op jit(solution)/shard_map/ppermute | solution.py:32
  8.4 1.9 %pad_maximum_fusion = bf16[16,32,512]{2,1,0:T(8,128)(2,1)} fusion(bf16[16,16,512]{2,1,0:T(8,128)(2,1)} %bitcast.25, bf16[16,16,512]{2,1,0:T(8,128)(2,1)} %bitcast.26), kind=kLoop, calls=%fused_computation | loop fusion | flops 1048576 | bytes 1048576 | tf_op jit(solution)/shard_map/concatenate | solution.py:380
  10.2 10.3 %all-to-all-start = ((bf16[16,32,512]{2,1,0:T(8,128)(2,1)}), bf16[16,32,512]{2,1,0:T(8,128)(2,1)S(1)}, u32[]{:S(2)}, u32[]{:S(2)}) async-start(bf16[16,32,512]{2,1,0:T(8,128)(2,1)} %pad_maximum_fusion), calls=%async_computation | async-start | bytes 1048576 | tf_op jit(solution)/shard_map/all_to_all | solution.py:364
  20.5 0.0 collective-permute-done.3.refs_2_
  20.6 0.0 copy-start.13
  20.6 1.1 collective-permute-start.5
  21.7 10.9 %all-gather = bf16[1024,256]{0,1:T(8,128)(2,1)S(1)} all-gather(bf16[256,256]{0,1:T(8,128)(2,1)S(1)} %bitcast.29), channel_id=2, replica_groups={{0,64,128,192},{16,80,144,208},{32,96,160,224},{48,112,176,240},{1,65,1..., dimensions={0}, use_global_device_ids=true | all-gather | bytes 655360 | tf_op jit(solution)/shard_map/all_gather | solution.py:388
  32.6 0.2 copy.14
  32.8 0.0 collective-permute-done.2.refs_2_
  32.9 3.0 %collective-permute-done.refs_0_ = bf16[256,512]{1,0:T(8,128)(2,1)S(1)} collective-permute-done((bf16[256,512]{1,0:T(8,128)(2,1)}, bf16[256,512]{1,0:T(8,128)(2,1)S(1)}, u32[]{:S(2)}, u32[]{:S(2)}) %collective-permute-start) | collective-permute-done | bytes 262176 | tf_op jit(solution)/shard_map/ppermute | solution.py:32
  35.8 0.1 stack.25.refs_1_
  35.9 0.0 collective-permute-done.5.refs_4_
  35.9 0.0 copy-start.15
  35.9 3.0 %collective-permute-start.8 = (bf16[3,256,512]{2,1,0:T(8,128)(2,1)S(1)}, bf16[3,256,512]{2,1,0:T(8,128)(2,1)}, u32[]{:S(2)}, u32[]{:S(2)}) collective-permute-start(bf16[3,256,512]{2,1,0:T(8,128)(2,1)S(1)} %stack.25.refs_1_), channel_id=1, source_target_pairs={{0,8},{1,9},{2,10},{3,11},{4,12},{5,13},{6,14},{7,15},{8,0},{9,1},... | collective-permute-start | bytes 2359304 | tf_op jit(solution)/shard_map/ppermute | solution.py:32
  39.0 2.1 %collective-permute-start.7 = (bf16[3,256,512]{2,1,0:T(8,128)(2,1)S(1)}, bf16[3,256,512]{2,1,0:T(8,128)(2,1)}, u32[]{:S(2)}, u32[]{:S(2)}) collective-permute-start(bf16[3,256,512]{2,1,0:T(8,128)(2,1)S(1)} %stack.25.refs_1_), channel_id=1, source_target_pairs={{0,12},{1,13},{2,14},{3,15},{4,0},{5,1},{6,2},{7,3},{8,4},{9,5},{1... | collective-permute-start | bytes 2359304 | tf_op jit(solution)/shard_map/ppermute | solution.py:32
  41.0 0.5 collective-permute-start.6
  41.5 0.0 all-to-all-done.xf_ref
  41.5 13.3 %collective-permute-start.9 = (bf16[4,256,256]{2,1,0:T(8,128)(2,1)S(1)}, bf16[4,256,256]{2,1,0:T(8,128)(2,1)S(1)}, u32[]{:S(2)}, u32[]{:S(2)}) collective-permute-start(bf16[4,256,256]{2,1,0:T(8,128)(2,1)S(1)} %bitcast.20), channel_id=1, source_target_pairs={{0,32},{16,48},{32,0},{48,16},{64,96},{80,112},{96,64},{112,80},{1... | collective-permute-start | bytes 1572872 | tf_op jit(solution)/shard_map/ppermute | solution.py:32
  54.8 7.3 %collective-permute-start.10 = (bf16[4,256,256]{2,1,0:T(8,128)(2,1)S(1)}, bf16[4,256,256]{2,1,0:T(8,128)(2,1)}, u32[]{:S(2)}, u32[]{:S(2)}) collective-permute-start(bf16[4,256,256]{2,1,0:T(8,128)(2,1)S(1)} %bitcast.21), channel_id=1, source_target_pairs={{0,16},{16,0},{32,48},{48,32},{64,80},{80,64},{96,112},{112,96},{1... | collective-permute-start | bytes 1572872 | tf_op jit(solution)/shard_map/ppermute | solution.py:32
  62.1 5.6 %conv.1 = (bf16[16,16,512]{2,1,0:T(8,128)(2,1)}, f32[4,1024,128]{2,1,0:T(8,128)}) custom-call(bf16[16,32,512]{2,1,0:T(8,128)(2,1)} %copy-done.9, bf16[128,128]{1,0:T(8,128)(2,1)} %constant.70.clone.refs_0_.first_ref, bf16[768,256]{1,0:T(8,128)(2,1)} %constant.71.clone.refs_1_.second_ref, bf16[768,256]{1,0:T(8,128)(2,1)} %constant.72.clone.refs_2_.back_ref, ...), custom_call_target="tpu_custom_call" | custom-call | flops 1000000000 | bytes 4194304 | tf_op jit(solution)/shard_map/conv/pallas_call | solution.py:228
  67.8 4.6 %all-to-all-start.1 = ((bf16[16,16,512]{2,1,0:T(8,128)(2,1)}), bf16[16,16,512]{2,1,0:T(8,128)(2,1)S(1)}, u32[]{:S(2)}, u32[]{:S(2)}) async-start(bf16[16,16,512]{2,1,0:T(8,128)(2,1)} %get-tuple-element.34), calls=%async_computation.1 | async-start | bytes 524288 | tf_op jit(solution)/shard_map/all_to_all | solution.py:364
  72.4 0.0 collective-permute-done.9.refs_9_
  72.5 0.4 collective-permute-start.14
  72.9 0.0 collective-permute-done.8.refs_7_
  72.9 0.1 collective-permute-start.13
  73.1 1.8 %collective-permute-done.7.refs_5_ = bf16[3,256,512]{2,1,0:T(8,128)(2,1)} collective-permute-done((bf16[3,256,512]{2,1,0:T(8,128)(2,1)S(1)}, bf16[3,256,512]{2,1,0:T(8,128)(2,1)}, u32[]{:S(2)}, u32[]{:S(2)}) %collective-permute-start.7) | collective-permute-done | bytes 786464 | tf_op jit(solution)/shard_map/ppermute | solution.py:32
  74.9 2.1 %collective-permute-start.12 = (bf16[1,256,256]{2,1,0:T(8,128)(2,1)S(1)}, bf16[1,256,256]{2,1,0:T(8,128)(2,1)S(1)}, u32[]{:S(2)}, u32[]{:S(2)}) collective-permute-start(bf16[1,256,256]{2,1,0:T(8,128)(2,1)S(1)} %get-tuple-element.47), channel_id=1, source_target_pairs={{0,16},{16,0},{32,48},{48,32},{64,80},{80,64},{96,112},{112,96},{1... | collective-permute-start | bytes 393224 | tf_op jit(solution)/shard_map/ppermute | solution.py:32
  77.0 0.0 collective-permute-done.6.refs_3_
  77.0 0.0 collective-permute-start.11
  77.0 0.6 stack.24.where_ref
  77.6 4.8 %all-to-all-done.1 = bf16[16,16,512]{2,1,0:T(8,128)(2,1)S(1)} async-done(((bf16[16,16,512]{2,1,0:T(8,128)(2,1)}), bf16[16,16,512]{2,1,0:T(8,128)(2,1)S(1)}, u32[]{:S(2)}, u32[]{:S(2)}) %all-to-all-start.1) | async-done | bytes 262176 | tf_op jit(solution)/shard_map/all_to_all | solution.py:364
  82.4 0.0 collective-permute-done.10.refs_10_
  82.4 0.0 collective-permute-done.14.refs_14_
  82.5 0.0 collective-permute-done.12.refs_12_
  82.5 0.0 collective-permute-done.11.refs_11_
  82.5 0.7 copy-done.17
  83.1 0.0 copy-done.18
  83.2 0.7 copy-done.19
  83.9 6.9 %products.1 = (bf16[256,512]{1,0:T(8,128)(2,1)}, bf16[256,512]{1,0:T(8,128)(2,1)}, bf16[8,256,256]{2,1,0:T(8,128)(2,1)}, bf16[8,256,256]{2,1,0:T(8,128)(2,1)}) custom-call(s32[5]{0:T(128)} %stack.24.where_ref, bf16[256,512]{1,0:T(8,128)(2,1)} %refs_0_.2, bf16[3,256,512]{2,1,0:T(8,128)(2,1)} %copy-done, bf16[256,512]{1,0:T(8,128)(2,1)} %copy-done.13, ...), custom_call_target="tpu_custom_call" | custom-call | flops 2147483648 | bytes 9437184 | tf_op jit(solution)/shard_map/products/pallas_call | solution.py:351
  90.8 0.0 copy-start.1
  90.8 0.0 copy-start.2
  90.8 0.0 copy-start.3
  90.8 0.0 copy-start.4
  90.8 0.0 copy-start.5
  90.8 0.1 collective-permute-start.15
  90.9 11.6 %all-to-all-start.2 = ((bf16[16,16,512]{2,1,0:T(8,128)(2,1)}), bf16[16,16,512]{2,1,0:T(8,128)(2,1)S(1)}, u32[]{:S(2)}, u32[]{:S(2)}) async-start(bf16[16,16,512]{2,1,0:T(8,128)(2,1)} %bitcast.24), calls=%async_computation.2 | async-start | bytes 524288 | tf_op jit(solution)/shard_map/all_to_all | solution.py:364
  102.5 0.0 collective-permute-done.15
  102.5 2.3 %add_convert_fusion.3 = (bf16[2,256,256]{2,1,0:T(8,128)(2,1)}, bf16[2,256,256]{2,1,0:T(8,128)(2,1)}, bf16[2,256,256]{2,1,0:T(8,128)(2,1)S(1)}) fusion(bf16[8,256,256]{2,1,0:T(8,128)(2,1)} %collective-permute-done.15, bf16[8,256,256]{2,1,0:T(8,128)(2,1)} %get-tuple-element.38), kind=kLoop, calls=%fused_computation.4 | loop fusion | flops 1572864 | bytes 2359296 | tf_op jit(solution)/shard_map/convert_element_type | solution.py:371
  104.9 1.2 collective-permute-start.16
  106.1 0.3 collective-permute-start.18
  106.3 1.8 %collective-permute-start.17 = (bf16[2,256,256]{2,1,0:T(8,128)(2,1)S(1)}, bf16[2,256,256]{2,1,0:T(8,128)(2,1)}, u32[]{:S(2)}, u32[]{:S(2)}) collective-permute-start(bf16[2,256,256]{2,1,0:T(8,128)(2,1)S(1)} %get-tuple-element.42), channel_id=1, source_target_pairs={{0,128},{16,144},{32,160},{48,176},{64,192},{80,208},{96,224},{112... | collective-permute-start | bytes 786440 | tf_op jit(solution)/shard_map/ppermute | solution.py:32
  108.1 4.4 %all-to-all-done.2.p_ref = bf16[16,16,512]{2,1,0:T(8,128)(2,1)S(1)} async-done(((bf16[16,16,512]{2,1,0:T(8,128)(2,1)}), bf16[16,16,512]{2,1,0:T(8,128)(2,1)S(1)}, u32[]{:S(2)}, u32[]{:S(2)}) %all-to-all-start.2) | async-done | bytes 262176 | tf_op jit(solution)/shard_map/all_to_all | solution.py:364
  112.6 3.9 %grads.1 = bf16[16,32,512]{2,1,0:T(8,128)(2,1)} custom-call(bf16[16,16,512]{2,1,0:T(8,128)(2,1)S(1)} %all-to-all-done.2.p_ref, bf16[128,128]{1,0:T(8,128)(2,1)S(1)} %copy-done.5, bf16[768,256]{1,0:T(8,128)(2,1)S(1)} %copy-done.2, bf16[768,256]{1,0:T(8,128)(2,1)S(1)} %copy-done.1, bf16[64,384]{1,0:T(8,128)(2,1)S(1)} %copy-done.4, ...), custom_call_target="tpu_custom_call" | custom-call | flops 10000000000 | bytes 4194304 | tf_op jit(solution)/shard_map/grads/pallas_call | solution.py:244
  116.5 5.8 %all-to-all-start.3 = ((bf16[16,32,512]{2,1,0:T(8,128)(2,1)}), bf16[16,32,512]{2,1,0:T(8,128)(2,1)S(1)}, u32[]{:S(2)}, u32[]{:S(2)}) async-start(bf16[16,32,512]{2,1,0:T(8,128)(2,1)} %grads.1), calls=%async_computation.3 | async-start | bytes 1048576 | tf_op jit(solution)/shard_map/all_to_all | solution.py:364
  122.3 0.0 collective-permute-done.16
  122.3 1.4 %add_convert_fusion = bf16[2,256,256]{2,1,0:T(8,128)(2,1)S(1)} fusion(bf16[2,256,256]{2,1,0:T(8,128)(2,1)} %collective-permute-done.18, bf16[2,256,256]{2,1,0:T(8,128)(2,1)} %collective-permute-done.17, bf16[2,256,256]{2,1,0:T(8,128)(2,1)} %collective-permute-done.16, bf16[8,256,256]{2,1,0:T(8,128)(2,1)} %collective-permute-done.15, ...), kind=kLoop, calls=%fused_computation.1 | loop fusion | flops 1572864 | bytes 1572864 | tf_op jit(solution)/shard_map/convert_element_type | solution.py:371
  123.8 5.2 %collective-permute-start.19 = (bf16[256,256]{1,0:T(8,128)(2,1)S(1)}, bf16[256,256]{1,0:T(8,128)(2,1)S(1)}, u32[]{:S(2)}, u32[]{:S(2)}) collective-permute-start(bf16[256,256]{1,0:T(8,128)(2,1)S(1)} %slice_bitcast_fusion), channel_id=1, source_target_pairs={{0,32},{16,48},{32,0},{48,16},{64,96},{80,112},{96,64},{112,80},{1... | collective-permute-start | bytes 393224 | tf_op jit(solution)/shard_map/ppermute | solution.py:32
  128.9 7.8 %collective-permute-done.19 = bf16[256,256]{1,0:T(8,128)(2,1)S(1)} collective-permute-done((bf16[256,256]{1,0:T(8,128)(2,1)S(1)}, bf16[256,256]{1,0:T(8,128)(2,1)S(1)}, u32[]{:S(2)}, u32[]{:S(2)}) %collective-permute-start.19) | collective-permute-done | bytes 131104 | tf_op jit(solution)/shard_map/ppermute | solution.py:32
  136.8 0.7 fusion
  137.5 0.8 fusion.1
  (38 shorter events, 0.1 us)
Async XLA Ops:
  0.6 19.9 %copy-start.12 = (bf16[256,512]{1,0:T(8,128)(2,1)S(1)}, bf16[256,512]{1,0:T(8,128)(2,1)}, u32[]{:S(2)}) copy-start(bf16[256,512]{1,0:T(8,128)(2,1)} %refs_0_.2) | copy-start | bytes 786436
  0.6 21.1 %copy-start.11 = (bf16[256,256]{1,0:T(8,128)(2,1)S(1)}, bf16[256,256]{1,0:T(8,128)(2,1)}, u32[]{:S(2)}) copy-start(bf16[256,256]{1,0:T(8,128)(2,1)} %param.14) | copy-start | bytes 393220
  0.7 19.9 %collective-permute-start.3 = (bf16[256,512]{1,0:T(8,128)(2,1)}, bf16[256,512]{1,0:T(8,128)(2,1)S(1)}, u32[]{:S(2)}, u32[]{:S(2)}) collective-permute-start(bf16[256,512]{1,0:T(8,128)(2,1)} %refs_0_.2), channel_id=1, source_target_pairs={{0,4},{1,5},{2,6},{3,7},{4,8},{5,9},{6,10},{7,11},{8,12},{9,13},{1... | collective-permute-start | bytes 786440 | tf_op jit(solution)/shard_map/ppermute | solution.py:32
  2.0 30.8 %collective-permute-start.2 = (bf16[256,512]{1,0:T(8,128)(2,1)}, bf16[256,512]{1,0:T(8,128)(2,1)S(1)}, u32[]{:S(2)}, u32[]{:S(2)}) collective-permute-start(bf16[256,512]{1,0:T(8,128)(2,1)} %refs_0_.2), channel_id=1, source_target_pairs={{0,3},{1,0},{2,1},{3,2},{4,7},{5,4},{6,5},{7,6},{8,11},{9,8},{10,9... | collective-permute-start | bytes 786440 | tf_op jit(solution)/shard_map/ppermute | solution.py:32
  2.0 30.8 %collective-permute-start.1 = (bf16[256,512]{1,0:T(8,128)(2,1)}, bf16[256,512]{1,0:T(8,128)(2,1)S(1)}, u32[]{:S(2)}, u32[]{:S(2)}) collective-permute-start(bf16[256,512]{1,0:T(8,128)(2,1)} %refs_0_.2), channel_id=1, source_target_pairs={{0,2},{1,3},{2,0},{3,1},{4,6},{5,7},{6,4},{7,5},{8,10},{9,11},{10,... | collective-permute-start | bytes 786440 | tf_op jit(solution)/shard_map/ppermute | solution.py:32
  5.7 30.1 %collective-permute-start = (bf16[256,512]{1,0:T(8,128)(2,1)}, bf16[256,512]{1,0:T(8,128)(2,1)S(1)}, u32[]{:S(2)}, u32[]{:S(2)}) collective-permute-start(bf16[256,512]{1,0:T(8,128)(2,1)} %refs_0_.2), channel_id=1, source_target_pairs={{0,1},{1,2},{2,3},{3,0},{4,5},{5,6},{6,7},{7,4},{8,9},{9,10},{10,1... | collective-permute-start | bytes 786440 | tf_op jit(solution)/shard_map/ppermute | solution.py:32
  5.7 30.2 %collective-permute-start.4 = (bf16[256,512]{1,0:T(8,128)(2,1)}, bf16[256,512]{1,0:T(8,128)(2,1)S(1)}, u32[]{:S(2)}, u32[]{:S(2)}) collective-permute-start(bf16[256,512]{1,0:T(8,128)(2,1)} %refs_0_.2), channel_id=1, source_target_pairs={{0,8},{1,9},{2,10},{3,11},{4,12},{5,13},{6,14},{7,15},{8,0},{9,1},... | collective-permute-start | bytes 786440 | tf_op jit(solution)/shard_map/ppermute | solution.py:32
  10.2 31.3 %all-to-all-start = ((bf16[16,32,512]{2,1,0:T(8,128)(2,1)}), bf16[16,32,512]{2,1,0:T(8,128)(2,1)S(1)}, u32[]{:S(2)}, u32[]{:S(2)}) async-start(bf16[16,32,512]{2,1,0:T(8,128)(2,1)} %pad_maximum_fusion), calls=%async_computation | async-start | bytes 1048576 | tf_op jit(solution)/shard_map/all_to_all | solution.py:364
  20.6 1.2 copy-start.13
  20.6 15.4 %collective-permute-start.5 = (bf16[256,512]{1,0:T(8,128)(2,1)S(1)}, bf16[256,512]{1,0:T(8,128)(2,1)S(1)}, u32[]{:S(2)}, u32[]{:S(2)}) collective-permute-start(bf16[256,512]{1,0:T(8,128)(2,1)S(1)} %copy-done.12), channel_id=1, source_target_pairs={{0,12},{1,13},{2,14},{3,15},{4,0},{5,1},{6,2},{7,3},{8,4},{9,5},{1... | collective-permute-start | bytes 786440 | tf_op jit(solution)/shard_map/ppermute | solution.py:32
  32.8 22.0 %copy-start.7 = (bf16[1024,256]{1,0:T(8,128)(2,1)}, bf16[1024,256]{1,0:T(8,128)(2,1)S(1)}, u32[]{:S(2)}) copy-start(bf16[1024,256]{1,0:T(8,128)(2,1)S(1)} %copy.14) | copy-start | bytes 1572868
  35.9 31.9 %copy-start = (bf16[3,256,512]{2,1,0:T(8,128)(2,1)}, bf16[3,256,512]{2,1,0:T(8,128)(2,1)S(1)}, u32[]{:S(2)}) copy-start(bf16[3,256,512]{2,1,0:T(8,128)(2,1)S(1)} %stack.25.refs_1_) | copy-start | bytes 2359300
  35.9 5.6 %copy-start.14 = (bf16[256,512]{1,0:T(8,128)(2,1)}, bf16[256,512]{1,0:T(8,128)(2,1)S(1)}, u32[]{:S(2)}) copy-start(bf16[256,512]{1,0:T(8,128)(2,1)S(1)} %collective-permute-done.4.refs_6_) | copy-start | bytes 786436
  35.9 31.8 %copy-start.15 = (bf16[256,512]{1,0:T(8,128)(2,1)}, bf16[256,512]{1,0:T(8,128)(2,1)S(1)}, u32[]{:S(2)}) copy-start(bf16[256,512]{1,0:T(8,128)(2,1)S(1)} %collective-permute-done.5.refs_4_) | copy-start | bytes 786436
  35.9 37.0 %collective-permute-start.8 = (bf16[3,256,512]{2,1,0:T(8,128)(2,1)S(1)}, bf16[3,256,512]{2,1,0:T(8,128)(2,1)}, u32[]{:S(2)}, u32[]{:S(2)}) collective-permute-start(bf16[3,256,512]{2,1,0:T(8,128)(2,1)S(1)} %stack.25.refs_1_), channel_id=1, source_target_pairs={{0,8},{1,9},{2,10},{3,11},{4,12},{5,13},{6,14},{7,15},{8,0},{9,1},... | collective-permute-start | bytes 2359304 | tf_op jit(solution)/shard_map/ppermute | solution.py:32
  39.0 36.0 %collective-permute-start.7 = (bf16[3,256,512]{2,1,0:T(8,128)(2,1)S(1)}, bf16[3,256,512]{2,1,0:T(8,128)(2,1)}, u32[]{:S(2)}, u32[]{:S(2)}) collective-permute-start(bf16[3,256,512]{2,1,0:T(8,128)(2,1)S(1)} %stack.25.refs_1_), channel_id=1, source_target_pairs={{0,12},{1,13},{2,14},{3,15},{4,0},{5,1},{6,2},{7,3},{8,4},{9,5},{1... | collective-permute-start | bytes 2359304 | tf_op jit(solution)/shard_map/ppermute | solution.py:32
  41.0 36.0 %collective-permute-start.6 = (bf16[3,256,512]{2,1,0:T(8,128)(2,1)S(1)}, bf16[3,256,512]{2,1,0:T(8,128)(2,1)}, u32[]{:S(2)}, u32[]{:S(2)}) collective-permute-start(bf16[3,256,512]{2,1,0:T(8,128)(2,1)S(1)} %stack.25.refs_1_), channel_id=1, source_target_pairs={{0,4},{1,5},{2,6},{3,7},{4,8},{5,9},{6,10},{7,11},{8,12},{9,13},{1... | collective-permute-start | bytes 2359304 | tf_op jit(solution)/shard_map/ppermute | solution.py:32
  41.5 20.6 %copy-start.9 = (bf16[16,32,512]{2,1,0:T(8,128)(2,1)}, bf16[16,32,512]{2,1,0:T(8,128)(2,1)S(1)}, u32[]{:S(2)}) copy-start(bf16[16,32,512]{2,1,0:T(8,128)(2,1)S(1)} %all-to-all-done.xf_ref) | copy-start | bytes 1572868
  41.5 30.9 %collective-permute-start.9 = (bf16[4,256,256]{2,1,0:T(8,128)(2,1)S(1)}, bf16[4,256,256]{2,1,0:T(8,128)(2,1)S(1)}, u32[]{:S(2)}, u32[]{:S(2)}) collective-permute-start(bf16[4,256,256]{2,1,0:T(8,128)(2,1)S(1)} %bitcast.20), channel_id=1, source_target_pairs={{0,32},{16,48},{32,0},{48,16},{64,96},{80,112},{96,64},{112,80},{1... | collective-permute-start | bytes 1572872 | tf_op jit(solution)/shard_map/ppermute | solution.py:32
  54.8 27.6 %collective-permute-start.10 = (bf16[4,256,256]{2,1,0:T(8,128)(2,1)S(1)}, bf16[4,256,256]{2,1,0:T(8,128)(2,1)}, u32[]{:S(2)}, u32[]{:S(2)}) collective-permute-start(bf16[4,256,256]{2,1,0:T(8,128)(2,1)S(1)} %bitcast.21), channel_id=1, source_target_pairs={{0,16},{16,0},{32,48},{48,32},{64,80},{80,64},{96,112},{112,96},{1... | collective-permute-start | bytes 1572872 | tf_op jit(solution)/shard_map/ppermute | solution.py:32
  67.8 14.6 %all-to-all-start.1 = ((bf16[16,16,512]{2,1,0:T(8,128)(2,1)}), bf16[16,16,512]{2,1,0:T(8,128)(2,1)S(1)}, u32[]{:S(2)}, u32[]{:S(2)}) async-start(bf16[16,16,512]{2,1,0:T(8,128)(2,1)} %get-tuple-element.34), calls=%async_computation.1 | async-start | bytes 524288 | tf_op jit(solution)/shard_map/all_to_all | solution.py:364
  72.4 11.4 %copy-start.8 = (bf16[4,256,256]{2,1,0:T(8,128)(2,1)}, bf16[4,256,256]{2,1,0:T(8,128)(2,1)S(1)}, u32[]{:S(2)}) copy-start(bf16[4,256,256]{2,1,0:T(8,128)(2,1)S(1)} %collective-permute-done.9.refs_9_) | copy-start | bytes 1572868
  72.5 9.9 %collective-permute-start.14 = (bf16[1,256,256]{2,1,0:T(8,128)(2,1)S(1)}, bf16[1,256,256]{2,1,0:T(8,128)(2,1)S(1)}, u32[]{:S(2)}, u32[]{:S(2)}) collective-permute-start(bf16[1,256,256]{2,1,0:T(8,128)(2,1)S(1)} %get-tuple-element.45), channel_id=1, source_target_pairs={{0,16},{16,0},{32,48},{48,32},{64,80},{80,64},{96,112},{112,96},{1... | collective-permute-start | bytes 393224 | tf_op jit(solution)/shard_map/ppermute | solution.py:32
  72.9 9.5 %collective-permute-start.13 = (bf16[1,256,256]{2,1,0:T(8,128)(2,1)S(1)}, bf16[1,256,256]{2,1,0:T(8,128)(2,1)S(1)}, u32[]{:S(2)}, u32[]{:S(2)}) collective-permute-start(bf16[1,256,256]{2,1,0:T(8,128)(2,1)S(1)} %get-tuple-element.46), channel_id=1, source_target_pairs={{0,16},{16,0},{32,48},{48,32},{64,80},{80,64},{96,112},{112,96},{1... | collective-permute-start | bytes 393224 | tf_op jit(solution)/shard_map/ppermute | solution.py:32
  74.9 7.5 %collective-permute-start.12 = (bf16[1,256,256]{2,1,0:T(8,128)(2,1)S(1)}, bf16[1,256,256]{2,1,0:T(8,128)(2,1)S(1)}, u32[]{:S(2)}, u32[]{:S(2)}) collective-permute-start(bf16[1,256,256]{2,1,0:T(8,128)(2,1)S(1)} %get-tuple-element.47), channel_id=1, source_target_pairs={{0,16},{16,0},{32,48},{48,32},{64,80},{80,64},{96,112},{112,96},{1... | collective-permute-start | bytes 393224 | tf_op jit(solution)/shard_map/ppermute | solution.py:32
  77.0 5.5 %collective-permute-start.11 = (bf16[1,256,256]{2,1,0:T(8,128)(2,1)S(1)}, bf16[1,256,256]{2,1,0:T(8,128)(2,1)S(1)}, u32[]{:S(2)}, u32[]{:S(2)}) collective-permute-start(bf16[1,256,256]{2,1,0:T(8,128)(2,1)S(1)} %get-tuple-element.48), channel_id=1, source_target_pairs={{0,16},{16,0},{32,48},{48,32},{64,80},{80,64},{96,112},{112,96},{1... | collective-permute-start | bytes 393224 | tf_op jit(solution)/shard_map/ppermute | solution.py:32
  82.4 1.4 %copy-start.10 = (bf16[16,16,512]{2,1,0:T(8,128)(2,1)}, bf16[16,16,512]{2,1,0:T(8,128)(2,1)S(1)}, u32[]{:S(2)}) copy-start(bf16[16,16,512]{2,1,0:T(8,128)(2,1)S(1)} %all-to-all-done.1) | copy-start | bytes 786436
  82.4 1.4 %copy-start.16 = (bf16[1,256,256]{2,1,0:T(8,128)(2,1)}, bf16[1,256,256]{2,1,0:T(8,128)(2,1)S(1)}, u32[]{:S(2)}) copy-start(bf16[1,256,256]{2,1,0:T(8,128)(2,1)S(1)} %collective-permute-done.14.refs_14_) | copy-start | bytes 393220
  82.4 0.7 copy-start.17
  82.5 0.7 copy-start.18
  83.2 0.7 copy-start.19
  83.9 28.7 %copy-start.6 = (f32[4,1024,128]{2,1,0:T(8,128)S(1)}, f32[4,1024,128]{2,1,0:T(8,128)}, u32[]{:S(2)}) copy-start(f32[4,1024,128]{2,1,0:T(8,128)} %get-tuple-element.36.spec_ref) | copy-start | bytes 6291460
  90.8 21.8 %copy-start.1 = (bf16[768,256]{1,0:T(8,128)(2,1)S(1)}, bf16[768,256]{1,0:T(8,128)(2,1)}, u32[]{:S(2)}) copy-start(bf16[768,256]{1,0:T(8,128)(2,1)} %constant.72.clone.refs_2_.back_ref) | copy-start | bytes 1179652
  90.8 21.7 %copy-start.2 = (bf16[768,256]{1,0:T(8,128)(2,1)S(1)}, bf16[768,256]{1,0:T(8,128)(2,1)}, u32[]{:S(2)}) copy-start(bf16[768,256]{1,0:T(8,128)(2,1)} %constant.71.clone.refs_1_.second_ref) | copy-start | bytes 1179652
  90.8 21.7 %copy-start.3 = (f32[2,64,128]{2,1,0:T(8,128)S(1)}, f32[2,64,128]{2,1,0:T(8,128)}, u32[]{:S(2)}) copy-start(f32[2,64,128]{2,1,0:T(8,128)} %constant.74.clone.refs_4_.turn_ref) | copy-start | bytes 196612
  90.8 21.7 %copy-start.4 = (bf16[64,384]{1,0:T(8,128)(2,1)S(1)}, bf16[64,384]{1,0:T(8,128)(2,1)}, u32[]{:S(2)}) copy-start(bf16[64,384]{1,0:T(8,128)(2,1)} %constant.73.clone.refs_3_.last_ref) | copy-start | bytes 147460
  90.8 21.7 %copy-start.5 = (bf16[128,128]{1,0:T(8,128)(2,1)S(1)}, bf16[128,128]{1,0:T(8,128)(2,1)}, u32[]{:S(2)}) copy-start(bf16[128,128]{1,0:T(8,128)(2,1)} %constant.70.clone.refs_0_.first_ref) | copy-start | bytes 98308
  90.8 11.7 %collective-permute-start.15 = (bf16[8,256,256]{2,1,0:T(8,128)(2,1)}, bf16[8,256,256]{2,1,0:T(8,128)(2,1)}, u32[]{:S(2)}, u32[]{:S(2)}) collective-permute-start(bf16[8,256,256]{2,1,0:T(8,128)(2,1)} %get-tuple-element.39), channel_id=1, source_target_pairs={{0,16},{16,0},{32,48},{48,32},{64,80},{80,64},{96,112},{112,96},{1... | collective-permute-start | bytes 3145736 | tf_op jit(solution)/shard_map/ppermute | solution.py:32
  90.9 21.6 %all-to-all-start.2 = ((bf16[16,16,512]{2,1,0:T(8,128)(2,1)}), bf16[16,16,512]{2,1,0:T(8,128)(2,1)S(1)}, u32[]{:S(2)}, u32[]{:S(2)}) async-start(bf16[16,16,512]{2,1,0:T(8,128)(2,1)} %bitcast.24), calls=%async_computation.2 | async-start | bytes 524288 | tf_op jit(solution)/shard_map/all_to_all | solution.py:364
  104.9 17.4 %collective-permute-start.16 = (bf16[2,256,256]{2,1,0:T(8,128)(2,1)}, bf16[2,256,256]{2,1,0:T(8,128)(2,1)}, u32[]{:S(2)}, u32[]{:S(2)}) collective-permute-start(bf16[2,256,256]{2,1,0:T(8,128)(2,1)} %get-tuple-element.40), channel_id=1, source_target_pairs={{0,64},{16,80},{32,96},{48,112},{64,128},{80,144},{96,160},{112,17... | collective-permute-start | bytes 786440 | tf_op jit(solution)/shard_map/ppermute | solution.py:32
  106.1 16.2 %collective-permute-start.18 = (bf16[2,256,256]{2,1,0:T(8,128)(2,1)}, bf16[2,256,256]{2,1,0:T(8,128)(2,1)}, u32[]{:S(2)}, u32[]{:S(2)}) collective-permute-start(bf16[2,256,256]{2,1,0:T(8,128)(2,1)} %get-tuple-element.41), channel_id=1, source_target_pairs={{0,192},{16,208},{32,224},{48,240},{64,0},{80,16},{96,32},{112,48}... | collective-permute-start | bytes 786440 | tf_op jit(solution)/shard_map/ppermute | solution.py:32
  106.3 16.0 %collective-permute-start.17 = (bf16[2,256,256]{2,1,0:T(8,128)(2,1)S(1)}, bf16[2,256,256]{2,1,0:T(8,128)(2,1)}, u32[]{:S(2)}, u32[]{:S(2)}) collective-permute-start(bf16[2,256,256]{2,1,0:T(8,128)(2,1)S(1)} %get-tuple-element.42), channel_id=1, source_target_pairs={{0,128},{16,144},{32,160},{48,176},{64,192},{80,208},{96,224},{112... | collective-permute-start | bytes 786440 | tf_op jit(solution)/shard_map/ppermute | solution.py:32
  116.5 21.0 %all-to-all-start.3 = ((bf16[16,32,512]{2,1,0:T(8,128)(2,1)}), bf16[16,32,512]{2,1,0:T(8,128)(2,1)S(1)}, u32[]{:S(2)}, u32[]{:S(2)}) async-start(bf16[16,32,512]{2,1,0:T(8,128)(2,1)} %grads.1), calls=%async_computation.3 | async-start | bytes 1048576 | tf_op jit(solution)/shard_map/all_to_all | solution.py:364
  123.8 13.0 %collective-permute-start.19 = (bf16[256,256]{1,0:T(8,128)(2,1)S(1)}, bf16[256,256]{1,0:T(8,128)(2,1)S(1)}, u32[]{:S(2)}, u32[]{:S(2)}) collective-permute-start(bf16[256,256]{1,0:T(8,128)(2,1)S(1)} %slice_bitcast_fusion), channel_id=1, source_target_pairs={{0,32},{16,48},{32,0},{48,16},{64,96},{80,112},{96,64},{112,80},{1... | collective-permute-start | bytes 393224 | tf_op jit(solution)/shard_map/ppermute | solution.py:32
